TPU v7x, 32 devices: a whole 2x2x4 slice. The times are simulated.
32 devices in a mesh: dp: 8 (over y, x, core), tensor: 4 (over z).
Axes of the slice: x: 2, y: 2, z: 4, core: 2. Of those that a mesh axis runs over, the one named last changes fastest.
Arguments:
- block_input: float32 [8192, 1536], P(('dp', 'tensor')), may hold values from -17 to 17
- positions: int32 [8192], P('dp'), may hold values from 0 to 2047, as said below
- attn_gain: float32 [1536], replicated, may hold values from 0.5 to 1.5
- w_query: bfloat16 [1536, 1536], P(None, 'tensor'), may hold values from -0.102062073 to 0.102062073
- key_weight: bfloat16 [1536, 768], P(None, 'tensor'), may hold values from -3.0873777 to 3.0873777
- value_weight: bfloat16 [1536, 768], P(None, 'tensor'), may hold values from -0.15625 to 0.15625
- w_out: bfloat16 [1536, 1536], P('tensor'), may hold values from -1.25 to 1.25
- mlp_gain: float32 [1536], replicated, may hold values from 0.5 to 1.5
- w_gate: bfloat16 [1536, 4096], P(None, 'tensor'), may hold values from -0.15625 to 0.15625
- w_up: bfloat16 [1536, 4096], P(None, 'tensor'), may hold values from -0.15625 to 0.15625
- w_down: bfloat16 [4096, 1536], P('tensor'), may hold values from -0.09375 to 0.09375
- out_grad: float32 [8192, 1536], P(('dp', 'tensor')), may hold values from -30 to 30
Outputs:
- block_output: float32 [8192, 1536], P(('dp', 'tensor'))
- input_grad: float32 [8192, 1536], P(('dp', 'tensor'))
- grad_query: float32 [1536, 1536], P(None, 'tensor')
- grad_key: float32 [1536, 768], P(None, 'tensor')
- grad_value: float32 [1536, 768], P(None, 'tensor')
- grad_out: float32 [1536, 1536], P('tensor')
- grad_gate: float32 [1536, 4096], P(None, 'tensor')
- grad_up: float32 [1536, 4096], P(None, 'tensor')
- grad_down: float32 [4096, 1536], P('tensor')
- grad_attn_gain: float32 [1536], replicated
- grad_mlp_gain: float32 [1536], replicated
Inputs may be any that keep to these rules, and one draw needn't show every extreme that they name: positions[t] is t minus the index of the first token of t's document, so each document starts at 0; documents hold 1 to 2048 tokens and one of them exactly 2048.
All inputs are finite; a program needn't handle non-finite values.
Results may differ from a plain program's by a relative error of at most 0.014.
The roundings to bfloat16 on the way count: a program that leaves them out, or rounds other values in their place, can miss the bound.
Values may be sent and summed in bfloat16 or wider, within the bound.
No kernel may reach another device: no remote copies, remote signals or barrier semaphores. Data moves between devices by JAX's collectives and lax.ppermute only.
A program may use at most 192 MiB of HBM per device.

v0:
```python
import jax
import jax.numpy as jnp
from jax import lax
from jax.sharding import PartitionSpec as P

QUERY_HEADS = 16
KEY_VALUE_HEADS = 8
HEAD_SIZE = 96
LONGEST_DOCUMENT = 2048


epsilon = 1e-05
rope_base = 100000.0


def from_behind(value, axis, steps):
    count = lax.axis_size(axis)
    leading, last = (max(0, -steps), min(count, count - steps))
    return lax.ppermute(value, axis, [(source, source + steps) for source in range(leading, last)])


def rope_tables(positions):
    half_size = HEAD_SIZE // 2
    frequency = rope_base ** (-jnp.arange(half_size, dtype=jnp.float32) * 2.0 / HEAD_SIZE)
    angles = positions.astype(jnp.float32)[:, None] * frequency[None, :]
    return (jnp.cos(angles), jnp.sin(angles))


def apply_rotation(values, cosine_table, sine_table):
    half_size = HEAD_SIZE // 2
    first_half = values[..., :half_size]
    second_half = values[..., half_size:]
    cos_rows = cosine_table[:, None, :]
    sin_rows = sine_table[:, None, :]
    return jnp.concatenate(
        [
            first_half * cos_rows - second_half * sin_rows,
            second_half * cos_rows + first_half * sin_rows,
        ],
        axis=-1,
    )


def rotation_backward(grads, cosine_table, sine_table):
    half_size = HEAD_SIZE // 2
    first_half = grads[..., :half_size]
    second_half = grads[..., half_size:]
    cos_rows = cosine_table[:, None, :]
    sin_rows = sine_table[:, None, :]
    return jnp.concatenate(
        [
            first_half * cos_rows + second_half * sin_rows,
            second_half * cos_rows - first_half * sin_rows,
        ],
        axis=-1,
    )


def normalize(rows, gain):
    inv_rms = lax.rsqrt(jnp.mean(rows * rows, axis=-1, keepdims=True) + epsilon)
    return ((rows * inv_rms * gain).astype(jnp.bfloat16), inv_rms)


def normalize_back(rows, inv_rms, gain, normed_grad):
    weighted = normed_grad * gain
    inner = jnp.mean(weighted * rows, axis=-1, keepdims=True)
    rows_grad = inv_rms * weighted - rows * inv_rms**3 * inner
    gain_grad = jnp.sum(normed_grad * rows * inv_rms, axis=0)
    return (rows_grad, gain_grad)


def masked_scores(query_block, tile_keys, index_block, start_block, tile_index):
    score_scale = HEAD_SIZE ** (-0.5)
    scores = (
        jnp.einsum("igrd,jgd->grij", query_block, tile_keys, preferred_element_type=jnp.float32)
        * score_scale
    )
    allowed = (tile_index[None, :] <= index_block[:, None]) & (
        tile_index[None, :] >= start_block[:, None]
    )
    return jnp.where(allowed[None, None], scores, -1e30)


def per_device(
    block_input,
    positions,
    attn_gain,
    w_query,
    key_weight,
    value_weight,
    w_out,
    mlp_gain,
    w_gate,
    w_up,
    w_down,
    out_grad,
):
    stretch = positions.shape[0]
    reach = LONGEST_DOCUMENT // stretch
    tiles = reach + 1
    span = tiles * stretch
    query_group = QUERY_HEADS // KEY_VALUE_HEADS
    query_width = w_query.shape[1]
    kv_width = key_weight.shape[1]
    kv_heads = kv_width // HEAD_SIZE
    block_rows = min(512, stretch)
    blocks = stretch // block_rows
    score_scale = HEAD_SIZE ** (-0.5)
    base_index = lax.axis_index("dp") * stretch
    query_index = base_index + jnp.arange(stretch, dtype=jnp.int32)
    key_index = base_index - reach * stretch + jnp.arange(span, dtype=jnp.int32)
    doc_starts = query_index - positions
    cosine_table, sine_table = rope_tables(positions)
    normed_own, inv_rms_attn = normalize(block_input, attn_gain)
    attention_normed = lax.all_gather(normed_own, "tensor", axis=0, tiled=True)
    w_joined = jnp.concatenate([w_query, key_weight, value_weight], axis=1)
    projected = jnp.dot(attention_normed, w_joined, preferred_element_type=jnp.float32)
    query_rows = apply_rotation(
        projected[:, :query_width].reshape(stretch, -1, HEAD_SIZE), cosine_table, sine_table
    ).astype(jnp.bfloat16)
    keys_local = apply_rotation(
        projected[:, query_width : query_width + kv_width].reshape(stretch, kv_heads, HEAD_SIZE),
        cosine_table,
        sine_table,
    ).astype(jnp.bfloat16)
    values_local = projected[:, query_width + kv_width :].astype(jnp.bfloat16)
    key_value = jnp.concatenate([keys_local.reshape(stretch, kv_width), values_local], axis=1)
    pieces = [from_behind(key_value, "dp", distance) for distance in range(reach, 0, -1)]
    window = jnp.concatenate(pieces + [key_value], axis=0)
    key_tiles = window[:, :kv_width].reshape(tiles, stretch, kv_heads, HEAD_SIZE)
    value_tiles = window[:, kv_width:].reshape(tiles, stretch, kv_heads, HEAD_SIZE)
    index_tiles = key_index.reshape(tiles, stretch)
    query_blocks = query_rows.reshape(blocks, block_rows, kv_heads, query_group, HEAD_SIZE)
    index_blocks = query_index.reshape(blocks, block_rows)
    start_blocks = doc_starts.reshape(blocks, block_rows)

    def forward_block(inputs):
        query_block, index_block, start_block = inputs

        def gather_stats(carry, tile):
            run_max, run_sum = carry
            tile_keys, tile_index = tile
            scores = masked_scores(query_block, tile_keys, index_block, start_block, tile_index)
            new_max = jnp.maximum(run_max, jnp.max(scores, axis=-1, keepdims=True))
            run_sum = run_sum * jnp.exp(run_max - new_max) + jnp.sum(
                jnp.exp(scores - new_max), axis=-1, keepdims=True
            )
            return ((new_max, run_sum), None)

        stat_shape = (kv_heads, query_group, block_rows, 1)
        start_stats = (jnp.full(stat_shape, -1e30, jnp.float32), jnp.zeros(stat_shape, jnp.float32))
        (run_max, run_sum), unused = lax.scan(gather_stats, start_stats, (key_tiles, index_tiles))
        log_total = run_max + jnp.log(run_sum)

        def add_values(total, tile):
            tile_keys, tile_values, tile_index = tile
            scores = masked_scores(query_block, tile_keys, index_block, start_block, tile_index)
            weights = jnp.exp(scores - log_total).astype(jnp.bfloat16)
            return (
                total
                + jnp.einsum(
                    "grij,jgd->igrd", weights, tile_values, preferred_element_type=jnp.float32
                ),
                None,
            )

        mixed_total, unused = lax.scan(
            add_values,
            jnp.zeros((block_rows, kv_heads, query_group, HEAD_SIZE), jnp.float32),
            (key_tiles, value_tiles, index_tiles),
        )
        return (mixed_total.astype(jnp.bfloat16), log_total)

    mixed_blocks, log_blocks = lax.map(forward_block, (query_blocks, index_blocks, start_blocks))
    attended = mixed_blocks.reshape(stretch, query_width)
    rows = attended
    residual = block_input + lax.psum_scatter(
        jnp.dot(rows, w_out, preferred_element_type=jnp.float32),
        "tensor",
        scatter_dimension=0,
        tiled=True,
    )
    mlp_normed_own, inv_rms_mlp = normalize(residual, mlp_gain)
    normed_mlp = lax.all_gather(mlp_normed_own, "tensor", axis=0, tiled=True)
    gate_pre = jnp.dot(normed_mlp, w_gate, preferred_element_type=jnp.float32)
    up_proj = jnp.dot(normed_mlp, w_up, preferred_element_type=jnp.float32)
    sigmoid_gate = jax.nn.sigmoid(gate_pre)
    silu_gate = gate_pre * sigmoid_gate
    hidden = (silu_gate * up_proj).astype(jnp.bfloat16)
    rows = hidden
    block_output = residual + lax.psum_scatter(
        jnp.dot(rows, w_down, preferred_element_type=jnp.float32).astype(jnp.bfloat16),
        "tensor",
        scatter_dimension=0,
        tiled=True,
    ).astype(jnp.float32)
    out_low = lax.all_gather(out_grad.astype(jnp.bfloat16), "tensor", axis=0, tiled=True)
    grad_down = jnp.dot(hidden.T, out_low, preferred_element_type=jnp.float32)
    hidden_grad = jnp.dot(out_low, w_down.T, preferred_element_type=jnp.float32)
    gate_grad = (
        hidden_grad * up_proj * sigmoid_gate * (1.0 + gate_pre * (1.0 - sigmoid_gate))
    ).astype(jnp.bfloat16)
    up_grad = (hidden_grad * silu_gate).astype(jnp.bfloat16)
    grad_gate = jnp.dot(normed_mlp.T, gate_grad, preferred_element_type=jnp.float32)
    grad_up = jnp.dot(normed_mlp.T, up_grad, preferred_element_type=jnp.float32)
    mlp_normed_grad = lax.psum_scatter(
        jnp.dot(gate_grad, w_gate.T, preferred_element_type=jnp.float32)
        + jnp.dot(up_grad, w_up.T, preferred_element_type=jnp.float32),
        "tensor",
        scatter_dimension=0,
        tiled=True,
    )
    residual_part, mlp_gain_grad = normalize_back(residual, inv_rms_mlp, mlp_gain, mlp_normed_grad)
    residual_grad = out_grad + residual_part
    residual_low = lax.all_gather(residual_grad.astype(jnp.bfloat16), "tensor", axis=0, tiled=True)
    grad_out = jnp.dot(attended.T, residual_low, preferred_element_type=jnp.float32)
    attended_gradient = jnp.dot(residual_low, w_out.T, preferred_element_type=jnp.float32).astype(
        jnp.bfloat16
    )
    grad_blocks = attended_gradient.reshape(blocks, block_rows, kv_heads, query_group, HEAD_SIZE)

    def backward_block(carry, inputs):
        key_gradient_total, value_gradient_total = carry
        query_block, index_block, start_block, log_total, mixed_block, grad_block = inputs
        row_inner = jnp.einsum(
            "igrd,igrd->gri", grad_block, mixed_block, preferred_element_type=jnp.float32
        )

        def tile_step(query_total, tile):
            tile_keys, tile_values, tile_index = tile
            scores = masked_scores(query_block, tile_keys, index_block, start_block, tile_index)
            weights = jnp.exp(scores - log_total)
            weights_low = weights.astype(jnp.bfloat16)
            weight_grad = jnp.einsum(
                "igrd,jgd->grij", grad_block, tile_values, preferred_element_type=jnp.float32
            )
            score_grad = (weights * (weight_grad - row_inner[..., None]) * score_scale).astype(
                jnp.bfloat16
            )
            query_total = query_total + jnp.einsum(
                "grij,jgd->igrd", score_grad, tile_keys, preferred_element_type=jnp.float32
            )
            key_part = jnp.einsum(
                "grij,igrd->jgd", score_grad, query_block, preferred_element_type=jnp.float32
            )
            value_part = jnp.einsum(
                "grij,igrd->jgd", weights_low, grad_block, preferred_element_type=jnp.float32
            )
            return (query_total, (key_part, value_part))

        query_grad, (key_parts, value_parts) = lax.scan(
            tile_step,
            jnp.zeros((block_rows, kv_heads, query_group, HEAD_SIZE), jnp.float32),
            (key_tiles, value_tiles, index_tiles),
        )
        key_gradient_total = key_gradient_total + key_parts.reshape(span, kv_heads, HEAD_SIZE)
        value_gradient_total = value_gradient_total + value_parts.reshape(span, kv_heads, HEAD_SIZE)
        return ((key_gradient_total, value_gradient_total), query_grad)

    empty_window = jnp.zeros((span, kv_heads, HEAD_SIZE), jnp.float32)
    (key_gradient_total, value_gradient_total), query_grads = lax.scan(
        backward_block,
        (empty_window, empty_window),
        (query_blocks, index_blocks, start_blocks, log_blocks, mixed_blocks, grad_blocks),
    )
    window_grad = jnp.concatenate(
        [key_gradient_total.reshape(span, kv_width), value_gradient_total.reshape(span, kv_width)],
        axis=1,
    )
    total_grad = window_grad[reach * stretch :]
    for distance in range(1, reach + 1):
        rows_from = (reach - distance) * stretch
        total_grad = total_grad + from_behind(
            window_grad[rows_from : rows_from + stretch], "dp", -distance
        )
    query_grad = rotation_backward(
        query_grads.reshape(stretch, -1, HEAD_SIZE), cosine_table, sine_table
    ).reshape(stretch, query_width)
    key_gradient = rotation_backward(
        total_grad[:, :kv_width].reshape(stretch, kv_heads, HEAD_SIZE), cosine_table, sine_table
    ).reshape(stretch, kv_width)
    projected_grad = jnp.concatenate(
        [query_grad, key_gradient, total_grad[:, kv_width:]], axis=1
    ).astype(jnp.bfloat16)
    grad_joined = jnp.dot(attention_normed.T, projected_grad, preferred_element_type=jnp.float32)
    grad_query = grad_joined[:, :query_width]
    grad_key = grad_joined[:, query_width : query_width + kv_width]
    grad_value = grad_joined[:, query_width + kv_width :]
    rows = projected_grad
    attn_normed_grad = lax.psum_scatter(
        jnp.dot(rows, w_joined.T, preferred_element_type=jnp.float32),
        "tensor",
        scatter_dimension=0,
        tiled=True,
    )
    input_part, attn_gain_grad = normalize_back(
        block_input, inv_rms_attn, attn_gain, attn_normed_grad
    )
    input_grad = residual_grad + input_part
    grad_attn_gain, grad_mlp_gain = lax.psum((attn_gain_grad, mlp_gain_grad), ("dp", "tensor"))
    grad_query, grad_key, grad_value, grad_out, grad_gate, grad_up, grad_down = lax.psum(
        (grad_query, grad_key, grad_value, grad_out, grad_gate, grad_up, grad_down), "dp"
    )
    return (
        block_output,
        input_grad,
        grad_query,
        grad_key,
        grad_value,
        grad_out,
        grad_gate,
        grad_up,
        grad_down,
        grad_attn_gain,
        grad_mlp_gain,
    )


def solution(mesh):
    in_specs = (
        P(("dp", "tensor"), None),
        P("dp"),
        P(),
        P(None, "tensor"),
        P(None, "tensor"),
        P(None, "tensor"),
        P("tensor", None),
        P(),
        P(None, "tensor"),
        P(None, "tensor"),
        P("tensor", None),
        P(("dp", "tensor"), None),
    )
    out_specs = (
        P(("dp", "tensor"), None),
        P(("dp", "tensor"), None),
        P(None, "tensor"),
        P(None, "tensor"),
        P(None, "tensor"),
        P("tensor", None),
        P(None, "tensor"),
        P(None, "tensor"),
        P("tensor", None),
        P(),
        P(),
    )
    return jax.shard_map(
        per_device, mesh=mesh, in_specs=in_specs, out_specs=out_specs, check_vma=False
    )
```

profile of v0, /device:TPU:0, one launch (start us, length us, event | category | flops | bytes accessed | tf_op | source)
XLA Modules:
  0.0 1581.0 jit_solution(6399009617958249321)
XLA Ops:
  17.3 61.0 %all-gather.5.cloned.1.call-done = bf16[1024,1536]{1,0:T(8,128)(2,1)} async-done(((bf16[256,1536]{1,0:T(8,128)(2,1)}), bf16[1024,1536]{1,0:T(8,128)(2,1)}) %all-gather.5.cloned.1.call-update) | async-done | bytes 3145744 | tf_op jit(solution)/shard_map/all_gather | solution.py:115
  78.3 5.4 fusion.67
  103.8 5.8 copy.51
  117.1 6.2 copy.52
  130.5 174.1 %while.72 = (s32[]{:T(128)}, bf16[2,512,2,2,96]{1,4,3,2,0:T(8,128)(2,1)}, f32[2,2,2,512,1]{3,2,1,4,0:T(2,128)}, bf16[2,512,2,2,96]{4,3,2,1,0:T(2,128)(2,1)}, s32...) while((s32[]{:T(128)}, ...), condition=%wide.region_8.9_spmd.clone, body=%wide.region_1.8_spmd.clone.sunk | while | flops 1234785280 | bytes 31464144 | solution.py:174
  134.5 4.8 copy.111
  139.9 41.8 %while.75 = (s32[]{:T(128)}, f32[2,2,512,1]{2,1,0,3:T(2,128)S(1)}, f32[2,2,512,1]{2,1,0,3:T(2,128)S(1)}, s32[3,1024]{1,0:T(4,128)}, s32[512]{0:T(512)}, /*index=...) while((s32[]{:T(128)}, f32[2,2,512,1]{2,1,0,3:T(2,128)S(1)}, ...), condition=%wide.region_5.5_spmd.clone, body=%wide.region_2.4_spmd.clone.sunk | while | flops 418916352 | bytes 21357200 | solution.py:152
  141.8 6.9 fusion.154
  155.8 6.8 fusion.154
  169.7 6.8 fusion.154
  182.4 32.9 %while.76 = (s32[]{:T(128)}, f32[512,2,2,96]{0,3,2,1:T(8,128)}, bf16[3,1024,2,96]{1,3,2,0:T(8,128)(2,1)}, s32[3,1024]{1,0:T(4,128)}, s32[512]{0:T(512)}, /*index...) while((s32[]{:T(128)}, f32[512,2,2,96]{0,3,2,1:T(8,128)}, ...), condition=%wide.region_7.7_spmd.clone, body=%wide.region_6.6_spmd.clone.sunk | while | flops 815661056 | bytes 4874879 | solution.py:167
  187.3 6.0 fusion.159
  198.1 6.2 fusion.159
  209.2 6.2 fusion.159
  221.4 4.8 copy.111
  226.8 41.8 %while.75 = (s32[]{:T(128)}, f32[2,2,512,1]{2,1,0,3:T(2,128)S(1)}, f32[2,2,512,1]{2,1,0,3:T(2,128)S(1)}, s32[3,1024]{1,0:T(4,128)}, s32[512]{0:T(512)}, /*index=...) while((s32[]{:T(128)}, f32[2,2,512,1]{2,1,0,3:T(2,128)S(1)}, ...), condition=%wide.region_5.5_spmd.clone, body=%wide.region_2.4_spmd.clone.sunk | while | flops 418916352 | bytes 21357200 | solution.py:152
  228.7 6.8 fusion.154
  242.6 6.8 fusion.154
  256.6 6.8 fusion.154
  269.3 32.9 %while.76 = (s32[]{:T(128)}, f32[512,2,2,96]{0,3,2,1:T(8,128)}, bf16[3,1024,2,96]{1,3,2,0:T(8,128)(2,1)}, s32[3,1024]{1,0:T(4,128)}, s32[512]{0:T(512)}, /*index...) while((s32[]{:T(128)}, f32[512,2,2,96]{0,3,2,1:T(8,128)}, ...), condition=%wide.region_7.7_spmd.clone, body=%wide.region_6.6_spmd.clone.sunk | while | flops 815661056 | bytes 4874879 | solution.py:167
  274.1 5.9 fusion.159
  284.9 6.2 fusion.159
  296.0 6.2 fusion.159
  312.2 116.4 %reduce-scatter.5.cloned.1.call-done = f32[256,1536]{1,0:T(8,128)} async-done(((f32[1024,1536]{1,0:T(8,128)}), f32[256,1536]{1,0:T(8,128)}) %reduce-scatter.5.cloned.1.call-update) | async-done | bytes 1572880 | tf_op jit(solution)/shard_map/reduce_scatter | solution.py:177
  435.5 61.6 %all-gather.7.cloned.1.call-done = bf16[1024,1536]{1,0:T(8,128)(2,1)} async-done(((bf16[256,1536]{1,0:T(8,128)(2,1)}), bf16[1024,1536]{1,0:T(8,128)(2,1)}) %all-gather.7.cloned.1.call-update) | async-done | bytes 3145744 | tf_op jit(solution)/shard_map/all_gather | solution.py:184
  497.1 8.4 fusion.76
  505.5 4.9 fusion.77
  510.4 50.8 %all-gather.9.cloned.1.call-done = bf16[1024,1536]{1,0:T(8,128)(2,1)} async-done(((bf16[256,1536]{1,0:T(8,128)(2,1)}), bf16[1024,1536]{1,0:T(8,128)(2,1)}) %all-gather.9.cloned.1.call-update) | async-done | bytes 3145744 | tf_op jit(solution)/shard_map/all_gather | solution.py:197
  561.2 9.6 multiply_convert_fusion
  574.3 5.5 convolution_add_fusion
  579.9 6.4 convolution_convert_fusion
  586.3 103.1 %reduce-scatter.9.cloned.1.call-done = f32[256,1536]{1,0:T(8,128)} async-done(((f32[1024,1536]{1,0:T(8,128)}), f32[256,1536]{1,0:T(8,128)}) %reduce-scatter.9.cloned.1.call-update) | async-done | bytes 1572880 | tf_op jit(solution)/shard_map/reduce_scatter | solution.py:206
  691.8 61.3 %reduce-scatter.7.cloned.1.call-done = bf16[256,1536]{1,0:T(8,128)(2,1)} async-done(((bf16[1024,1536]{1,0:T(8,128)(2,1)}), bf16[256,1536]{1,0:T(8,128)(2,1)}) %reduce-scatter.7.cloned.1.call-update) | async-done | bytes 786448 | tf_op jit(solution)/shard_map/reduce_scatter | solution.py:191
  761.3 59.4 %all-gather.11.cloned.1.call-done = bf16[1024,1536]{1,0:T(8,128)(2,1)} async-done(((bf16[256,1536]{1,0:T(8,128)(2,1)}), bf16[1024,1536]{1,0:T(8,128)(2,1)}) %all-gather.11.cloned.1.call-update) | async-done | bytes 3145744 | tf_op jit(solution)/shard_map/all_gather | solution.py:215
  827.5 212.7 %while.74 = (s32[]{:T(128)}, f32[3072,2,96]{2,1,0:T(2,128)}, f32[3072,2,96]{2,1,0:T(2,128)}, f32[2,512,2,2,96]{1,0,4,3,2:T(2,128)}, bf16[2,512,2,2,96]{1,4,3,2,0...) while((s32[]{:T(128)}, f32[3072,2,96]{2,1,0:T(2,128)}, ...), condition=%wide.region_17.18_spmd.clone, body=%wide.region_14.17_spmd.clone.sunk | while | flops 2041453568 | bytes 130652224 | solution.py:261
  837.1 61.1 %while.77 = (s32[]{:T(128)}, f32[512,2,2,96]{0,3,2,1:T(8,128)S(1)}, f32[3,1024,2,96]{1,3,2,0:T(8,128)}, f32[3,1024,2,96]{1,3,2,0:T(8,128)}, bf16[3,1024,2,96]{1,...) while((s32[]{:T(128)}, f32[512,2,2,96]{0,3,2,1:T(8,128)S(1)}, ...), condition=%wide.region_16.16_spmd.clone, body=%wide.region_15.15_spmd.clone.sunk | while | flops 2038300672 | bytes 95594200 | solution.py:251
  850.9 6.6 fusion.152
  859.3 4.6 fusion.149
  871.3 6.6 fusion.152
  879.7 4.6 fusion.149
  891.6 6.6 fusion.152
  898.2 5.5 copy.116
  903.7 5.5 copy.117
  909.2 7.9 bitcast_add_fusion.5
  917.9 15.0 dynamic_update_slice.35
  942.5 61.1 %while.77 = (s32[]{:T(128)}, f32[512,2,2,96]{0,3,2,1:T(8,128)S(1)}, f32[3,1024,2,96]{1,3,2,0:T(8,128)}, f32[3,1024,2,96]{1,3,2,0:T(8,128)}, bf16[3,1024,2,96]{1,...) while((s32[]{:T(128)}, f32[512,2,2,96]{0,3,2,1:T(8,128)S(1)}, ...), condition=%wide.region_16.16_spmd.clone, body=%wide.region_15.15_spmd.clone.sunk | while | flops 2038300672 | bytes 95594200 | solution.py:251
  956.2 6.6 fusion.152
  964.7 4.6 fusion.149
  976.6 6.6 fusion.152
  985.0 4.6 fusion.149
  997.0 6.6 fusion.152
  1003.6 5.5 copy.116
  1009.0 5.5 copy.117
  1014.5 9.9 bitcast_add_fusion.5
  1025.2 15.0 dynamic_update_slice.35
  1040.2 5.6 copy.62
  1060.8 48.8 %collective-permute-done.3 = f32[1024,384]{0,1:T(8,128)} collective-permute-done((f32[1024,384]{0,1:T(8,128)}, f32[1024,384]{0,1:T(8,128)}, u32[]{:S(2)}, u32[]{:S(2)}) %collective-permute-start.3) | collective-permute-done | bytes 1572896 | tf_op jit(solution)/shard_map/ppermute | solution.py:19
  1113.9 5.7 fusion.66
  1119.7 8.9 fusion.80
  1128.6 5.7 fusion.81
  1134.2 5.6 fusion.82
  1148.5 80.7 %reduce-scatter.11.cloned.1.call-done = f32[256,1536]{1,0:T(8,128)} async-done(((f32[1024,1536]{1,0:T(8,128)}), f32[256,1536]{1,0:T(8,128)}) %reduce-scatter.11.cloned.1.call-update) | async-done | bytes 1572880 | tf_op jit(solution)/shard_map/reduce_scatter | solution.py:290
  1231.1 41.7 %all-reduce = (f32[1536]{0:T(1024)}, f32[1536]{0:T(1024)}) all-reduce(f32[1536]{0:T(1024)S(1)} %get-tuple-element.578, f32[1536]{0:T(1024)S(1)} %copy-done.39), channel_id=1, replica_groups=mesh['dp'=8,'tensor'=4] {'dp','tensor'}, use_global_device_ids=true, to_apply=%region_28.29 | all-reduce | flops 3072 | bytes 24576 | tf_op jit(solution)/shard_map/psum | solution.py:300
  1275.8 276.3 %all-reduce.4.cloned.1.call-done = (f32[1536,384]{0,1:T(8,128)}, f32[1536,192]{0,1:T(8,128)}, f32[1536,192]{0,1:T(8,128)}, f32[384,1536]{1,0:T(8,128)}, f32[1536...) async-done(((f32[1536,384]{0,1:T(8,128)}, f32[1536,192]{0,1:T(8,128)}, f32[1536,192]{0,1:T(8,128)}, f32[384,1536]{1,0:T(8,128)}, f32[1536,1024]{1,0:T(8,128)}, ...) | async-done | bytes 25952272 | tf_op jit(solution)/shard_map/psum | solution.py:301
  (395 shorter events, 305.5 us)
Async XLA Ops:
  7.2 554.0 %copy-start = (bf16[1024,1536]{1,0:T(8,128)(2,1)S(1)}, bf16[1024,1536]{1,0:T(8,128)(2,1)}, u32[]{:S(2)}) copy-start(bf16[1024,1536]{1,0:T(8,128)(2,1)} %param.32) | copy-start | bytes 9437188
  7.2 71.1 %all-gather.5.cloned.1.call-start = ((), (), s32[]{:S(2)}) async-start(), calls=%async_computation.4 | async-start | bytes 3932160 | tf_op jit(solution)/shard_map/all_gather | solution.py:115
  12.0 416.6 %reduce-scatter.5.cloned.1.call-start = ((), (), s32[]{:S(2)}) async-start(), calls=%async_computation.5 | async-start | bytes 7864320 | tf_op jit(solution)/shard_map/reduce_scatter | solution.py:177
  17.3 75.8 %copy-start.16 = (f32[1024,48]{0,1:T(8,128)}, f32[1024,48]{0,1:T(8,128)S(1)}, u32[]{:S(2)}) copy-start(f32[1024,48]{0,1:T(8,128)S(1)} %get-tuple-element.725) | copy-start | bytes 589828
  17.3 75.8 %copy-start.18 = (f32[1024,48]{0,1:T(8,128)}, f32[1024,48]{0,1:T(8,128)S(1)}, u32[]{:S(2)}) copy-start(f32[1024,48]{0,1:T(8,128)S(1)} %get-tuple-element.726) | copy-start | bytes 589828
  86.4 23.1 %collective-permute-start = (bf16[1024,384]{0,1:T(8,128)(2,1)}, bf16[1024,384]{0,1:T(8,128)(2,1)}, u32[]{:S(2)}, u32[]{:S(2)}) collective-permute-start(bf16[1024,384]{0,1:T(8,128)(2,1)} %pad_maximum_fusion.3), channel_id=1, source_target_pairs={{0,8},{4,12},{8,16},{12,20},{16,24},{20,28},{1,9},{5,13},{9,17},{1... | collective-permute-start | bytes 2359304 | tf_op jit(solution)/shard_map/ppermute | solution.py:19
  90.7 18.8 %collective-permute-start.1 = (bf16[1024,384]{0,1:T(8,128)(2,1)}, bf16[1024,384]{0,1:T(8,128)(2,1)}, u32[]{:S(2)}, u32[]{:S(2)}) collective-permute-start(bf16[1024,384]{0,1:T(8,128)(2,1)} %pad_maximum_fusion.3), channel_id=1, source_target_pairs={{0,4},{4,8},{8,12},{12,16},{16,20},{20,24},{24,28},{1,5},{5,9},{9,... | collective-permute-start | bytes 2359304 | tf_op jit(solution)/shard_map/ppermute | solution.py:19
  95.6 13.9 copy-start.21
  141.8 6.9 copy-start.4
  155.8 6.9 copy-start.4
  169.7 6.9 copy-start.4
  182.4 34.9 %copy-start.34 = (s32[2,512]{1,0:T(2,128)S(1)}, s32[2,512]{1,0:T(2,128)}, u32[]{:S(2)}) copy-start(s32[2,512]{1,0:T(2,128)} %copy-done.33) | copy-start | bytes 12292 | tf_op jit(solution)/shard_map/while
  182.4 34.9 %copy-start.36 = (s32[2,512]{1,0:T(2,128)S(1)}, s32[2,512]{1,0:T(2,128)}, u32[]{:S(2)}) copy-start(s32[2,512]{1,0:T(2,128)} %copy-done.35) | copy-start | bytes 12292 | tf_op jit(solution)/shard_map/while
  228.7 6.9 copy-start.4
  242.6 6.9 copy-start.4
  256.6 6.9 copy-start.4
  269.3 34.9 %copy-start.34 = (s32[2,512]{1,0:T(2,128)S(1)}, s32[2,512]{1,0:T(2,128)}, u32[]{:S(2)}) copy-start(s32[2,512]{1,0:T(2,128)} %copy-done.33) | copy-start | bytes 12292 | tf_op jit(solution)/shard_map/while
  269.3 34.9 %copy-start.36 = (s32[2,512]{1,0:T(2,128)S(1)}, s32[2,512]{1,0:T(2,128)}, u32[]{:S(2)}) copy-start(s32[2,512]{1,0:T(2,128)} %copy-done.35) | copy-start | bytes 12292 | tf_op jit(solution)/shard_map/while
  312.2 119.7 %copy-start.37 = (f32[1536]{0:T(1024)S(1)}, f32[1536]{0:T(1024)}, u32[]{:S(2)}) copy-start(f32[1536]{0:T(1024)} %param.29) | copy-start | bytes 18436
  312.2 184.9 %all-gather.7.cloned.1.call-start = ((), (), s32[]{:S(2)}) async-start(), calls=%async_computation.6 | async-start | bytes 3932160 | tf_op jit(solution)/shard_map/all_gather | solution.py:184
  433.0 128.2 %all-gather.9.cloned.1.call-start = ((), (), s32[]{:S(2)}) async-start(), calls=%async_computation.8 | async-start | bytes 3932160 | tf_op jit(solution)/shard_map/all_gather | solution.py:197
  435.4 254.0 %reduce-scatter.9.cloned.1.call-start = ((), (), s32[]{:S(2)}) async-start(), calls=%async_computation.9 | async-start | bytes 7864320 | tf_op jit(solution)/shard_map/reduce_scatter | solution.py:206
  497.1 8.4 copy-start.45
  497.1 8.4 copy-start.48
  561.2 9.6 copy-start.44
  579.8 173.3 %reduce-scatter.7.cloned.1.call-start = ((), (), s32[]{:S(2)}) async-start(), calls=%async_computation.7 | async-start | bytes 3932160 | tf_op jit(solution)/shard_map/reduce_scatter | solution.py:191
  586.2 103.2 %copy-start.9 = (f32[256,1536]{1,0:T(8,128)S(1)}, f32[256,1536]{1,0:T(8,128)}, u32[]{:S(2)}) copy-start(f32[256,1536]{1,0:T(8,128)} %copy-done.8) | copy-start | bytes 4718596
  586.3 166.8 %copy-start.13 = (f32[256,1536]{1,0:T(8,128)S(1)}, f32[256,1536]{1,0:T(8,128)}, u32[]{:S(2)}) copy-start(f32[256,1536]{1,0:T(8,128)} %param.33) | copy-start | bytes 4718596
  586.3 234.4 %all-gather.11.cloned.1.call-start = ((), (), s32[]{:S(2)}) async-start(), calls=%async_computation.10 | async-start | bytes 3932160 | tf_op jit(solution)/shard_map/all_gather | solution.py:215
  757.1 63.5 %copy-start.28 = (bf16[384,1536]{1,0:T(8,128)(2,1)S(1)}, bf16[384,1536]{1,0:T(8,128)(2,1)}, u32[]{:S(2)}) copy-start(bf16[384,1536]{1,0:T(8,128)(2,1)} %param.28) | copy-start | bytes 3538948
  757.1 472.1 %reduce-scatter.11.cloned.1.call-start = ((), (), s32[]{:S(2)}) async-start(), calls=%async_computation.11 | async-start | bytes 7864320 | tf_op jit(solution)/shard_map/reduce_scatter | solution.py:290
  831.6 5.5 copy-start.11
  838.4 5.1 copy-start.3
  858.8 5.1 copy-start.3
  879.2 5.1 copy-start.3
  936.9 5.5 copy-start.11
  943.8 5.1 copy-start.3
  964.1 5.1 copy-start.3
  984.5 5.1 copy-start.3
  1040.2 5.6 copy-start.5
  1049.7 6.8 copy-start.26
  1053.7 5.2 copy-start.17
  1053.7 5.2 copy-start.19
  1053.7 7.1 collective-permute-start.2
  1055.1 54.5 %collective-permute-start.3 = (f32[1024,384]{0,1:T(8,128)}, f32[1024,384]{0,1:T(8,128)}, u32[]{:S(2)}, u32[]{:S(2)}) collective-permute-start(f32[1024,384]{0,1:T(8,128)} %get-tuple-element.713), channel_id=1, source_target_pairs={{8,0},{12,4},{16,8},{20,12},{24,16},{28,20},{9,1},{13,5},{17,9},{2... | collective-permute-start | bytes 4718600 | tf_op jit(solution)/shard_map/ppermute | solution.py:19
  1058.9 50.7 %copy-start.10 = (f32[3072,2,96]{0,2,1:T(8,128)S(1)}, f32[3072,2,96]{0,2,1:T(8,128)}, u32[]{:S(2)}) copy-start(f32[3072,2,96]{0,2,1:T(8,128)} %copy.62) | copy-start | bytes 7077892
  1060.8 51.7 %copy-start.29 = (bf16[1024,4,96]{0,2,1:T(8,128)(2,1)}, bf16[1024,4,96]{0,2,1:T(8,128)(2,1)S(1)}, u32[]{:S(2)}) copy-start(bf16[1024,4,96]{0,2,1:T(8,128)(2,1)S(1)} %pad_maximum_fusion.4) | copy-start | bytes 2359300
  1119.6 8.9 copy-start.55
  1119.6 432.4 %all-reduce.4.cloned.1.call-start = ((), (), s32[]{:S(2)}) async-start(), calls=%async_computation.12 | async-start | bytes 51904512 | tf_op jit(solution)/shard_map/psum | solution.py:301
  1119.7 8.9 copy-start.49
  1128.6 5.7 copy-start.50
  1128.6 5.7 copy-start.53
  1134.2 5.6 copy-start.24
  1134.2 5.6 copy-start.51
  1148.4 80.8 %copy-start.7 = (f32[256,1536]{1,0:T(8,128)S(1)}, f32[256,1536]{1,0:T(8,128)}, u32[]{:S(2)}) copy-start(f32[256,1536]{1,0:T(8,128)} %param.22) | copy-start | bytes 4718596
  1148.4 80.8 %copy-start.38 = (f32[1536]{0:T(1024)S(1)}, f32[1536]{0:T(1024)}, u32[]{:S(2)}) copy-start(f32[1536]{0:T(1024)} %param.24) | copy-start | bytes 18436
  1148.4 80.8 %copy-start.41 = (f32[256]{0:T(256)S(1)}, f32[256]{0:T(256)}, u32[]{:S(2)}) copy-start(f32[256]{0:T(256)} %copy-done.40) | copy-start | bytes 3076
  1148.5 82.6 %copy-start.39 = (f32[1536]{0:T(1024)S(1)}, f32[1536]{0:T(1024)}, u32[]{:S(2)}) copy-start(f32[1536]{0:T(1024)} %get-tuple-element.576) | copy-start | bytes 18436
  1148.5 124.3 %copy-start.14 = (f32[256,1536]{1,0:T(8,128)S(1)}, f32[256,1536]{1,0:T(8,128)}, u32[]{:S(2)}) copy-start(f32[256,1536]{1,0:T(8,128)} %get-tuple-element.696) | copy-start | bytes 4718596
  1148.5 124.3 %copy-start.42 = (f32[256]{0:T(256)S(1)}, f32[256]{0:T(256)}, u32[]{:S(2)}) copy-start(f32[256]{0:T(256)} %get-tuple-element.729) | copy-start | bytes 3076
  1555.1 5.0 copy-start.25
  1560.1 5.1 slice-start.2
  1561.5 4.6 slice-start.3
  1561.5 7.6 slice-start
  (31 other events, 65.7 us)
Sparse Core Ops, SparseCore 0:
  12.1 66.1 all-gather.4
  312.3 116.2 reduce-scatter.4
  433.1 63.9 all-gather.6
  499.1 62.0 all-gather.8
  579.9 109.4 reduce-scatter.8
  692.1 60.8 reduce-scatter.6
  757.3 63.3 all-gather.10
  1119.7 109.4 reduce-scatter.10
  1235.0 316.9 all-reduce.3
where the time goes:
time: 1590 us; the launch traced here: 1580 us
  waiting for transfers between devices  919 us (58%)
  matrix products  268 us (17%)
  local copies, waits for them, and re-layouts  207 us (13%)
  other arithmetic  119 us (7%)
  blocking collectives  41.7 us (3%)
    psum x1, waiting for transfers between devices, per_device(): lax.psum((grad_query, grad_key, grad_value, grad_out, grad_gate, grad_up,...  276 us
    reduce_scatter x1, waiting for transfers between devices, per_device(): lax.psum_scatter(jnp.dot(rows, w_out, preferred_element_type=jnp.float32)...  116 us
    reduce_scatter x1, waiting for transfers between devices, per_device(): lax.psum_scatter(jnp.dot(gate_grad, w_gate.T, preferred_element_type=jnp....  103 us
    reduce_scatter x1, waiting for transfers between devices, per_device(): lax.psum_scatter(jnp.dot(rows, w_joined.T, preferred_element_type=jnp.flo...  80.7 us
    all_gather x1, waiting for transfers between devices, per_device(): normed_mlp = lax.all_gather(mlp_normed_own, 'tensor', axis=0, tiled=True)  61.6 us
    reduce_scatter x1, waiting for transfers between devices, per_device(): lax.psum_scatter(jnp.dot(rows, w_down, preferred_element_type=jnp.float32...  61.3 us
    all_gather x1, waiting for transfers between devices, per_device(): attention_normed = lax.all_gather(normed_own, 'tensor', axis=0, tiled=True)  61 us
    all_gather x1, waiting for transfers between devices, per_device(): lax.all_gather(residual_grad.astype(jnp.bfloat16), 'tensor', axis=0, tile...  59.4 us
  transfers between devices with their start and end apart: 13, of which 10 were waited for; matrix products, arithmetic and copies ran while one was open for 5% of the time, Pallas kernels for 0%

commit v1 on v0

v1 whole, which is shorter than its diff:
```python
import functools
import math

import jax
import jax.numpy as jnp
from jax import lax
from jax.experimental import pallas as pl
from jax.experimental.pallas import tpu as pltpu
from jax.sharding import PartitionSpec as P

QUERY_HEADS = 16
KEY_VALUE_HEADS = 8
HEAD_SIZE = 96
LONGEST_DOCUMENT = 2048

LANES = 128
HALF_LANES = LANES // 2
FAR = -1e30

epsilon = 1e-05
rope_base = 100000.0

f32 = jnp.float32
bf16 = jnp.bfloat16


def from_behind(value, axis, steps):
    count = lax.axis_size(axis)
    leading, last = (max(0, -steps), min(count, count - steps))
    return lax.ppermute(value, axis, [(source, source + steps) for source in range(leading, last)])


def exchange(value, axis, distance):
    count = lax.axis_size(axis)
    return lax.ppermute(value, axis, [(i, i ^ distance) for i in range(count)])


def rope_tables(positions):
    half_size = HEAD_SIZE // 2
    frequency = rope_base ** (-jnp.arange(half_size, dtype=f32) * 2.0 / HEAD_SIZE)
    rest = jnp.zeros((HALF_LANES - half_size,), f32)
    spread = jnp.concatenate([frequency, rest, frequency, rest])
    sign = jnp.where(jnp.arange(LANES) < HALF_LANES, -1.0, 1.0).astype(f32)
    angles = positions.astype(f32)[:, None] * spread[None, :]
    return (jnp.cos(angles), jnp.sin(angles) * sign[None, :])


def spread_matrix(heads, dtype=bf16):
    half_size = HEAD_SIZE // 2
    rows = jnp.arange(heads * HEAD_SIZE, dtype=jnp.int32)
    inner = rows % HEAD_SIZE
    lane = (rows // HEAD_SIZE) * LANES + jnp.where(
        inner < half_size, inner, inner - half_size + HALF_LANES
    )
    columns = jnp.arange(heads * LANES, dtype=jnp.int32)
    return (lane[:, None] == columns[None, :]).astype(dtype)


def normalize(rows, gain):
    inv_rms = lax.rsqrt(jnp.mean(rows * rows, axis=-1, keepdims=True) + epsilon)
    return ((rows * inv_rms * gain).astype(bf16), inv_rms)


def normalize_back(rows, inv_rms, gain, normed_grad):
    weighted = normed_grad * gain
    inner = jnp.mean(weighted * rows, axis=-1, keepdims=True)
    return inv_rms * weighted - rows * inv_rms**3 * inner


def turn(value, cosine, sine):
    return value * cosine + pltpu.roll(value, HALF_LANES, 1) * sine


def turn_back(value, cosine, sine):
    return value * cosine - pltpu.roll(value, HALF_LANES, 1) * sine


def project_kernel(rotated, rows_ref, weight_ref, cosine_ref, sine_ref, out_ref):
    product = jnp.dot(rows_ref[...], weight_ref[...], preferred_element_type=f32)
    cosine = cosine_ref[...]
    sine = sine_ref[...]
    for head in range(out_ref.shape[1] // LANES):
        part = product[:, head * LANES : (head + 1) * LANES]
        if head < rotated:
            part = turn(part, cosine, sine)
        out_ref[:, head * LANES : (head + 1) * LANES] = part.astype(bf16)


def project(rows, weight, cosine, sine, rotated, block):
    count, depth = rows.shape
    width = weight.shape[1]
    return pl.pallas_call(
        functools.partial(project_kernel, rotated),
        grid=(count // block,),
        in_specs=[
            pl.BlockSpec((block, depth), lambda i: (i, 0)),
            pl.BlockSpec((depth, width), lambda i: (0, 0)),
            pl.BlockSpec((block, LANES), lambda i: (i, 0)),
            pl.BlockSpec((block, LANES), lambda i: (i, 0)),
        ],
        out_specs=pl.BlockSpec((block, width), lambda i: (i, 0)),
        out_shape=jax.ShapeDtypeStruct((count, width), bf16),
        cost_estimate=pl.CostEstimate(
            flops=2 * count * depth * width,
            bytes_accessed=2 * (count * depth + depth * width + count * width),
            transcendentals=0,
        ),
        name="project",
    )(rows, weight, cosine, sine)


def pair_rows(ref, group):
    return jnp.concatenate([ref[:, h * LANES : (h + 1) * LANES] for h in range(group)], axis=0)


def place_row(ref, group):
    row = ref[0]
    return jnp.concatenate([row] * group, axis=1)


def masked(scores, first, last, base):
    index = lax.broadcasted_iota(jnp.int32, scores.shape, 0)
    allowed = (index >= first - base) & (index <= last - base)
    return jnp.where(allowed, scores, FAR)


def bounds(low_ref, query_block, rows, tile_rows, offset):
    high = (offset + (query_block + 1) * rows - 1) // tile_rows + 1
    return low_ref[query_block], high


def attend_kernel(tiles, group, factor, low_ref, query_ref, first_ref, *refs):
    keys = refs[:tiles]
    values = refs[tiles : 2 * tiles]
    out_ref, log_ref, key_window, value_turned, top, total, mixed = refs[2 * tiles :]
    query_block = pl.program_id(1)
    rows = query_ref.shape[0]
    stretch = keys[0].shape[0]
    tile_rows = key_window.shape[1]
    per_tile = stretch // tile_rows

    @pl.when(query_block == 0)
    def _():
        for tile in range(tiles):
            for part in range(per_tile):
                at = pl.ds(part * tile_rows, tile_rows)
                key_window[tile * per_tile + part] = keys[tile][at, :]
                value_turned[tile * per_tile + part] = values[tile][at, :].T

    offset = (tiles - 1) * stretch
    query = pair_rows(query_ref, group)
    first = place_row(first_ref, group)
    lane = lax.broadcasted_iota(jnp.int32, (1, rows), 1)
    last = jnp.concatenate([lane] * group, axis=1) + (offset + query_block * rows)
    top[...] = jnp.full_like(top, FAR)
    total[...] = jnp.zeros_like(total)
    mixed[...] = jnp.zeros_like(mixed)
    low, high = bounds(low_ref, query_block, rows, tile_rows, offset)

    def step(tile, unused):
        scores = lax.dot_general(
            key_window[tile], query, (((1,), (1,)), ((), ())), preferred_element_type=f32
        )
        scores = masked(scores, first, last, tile * tile_rows)
        before = top[...]
        after = jnp.maximum(before, jnp.max(scores, axis=0, keepdims=True))
        weights = jnp.exp2(scores * factor - after * factor)
        fade = jnp.exp2((before - after) * factor)
        top[...] = after
        total[...] = total[...] * fade + jnp.sum(weights, axis=0, keepdims=True)
        mixed[...] = mixed[...] * fade + jnp.dot(
            value_turned[tile], weights.astype(bf16), preferred_element_type=f32
        )
        return unused

    lax.fori_loop(low, high, step, 0)
    result = (mixed[...] / total[...]).T.astype(bf16)
    for head in range(group):
        out_ref[:, head * LANES : (head + 1) * LANES] = result[head * rows : (head + 1) * rows]
    log_ref[0, 0] = top[...] * factor + jnp.log2(total[...])


def window_specs(tiles, stretch, first_column):
    return [
        pl.BlockSpec((stretch, LANES), lambda g, i, *s, c=c: (0, c + g)) for c in first_column
    ]


def attend(queries_joined, windows, firsts, low, kv_heads, group, rows, tile_rows):
    stretch = queries_joined.shape[0]
    tiles = len(windows)
    blocks = stretch // rows
    pairs = group * rows
    window_tiles = tiles * stretch // tile_rows
    factor = HEAD_SIZE ** (-0.5) * math.log2(math.e)
    key_columns = [at for _, at in windows]
    value_columns = [at + kv_heads for _, at in windows]
    arrays = [a for a, _ in windows]
    grid_spec = pltpu.PrefetchScalarGridSpec(
        num_scalar_prefetch=1,
        grid=(kv_heads, blocks),
        in_specs=[
            pl.BlockSpec((rows, group * LANES), lambda g, i, *s: (i, g)),
            pl.BlockSpec((1, 1, rows), lambda g, i, *s: (i, 0, 0)),
        ]
        + window_specs(tiles, stretch, key_columns)
        + window_specs(tiles, stretch, value_columns),
        out_specs=[
            pl.BlockSpec((rows, group * LANES), lambda g, i, *s: (i, g)),
            pl.BlockSpec((1, 1, 1, pairs), lambda g, i, *s: (g, i, 0, 0)),
        ],
        scratch_shapes=[
            pltpu.VMEM((window_tiles, tile_rows, LANES), bf16),
            pltpu.VMEM((window_tiles, LANES, tile_rows), bf16),
            pltpu.VMEM((1, pairs), f32),
            pltpu.VMEM((1, pairs), f32),
            pltpu.VMEM((LANES, pairs), f32),
        ],
    )
    work = stretch * stretch * kv_heads * group
    return pl.pallas_call(
        functools.partial(attend_kernel, tiles, group, factor),
        grid_spec=grid_spec,
        out_shape=[
            jax.ShapeDtypeStruct((stretch, kv_heads * group * LANES), bf16),
            jax.ShapeDtypeStruct((kv_heads, blocks, 1, pairs), f32),
        ],
        cost_estimate=pl.CostEstimate(
            flops=16 * LANES * work, bytes_accessed=8 * stretch * stretch, transcendentals=work
        ),
        name="attend",
    )(low, queries_joined, firsts, *arrays, *arrays)


def attend_back_kernel(tiles, group, factor, scale, low_ref, query_ref, first_ref, *refs):
    mixed_ref, grad_ref, log_ref, cosine_ref, sine_ref = refs[:5]
    keys = refs[5 : 5 + tiles]
    values = refs[5 + tiles : 5 + 2 * tiles]
    (
        query_out,
        key_out,
        value_out,
        key_window,
        value_window,
        key_turned,
        query_total,
    ) = refs[5 + 2 * tiles :]
    query_block = pl.program_id(1)
    rows = query_ref.shape[0]
    stretch = keys[0].shape[0]
    tile_rows = key_window.shape[1]
    per_tile = stretch // tile_rows

    @pl.when(query_block == 0)
    def _():
        key_out[...] = jnp.zeros_like(key_out)
        value_out[...] = jnp.zeros_like(value_out)
        for tile in range(tiles):
            for part in range(per_tile):
                at = pl.ds(part * tile_rows, tile_rows)
                key_window[tile * per_tile + part] = keys[tile][at, :]
                key_turned[tile * per_tile + part] = keys[tile][at, :].T
                value_window[tile * per_tile + part] = values[tile][at, :]

    offset = (tiles - 1) * stretch
    query = pair_rows(query_ref, group)
    grad = pair_rows(grad_ref, group)
    mixed = pair_rows(mixed_ref, group)
    inner = jnp.sum((grad.astype(f32) * mixed.astype(f32)).T, axis=0, keepdims=True)
    log_total = log_ref[0, 0]
    first = place_row(first_ref, group)
    lane = lax.broadcasted_iota(jnp.int32, (1, rows), 1)
    last = jnp.concatenate([lane] * group, axis=1) + (offset + query_block * rows)
    query_total[...] = jnp.zeros_like(query_total)
    low, high = bounds(low_ref, query_block, rows, tile_rows, offset)
    both_last = (((1,), (1,)), ((), ()))

    def step(tile, unused):
        scores = lax.dot_general(key_window[tile], query, both_last, preferred_element_type=f32)
        scores = masked(scores, first, last, tile * tile_rows)
        weights = jnp.exp2(scores * factor - log_total)
        weight_grad = lax.dot_general(
            value_window[tile], grad, both_last, preferred_element_type=f32
        )
        score_grad = (weights * (weight_grad - inner) * scale).astype(bf16)
        at = pl.ds(pl.multiple_of(tile * tile_rows, tile_rows), tile_rows)
        value_out[at, :] += jnp.dot(weights.astype(bf16), grad, preferred_element_type=f32)
        key_out[at, :] += jnp.dot(score_grad, query, preferred_element_type=f32)
        query_total[...] += jnp.dot(key_turned[tile], score_grad, preferred_element_type=f32)
        return unused

    lax.fori_loop(low, high, step, 0)
    result = query_total[...].T
    for head in range(group):
        part = result[head * rows : (head + 1) * rows]
        query_out[:, head * LANES : (head + 1) * LANES] = turn_back(
            part, cosine_ref[...], sine_ref[...]
        ).astype(bf16)


def attend_back(
    queries_joined, windows, firsts, low, mixed, grads, logs, cosine, sine,
    kv_heads, group, rows, tile_rows,
):
    stretch = queries_joined.shape[0]
    tiles = len(windows)
    blocks = stretch // rows
    pairs = group * rows
    window_tiles = tiles * stretch // tile_rows
    scale = HEAD_SIZE ** (-0.5)
    factor = scale * math.log2(math.e)
    key_columns = [at for _, at in windows]
    value_columns = [at + kv_heads for _, at in windows]
    arrays = [a for a, _ in windows]
    heads_spec = pl.BlockSpec((rows, group * LANES), lambda g, i, *s: (i, g))
    table_spec = pl.BlockSpec((rows, LANES), lambda g, i, *s: (i, 0))
    total_spec = pl.BlockSpec((tiles * stretch, LANES), lambda g, i, *s: (0, g))
    grid_spec = pltpu.PrefetchScalarGridSpec(
        num_scalar_prefetch=1,
        grid=(kv_heads, blocks),
        in_specs=[
            heads_spec,
            pl.BlockSpec((1, 1, rows), lambda g, i, *s: (i, 0, 0)),
            heads_spec,
            heads_spec,
            pl.BlockSpec((1, 1, 1, pairs), lambda g, i, *s: (g, i, 0, 0)),
            table_spec,
            table_spec,
        ]
        + window_specs(tiles, stretch, key_columns)
        + window_specs(tiles, stretch, value_columns),
        out_specs=[heads_spec, total_spec, total_spec],
        scratch_shapes=[
            pltpu.VMEM((window_tiles, tile_rows, LANES), bf16),
            pltpu.VMEM((window_tiles, tile_rows, LANES), bf16),
            pltpu.VMEM((window_tiles, LANES, tile_rows), bf16),
            pltpu.VMEM((LANES, pairs), f32),
        ],
    )
    work = stretch * stretch * kv_heads * group
    return pl.pallas_call(
        functools.partial(attend_back_kernel, tiles, group, factor, scale),
        grid_spec=grid_spec,
        out_shape=[
            jax.ShapeDtypeStruct((stretch, kv_heads * group * LANES), bf16),
            jax.ShapeDtypeStruct((tiles * stretch, kv_heads * LANES), f32),
            jax.ShapeDtypeStruct((tiles * stretch, kv_heads * LANES), f32),
        ],
        cost_estimate=pl.CostEstimate(
            flops=40 * LANES * work, bytes_accessed=16 * stretch * stretch, transcendentals=work
        ),
        name="attend_back",
    )(low, queries_joined, firsts, mixed, grads, logs, cosine, sine, *arrays, *arrays)


def gather_back_kernel(kv_heads, parts, key_ref, value_ref, cosine_ref, sine_ref, *refs):
    out_ref = refs[2 * parts]
    for head in range(kv_heads):
        at = pl.ds(head * LANES, LANES)
        key = key_ref[:, at]
        value = value_ref[:, at]
        for part in range(parts):
            key = key + refs[2 * part][:, at].astype(f32)
            value = value + refs[2 * part + 1][:, at].astype(f32)
        out_ref[:, at] = turn_back(key, cosine_ref[...], sine_ref[...]).astype(bf16)
        out_ref[:, pl.ds((kv_heads + head) * LANES, LANES)] = value.astype(bf16)


def gather_back(key_totals, value_totals, received, cosine, sine, kv_heads, stretch, block):
    skipped = key_totals.shape[0] // block - stretch // block
    width = kv_heads * LANES
    own = pl.BlockSpec((block, width), lambda i: (i + skipped, 0))
    other = pl.BlockSpec((block, width), lambda i: (i, 0))
    table = pl.BlockSpec((block, LANES), lambda i: (i, 0))
    flat = [array for pair in received for array in pair]
    return pl.pallas_call(
        functools.partial(gather_back_kernel, kv_heads, len(received)),
        grid=(stretch // block,),
        in_specs=[own, own, table, table] + [other] * len(flat),
        out_specs=pl.BlockSpec((block, 2 * width), lambda i: (i, 0)),
        out_shape=jax.ShapeDtypeStruct((stretch, 2 * width), bf16),
        name="gather_back",
    )(key_totals, value_totals, cosine, sine, *flat)


def product_over(left, right, axis, order):
    count = lax.axis_size(axis)
    index = lax.axis_index(axis)
    size = left.shape[1] // 2

    def times(offset):
        part = lax.dynamic_slice_in_dim(left, offset, size, 1)
        return jnp.dot(part.T, right, preferred_element_type=f32)

    kept = None
    for place in order:
        bit = (index >> place) & 1
        if kept is None:
            sent = times((1 - bit) * size).astype(bf16)
            got = exchange(sent, axis, 1 << place)
            kept = times(bit * size) + got.astype(f32)
        else:
            size //= 2
            sent = lax.dynamic_slice_in_dim(kept, (1 - bit) * size, size, 0).astype(bf16)
            got = exchange(sent, axis, 1 << place)
            kept = lax.dynamic_slice_in_dim(kept, bit * size, size, 0) + got.astype(f32)
    whole = kept.astype(bf16)
    for place in reversed(order):
        bit = (index >> place) & 1
        got = exchange(whole, axis, 1 << place)
        whole = jnp.where(
            bit == 1,
            jnp.concatenate([got, whole], axis=0),
            jnp.concatenate([whole, got], axis=0),
        )
    return whole.astype(f32)


def sum_everywhere(value, axes):
    for axis in axes:
        count = lax.axis_size(axis)
        place = 1
        while place < count:
            value = value + exchange(value, axis, place)
            place *= 2
    return value


def scatter_sum(product):
    return lax.psum_scatter(
        product.astype(bf16), "tensor", scatter_dimension=0, tiled=True
    ).astype(f32)


def gather_rows(rows):
    return lax.all_gather(rows, "tensor", axis=0, tiled=True)


def after(value, *others):
    return lax.optimization_barrier((value,) + others)[0]


def per_device(
    block_input,
    positions,
    attn_gain,
    w_query,
    key_weight,
    value_weight,
    w_out,
    mlp_gain,
    w_gate,
    w_up,
    w_down,
    out_grad,
):
    stretch = positions.shape[0]
    reach = LONGEST_DOCUMENT // stretch
    heads = w_query.shape[1] // HEAD_SIZE
    kv_heads = key_weight.shape[1] // HEAD_SIZE
    group = heads // kv_heads
    rows = min(256, stretch)
    tile_rows = min(512, stretch)
    blocks = stretch // rows
    places = list(range((lax.axis_size("dp") - 1).bit_length()))
    crossed = places[:1] + places[:0:-1]

    normed_own, inv_rms_attn = normalize(block_input, attn_gain)
    attention_normed = gather_rows(normed_own)
    out_low = gather_rows(after(out_grad.astype(bf16), attention_normed))

    query_spread = spread_matrix(heads)
    kv_spread = spread_matrix(2 * kv_heads)
    all_spread = spread_matrix(heads + 2 * kv_heads)
    w_joined = jnp.dot(
        jnp.concatenate([w_query, key_weight, value_weight], axis=1), all_spread,
        preferred_element_type=bf16,
    )
    w_out_spread = jnp.dot(query_spread.T, w_out, preferred_element_type=bf16)
    cosine, sine = rope_tables(positions)
    local = jnp.arange(stretch, dtype=jnp.int32)
    window_first = reach * stretch + local - positions
    firsts = window_first.reshape(blocks, 1, rows)
    low = jnp.min(window_first.reshape(blocks, rows), axis=1) // tile_rows

    joined = project(attention_normed, w_joined, cosine, sine, heads + kv_heads, rows)
    key_value = joined[:, heads * LANES :]
    windows = [(from_behind(key_value, "dp", d), 0) for d in range(reach, 0, -1)]
    windows = windows + [(joined, heads)]
    attended, logs = attend(joined, windows, firsts, low, kv_heads, group, rows, tile_rows)

    residual = block_input + scatter_sum(
        jnp.dot(attended, w_out_spread, preferred_element_type=f32)
    )
    mlp_normed_own, inv_rms_mlp = normalize(residual, mlp_gain)
    normed_mlp = gather_rows(mlp_normed_own)
    gate_pre = jnp.dot(normed_mlp, w_gate, preferred_element_type=f32)
    up_proj = jnp.dot(normed_mlp, w_up, preferred_element_type=f32)
    sigmoid_gate = jax.nn.sigmoid(gate_pre)
    silu_gate = gate_pre * sigmoid_gate
    hidden = (silu_gate * up_proj).astype(bf16)
    hidden_grad = jnp.dot(out_low, w_down.T, preferred_element_type=f32)
    gate_grad = (
        hidden_grad * up_proj * sigmoid_gate * (1.0 + gate_pre * (1.0 - sigmoid_gate))
    ).astype(bf16)
    up_grad = (hidden_grad * silu_gate).astype(bf16)
    mlp_normed_grad = scatter_sum(
        jnp.dot(gate_grad, w_gate.T, preferred_element_type=f32)
        + jnp.dot(up_grad, w_up.T, preferred_element_type=f32)
    )
    residual_part = normalize_back(residual, inv_rms_mlp, mlp_gain, mlp_normed_grad)
    residual_grad = out_grad + residual_part
    residual_low = gather_rows(residual_grad.astype(bf16))

    down_product = after(
        jnp.dot(hidden, w_down, preferred_element_type=f32).astype(bf16), residual_low
    )
    block_output = residual + scatter_sum(down_product)

    grad_gate = product_over(normed_mlp, gate_grad, "dp", places)
    grad_up = product_over(normed_mlp, up_grad, "dp", crossed)
    grad_down = product_over(hidden, out_low, "dp", places)

    attended_plain = jnp.dot(attended, query_spread.T, preferred_element_type=bf16)
    grad_out = product_over(attended_plain, residual_low, "dp", crossed)
    attended_gradient = jnp.dot(residual_low, w_out_spread.T, preferred_element_type=f32).astype(
        bf16
    )
    query_grad, key_totals, value_totals = attend_back(
        joined, windows, firsts, low, attended, attended_gradient, logs, cosine, sine,
        kv_heads, group, rows, tile_rows,
    )
    received = []
    for distance in range(1, reach + 1):
        begin = (reach - distance) * stretch
        received.append(
            [
                from_behind(total[begin : begin + stretch].astype(bf16), "dp", -distance)
                for total in (key_totals, value_totals)
            ]
        )
    key_value_grad = gather_back(
        key_totals, value_totals, received, cosine, sine, kv_heads, stretch, rows
    )
    split = heads * LANES
    attn_normed_part = jnp.dot(
        query_grad, w_joined[:, :split].T, preferred_element_type=f32
    ) + jnp.dot(key_value_grad, w_joined[:, split:].T, preferred_element_type=f32)
    attn_normed_grad = scatter_sum(attn_normed_part)
    input_part = normalize_back(block_input, inv_rms_attn, attn_gain, attn_normed_grad)
    input_grad = residual_grad + input_part

    query_plain = jnp.dot(query_grad, query_spread.T, preferred_element_type=bf16)
    kv_plain = jnp.dot(key_value_grad, kv_spread.T, preferred_element_type=bf16)
    grad_query = product_over(attention_normed, query_plain, "dp", places)
    grad_key_value = product_over(attention_normed, kv_plain, "dp", crossed)
    grad_key = grad_key_value[:, : kv_heads * HEAD_SIZE]
    grad_value = grad_key_value[:, kv_heads * HEAD_SIZE :]

    mlp_gain_part = jnp.sum(mlp_normed_grad * residual * inv_rms_mlp, axis=0, keepdims=True)
    attn_gain_part = jnp.sum(attn_normed_grad * block_input * inv_rms_attn, axis=0, keepdims=True)
    grad_mlp_gain = sum_everywhere(mlp_gain_part, ("tensor", "dp"))[0]
    grad_attn_gain = sum_everywhere(attn_gain_part, ("tensor", "dp"))[0]
    return (
        block_output,
        input_grad,
        grad_query,
        grad_key,
        grad_value,
        grad_out,
        grad_gate,
        grad_up,
        grad_down,
        grad_attn_gain,
        grad_mlp_gain,
    )


def solution(mesh):
    in_specs = (
        P(("dp", "tensor"), None),
        P("dp"),
        P(),
        P(None, "tensor"),
        P(None, "tensor"),
        P(None, "tensor"),
        P("tensor", None),
        P(),
        P(None, "tensor"),
        P(None, "tensor"),
        P("tensor", None),
        P(("dp", "tensor"), None),
    )
    out_specs = (
        P(("dp", "tensor"), None),
        P(("dp", "tensor"), None),
        P(None, "tensor"),
        P(None, "tensor"),
        P(None, "tensor"),
        P("tensor", None),
        P(None, "tensor"),
        P(None, "tensor"),
        P("tensor", None),
        P(),
        P(),
    )
    return jax.shard_map(
        per_device, mesh=mesh, in_specs=in_specs, out_specs=out_specs, check_vma=False
    )
```

time: 1590 us -> 785 us (0.49)
  waiting for transfers between devices: 919 us -> 443 us
  local copies, waits for them, and re-layouts: 207 us -> 24 us
  matrix products: 268 us -> 105 us
  starting transfers between devices: 9.65 us -> 80 us
  other arithmetic: 119 us -> 71.7 us
  Pallas kernels: 0 us -> 45.4 us
  blocking collectives: 41.7 us -> 0 us
    psum x1 -> x0, waiting for transfers between devices: 276 us -> none  [per_device(): lax.psum((grad_query, grad_key, grad_value, grad_out, grad_gate, grad_up,...]
    reduce_scatter x4, waiting for transfers between devices: 361 us -> 144 us  [scatter_sum(): lax.psum_scatter(product.astype(bf16), 'tensor', scatter_dimension=0, til...]
    dot_general x57 -> x27, matrix products: 268 us -> 105 us  [the longest x12 36.3 us: times(): return jnp.dot(part.T, right, preferred_element_type=f32)]
    ppermute x0 -> x46, starting transfers between devices: none -> 67 us  [exchange(): return lax.ppermute(value, axis, [(i, i ^ distance) for i in range(count)])]
    while x75 -> x0, local copies, waits for them, and re-layouts: 59.2 us -> none
    ppermute x0 -> x46, waiting for transfers between devices: none -> 53 us  [exchange(): return lax.ppermute(value, axis, [(i, i ^ distance) for i in range(count)])]
    pallas_call x0 -> x4, Pallas kernels: none -> 45.4 us  [the longest x1 20 us: attend_back(): pl.pallas_call(functools.partial(attend_back_kernel, tiles, group, factor...]
    unnamed x123 -> x100, local copies, waits for them, and re-layouts: 55.9 us -> 13.8 us
  transfers between devices with their start and end apart: 13 -> 60, of which waited for: 10 -> 28; matrix products, arithmetic and copies ran while one was open for 5% -> 20% of each run, Pallas kernels for 0% -> 3%
where the time goes in v1:
time: 785 us; the launch traced here: 784 us
  waiting for transfers between devices  443 us (56%)
  matrix products  105 us (13%)
  starting transfers between devices  80 us (10%)
  other arithmetic  71.7 us (9%)
  Pallas kernels  45.4 us (6%)
  local copies, waits for them, and re-layouts  24 us (3%)
  between operations  15.3 us (2%)
    all_gather x4, waiting for transfers between devices, gather_rows(): return lax.all_gather(rows, 'tensor', axis=0, tiled=True)  193 us
    reduce_scatter x4, waiting for transfers between devices, scatter_sum(): lax.psum_scatter(product.astype(bf16), 'tensor', scatter_dimension=0, til...  144 us
    ppermute x46, starting transfers between devices, exchange(): return lax.ppermute(value, axis, [(i, i ^ distance) for i in range(count)])  67 us
    ppermute x6, waiting for transfers between devices, from_behind(): lax.ppermute(value, axis, [(source, source + steps) for source in range(l...  53.1 us
    ppermute x46, waiting for transfers between devices, exchange(): return lax.ppermute(value, axis, [(i, i ^ distance) for i in range(count)])  53 us
    dot_general x12, matrix products, times(): return jnp.dot(part.T, right, preferred_element_type=f32)  36.3 us
    convert_element_type x6, other arithmetic, product_over(): return whole.astype(f32)  20.4 us
    pallas_call x1, Pallas kernels, attend_back(): pl.pallas_call(functools.partial(attend_back_kernel, tiles, group, factor...  20 us
  transfers between devices with their start and end apart: 60, of which 28 were waited for; matrix products, arithmetic and copies ran while one was open for 20% of the time, Pallas kernels for 3%

profile of v1, /device:TPU:0, one launch (start us, length us, event | category | flops | bytes accessed | tf_op | source)
XLA Modules:
  0.0 784.0 jit_solution(12870873998396373906)
XLA Ops:
  16.6 3.1 fusion.64
  19.7 6.3 fusion.4.weight_ref
  26.0 52.3 %all-gather.5.cloned.1.call-done.rows_ref = bf16[1024,1536]{1,0:T(8,128)(2,1)} async-done(((bf16[256,1536]{1,0:T(8,128)(2,1)}), bf16[1024,1536]{1,0:T(8,128)(2,1)}) %all-gather.5.cloned.1.call-update) | async-done | bytes 3145744 | tf_op jit(solution)/shard_map/all_gather | solution.py:436
  78.3 7.7 project.1.query_ref.refs_2_.refs_5_.refs_7_.refs_10_
  88.3 4.4 collective-permute-start
  95.6 3.5 fusion.63
  99.2 16.3 %collective-permute-done.refs_0_.refs_3_.refs_5_.refs_8_ = bf16[1024,512]{1,0:T(8,128)(2,1)} collective-permute-done((bf16[1024,512]{1,0:T(8,128)(2,1)}, bf16[1024,512]{1,0:T(8,128)(2,1)}, u32[]{:S(2)}, u32[]{:S(2)}) %collective-permute-start) | collective-permute-done | bytes 1048608 | tf_op jit(solution)/shard_map/ppermute | solution.py:30
  115.5 13.4 %attend.1 = (bf16[1024,512]{1,0:T(8,128)(2,1)}, f32[2,4,1,512]{3,2,1,0:T(1,128)}) custom-call(s32[4]{0:T(128)} %and_select_fusion.low_ref, bf16[1024,1024]{1,0:T(8,128)(2,1)} %project.1.query_ref.refs_2_.refs_5_.refs_7_.refs_10_, s32[4,1,256]{2,1,0:T(1,128)} %bitcast.35, bf16[1024,512]{1,0:T(8,128)(2,1)} %collective-permute-done.refs_0_.refs_3_.refs_5_.refs_8_, ...), custom_call_target="tpu_custom_call" | custom-call | flops 8589934592 | bytes 8388608 | tf_op jit(solution)/shard_map/attend/pallas_call | solution.py:221
  128.9 5.2 convolution_convert_fusion
  134.1 84.4 %reduce-scatter.5.cloned.1.call-done = bf16[256,1536]{1,0:T(8,128)(2,1)} async-done(((bf16[1024,1536]{1,0:T(8,128)(2,1)}), bf16[256,1536]{1,0:T(8,128)(2,1)}) %reduce-scatter.5.cloned.1.call-update) | async-done | bytes 786448 | tf_op jit(solution)/shard_map/reduce_scatter | solution.py:430
  222.7 2.4 convert_element_type.209
  225.7 60.5 %all-gather.7.cloned.1.call-done = bf16[1024,1536]{1,0:T(8,128)(2,1)} async-done(((bf16[256,1536]{1,0:T(8,128)(2,1)}), bf16[1024,1536]{1,0:T(8,128)(2,1)}) %all-gather.7.cloned.1.call-update) | async-done | bytes 3145744 | tf_op jit(solution)/shard_map/all_gather | solution.py:436
  286.2 8.4 %fusion.115 = f32[1024,1024]{1,0:T(8,128)} fusion(bf16[1024,1536]{1,0:T(8,128)(2,1)} %all-gather.7.cloned.1.call-done, bf16[1536,1024]{1,0:T(8,128)(2,1)} %param.20), kind=kOutput, calls=%fused_computation.199 | convolution fusion | flops 3221225472 | bytes 10485760 | tf_op jit(solution)/shard_map/dot_general | solution.py:497
  294.6 4.9 fusion.116
  299.5 50.8 %all-gather.9.cloned.1.call-done = bf16[1024,1536]{1,0:T(8,128)(2,1)} async-done(((bf16[256,1536]{1,0:T(8,128)(2,1)}), bf16[1024,1536]{1,0:T(8,128)(2,1)}) %all-gather.9.cloned.1.call-update) | async-done | bytes 3145744 | tf_op jit(solution)/shard_map/all_gather | solution.py:436
  350.3 9.5 %multiply_convert_fusion = (bf16[1024,1024]{1,0:T(8,128)(2,1)S(1)}, bf16[1024,1024]{1,0:T(8,128)(2,1)S(1)}, bf16[1024,1024]{1,0:T(8,128)(2,1)}) fusion(f32[1024,1024]{1,0:T(8,128)} %fusion.115, f32[1024,1024]{1,0:T(8,128)} %fusion.116, bf16[1024,1536]{1,0:T(8,128)(2,1)} %all-gather.9.cloned.1.call-done, bf16[1024,1536]{1,0:T(8,128)(2,1)S(1)} %copy-done), kind=kOutput, calls=%fused_computation.2 | convolution fusion | flops 3236954112 | bytes 20971520 | tf_op jit(solution)/shard_map/dot_general | solution.py:502
  359.8 3.5 fusion.117
  363.3 4.9 add_convert_fusion.1
  368.3 59.2 %reduce-scatter.7.cloned.1.call-done = bf16[256,1536]{1,0:T(8,128)(2,1)} async-done(((bf16[1024,1536]{1,0:T(8,128)(2,1)}), bf16[256,1536]{1,0:T(8,128)(2,1)}) %reduce-scatter.7.cloned.1.call-update) | async-done | bytes 786448 | tf_op jit(solution)/shard_map/reduce_scatter | solution.py:430
  429.8 3.3 fusion.109
  433.3 5.3 convolution_convert_fusion.2
  438.6 5.6 convolution_convert_fusion.4
  444.7 3.0 convolution_convert_fusion.5
  447.7 4.7 convert_add_fusion
  455.1 3.3 convert_add_fusion.1
  461.0 3.3 convert_add_fusion.2
  466.9 29.7 %all-gather.11.cloned.1.call-done = bf16[1024,1536]{1,0:T(8,128)(2,1)} async-done(((bf16[256,1536]{1,0:T(8,128)(2,1)}), bf16[1024,1536]{1,0:T(8,128)(2,1)}) %all-gather.11.cloned.1.call-update) | async-done | bytes 3145744 | tf_op jit(solution)/shard_map/all_gather | solution.py:436
  496.6 5.1 convolution_convert_fusion.6.refs_1_
  501.7 20.0 %attend_back.1 = (bf16[1024,512]{1,0:T(8,128)(2,1)}, f32[3072,256]{1,0:T(8,128)}, f32[3072,256]{1,0:T(8,128)}) custom-call(s32[4]{0:T(128)} %and_select_fusion.low_ref, bf16[1024,1024]{1,0:T(8,128)(2,1)} %project.1.query_ref.refs_2_.refs_5_.refs_7_.refs_10_, s32[4,1,256]{2,1,0:T(1,128)} %bitcast.36, bf16[1024,512]{1,0:T(8,128)(2,1)} %get-tuple-element.18.refs_0_, ...), custom_call_target="tpu_custom_call" | custom-call | flops 21474836480 | bytes 16777216 | tf_op jit(solution)/shard_map/attend_back/pallas_call | solution.py:341
  529.6 2.5 convert_add_fusion.3
  532.1 9.7 %collective-permute-done.2.refs_0_ = bf16[1024,256]{1,0:T(8,128)(2,1)} collective-permute-done((bf16[1024,256]{1,0:T(8,128)(2,1)S(1)}, bf16[1024,256]{1,0:T(8,128)(2,1)}, u32[]{:S(2)}, u32[]{:S(2)}) %collective-permute-start.2) | collective-permute-done | bytes 524320 | tf_op jit(solution)/shard_map/ppermute | solution.py:30
  541.8 8.8 %collective-permute-start.25 = (bf16[384,1024]{1,0:T(8,128)(2,1)}, bf16[384,1024]{1,0:T(8,128)(2,1)}, u32[]{:S(2)}, u32[]{:S(2)}) collective-permute-start(bf16[384,1024]{1,0:T(8,128)(2,1)} %dynamic-slice_convert_fusion.2), channel_id=1, source_target_pairs={{0,8},{4,12},{8,0},{12,4},{16,24},{20,28},{24,16},{28,20},{1,9},{5... | collective-permute-start | bytes 2359304 | tf_op jit(solution)/shard_map/ppermute | solution.py:35
  550.6 15.9 %collective-permute-done.4.refs_2_ = bf16[1024,256]{1,0:T(8,128)(2,1)} collective-permute-done((bf16[1024,256]{1,0:T(8,128)(2,1)S(1)}, bf16[1024,256]{1,0:T(8,128)(2,1)}, u32[]{:S(2)}, u32[]{:S(2)}) %collective-permute-start.4) | collective-permute-done | bytes 524320 | tf_op jit(solution)/shard_map/ppermute | solution.py:30
  566.5 11.2 %collective-permute-done.5.refs_3_ = bf16[1024,256]{1,0:T(8,128)(2,1)} collective-permute-done((bf16[1024,256]{1,0:T(8,128)(2,1)S(1)}, bf16[1024,256]{1,0:T(8,128)(2,1)}, u32[]{:S(2)}, u32[]{:S(2)}) %collective-permute-start.5) | collective-permute-done | bytes 524320 | tf_op jit(solution)/shard_map/ppermute | solution.py:30
  577.7 4.4 gather_back.1
  582.1 3.7 fusion.24
  585.8 3.6 add_convert_fusion
  590.7 14.5 %collective-permute-start.38 = (bf16[128,1536]{1,0:T(8,128)(2,1)S(1)}, bf16[128,1536]{1,0:T(8,128)(2,1)S(1)}, u32[]{:S(2)}, u32[]{:S(2)}) collective-permute-start(bf16[128,1536]{1,0:T(8,128)(2,1)S(1)} %dynamic-slice_convert_fusion.3), channel_id=1, source_target_pairs={{0,16},{4,20},{8,24},{12,28},{16,0},{20,4},{24,8},{28,12},{1,17},{... | collective-permute-start | bytes 1179656 | tf_op jit(solution)/shard_map/ppermute | solution.py:35
  609.4 2.6 collective-permute-done.38
  612.0 2.4 collective-permute-start.39
  615.9 3.0 collective-permute-done.32
  619.0 2.5 collective-permute-start.33
  625.3 7.0 collective-permute-start.40
  639.3 3.3 collective-permute-done.40
  642.6 3.4 maximum_select_fusion.5
  646.1 4.1 collective-permute-done.27
  655.4 5.3 convolution_convert_fusion.1
  662.5 5.3 collective-permute-done.28
  667.8 3.8 maximum_select_fusion.3
  672.2 4.9 fusion.3
  679.0 5.0 fusion.2
  691.1 2.6 fusion.49
  700.9 4.9 collective-permute-done.19
  706.5 3.6 collective-permute-done.7
  714.2 2.8 collective-permute-done.8
  717.1 5.9 collective-permute-done.13
  727.2 2.7 collective-permute-done.14
  731.2 4.0 collective-permute-done.10
  738.1 5.3 fusion.1
  755.2 2.6 collective-permute-start.43
  760.0 2.9 copy.29
  762.8 2.9 copy.30
  765.9 3.1 convert_add_fusion.6
  769.3 3.4 collective-permute-done.45
  (279 shorter events, 111.6 us)
Async XLA Ops:
  7.2 343.1 %copy-start = (bf16[1024,1536]{1,0:T(8,128)(2,1)S(1)}, bf16[1024,1536]{1,0:T(8,128)(2,1)}, u32[]{:S(2)}) copy-start(bf16[1024,1536]{1,0:T(8,128)(2,1)} %param.22) | copy-start | bytes 9437188
  7.2 71.1 %all-gather.5.cloned.1.call-start = ((), (), s32[]{:S(2)}) async-start(), calls=%async_computation.4 | async-start | bytes 3932160 | tf_op jit(solution)/shard_map/all_gather | solution.py:436
  12.0 206.6 %reduce-scatter.5.cloned.1.call-start = ((), (), s32[]{:S(2)}) async-start(), calls=%async_computation.5 | async-start | bytes 3932160 | tf_op jit(solution)/shard_map/reduce_scatter | solution.py:430
  16.6 78.3 %copy-start.27 = (s32[1024]{0:T(1024)}, s32[1024]{0:T(1024)S(1)}, u32[]{:S(2)}) copy-start(s32[1024]{0:T(1024)S(1)} %get-tuple-element.67) | copy-start | bytes 12292
  88.3 27.2 %collective-permute-start = (bf16[1024,512]{1,0:T(8,128)(2,1)}, bf16[1024,512]{1,0:T(8,128)(2,1)}, u32[]{:S(2)}, u32[]{:S(2)}) collective-permute-start(bf16[1024,512]{1,0:T(8,128)(2,1)} %slice.40), channel_id=1, source_target_pairs={{0,8},{4,12},{8,16},{12,20},{16,24},{20,28},{1,9},{5,13},{9,17},{1... | collective-permute-start | bytes 3145736 | tf_op jit(solution)/shard_map/ppermute | solution.py:30
  92.6 22.9 %collective-permute-start.1 = (bf16[1024,512]{1,0:T(8,128)(2,1)}, bf16[1024,512]{1,0:T(8,128)(2,1)}, u32[]{:S(2)}, u32[]{:S(2)}) collective-permute-start(bf16[1024,512]{1,0:T(8,128)(2,1)} %slice.40), channel_id=1, source_target_pairs={{0,4},{4,8},{8,12},{12,16},{16,20},{20,24},{24,28},{1,5},{5,9},{9,... | collective-permute-start | bytes 3145736 | tf_op jit(solution)/shard_map/ppermute | solution.py:30
  134.1 87.5 %copy-start.25 = (f32[1536]{0:T(1024)S(1)}, f32[1536]{0:T(1024)}, u32[]{:S(2)}) copy-start(f32[1536]{0:T(1024)} %param.19) | copy-start | bytes 18436
  134.1 152.1 %all-gather.7.cloned.1.call-start = ((), (), s32[]{:S(2)}) async-start(), calls=%async_computation.6 | async-start | bytes 3932160 | tf_op jit(solution)/shard_map/all_gather | solution.py:436
  222.7 127.6 %all-gather.9.cloned.1.call-start = ((), (), s32[]{:S(2)}) async-start(), calls=%async_computation.7 | async-start | bytes 3932160 | tf_op jit(solution)/shard_map/all_gather | solution.py:436
  225.1 202.3 %reduce-scatter.7.cloned.1.call-start = ((), (), s32[]{:S(2)}) async-start(), calls=%async_computation.8 | async-start | bytes 3932160 | tf_op jit(solution)/shard_map/reduce_scatter | solution.py:430
  368.2 128.3 %all-gather.11.cloned.1.call-start = ((), (), s32[]{:S(2)}) async-start(), calls=%async_computation.9 | async-start | bytes 3932160 | tf_op jit(solution)/shard_map/all_gather | solution.py:436
  433.1 316.3 %reduce-scatter.11.cloned.1.call-start = ((), (), s32[]{:S(2)}) async-start(), calls=%async_computation.11 | async-start | bytes 3932160 | tf_op jit(solution)/shard_map/reduce_scatter | solution.py:430
  438.6 9.1 %collective-permute-start.36 = (bf16[512,1536]{1,0:T(8,128)(2,1)}, bf16[512,1536]{1,0:T(8,128)(2,1)}, u32[]{:S(2)}, u32[]{:S(2)}) collective-permute-start(bf16[512,1536]{1,0:T(8,128)(2,1)} %convolution_convert_fusion.2), channel_id=1, source_target_pairs={{0,4},{4,0},{8,12},{12,8},{16,20},{20,16},{24,28},{28,24},{1,5},{5... | collective-permute-start | bytes 4718600 | tf_op jit(solution)/shard_map/ppermute | solution.py:35
  444.1 10.9 %collective-permute-start.30 = (bf16[768,1024]{1,0:T(8,128)(2,1)}, bf16[768,1024]{1,0:T(8,128)(2,1)}, u32[]{:S(2)}, u32[]{:S(2)}) collective-permute-start(bf16[768,1024]{1,0:T(8,128)(2,1)} %convolution_convert_fusion.4), channel_id=1, source_target_pairs={{0,4},{4,0},{8,12},{12,8},{16,20},{20,16},{24,28},{28,24},{1,5},{5... | collective-permute-start | bytes 4718600 | tf_op jit(solution)/shard_map/ppermute | solution.py:35
  447.7 13.3 %collective-permute-start.24 = (bf16[768,1024]{1,0:T(8,128)(2,1)}, bf16[768,1024]{1,0:T(8,128)(2,1)}, u32[]{:S(2)}, u32[]{:S(2)}) collective-permute-start(bf16[768,1024]{1,0:T(8,128)(2,1)} %convolution_convert_fusion.5), channel_id=1, source_target_pairs={{0,4},{4,0},{8,12},{12,8},{16,20},{20,16},{24,28},{28,24},{1,5},{5... | collective-permute-start | bytes 4718600 | tf_op jit(solution)/shard_map/ppermute | solution.py:35
  453.6 74.7 %collective-permute-start.37 = (bf16[256,1536]{1,0:T(8,128)(2,1)}, bf16[256,1536]{1,0:T(8,128)(2,1)}, u32[]{:S(2)}, u32[]{:S(2)}) collective-permute-start(bf16[256,1536]{1,0:T(8,128)(2,1)} %dynamic-slice_convert_fusion), channel_id=1, source_target_pairs={{0,8},{4,12},{8,0},{12,4},{16,24},{20,28},{24,16},{28,20},{1,9},{5... | collective-permute-start | bytes 2359304 | tf_op jit(solution)/shard_map/ppermute | solution.py:35
  459.5 145.6 %collective-permute-start.31 = (bf16[384,1024]{1,0:T(8,128)(2,1)}, bf16[384,1024]{1,0:T(8,128)(2,1)}, u32[]{:S(2)}, u32[]{:S(2)}) collective-permute-start(bf16[384,1024]{1,0:T(8,128)(2,1)} %dynamic-slice_convert_fusion.1), channel_id=1, source_target_pairs={{0,16},{4,20},{8,24},{12,28},{16,0},{20,4},{24,8},{28,12},{1,17},{... | collective-permute-start | bytes 2359304 | tf_op jit(solution)/shard_map/ppermute | solution.py:35
  524.0 17.8 %collective-permute-start.2 = (bf16[1024,256]{1,0:T(8,128)(2,1)S(1)}, bf16[1024,256]{1,0:T(8,128)(2,1)}, u32[]{:S(2)}, u32[]{:S(2)}) collective-permute-start(bf16[1024,256]{1,0:T(8,128)(2,1)S(1)} %get-tuple-element.63), channel_id=1, source_target_pairs={{4,0},{8,4},{12,8},{16,12},{20,16},{24,20},{28,24},{5,1},{9,5},{13... | collective-permute-start | bytes 1572872 | tf_op jit(solution)/shard_map/ppermute | solution.py:30
  525.5 25.1 %collective-permute-start.3 = (bf16[1024,256]{1,0:T(8,128)(2,1)S(1)}, bf16[1024,256]{1,0:T(8,128)(2,1)}, u32[]{:S(2)}, u32[]{:S(2)}) collective-permute-start(bf16[1024,256]{1,0:T(8,128)(2,1)S(1)} %get-tuple-element.61), channel_id=1, source_target_pairs={{4,0},{8,4},{12,8},{16,12},{20,16},{24,20},{28,24},{5,1},{9,5},{13... | collective-permute-start | bytes 1572872 | tf_op jit(solution)/shard_map/ppermute | solution.py:30
  527.0 39.5 %collective-permute-start.4 = (bf16[1024,256]{1,0:T(8,128)(2,1)S(1)}, bf16[1024,256]{1,0:T(8,128)(2,1)}, u32[]{:S(2)}, u32[]{:S(2)}) collective-permute-start(bf16[1024,256]{1,0:T(8,128)(2,1)S(1)} %get-tuple-element.62), channel_id=1, source_target_pairs={{8,0},{12,4},{16,8},{20,12},{24,16},{28,20},{9,1},{13,5},{17,9},{2... | collective-permute-start | bytes 1572872 | tf_op jit(solution)/shard_map/ppermute | solution.py:30
  528.3 49.4 %collective-permute-start.5 = (bf16[1024,256]{1,0:T(8,128)(2,1)S(1)}, bf16[1024,256]{1,0:T(8,128)(2,1)}, u32[]{:S(2)}, u32[]{:S(2)}) collective-permute-start(bf16[1024,256]{1,0:T(8,128)(2,1)S(1)} %get-tuple-element.60), channel_id=1, source_target_pairs={{8,0},{12,4},{16,8},{20,12},{24,16},{28,20},{9,1},{13,5},{17,9},{2... | collective-permute-start | bytes 1572872 | tf_op jit(solution)/shard_map/ppermute | solution.py:30
  541.8 72.6 %collective-permute-start.25 = (bf16[384,1024]{1,0:T(8,128)(2,1)}, bf16[384,1024]{1,0:T(8,128)(2,1)}, u32[]{:S(2)}, u32[]{:S(2)}) collective-permute-start(bf16[384,1024]{1,0:T(8,128)(2,1)} %dynamic-slice_convert_fusion.2), channel_id=1, source_target_pairs={{0,8},{4,12},{8,0},{12,4},{16,24},{20,28},{24,16},{28,20},{1,9},{5... | collective-permute-start | bytes 2359304 | tf_op jit(solution)/shard_map/ppermute | solution.py:35
  589.4 176.4 %reduce-scatter.9.cloned.1.call-start = ((), (), s32[]{:S(2)}) async-start(), calls=%async_computation.10 | async-start | bytes 3932160 | tf_op jit(solution)/shard_map/reduce_scatter | solution.py:430
  590.7 21.3 %copy-start.13 = (f32[256,1536]{1,0:T(8,128)S(1)}, f32[256,1536]{1,0:T(8,128)}, u32[]{:S(2)}) copy-start(f32[256,1536]{1,0:T(8,128)} %convert_add_fusion.3) | copy-start | bytes 4718596
  590.7 21.3 %collective-permute-start.38 = (bf16[128,1536]{1,0:T(8,128)(2,1)S(1)}, bf16[128,1536]{1,0:T(8,128)(2,1)S(1)}, u32[]{:S(2)}, u32[]{:S(2)}) collective-permute-start(bf16[128,1536]{1,0:T(8,128)(2,1)S(1)} %dynamic-slice_convert_fusion.3), channel_id=1, source_target_pairs={{0,16},{4,20},{8,24},{12,28},{16,0},{20,4},{24,8},{28,12},{1,17},{... | collective-permute-start | bytes 1179656 | tf_op jit(solution)/shard_map/ppermute | solution.py:35
  607.2 11.6 %collective-permute-start.32 = (bf16[192,1024]{1,0:T(8,128)(2,1)S(1)}, bf16[192,1024]{1,0:T(8,128)(2,1)S(1)}, u32[]{:S(2)}, u32[]{:S(2)}) collective-permute-start(bf16[192,1024]{1,0:T(8,128)(2,1)S(1)} %dynamic-slice_convert_fusion.4), channel_id=1, source_target_pairs={{0,8},{4,12},{8,0},{12,4},{16,24},{20,28},{24,16},{28,20},{1,9},{5... | collective-permute-start | bytes 1179656 | tf_op jit(solution)/shard_map/ppermute | solution.py:35
  612.0 12.3 %collective-permute-start.39 = (bf16[128,1536]{1,0:T(8,128)(2,1)S(1)}, bf16[128,1536]{1,0:T(8,128)(2,1)S(1)}, u32[]{:S(2)}, u32[]{:S(2)}) collective-permute-start(bf16[128,1536]{1,0:T(8,128)(2,1)S(1)} %add_convert_fusion.2), channel_id=1, source_target_pairs={{0,16},{4,20},{8,24},{12,28},{16,0},{20,4},{24,8},{28,12},{1,17},{... | collective-permute-start | bytes 1179656 | tf_op jit(solution)/shard_map/ppermute | solution.py:35
  619.0 13.4 %collective-permute-start.33 = (bf16[192,1024]{1,0:T(8,128)(2,1)S(1)}, bf16[192,1024]{1,0:T(8,128)(2,1)}, u32[]{:S(2)}, u32[]{:S(2)}) collective-permute-start(bf16[192,1024]{1,0:T(8,128)(2,1)S(1)} %add_convert_fusion.3), channel_id=1, source_target_pairs={{0,8},{4,12},{8,0},{12,4},{16,24},{20,28},{24,16},{28,20},{1,9},{5... | collective-permute-start | bytes 1179656 | tf_op jit(solution)/shard_map/ppermute | solution.py:35
  622.3 12.3 %collective-permute-start.26 = (bf16[192,1024]{1,0:T(8,128)(2,1)}, bf16[192,1024]{1,0:T(8,128)(2,1)}, u32[]{:S(2)}, u32[]{:S(2)}) collective-permute-start(bf16[192,1024]{1,0:T(8,128)(2,1)} %dynamic-slice_convert_fusion.5), channel_id=1, source_target_pairs={{0,16},{4,20},{8,24},{12,28},{16,0},{20,4},{24,8},{28,12},{1,17},{... | collective-permute-start | bytes 1179656 | tf_op jit(solution)/shard_map/ppermute | solution.py:35
  625.3 17.3 %collective-permute-start.40 = (bf16[256,1536]{1,0:T(8,128)(2,1)}, bf16[256,1536]{1,0:T(8,128)(2,1)}, u32[]{:S(2)}, u32[]{:S(2)}) collective-permute-start(bf16[256,1536]{1,0:T(8,128)(2,1)} %maximum_select_fusion.11), channel_id=1, source_target_pairs={{0,8},{4,12},{8,0},{12,4},{16,24},{20,28},{24,16},{28,20},{1,9},{5... | collective-permute-start | bytes 2359304 | tf_op jit(solution)/shard_map/ppermute | solution.py:35
  633.9 19.5 %collective-permute-start.34 = (bf16[384,1024]{1,0:T(8,128)(2,1)S(1)}, bf16[384,1024]{1,0:T(8,128)(2,1)S(1)}, u32[]{:S(2)}, u32[]{:S(2)}) collective-permute-start(bf16[384,1024]{1,0:T(8,128)(2,1)S(1)} %maximum_select_fusion.10), channel_id=1, source_target_pairs={{0,16},{4,20},{8,24},{12,28},{16,0},{20,4},{24,8},{28,12},{1,17},{... | collective-permute-start | bytes 2359304 | tf_op jit(solution)/shard_map/ppermute | solution.py:35
  635.7 14.5 %collective-permute-start.27 = (bf16[192,1024]{1,0:T(8,128)(2,1)S(1)}, bf16[192,1024]{1,0:T(8,128)(2,1)S(1)}, u32[]{:S(2)}, u32[]{:S(2)}) collective-permute-start(bf16[192,1024]{1,0:T(8,128)(2,1)S(1)} %add_convert_fusion.4), channel_id=1, source_target_pairs={{0,16},{4,20},{8,24},{12,28},{16,0},{20,4},{24,8},{28,12},{1,17},{... | collective-permute-start | bytes 1179656 | tf_op jit(solution)/shard_map/ppermute | solution.py:35
  646.1 26.1 %collective-permute-start.41 = (bf16[512,1536]{1,0:T(8,128)(2,1)}, bf16[512,1536]{1,0:T(8,128)(2,1)}, u32[]{:S(2)}, u32[]{:S(2)}) collective-permute-start(bf16[512,1536]{1,0:T(8,128)(2,1)} %maximum_select_fusion.5), channel_id=1, source_target_pairs={{0,4},{4,0},{8,12},{12,8},{16,20},{20,16},{24,28},{28,24},{1,5},{5... | collective-permute-start | bytes 4718600 | tf_op jit(solution)/shard_map/ppermute | solution.py:35
  651.4 16.4 %collective-permute-start.28 = (bf16[384,1024]{1,0:T(8,128)(2,1)}, bf16[384,1024]{1,0:T(8,128)(2,1)}, u32[]{:S(2)}, u32[]{:S(2)}) collective-permute-start(bf16[384,1024]{1,0:T(8,128)(2,1)} %maximum_select_fusion.9), channel_id=1, source_target_pairs={{0,8},{4,12},{8,0},{12,4},{16,24},{20,28},{24,16},{28,20},{1,9},{5... | collective-permute-start | bytes 2359304 | tf_op jit(solution)/shard_map/ppermute | solution.py:35
  655.3 23.7 %collective-permute-start.35 = (bf16[768,1024]{1,0:T(8,128)(2,1)}, bf16[768,1024]{1,0:T(8,128)(2,1)}, u32[]{:S(2)}, u32[]{:S(2)}) collective-permute-start(bf16[768,1024]{1,0:T(8,128)(2,1)} %maximum_select_fusion.4), channel_id=1, source_target_pairs={{0,4},{4,0},{8,12},{12,8},{16,20},{20,16},{24,28},{28,24},{1,5},{5... | collective-permute-start | bytes 4718600 | tf_op jit(solution)/shard_map/ppermute | solution.py:35
  655.3 5.3 collective-permute-start.47
  660.6 11.0 %collective-permute-start.48 = (f32[1,1536]{1,0:T(1,128)S(1)}, f32[1,1536]{1,0:T(1,128)S(1)}, u32[]{:S(2)}, u32[]{:S(2)}) collective-permute-start(f32[1,1536]{1,0:T(1,128)S(1)} %reshape_add_fusion), channel_id=1, source_target_pairs={{0,2},{1,3},{2,0},{3,1},{4,6},{5,7},{6,4},{7,5},{8,10},{9,11},{10,... | collective-permute-start | bytes 18440 | tf_op jit(solution)/shard_map/ppermute | solution.py:35
  671.6 66.5 %collective-permute-start.29 = (bf16[768,1024]{1,0:T(8,128)(2,1)}, bf16[768,1024]{1,0:T(8,128)(2,1)}, u32[]{:S(2)}, u32[]{:S(2)}) collective-permute-start(bf16[768,1024]{1,0:T(8,128)(2,1)} %maximum_select_fusion.3), channel_id=1, source_target_pairs={{0,4},{4,0},{8,12},{12,8},{16,20},{20,16},{24,28},{28,24},{1,5},{5... | collective-permute-start | bytes 4718600 | tf_op jit(solution)/shard_map/ppermute | solution.py:35
  671.6 5.5 collective-permute-start.49
  677.2 6.8 collective-permute-start.50
  684.0 59.4 %collective-permute-start.51 = (f32[1,1536]{1,0:T(1,128)S(1)}, f32[1,1536]{1,0:T(1,128)S(1)}, u32[]{:S(2)}, u32[]{:S(2)}) collective-permute-start(f32[1,1536]{1,0:T(1,128)S(1)} %add.386), channel_id=1, source_target_pairs={{0,16},{4,20},{8,24},{12,28},{16,0},{20,4},{24,8},{28,12},{1,17},{... | collective-permute-start | bytes 18440 | tf_op jit(solution)/shard_map/ppermute | solution.py:35
  685.8 8.0 %collective-permute-start.18 = (bf16[192,1536]{1,0:T(8,128)(2,1)}, bf16[192,1536]{1,0:T(8,128)(2,1)}, u32[]{:S(2)}, u32[]{:S(2)}) collective-permute-start(bf16[192,1536]{1,0:T(8,128)(2,1)} %convolution_convert_fusion.3), channel_id=1, source_target_pairs={{0,4},{4,0},{8,12},{12,8},{16,20},{20,16},{24,28},{28,24},{1,5},{5... | collective-permute-start | bytes 1769480 | tf_op jit(solution)/shard_map/ppermute | solution.py:35
  688.5 9.5 %collective-permute-start.6 = (bf16[768,384]{1,0:T(8,128)(2,1)}, bf16[768,384]{1,0:T(8,128)(2,1)}, u32[]{:S(2)}, u32[]{:S(2)}) collective-permute-start(bf16[768,384]{1,0:T(8,128)(2,1)} %fusion.46), channel_id=1, source_target_pairs={{0,4},{4,0},{8,12},{12,8},{16,20},{20,16},{24,28},{28,24},{1,5},{5... | collective-permute-start | bytes 1769480 | tf_op jit(solution)/shard_map/ppermute | solution.py:35
  693.7 16.6 %collective-permute-start.12 = (bf16[768,384]{1,0:T(8,128)(2,1)S(1)}, bf16[768,384]{1,0:T(8,128)(2,1)S(1)}, u32[]{:S(2)}, u32[]{:S(2)}) collective-permute-start(bf16[768,384]{1,0:T(8,128)(2,1)S(1)} %fusion.49), channel_id=1, source_target_pairs={{0,4},{4,0},{8,12},{12,8},{16,20},{20,16},{24,28},{28,24},{1,5},{5... | collective-permute-start | bytes 1769480 | tf_op jit(solution)/shard_map/ppermute | solution.py:35
  695.9 9.9 %collective-permute-start.19 = (bf16[96,1536]{1,0:T(8,128)(2,1)S(1)}, bf16[96,1536]{1,0:T(8,128)(2,1)S(1)}, u32[]{:S(2)}, u32[]{:S(2)}) collective-permute-start(bf16[96,1536]{1,0:T(8,128)(2,1)S(1)} %dynamic-slice_convert_fusion.6), channel_id=1, source_target_pairs={{0,16},{4,20},{8,24},{12,28},{16,0},{20,4},{24,8},{28,12},{1,17},{... | collective-permute-start | bytes 884744 | tf_op jit(solution)/shard_map/ppermute | solution.py:35
  700.2 9.9 %collective-permute-start.7 = (bf16[384,384]{1,0:T(8,128)(2,1)S(1)}, bf16[384,384]{1,0:T(8,128)(2,1)S(1)}, u32[]{:S(2)}, u32[]{:S(2)}) collective-permute-start(bf16[384,384]{1,0:T(8,128)(2,1)S(1)} %dynamic-slice_convert_fusion.8), channel_id=1, source_target_pairs={{0,8},{4,12},{8,0},{12,4},{16,24},{20,28},{24,16},{28,20},{1,9},{5... | collective-permute-start | bytes 884744 | tf_op jit(solution)/shard_map/ppermute | solution.py:35
  706.0 7.5 collective-permute-start.20
  710.2 6.8 collective-permute-start.8
  711.4 11.6 %collective-permute-start.13 = (bf16[384,384]{1,0:T(8,128)(2,1)S(1)}, bf16[384,384]{1,0:T(8,128)(2,1)S(1)}, u32[]{:S(2)}, u32[]{:S(2)}) collective-permute-start(bf16[384,384]{1,0:T(8,128)(2,1)S(1)} %dynamic-slice_convert_fusion.7), channel_id=1, source_target_pairs={{0,16},{4,20},{8,24},{12,28},{16,0},{20,4},{24,8},{28,12},{1,17},{... | collective-permute-start | bytes 884744 | tf_op jit(solution)/shard_map/ppermute | solution.py:35
  713.5 10.7 %collective-permute-start.21 = (bf16[48,1536]{1,0:T(8,128)(2,1)S(1)}, bf16[48,1536]{1,0:T(8,128)(2,1)S(1)}, u32[]{:S(2)}, u32[]{:S(2)}) collective-permute-start(bf16[48,1536]{1,0:T(8,128)(2,1)S(1)} %add_convert_fusion.5), channel_id=1, source_target_pairs={{0,8},{4,12},{8,0},{12,4},{16,24},{20,28},{24,16},{28,20},{1,9},{5... | collective-permute-start | bytes 442376 | tf_op jit(solution)/shard_map/ppermute | solution.py:35
  717.0 8.2 %collective-permute-start.9 = (bf16[192,384]{1,0:T(8,128)(2,1)S(1)}, bf16[192,384]{1,0:T(8,128)(2,1)S(1)}, u32[]{:S(2)}, u32[]{:S(2)}) collective-permute-start(bf16[192,384]{1,0:T(8,128)(2,1)S(1)} %add_convert_fusion.7), channel_id=1, source_target_pairs={{0,16},{4,20},{8,24},{12,28},{16,0},{20,4},{24,8},{28,12},{1,17},{... | collective-permute-start | bytes 442376 | tf_op jit(solution)/shard_map/ppermute | solution.py:35
  723.1 6.8 collective-permute-start.14
  724.2 6.8 collective-permute-start.22
  725.3 9.9 %collective-permute-start.10 = (bf16[384,384]{1,0:T(8,128)(2,1)S(1)}, bf16[384,384]{1,0:T(8,128)(2,1)S(1)}, u32[]{:S(2)}, u32[]{:S(2)}) collective-permute-start(bf16[384,384]{1,0:T(8,128)(2,1)S(1)} %maximum_select_fusion.15), channel_id=1, source_target_pairs={{0,8},{4,12},{8,0},{12,4},{16,24},{20,28},{24,16},{28,20},{1,9},{5... | collective-permute-start | bytes 884744 | tf_op jit(solution)/shard_map/ppermute | solution.py:35
  729.9 6.8 collective-permute-start.15
  731.1 14.9 %collective-permute-start.23 = (bf16[192,1536]{1,0:T(8,128)(2,1)S(1)}, bf16[192,1536]{1,0:T(8,128)(2,1)S(1)}, u32[]{:S(2)}, u32[]{:S(2)}) collective-permute-start(bf16[192,1536]{1,0:T(8,128)(2,1)S(1)} %maximum_select_fusion.14), channel_id=1, source_target_pairs={{0,4},{4,0},{8,12},{12,8},{16,20},{20,16},{24,28},{28,24},{1,5},{5... | collective-permute-start | bytes 1769480 | tf_op jit(solution)/shard_map/ppermute | solution.py:35
  735.4 12.4 %collective-permute-start.11 = (bf16[768,384]{1,0:T(8,128)(2,1)S(1)}, bf16[768,384]{1,0:T(8,128)(2,1)S(1)}, u32[]{:S(2)}, u32[]{:S(2)}) collective-permute-start(bf16[768,384]{1,0:T(8,128)(2,1)S(1)} %maximum_select_fusion.12), channel_id=1, source_target_pairs={{0,4},{4,0},{8,12},{12,8},{16,20},{20,16},{24,28},{28,24},{1,5},{5... | collective-permute-start | bytes 1769480 | tf_op jit(solution)/shard_map/ppermute | solution.py:35
  736.8 8.2 %collective-permute-start.16 = (bf16[384,384]{1,0:T(8,128)(2,1)S(1)}, bf16[384,384]{1,0:T(8,128)(2,1)S(1)}, u32[]{:S(2)}, u32[]{:S(2)}) collective-permute-start(bf16[384,384]{1,0:T(8,128)(2,1)S(1)} %maximum_select_fusion.16), channel_id=1, source_target_pairs={{0,16},{4,20},{8,24},{12,28},{16,0},{20,4},{24,8},{28,12},{1,17},{... | collective-permute-start | bytes 884744 | tf_op jit(solution)/shard_map/ppermute | solution.py:35
  746.1 5.5 collective-permute-start.17
  751.5 3.7 collective-permute-start.42
  755.2 10.5 %collective-permute-start.43 = (f32[1,1536]{1,0:T(1,128)S(1)}, f32[1,1536]{1,0:T(1,128)S(1)}, u32[]{:S(2)}, u32[]{:S(2)}) collective-permute-start(f32[1,1536]{1,0:T(1,128)S(1)} %reshape_add_fusion.1), channel_id=1, source_target_pairs={{0,2},{1,3},{2,0},{3,1},{4,6},{5,7},{6,4},{7,5},{8,10},{9,11},{10,... | collective-permute-start | bytes 18440 | tf_op jit(solution)/shard_map/ppermute | solution.py:35
  765.7 3.2 collective-permute-start.44
  769.0 3.7 collective-permute-start.45
  772.7 3.7 collective-permute-start.46
  (44 other events, 212.0 us)
Sparse Core Ops, SparseCore 0:
  12.1 66.1 all-gather.4
  134.2 84.2 reduce-scatter.4
  222.8 63.3 all-gather.6
  288.2 62.0 all-gather.8
  368.4 59.0 reduce-scatter.6
  433.2 63.3 all-gather.10
  589.5 73.3 reduce-scatter.10
  689.1 58.8 reduce-scatter.8

commit v2 on v1

--- a/solution.py
+++ b/solution.py
@@ -8,14 +8,14 @@
 from jax.experimental.pallas import tpu as pltpu
 from jax.sharding import PartitionSpec as P
 
-QUERY_HEADS = 16
-KEY_VALUE_HEADS = 8
+
 HEAD_SIZE = 96
 LONGEST_DOCUMENT = 2048
 
 LANES = 128
 HALF_LANES = LANES // 2
 FAR = -1e30
+
 
 epsilon = 1e-05
 rope_base = 100000.0
@@ -180,7 +180,7 @@
     log_ref[0, 0] = top[...] * factor + jnp.log2(total[...])
 
 
-def window_specs(tiles, stretch, first_column):
+def window_specs(stretch, first_column):
     return [
         pl.BlockSpec((stretch, LANES), lambda g, i, *s, c=c: (0, c + g)) for c in first_column
     ]
@@ -203,8 +203,8 @@
             pl.BlockSpec((rows, group * LANES), lambda g, i, *s: (i, g)),
             pl.BlockSpec((1, 1, rows), lambda g, i, *s: (i, 0, 0)),
         ]
-        + window_specs(tiles, stretch, key_columns)
-        + window_specs(tiles, stretch, value_columns),
+        + window_specs(stretch, key_columns)
+        + window_specs(stretch, value_columns),
         out_specs=[
             pl.BlockSpec((rows, group * LANES), lambda g, i, *s: (i, g)),
             pl.BlockSpec((1, 1, 1, pairs), lambda g, i, *s: (g, i, 0, 0)),
@@ -232,10 +232,12 @@
     )(low, queries_joined, firsts, *arrays, *arrays)
 
 
-def attend_back_kernel(tiles, group, factor, scale, low_ref, query_ref, first_ref, *refs):
-    mixed_ref, grad_ref, log_ref, cosine_ref, sine_ref = refs[:5]
-    keys = refs[5 : 5 + tiles]
-    values = refs[5 + tiles : 5 + 2 * tiles]
+def attend_back_kernel(tiles, chunks, group, factor, scale, low_ref, query_ref, first_ref, *refs):
+    mixed_ref, log_ref, cosine_ref, sine_ref = refs[:4]
+    grad_refs = refs[4 : 4 + chunks]
+    refs = refs[4 + chunks :]
+    keys = refs[:tiles]
+    values = refs[tiles : 2 * tiles]
     (
         query_out,
         key_out,
@@ -244,7 +246,7 @@
         value_window,
         key_turned,
         query_total,
-    ) = refs[5 + 2 * tiles :]
+    ) = refs[2 * tiles :]
     query_block = pl.program_id(1)
     rows = query_ref.shape[0]
     stretch = keys[0].shape[0]
@@ -264,7 +266,9 @@
 
     offset = (tiles - 1) * stretch
     query = pair_rows(query_ref, group)
-    grad = pair_rows(grad_ref, group)
+    grad = jnp.concatenate(
+        [ref[:, h * LANES : (h + 1) * LANES] for h in range(group) for ref in grad_refs], axis=0
+    )
     mixed = pair_rows(mixed_ref, group)
     inner = jnp.sum((grad.astype(f32) * mixed.astype(f32)).T, axis=0, keepdims=True)
     log_total = log_ref[0, 0]
@@ -307,6 +311,7 @@
     blocks = stretch // rows
     pairs = group * rows
     window_tiles = tiles * stretch // tile_rows
+    chunks = len(grads)
     scale = HEAD_SIZE ** (-0.5)
     factor = scale * math.log2(math.e)
     key_columns = [at for _, at in windows]
@@ -322,13 +327,13 @@
             heads_spec,
             pl.BlockSpec((1, 1, rows), lambda g, i, *s: (i, 0, 0)),
             heads_spec,
-            heads_spec,
             pl.BlockSpec((1, 1, 1, pairs), lambda g, i, *s: (g, i, 0, 0)),
             table_spec,
             table_spec,
         ]
-        + window_specs(tiles, stretch, key_columns)
-        + window_specs(tiles, stretch, value_columns),
+        + [pl.BlockSpec((rows // chunks, group * LANES), lambda g, i, *s: (i, g))] * chunks
+        + window_specs(stretch, key_columns)
+        + window_specs(stretch, value_columns),
         out_specs=[heads_spec, total_spec, total_spec],
         scratch_shapes=[
             pltpu.VMEM((window_tiles, tile_rows, LANES), bf16),
@@ -339,7 +344,7 @@
     )
     work = stretch * stretch * kv_heads * group
     return pl.pallas_call(
-        functools.partial(attend_back_kernel, tiles, group, factor, scale),
+        functools.partial(attend_back_kernel, tiles, chunks, group, factor, scale),
         grid_spec=grid_spec,
         out_shape=[
             jax.ShapeDtypeStruct((stretch, kv_heads * group * LANES), bf16),
@@ -350,7 +355,7 @@
             flops=40 * LANES * work, bytes_accessed=16 * stretch * stretch, transcendentals=work
         ),
         name="attend_back",
-    )(low, queries_joined, firsts, mixed, grads, logs, cosine, sine, *arrays, *arrays)
+    )(low, queries_joined, firsts, mixed, logs, cosine, sine, *grads, *arrays, *arrays)
 
 
 def gather_back_kernel(kv_heads, parts, key_ref, value_ref, cosine_ref, sine_ref, *refs):
@@ -383,37 +388,45 @@
     )(key_totals, value_totals, cosine, sine, *flat)
 
 
-def product_over(left, right, axis, order):
-    count = lax.axis_size(axis)
-    index = lax.axis_index(axis)
-    size = left.shape[1] // 2
-
-    def times(offset):
-        part = lax.dynamic_slice_in_dim(left, offset, size, 1)
-        return jnp.dot(part.T, right, preferred_element_type=f32)
-
-    kept = None
-    for place in order:
-        bit = (index >> place) & 1
-        if kept is None:
-            sent = times((1 - bit) * size).astype(bf16)
-            got = exchange(sent, axis, 1 << place)
-            kept = times(bit * size) + got.astype(f32)
-        else:
+class SharedProduct:
+
+    def __init__(self, left, right, axis, order):
+        self.left, self.right, self.axis, self.order = left, right, axis, order
+        self.size = left.shape[1] // 2
+        self.sent = self.times(0, True).astype(bf16)
+
+    def bit(self, place):
+        return (lax.axis_index(self.axis) >> place) & 1
+
+    def times(self, place, other):
+        bit = self.bit(self.order[place])
+        offset = ((1 - bit) if other else bit) * self.size
+        part = lax.dynamic_slice_in_dim(self.left, offset, self.size, 1)
+        return jnp.dot(part.T, self.right, preferred_element_type=f32)
+
+    def meet(self):
+        got = exchange(self.sent, self.axis, 1 << self.order[0])
+        self.kept = self.times(0, False) + got.astype(f32)
+        return self.kept
+
+    def finish(self):
+        axis, kept, size = self.axis, self.kept, self.size
+        for place in self.order[1:]:
+            bit = self.bit(place)
             size //= 2
             sent = lax.dynamic_slice_in_dim(kept, (1 - bit) * size, size, 0).astype(bf16)
             got = exchange(sent, axis, 1 << place)
             kept = lax.dynamic_slice_in_dim(kept, bit * size, size, 0) + got.astype(f32)
-    whole = kept.astype(bf16)
-    for place in reversed(order):
-        bit = (index >> place) & 1
-        got = exchange(whole, axis, 1 << place)
-        whole = jnp.where(
-            bit == 1,
-            jnp.concatenate([got, whole], axis=0),
-            jnp.concatenate([whole, got], axis=0),
-        )
-    return whole.astype(f32)
+        whole = kept.astype(bf16)
+        for place in reversed(self.order):
+            bit = self.bit(place)
+            got = exchange(whole, axis, 1 << place)
+            whole = jnp.where(
+                bit == 1,
+                jnp.concatenate([got, whole], axis=0),
+                jnp.concatenate([whole, got], axis=0),
+            )
+        return whole.astype(f32)
 
 
 def sum_everywhere(value, axes):
@@ -430,6 +443,33 @@
     return lax.psum_scatter(
         product.astype(bf16), "tensor", scatter_dimension=0, tiled=True
     ).astype(f32)
+
+
+def chain_scatter(product, axis, fillers=()):
+    count = lax.axis_size(axis)
+    index = lax.axis_index(axis)
+    rows = product.shape[0] // count
+
+    def piece(offset):
+        start = lax.rem(index + offset, count) * rows
+        return lax.dynamic_slice_in_dim(product, start, rows, 0).astype(f32)
+
+    right = left = None
+    for step in range(1, count):
+        to_right = piece((count - step) % count)
+        to_left = piece(step % count)
+        if right is not None:
+            to_right = to_right + right.astype(f32)
+            to_left = to_left + left.astype(f32)
+        others = fillers[step - 2] if 0 <= step - 2 < len(fillers) else ()
+        to_right, to_left = lax.optimization_barrier(
+            (to_right.astype(bf16), to_left.astype(bf16)) + tuple(others)
+        )[:2]
+        right = lax.ppermute(to_right, axis, [(i, i + 1) for i in range(min(step, count - 1))])
+        left = lax.ppermute(
+            to_left, axis, [(i, i - 1) for i in range(max(count - step, 1), count)]
+        )
+    return piece(0) + right.astype(f32) + left.astype(f32)
 
 
 def gather_rows(rows):
@@ -459,11 +499,24 @@
     heads = w_query.shape[1] // HEAD_SIZE
     kv_heads = key_weight.shape[1] // HEAD_SIZE
     group = heads // kv_heads
-    rows = min(256, stretch)
+    rows = block_input.shape[0]
     tile_rows = min(512, stretch)
     blocks = stretch // rows
+    chunks = 2
+    part_rows = rows // chunks
     places = list(range((lax.axis_size("dp") - 1).bit_length()))
     crossed = places[:1] + places[:0:-1]
+
+    def own_parts(value):
+        return [value[c * part_rows : (c + 1) * part_rows] for c in range(chunks)]
+
+    def whole_parts(value):
+        cut = value.reshape(blocks, chunks, part_rows, value.shape[1])
+        return [cut[:, c].reshape(blocks * part_rows, value.shape[1]) for c in range(chunks)]
+
+    def whole_order(parts):
+        cut = [part.reshape(blocks, 1, part_rows, part.shape[1]) for part in parts]
+        return jnp.concatenate(cut, axis=1).reshape(stretch, parts[0].shape[1])
 
     normed_own, inv_rms_attn = normalize(block_input, attn_gain)
     attention_normed = gather_rows(normed_own)
@@ -489,45 +542,93 @@
     windows = windows + [(joined, heads)]
     attended, logs = attend(joined, windows, firsts, low, kv_heads, group, rows, tile_rows)
 
-    residual = block_input + scatter_sum(
-        jnp.dot(attended, w_out_spread, preferred_element_type=f32)
-    )
-    mlp_normed_own, inv_rms_mlp = normalize(residual, mlp_gain)
-    normed_mlp = gather_rows(mlp_normed_own)
-    gate_pre = jnp.dot(normed_mlp, w_gate, preferred_element_type=f32)
-    up_proj = jnp.dot(normed_mlp, w_up, preferred_element_type=f32)
-    sigmoid_gate = jax.nn.sigmoid(gate_pre)
-    silu_gate = gate_pre * sigmoid_gate
-    hidden = (silu_gate * up_proj).astype(bf16)
-    hidden_grad = jnp.dot(out_low, w_down.T, preferred_element_type=f32)
-    gate_grad = (
-        hidden_grad * up_proj * sigmoid_gate * (1.0 + gate_pre * (1.0 - sigmoid_gate))
-    ).astype(bf16)
-    up_grad = (hidden_grad * silu_gate).astype(bf16)
-    mlp_normed_grad = scatter_sum(
-        jnp.dot(gate_grad, w_gate.T, preferred_element_type=f32)
-        + jnp.dot(up_grad, w_up.T, preferred_element_type=f32)
-    )
-    residual_part = normalize_back(residual, inv_rms_mlp, mlp_gain, mlp_normed_grad)
-    residual_grad = out_grad + residual_part
-    residual_low = gather_rows(residual_grad.astype(bf16))
+    out_parts = whole_parts(out_low)
+    mixed_product = jnp.dot(attended, w_out_spread, preferred_element_type=f32).astype(bf16)
+    residuals, inv_rms_mlps, normed_mlps, c_normed = [], [], [], []
+    for part, product in zip(own_parts(block_input), whole_parts(mixed_product)):
+        if c_normed:
+            product = after(product, c_normed[-1])
+        residual = part + chain_scatter(product, "tensor")
+        mlp_normed_own, inv_rms_mlp = normalize(residual, mlp_gain)
+        c_normed.append(mlp_normed_own)
+        residuals.append(residual)
+        inv_rms_mlps.append(inv_rms_mlp)
+        normed_mlps.append(gather_rows(mlp_normed_own))
+
+    hiddens, gate_grads, up_grads, residual_grads, residual_lows = [], [], [], [], []
+    own_lows = []
+    gate_pres = [jnp.dot(part, w_gate, preferred_element_type=f32) for part in normed_mlps]
+    up_projs = [jnp.dot(part, w_up, preferred_element_type=f32) for part in normed_mlps]
+    mlp_gain_part = 0.0
+    for c in range(chunks):
+        gate_pre, up_proj = gate_pres[c], up_projs[c]
+        sigmoid_gate = jax.nn.sigmoid(gate_pre)
+        silu_gate = gate_pre * sigmoid_gate
+        hiddens.append((silu_gate * up_proj).astype(bf16))
+        hidden_grad = jnp.dot(out_parts[c], w_down.T, preferred_element_type=f32)
+        gate_grad = (
+            hidden_grad * up_proj * sigmoid_gate * (1.0 + gate_pre * (1.0 - sigmoid_gate))
+        ).astype(bf16)
+        up_grad = (hidden_grad * silu_gate).astype(bf16)
+        gate_grads.append(gate_grad)
+        up_grads.append(up_grad)
+        product = (
+            jnp.dot(gate_grad, w_gate.T, preferred_element_type=f32)
+            + jnp.dot(up_grad, w_up.T, preferred_element_type=f32)
+        ).astype(bf16)
+        fillers = ()
+        if c + 1 < chunks:
+            product = after(product, c_normed[c + 1])
+            fillers = ((), (gate_pres[c + 1], up_projs[c + 1]))
+        else:
+            normed_joined = jnp.concatenate(normed_mlps, axis=0)
+            shared = [
+                SharedProduct(normed_joined, jnp.concatenate(gate_grads, axis=0), "dp", places),
+                SharedProduct(normed_joined, jnp.concatenate(up_grads, axis=0), "dp", crossed),
+                SharedProduct(
+                    jnp.concatenate(hiddens, axis=0), jnp.concatenate(out_parts, axis=0),
+                    "dp", places,
+                ),
+            ]
+            fillers = ([p.sent for p in shared], [p.meet() for p in shared])
+        if c > 0:
+            product = after(product, own_lows[-1])
+        mlp_normed_grad = chain_scatter(product, "tensor", fillers)
+        residual_part = normalize_back(residuals[c], inv_rms_mlps[c], mlp_gain, mlp_normed_grad)
+        residual_grad = own_parts(out_grad)[c] + residual_part
+        residual_grads.append(residual_grad)
+        own_lows.append(residual_grad.astype(bf16))
+        residual_lows.append(gather_rows(own_lows[-1]))
+        mlp_gain_part = mlp_gain_part + jnp.sum(
+            mlp_normed_grad * residuals[c] * inv_rms_mlps[c], axis=0, keepdims=True
+        )
+
+    grad_gate, grad_up, grad_down = [p.finish() for p in shared]
+    grad_mlp_gain = sum_everywhere(mlp_gain_part, ("tensor", "dp"))[0]
 
     down_product = after(
-        jnp.dot(hidden, w_down, preferred_element_type=f32).astype(bf16), residual_low
-    )
-    block_output = residual + scatter_sum(down_product)
-
-    grad_gate = product_over(normed_mlp, gate_grad, "dp", places)
-    grad_up = product_over(normed_mlp, up_grad, "dp", crossed)
-    grad_down = product_over(hidden, out_low, "dp", places)
-
-    attended_plain = jnp.dot(attended, query_spread.T, preferred_element_type=bf16)
-    grad_out = product_over(attended_plain, residual_low, "dp", crossed)
-    attended_gradient = jnp.dot(residual_low, w_out_spread.T, preferred_element_type=f32).astype(
-        bf16
-    )
+        whole_order(
+            [jnp.dot(h, w_down, preferred_element_type=f32).astype(bf16) for h in hiddens]
+        ),
+        *residual_lows,
+    )
+    block_scattered = scatter_sum(down_product)
+    block_output = jnp.concatenate(residuals, axis=0) + block_scattered
+
+    attended_plain = jnp.concatenate(
+        whole_parts(jnp.dot(attended, query_spread.T, preferred_element_type=bf16)), axis=0
+    )
+    out_shared = SharedProduct(
+        attended_plain, jnp.concatenate(residual_lows, axis=0), "dp", crossed
+    )
+    out_shared.meet()
+    grad_out = out_shared.finish()
+    attended_gradients = [
+        jnp.dot(low_rows, w_out_spread.T, preferred_element_type=f32).astype(bf16)
+        for low_rows in residual_lows
+    ]
     query_grad, key_totals, value_totals = attend_back(
-        joined, windows, firsts, low, attended, attended_gradient, logs, cosine, sine,
+        joined, windows, firsts, low, attended, attended_gradients, logs, cosine, sine,
         kv_heads, group, rows, tile_rows,
     )
     received = []
@@ -543,23 +644,34 @@
         key_totals, value_totals, received, cosine, sine, kv_heads, stretch, rows
     )
     split = heads * LANES
-    attn_normed_part = jnp.dot(
-        query_grad, w_joined[:, :split].T, preferred_element_type=f32
-    ) + jnp.dot(key_value_grad, w_joined[:, split:].T, preferred_element_type=f32)
-    attn_normed_grad = scatter_sum(attn_normed_part)
-    input_part = normalize_back(block_input, inv_rms_attn, attn_gain, attn_normed_grad)
-    input_grad = residual_grad + input_part
-
+    attn_normed_part = (
+        jnp.dot(query_grad, w_joined[:, :split].T, preferred_element_type=f32)
+        + jnp.dot(key_value_grad, w_joined[:, split:].T, preferred_element_type=f32)
+    ).astype(bf16)
     query_plain = jnp.dot(query_grad, query_spread.T, preferred_element_type=bf16)
     kv_plain = jnp.dot(key_value_grad, kv_spread.T, preferred_element_type=bf16)
-    grad_query = product_over(attention_normed, query_plain, "dp", places)
-    grad_key_value = product_over(attention_normed, kv_plain, "dp", crossed)
+    query_shared = SharedProduct(attention_normed, query_plain, "dp", places)
+    kv_shared = SharedProduct(attention_normed, kv_plain, "dp", crossed)
+    attn_gain_part = (
+        jnp.sum(
+            attn_normed_part.astype(f32) * attention_normed.astype(f32), axis=0, keepdims=True
+        )
+        / attn_gain
+    )
+    attn_normed_grad = chain_scatter(
+        attn_normed_part, "tensor",
+        (
+            [query_shared.sent, kv_shared.sent, attn_gain_part],
+            [query_shared.meet(), kv_shared.meet()],
+        ),
+    )
+    input_part = normalize_back(block_input, inv_rms_attn, attn_gain, attn_normed_grad)
+    input_grad = jnp.concatenate(residual_grads, axis=0) + input_part
+    grad_query = query_shared.finish()
+    grad_key_value = kv_shared.finish()
     grad_key = grad_key_value[:, : kv_heads * HEAD_SIZE]
     grad_value = grad_key_value[:, kv_heads * HEAD_SIZE :]
 
-    mlp_gain_part = jnp.sum(mlp_normed_grad * residual * inv_rms_mlp, axis=0, keepdims=True)
-    attn_gain_part = jnp.sum(attn_normed_grad * block_input * inv_rms_attn, axis=0, keepdims=True)
-    grad_mlp_gain = sum_everywhere(mlp_gain_part, ("tensor", "dp"))[0]
     grad_attn_gain = sum_everywhere(attn_gain_part, ("tensor", "dp"))[0]
     return (
         block_output,
@@ -604,6 +716,7 @@
         P(),
         P(),
     )
+
     return jax.shard_map(
         per_device, mesh=mesh, in_specs=in_specs, out_specs=out_specs, check_vma=False
     )

time: 785 us -> 820 us (1.045); the launches traced: 784 us -> 809 us
  starting transfers between devices: 80 us -> 175 us
  waiting for transfers between devices: 443 us -> 357 us
  local copies, waits for them, and re-layouts: 24 us -> 41.4 us
  matrix products: 105 us -> 91.8 us
  other arithmetic: 71.7 us -> 82.9 us
    reduce_scatter x4 -> x1, waiting for transfers between devices: 144 us -> 0.01 us  [scatter_sum(): lax.psum_scatter(product.astype(bf16), 'tensor', scatter_dimension=0, til...]
    ppermute x0 -> x30, starting transfers between devices: none -> 103 us  [the longest x15 87.9 us: chain_scatter(): lax.ppermute(to_right, axis, [(i, i + 1) for i in range(min(step, count -...]
    ppermute x0 -> x30, waiting for transfers between devices: none -> 76.6 us  [the longest x15 49.5 us: chain_scatter(): lax.ppermute(to_right, axis, [(i, i + 1) for i in range(min(step, count -...]
    all_gather x4 -> x6, waiting for transfers between devices: 193 us -> 142 us  [gather_rows(): return lax.all_gather(rows, 'tensor', axis=0, tiled=True)]
    ppermute x46, waiting for transfers between devices: 53 us -> 99.7 us  [exchange(): return lax.ppermute(value, axis, [(i, i ^ distance) for i in range(count)])]
    ppermute x6, waiting for transfers between devices: 53.1 us -> 38.4 us  [from_behind(): lax.ppermute(value, axis, [(source, source + steps) for source in range(l...]
    convert_element_type x13 -> x29, other arithmetic: 25.1 us -> 36.7 us  [the longest x6 17.1 us: finish(): return whole.astype(f32)]
    dot_general x18 -> x23, matrix products: 74.7 us -> 64.6 us  [the longest x12 31.9 us: times(): return jnp.dot(part.T, self.right, preferred_element_type=f32)]
  transfers between devices with their start and end apart: 60 -> 89, of which waited for: 28 -> 44; matrix products, arithmetic and copies ran while one was open for 20% -> 20% of each run, Pallas kernels for 3% -> 3%
where the time goes in v2:
time: 820 us; the launch traced here: 809 us
  waiting for transfers between devices  357 us (44%)
  starting transfers between devices  175 us (21%)
  matrix products  91.8 us (11%)
  other arithmetic  82.9 us (10%)
  Pallas kernels  45.2 us (6%)
  local copies, waits for them, and re-layouts  41.4 us (5%)
  between operations  16.2 us (2%)
    all_gather x6, waiting for transfers between devices, gather_rows(): return lax.all_gather(rows, 'tensor', axis=0, tiled=True)  142 us
    ppermute x46, waiting for transfers between devices, exchange(): return lax.ppermute(value, axis, [(i, i ^ distance) for i in range(count)])  99.7 us
    ppermute x15, starting transfers between devices, chain_scatter(): lax.ppermute(to_right, axis, [(i, i + 1) for i in range(min(step, count -...  87.9 us
    ppermute x46, starting transfers between devices, exchange(): return lax.ppermute(value, axis, [(i, i ^ distance) for i in range(count)])  59.1 us
    ppermute x15, waiting for transfers between devices, chain_scatter(): lax.ppermute(to_right, axis, [(i, i + 1) for i in range(min(step, count -...  49.5 us
    ppermute x6, waiting for transfers between devices, from_behind(): lax.ppermute(value, axis, [(source, source + steps) for source in range(l...  38.4 us
    dot_general x12, matrix products, times(): return jnp.dot(part.T, self.right, preferred_element_type=f32)  31.9 us
    ppermute x15, waiting for transfers between devices, chain_scatter(): lax.ppermute(to_left, axis, [(i, i - 1) for i in range(max(count - step,...  27.1 us
  transfers between devices with their start and end apart: 89, of which 44 were waited for; matrix products, arithmetic and copies ran while one was open for 20% of the time, Pallas kernels for 3%

profile of v2, /device:TPU:0, one launch (start us, length us, event | category | flops | bytes accessed | tf_op | source)
XLA Modules:
  0.0 809.3 jit_solution(18341030531093193280)
XLA Ops:
  19.7 6.3 fusion.3.weight_ref
  26.0 52.3 %all-gather.7.cloned.1.call-done.rows_ref = bf16[1024,1536]{1,0:T(8,128)(2,1)} async-done(((bf16[256,1536]{1,0:T(8,128)(2,1)}), bf16[1024,1536]{1,0:T(8,128)(2,1)}) %all-gather.7.cloned.1.call-update) | async-done | bytes 3145744 | tf_op jit(solution)/shard_map/all_gather | solution.py:476
  78.3 7.7 project.1.query_ref.refs_2_.refs_5_.refs_8_.refs_11_
  88.3 4.4 collective-permute-start
  95.7 3.5 fusion.62
  99.2 16.3 %collective-permute-done.refs_0_.refs_3_.refs_6_.refs_9_ = bf16[1024,512]{1,0:T(8,128)(2,1)} collective-permute-done((bf16[1024,512]{1,0:T(8,128)(2,1)}, bf16[1024,512]{1,0:T(8,128)(2,1)}, u32[]{:S(2)}, u32[]{:S(2)}) %collective-permute-start) | collective-permute-done | bytes 1048608 | tf_op jit(solution)/shard_map/ppermute | solution.py:30
  115.5 13.4 %attend.1 = (bf16[1024,512]{1,0:T(8,128)(2,1)}, f32[2,4,1,512]{3,2,1,0:T(1,128)}) custom-call(s32[4]{0:T(128)} %and_select_fusion.low_ref, bf16[1024,1024]{1,0:T(8,128)(2,1)} %project.1.query_ref.refs_2_.refs_5_.refs_8_.refs_11_, s32[4,1,256]{2,1,0:T(1,128)} %bitcast.85, bf16[1024,512]{1,0:T(8,128)(2,1)} %collective-permute-done.refs_0_.refs_3_.refs_6_.refs_9_, ...), custom_call_target="tpu_custom_call" | custom-call | flops 8589934592 | bytes 8388608 | tf_op jit(solution)/shard_map/attend/pallas_call | solution.py:221
  128.9 3.5 convolution_convert_fusion
  139.1 4.5 collective-permute-done.2
  145.0 4.5 collective-permute-start.4
  150.2 4.6 collective-permute-done.4
  158.8 6.9 collective-permute-start.6
  165.7 3.3 collective-permute-done.7
  179.5 4.6 collective-permute-start.8
  184.1 8.5 %collective-permute-done.8 = bf16[128,1536]{1,0:T(8,128)(2,1)S(1)} collective-permute-done((bf16[128,1536]{1,0:T(8,128)(2,1)S(1)}, bf16[128,1536]{1,0:T(8,128)(2,1)S(1)}, u32[]{:S(2)}, u32[]{:S(2)}) %collective-permute-start.8) | collective-permute-done | bytes 393248 | tf_op jit(solution)/shard_map/ppermute | solution.py:468
  193.7 4.4 collective-permute-start.10
  198.8 4.6 collective-permute-done.10
  204.9 7.3 collective-permute-start.12
  212.2 16.9 %collective-permute-done.13 = bf16[128,1536]{1,0:T(8,128)(2,1)S(1)} collective-permute-done((bf16[128,1536]{1,0:T(8,128)(2,1)S(1)}, bf16[128,1536]{1,0:T(8,128)(2,1)S(1)}, u32[]{:S(2)}, u32[]{:S(2)}) %collective-permute-start.13) | collective-permute-done | bytes 393248 | tf_op jit(solution)/shard_map/ppermute | solution.py:469
  232.7 14.3 %all-gather.9.cloned.1.call-done = bf16[512,1536]{1,0:T(8,128)(2,1)} async-done(((bf16[128,1536]{1,0:T(8,128)(2,1)}), bf16[512,1536]{1,0:T(8,128)(2,1)}) %all-gather.9.cloned.1.call-update) | async-done | bytes 1572880 | tf_op jit(solution)/shard_map/all_gather | solution.py:476
  246.9 5.5 fusion.127
  252.4 62.8 %all-gather.13.cloned.1.call-done = bf16[1024,1536]{1,0:T(8,128)(2,1)} async-done(((bf16[256,1536]{1,0:T(8,128)(2,1)}), bf16[1024,1536]{1,0:T(8,128)(2,1)}) %all-gather.13.cloned.1.call-update) | async-done | bytes 3145744 | tf_op jit(solution)/shard_map/all_gather | solution.py:476
  315.2 3.4 fusion.120
  321.2 3.7 multiply_convert_fusion.2
  337.0 5.5 collective-permute-done.14
  344.0 4.5 collective-permute-start.16
  351.5 14.3 %collective-permute-done.16 = bf16[128,1536]{1,0:T(8,128)(2,1)S(1)} collective-permute-done((bf16[128,1536]{1,0:T(8,128)(2,1)S(1)}, bf16[128,1536]{1,0:T(8,128)(2,1)S(1)}, u32[]{:S(2)}, u32[]{:S(2)}) %collective-permute-start.16) | collective-permute-done | bytes 393248 | tf_op jit(solution)/shard_map/ppermute | solution.py:468
  368.5 12.6 %all-gather.11.cloned.1.call-done = bf16[512,1536]{1,0:T(8,128)(2,1)} async-done(((bf16[128,1536]{1,0:T(8,128)(2,1)}), bf16[512,1536]{1,0:T(8,128)(2,1)}) %all-gather.11.cloned.1.call-update) | async-done | bytes 1572880 | tf_op jit(solution)/shard_map/all_gather | solution.py:476
  381.2 3.3 fusion.128
  386.9 3.5 multiply_convert_fusion
  391.7 4.6 collective-permute-start.18
  410.3 3.4 collective-permute-start.20
  413.7 5.0 convolution_convert_fusion.5
  431.3 3.5 collective-permute-done.22
  437.2 3.4 convert_add_fusion.2
  440.8 4.5 convert_add_fusion.1
  445.3 4.4 convert_add_fusion
  451.4 20.5 %collective-permute-start.27 = (bf16[128,1536]{1,0:T(8,128)(2,1)S(1)}, bf16[128,1536]{1,0:T(8,128)(2,1)S(1)}, u32[]{:S(2)}, u32[]{:S(2)}) collective-permute-start(bf16[128,1536]{1,0:T(8,128)(2,1)S(1)} %add_convert_fusion.7), channel_id=1, source_target_pairs={{0,1},{1,2},{2,3},{4,5},{5,6},{6,7},{8,9},{9,10},{10,11},{12,13},{... | collective-permute-start | bytes 1179656 | tf_op jit(solution)/shard_map/ppermute | solution.py:468
  491.9 18.0 %collective-permute-done.80 = f32[1,1536]{1,0:T(1,128)} collective-permute-done((f32[1,1536]{1,0:T(1,128)S(1)}, f32[1,1536]{1,0:T(1,128)}, u32[]{:S(2)}, u32[]{:S(2)}) %collective-permute-start.80) | collective-permute-done | bytes 6176 | tf_op jit(solution)/shard_map/ppermute | solution.py:35
  520.7 5.3 collective-permute-done.58
  528.9 5.6 collective-permute-done.68
  538.0 5.0 collective-permute-done.59
  546.2 5.2 collective-permute-done.69
  557.8 5.3 collective-permute-done.60
  565.0 3.3 maximum_select_fusion.4
  568.3 3.4 collective-permute-done.70
  578.4 19.7 %attend_back.1 = (bf16[1024,512]{1,0:T(8,128)(2,1)}, f32[3072,256]{1,0:T(8,128)}, f32[3072,256]{1,0:T(8,128)}) custom-call(s32[4]{0:T(128)} %and_select_fusion.low_ref, bf16[1024,1024]{1,0:T(8,128)(2,1)} %project.1.query_ref.refs_2_.refs_5_.refs_8_.refs_11_, s32[4,1,256]{2,1,0:T(1,128)} %bitcast.86, bf16[1024,512]{1,0:T(8,128)(2,1)} %get-tuple-element.51.refs_0_, ...), custom_call_target="tpu_custom_call" | custom-call | flops 21474836480 | bytes 16777216 | tf_op jit(solution)/shard_map/attend_back/pallas_call | solution.py:346
  609.1 6.5 collective-permute-done.29.refs_0_
  615.5 11.0 %collective-permute-start.66 = (bf16[768,1024]{1,0:T(8,128)(2,1)}, bf16[768,1024]{1,0:T(8,128)(2,1)}, u32[]{:S(2)}, u32[]{:S(2)}) collective-permute-start(bf16[768,1024]{1,0:T(8,128)(2,1)} %maximum_select_fusion.4), channel_id=1, source_target_pairs={{0,4},{4,0},{8,12},{12,8},{16,20},{20,16},{24,28},{28,24},{1,5},{5... | collective-permute-start | bytes 4718600 | tf_op jit(solution)/shard_map/ppermute | solution.py:35
  626.6 10.9 %collective-permute-start.37 = (bf16[768,384]{1,0:T(8,128)(2,1)}, bf16[768,384]{1,0:T(8,128)(2,1)}, u32[]{:S(2)}, u32[]{:S(2)}) collective-permute-start(bf16[768,384]{1,0:T(8,128)(2,1)} %fusion.38), channel_id=1, source_target_pairs={{0,4},{4,0},{8,12},{12,8},{16,20},{20,16},{24,28},{28,24},{1,5},{5... | collective-permute-start | bytes 1769480 | tf_op jit(solution)/shard_map/ppermute | solution.py:35
  637.5 10.0 %collective-permute-done.31.refs_2_ = bf16[1024,256]{1,0:T(8,128)(2,1)} collective-permute-done((bf16[1024,256]{1,0:T(8,128)(2,1)S(1)}, bf16[1024,256]{1,0:T(8,128)(2,1)}, u32[]{:S(2)}, u32[]{:S(2)}) %collective-permute-start.31) | collective-permute-done | bytes 524320 | tf_op jit(solution)/shard_map/ppermute | solution.py:30
  647.5 5.6 collective-permute-done.32.refs_3_
  653.2 4.4 gather_back.1
  684.7 7.6 collective-permute-done.41
  692.4 8.0 collective-permute-done.52
  700.8 4.8 collective-permute-done.42
  706.1 4.5 collective-permute-done.53
  716.2 5.1 fusion
  721.9 5.3 fusion.1
  730.6 6.1 collective-permute-done.46
  745.6 3.7 collective-permute-done.48
  763.4 15.4 %collective-permute-start.39 = (bf16[256,1536]{1,0:T(8,128)(2,1)}, bf16[256,1536]{1,0:T(8,128)(2,1)}, u32[]{:S(2)}, u32[]{:S(2)}) collective-permute-start(bf16[256,1536]{1,0:T(8,128)(2,1)} %add_convert_fusion.2), channel_id=1, source_target_pairs={{0,1},{1,2},{2,3},{4,5},{5,6},{6,7},{8,9},{9,10},{10,11},{12,13},{... | collective-permute-start | bytes 2359304 | tf_op jit(solution)/shard_map/ppermute | solution.py:468
  785.7 6.8 collective-permute-done.40
  795.8 3.5 maximum_add_fusion.1
  (479 shorter events, 242.8 us)
Async XLA Ops:
  7.2 71.1 %all-gather.7.cloned.1.call-start = ((), (), s32[]{:S(2)}) async-start(), calls=%async_computation.1 | async-start | bytes 3932160 | tf_op jit(solution)/shard_map/all_gather | solution.py:476
  12.0 235.0 %all-gather.9.cloned.1.call-start = ((), (), s32[]{:S(2)}) async-start(), calls=%async_computation.2 | async-start | bytes 1966080 | tf_op jit(solution)/shard_map/all_gather | solution.py:476
  88.3 27.2 %collective-permute-start = (bf16[1024,512]{1,0:T(8,128)(2,1)}, bf16[1024,512]{1,0:T(8,128)(2,1)}, u32[]{:S(2)}, u32[]{:S(2)}) collective-permute-start(bf16[1024,512]{1,0:T(8,128)(2,1)} %slice.80), channel_id=1, source_target_pairs={{0,8},{4,12},{8,16},{12,20},{16,24},{20,28},{1,9},{5,13},{9,17},{1... | collective-permute-start | bytes 3145736 | tf_op jit(solution)/shard_map/ppermute | solution.py:30
  92.7 22.8 %collective-permute-start.1 = (bf16[1024,512]{1,0:T(8,128)(2,1)}, bf16[1024,512]{1,0:T(8,128)(2,1)}, u32[]{:S(2)}, u32[]{:S(2)}) collective-permute-start(bf16[1024,512]{1,0:T(8,128)(2,1)} %slice.80), channel_id=1, source_target_pairs={{0,4},{4,8},{8,12},{12,16},{16,20},{20,24},{24,28},{1,5},{5,9},{9,... | collective-permute-start | bytes 3145736 | tf_op jit(solution)/shard_map/ppermute | solution.py:30
  145.0 9.8 %collective-permute-start.4 = (bf16[128,1536]{1,0:T(8,128)(2,1)S(1)}, bf16[128,1536]{1,0:T(8,128)(2,1)S(1)}, u32[]{:S(2)}, u32[]{:S(2)}) collective-permute-start(bf16[128,1536]{1,0:T(8,128)(2,1)S(1)} %get-tuple-element.54), channel_id=1, source_target_pairs={{0,1},{1,2},{4,5},{5,6},{8,9},{9,10},{12,13},{13,14},{16,17},{17,1... | collective-permute-start | bytes 1179656 | tf_op jit(solution)/shard_map/ppermute | solution.py:468
  157.5 11.5 %collective-permute-start.7 = (bf16[128,1536]{1,0:T(8,128)(2,1)}, bf16[128,1536]{1,0:T(8,128)(2,1)S(1)}, u32[]{:S(2)}, u32[]{:S(2)}) collective-permute-start(bf16[128,1536]{1,0:T(8,128)(2,1)} %add_convert_fusion.12), channel_id=1, source_target_pairs={{1,0},{2,1},{3,2},{5,4},{6,5},{7,6},{9,8},{10,9},{11,10},{13,12},{... | collective-permute-start | bytes 1179656 | tf_op jit(solution)/shard_map/ppermute | solution.py:469
  158.8 12.5 %collective-permute-start.6 = (bf16[128,1536]{1,0:T(8,128)(2,1)}, bf16[128,1536]{1,0:T(8,128)(2,1)}, u32[]{:S(2)}, u32[]{:S(2)}) collective-permute-start(bf16[128,1536]{1,0:T(8,128)(2,1)} %add_convert_fusion.13), channel_id=1, source_target_pairs={{0,1},{1,2},{2,3},{4,5},{5,6},{6,7},{8,9},{9,10},{10,11},{12,13},{... | collective-permute-start | bytes 1179656 | tf_op jit(solution)/shard_map/ppermute | solution.py:468
  175.0 140.2 %all-gather.13.cloned.1.call-start = ((), (), s32[]{:S(2)}) async-start(), calls=%async_computation.4 | async-start | bytes 3932160 | tf_op jit(solution)/shard_map/all_gather | solution.py:476
  177.4 203.7 %all-gather.11.cloned.1.call-start = ((), (), s32[]{:S(2)}) async-start(), calls=%async_computation.3 | async-start | bytes 1966080 | tf_op jit(solution)/shard_map/all_gather | solution.py:476
  179.5 13.1 %collective-permute-start.8 = (bf16[128,1536]{1,0:T(8,128)(2,1)S(1)}, bf16[128,1536]{1,0:T(8,128)(2,1)S(1)}, u32[]{:S(2)}, u32[]{:S(2)}) collective-permute-start(bf16[128,1536]{1,0:T(8,128)(2,1)S(1)} %get-tuple-element.59), channel_id=1, source_target_pairs={{0,1},{4,5},{8,9},{12,13},{16,17},{20,21},{24,25},{28,29}} | collective-permute-start | bytes 1179656 | tf_op jit(solution)/shard_map/ppermute | solution.py:468
  193.7 9.7 %collective-permute-start.10 = (bf16[128,1536]{1,0:T(8,128)(2,1)S(1)}, bf16[128,1536]{1,0:T(8,128)(2,1)S(1)}, u32[]{:S(2)}, u32[]{:S(2)}) collective-permute-start(bf16[128,1536]{1,0:T(8,128)(2,1)S(1)} %get-tuple-element.61), channel_id=1, source_target_pairs={{0,1},{1,2},{4,5},{5,6},{8,9},{9,10},{12,13},{13,14},{16,17},{17,1... | collective-permute-start | bytes 1179656 | tf_op jit(solution)/shard_map/ppermute | solution.py:468
  203.6 25.5 %collective-permute-start.13 = (bf16[128,1536]{1,0:T(8,128)(2,1)S(1)}, bf16[128,1536]{1,0:T(8,128)(2,1)S(1)}, u32[]{:S(2)}, u32[]{:S(2)}) collective-permute-start(bf16[128,1536]{1,0:T(8,128)(2,1)S(1)} %add_convert_fusion.10), channel_id=1, source_target_pairs={{1,0},{2,1},{3,2},{5,4},{6,5},{7,6},{9,8},{10,9},{11,10},{13,12},{... | collective-permute-start | bytes 1179656 | tf_op jit(solution)/shard_map/ppermute | solution.py:469
  204.9 24.5 %collective-permute-start.12 = (bf16[128,1536]{1,0:T(8,128)(2,1)S(1)}, bf16[128,1536]{1,0:T(8,128)(2,1)S(1)}, u32[]{:S(2)}, u32[]{:S(2)}) collective-permute-start(bf16[128,1536]{1,0:T(8,128)(2,1)S(1)} %add_convert_fusion.11), channel_id=1, source_target_pairs={{0,1},{1,2},{2,3},{4,5},{5,6},{6,7},{8,9},{9,10},{10,11},{12,13},{... | collective-permute-start | bytes 1179656 | tf_op jit(solution)/shard_map/ppermute | solution.py:468
  332.8 9.8 %collective-permute-start.14 = (bf16[128,1536]{1,0:T(8,128)(2,1)S(1)}, bf16[128,1536]{1,0:T(8,128)(2,1)}, u32[]{:S(2)}, u32[]{:S(2)}) collective-permute-start(bf16[128,1536]{1,0:T(8,128)(2,1)S(1)} %get-tuple-element.67), channel_id=1, source_target_pairs={{0,1},{4,5},{8,9},{12,13},{16,17},{20,21},{24,25},{28,29}} | collective-permute-start | bytes 1179656 | tf_op jit(solution)/shard_map/ppermute | solution.py:468
  334.8 218.4 %all-gather.15.cloned.1.call-start = ((), (), s32[]{:S(2)}) async-start(), calls=%async_computation.5 | async-start | bytes 1966080 | tf_op jit(solution)/shard_map/all_gather | solution.py:476
  344.0 21.8 %collective-permute-start.16 = (bf16[128,1536]{1,0:T(8,128)(2,1)S(1)}, bf16[128,1536]{1,0:T(8,128)(2,1)S(1)}, u32[]{:S(2)}, u32[]{:S(2)}) collective-permute-start(bf16[128,1536]{1,0:T(8,128)(2,1)S(1)} %get-tuple-element.69), channel_id=1, source_target_pairs={{0,1},{1,2},{4,5},{5,6},{8,9},{9,10},{12,13},{13,14},{16,17},{17,1... | collective-permute-start | bytes 1179656 | tf_op jit(solution)/shard_map/ppermute | solution.py:468
  350.7 17.0 %collective-permute-start.17 = (bf16[128,1536]{1,0:T(8,128)(2,1)S(1)}, bf16[128,1536]{1,0:T(8,128)(2,1)S(1)}, u32[]{:S(2)}, u32[]{:S(2)}) collective-permute-start(bf16[128,1536]{1,0:T(8,128)(2,1)S(1)} %get-tuple-element.70), channel_id=1, source_target_pairs={{2,1},{3,2},{6,5},{7,6},{10,9},{11,10},{14,13},{15,14},{18,17},{19... | collective-permute-start | bytes 1179656 | tf_op jit(solution)/shard_map/ppermute | solution.py:469
  390.4 15.0 %collective-permute-start.19 = (bf16[128,1536]{1,0:T(8,128)(2,1)S(1)}, bf16[128,1536]{1,0:T(8,128)(2,1)S(1)}, u32[]{:S(2)}, u32[]{:S(2)}) collective-permute-start(bf16[128,1536]{1,0:T(8,128)(2,1)S(1)} %copy-done.67), channel_id=1, source_target_pairs={{1,0},{2,1},{3,2},{5,4},{6,5},{7,6},{9,8},{10,9},{11,10},{13,12},{... | collective-permute-start | bytes 1179656 | tf_op jit(solution)/shard_map/ppermute | solution.py:469
  391.7 13.7 %collective-permute-start.18 = (bf16[128,1536]{1,0:T(8,128)(2,1)S(1)}, bf16[128,1536]{1,0:T(8,128)(2,1)S(1)}, u32[]{:S(2)}, u32[]{:S(2)}) collective-permute-start(bf16[128,1536]{1,0:T(8,128)(2,1)S(1)} %copy-done.66), channel_id=1, source_target_pairs={{0,1},{1,2},{2,3},{4,5},{5,6},{6,7},{8,9},{9,10},{10,11},{12,13},{... | collective-permute-start | bytes 1179656 | tf_op jit(solution)/shard_map/ppermute | solution.py:468
  409.4 12.9 %collective-permute-start.21 = (bf16[128,1536]{1,0:T(8,128)(2,1)S(1)}, bf16[128,1536]{1,0:T(8,128)(2,1)S(1)}, u32[]{:S(2)}, u32[]{:S(2)}) collective-permute-start(bf16[128,1536]{1,0:T(8,128)(2,1)S(1)} %get-tuple-element.75), channel_id=1, source_target_pairs={{3,2},{7,6},{11,10},{15,14},{19,18},{23,22},{27,26},{31,30}} | collective-permute-start | bytes 1179656 | tf_op jit(solution)/shard_map/ppermute | solution.py:469
  410.3 12.0 %collective-permute-start.20 = (bf16[128,1536]{1,0:T(8,128)(2,1)S(1)}, bf16[128,1536]{1,0:T(8,128)(2,1)S(1)}, u32[]{:S(2)}, u32[]{:S(2)}) collective-permute-start(bf16[128,1536]{1,0:T(8,128)(2,1)S(1)} %get-tuple-element.74), channel_id=1, source_target_pairs={{0,1},{4,5},{8,9},{12,13},{16,17},{20,21},{24,25},{28,29}} | collective-permute-start | bytes 1179656 | tf_op jit(solution)/shard_map/ppermute | solution.py:468
  418.7 18.5 %collective-permute-start.24 = (bf16[768,1024]{1,0:T(8,128)(2,1)}, bf16[768,1024]{1,0:T(8,128)(2,1)}, u32[]{:S(2)}, u32[]{:S(2)}) collective-permute-start(bf16[768,1024]{1,0:T(8,128)(2,1)} %convolution_convert_fusion.6), channel_id=1, source_target_pairs={{0,4},{4,0},{8,12},{12,8},{16,20},{20,16},{24,28},{28,24},{1,5},{5... | collective-permute-start | bytes 4718600 | tf_op jit(solution)/shard_map/ppermute | solution.py:35
  418.7 22.0 %collective-permute-start.25 = (bf16[768,1024]{1,0:T(8,128)(2,1)}, bf16[768,1024]{1,0:T(8,128)(2,1)}, u32[]{:S(2)}, u32[]{:S(2)}) collective-permute-start(bf16[768,1024]{1,0:T(8,128)(2,1)} %convolution_convert_fusion.5), channel_id=1, source_target_pairs={{0,4},{4,0},{8,12},{12,8},{16,20},{20,16},{24,28},{28,24},{1,5},{5... | collective-permute-start | bytes 4718600 | tf_op jit(solution)/shard_map/ppermute | solution.py:35
  424.3 10.5 %collective-permute-start.22 = (bf16[128,1536]{1,0:T(8,128)(2,1)}, bf16[128,1536]{1,0:T(8,128)(2,1)}, u32[]{:S(2)}, u32[]{:S(2)}) collective-permute-start(bf16[128,1536]{1,0:T(8,128)(2,1)} %get-tuple-element.76), channel_id=1, source_target_pairs={{0,1},{1,2},{4,5},{5,6},{8,9},{9,10},{12,13},{13,14},{16,17},{17,1... | collective-permute-start | bytes 1179656 | tf_op jit(solution)/shard_map/ppermute | solution.py:468
  430.4 14.9 %collective-permute-start.26 = (bf16[512,1536]{1,0:T(8,128)(2,1)}, bf16[512,1536]{1,0:T(8,128)(2,1)}, u32[]{:S(2)}, u32[]{:S(2)}) collective-permute-start(bf16[512,1536]{1,0:T(8,128)(2,1)} %convolution_convert_fusion.1), channel_id=1, source_target_pairs={{0,4},{4,0},{8,12},{12,8},{16,20},{20,16},{24,28},{28,24},{1,5},{5... | collective-permute-start | bytes 4718600 | tf_op jit(solution)/shard_map/ppermute | solution.py:35
  430.4 144.3 %all-gather.17.cloned.1.call-start = ((), (), s32[]{:S(2)}) async-start(), calls=%async_computation.6 | async-start | bytes 1966080 | tf_op jit(solution)/shard_map/all_gather | solution.py:476
  449.8 27.7 %collective-permute-start.28 = (bf16[128,1536]{1,0:T(8,128)(2,1)S(1)}, bf16[128,1536]{1,0:T(8,128)(2,1)S(1)}, u32[]{:S(2)}, u32[]{:S(2)}) collective-permute-start(bf16[128,1536]{1,0:T(8,128)(2,1)S(1)} %add_convert_fusion.6), channel_id=1, source_target_pairs={{1,0},{2,1},{3,2},{5,4},{6,5},{7,6},{9,8},{10,9},{11,10},{13,12},{... | collective-permute-start | bytes 1179656 | tf_op jit(solution)/shard_map/ppermute | solution.py:469
  451.4 26.3 %collective-permute-start.27 = (bf16[128,1536]{1,0:T(8,128)(2,1)S(1)}, bf16[128,1536]{1,0:T(8,128)(2,1)S(1)}, u32[]{:S(2)}, u32[]{:S(2)}) collective-permute-start(bf16[128,1536]{1,0:T(8,128)(2,1)S(1)} %add_convert_fusion.7), channel_id=1, source_target_pairs={{0,1},{1,2},{2,3},{4,5},{5,6},{6,7},{8,9},{9,10},{10,11},{12,13},{... | collective-permute-start | bytes 1179656 | tf_op jit(solution)/shard_map/ppermute | solution.py:468
  475.8 36.4 %collective-permute-start.57 = (bf16[384,1024]{1,0:T(8,128)(2,1)}, bf16[384,1024]{1,0:T(8,128)(2,1)}, u32[]{:S(2)}, u32[]{:S(2)}) collective-permute-start(bf16[384,1024]{1,0:T(8,128)(2,1)} %dynamic-slice_convert_fusion.2), channel_id=1, source_target_pairs={{0,8},{4,12},{8,0},{12,4},{16,24},{20,28},{24,16},{28,20},{1,9},{5... | collective-permute-start | bytes 2359304 | tf_op jit(solution)/shard_map/ppermute | solution.py:35
  481.6 33.5 %collective-permute-start.62 = (bf16[384,1024]{1,0:T(8,128)(2,1)}, bf16[384,1024]{1,0:T(8,128)(2,1)}, u32[]{:S(2)}, u32[]{:S(2)}) collective-permute-start(bf16[384,1024]{1,0:T(8,128)(2,1)} %dynamic-slice_convert_fusion.1), channel_id=1, source_target_pairs={{0,16},{4,20},{8,24},{12,28},{16,0},{20,4},{24,8},{28,12},{1,17},{... | collective-permute-start | bytes 2359304 | tf_op jit(solution)/shard_map/ppermute | solution.py:35
  486.3 31.8 %collective-permute-start.67 = (bf16[256,1536]{1,0:T(8,128)(2,1)}, bf16[256,1536]{1,0:T(8,128)(2,1)}, u32[]{:S(2)}, u32[]{:S(2)}) collective-permute-start(bf16[256,1536]{1,0:T(8,128)(2,1)} %dynamic-slice_convert_fusion), channel_id=1, source_target_pairs={{0,8},{4,12},{8,0},{12,4},{16,24},{20,28},{24,16},{28,20},{1,9},{5... | collective-permute-start | bytes 2359304 | tf_op jit(solution)/shard_map/ppermute | solution.py:35
  489.0 20.9 %collective-permute-start.80 = (f32[1,1536]{1,0:T(1,128)S(1)}, f32[1,1536]{1,0:T(1,128)}, u32[]{:S(2)}, u32[]{:S(2)}) collective-permute-start(f32[1,1536]{1,0:T(1,128)S(1)} %add.649), channel_id=1, source_target_pairs={{0,8},{4,12},{8,0},{12,4},{16,24},{20,28},{24,16},{28,20},{1,9},{5... | collective-permute-start | bytes 18440 | tf_op jit(solution)/shard_map/ppermute | solution.py:35
  491.9 307.4 %reduce-scatter.2.cloned.1.call-start = ((), (), s32[]{:S(2)}) async-start(), calls=%async_computation.7 | async-start | bytes 3932160 | tf_op jit(solution)/shard_map/reduce_scatter | solution.py:443
  510.7 26.7 %collective-permute-start.81 = (f32[1,1536]{1,0:T(1,128)S(1)}, f32[1,1536]{1,0:T(1,128)S(1)}, u32[]{:S(2)}, u32[]{:S(2)}) collective-permute-start(f32[1,1536]{1,0:T(1,128)S(1)} %add.650), channel_id=1, source_target_pairs={{0,16},{4,20},{8,24},{12,28},{16,0},{20,4},{24,8},{28,12},{1,17},{... | collective-permute-start | bytes 18440 | tf_op jit(solution)/shard_map/ppermute | solution.py:35
  514.2 11.9 %collective-permute-start.58 = (bf16[192,1024]{1,0:T(8,128)(2,1)S(1)}, bf16[192,1024]{1,0:T(8,128)(2,1)S(1)}, u32[]{:S(2)}, u32[]{:S(2)}) collective-permute-start(bf16[192,1024]{1,0:T(8,128)(2,1)S(1)} %dynamic-slice_convert_fusion.5), channel_id=1, source_target_pairs={{0,16},{4,20},{8,24},{12,28},{16,0},{20,4},{24,8},{28,12},{1,17},{... | collective-permute-start | bytes 1179656 | tf_op jit(solution)/shard_map/ppermute | solution.py:35
  516.6 10.4 %collective-permute-start.63 = (bf16[192,1024]{1,0:T(8,128)(2,1)S(1)}, bf16[192,1024]{1,0:T(8,128)(2,1)S(1)}, u32[]{:S(2)}, u32[]{:S(2)}) collective-permute-start(bf16[192,1024]{1,0:T(8,128)(2,1)S(1)} %dynamic-slice_convert_fusion.4), channel_id=1, source_target_pairs={{0,8},{4,12},{8,0},{12,4},{16,24},{20,28},{24,16},{28,20},{1,9},{5... | collective-permute-start | bytes 1179656 | tf_op jit(solution)/shard_map/ppermute | solution.py:35
  519.5 15.0 %collective-permute-start.68 = (bf16[128,1536]{1,0:T(8,128)(2,1)S(1)}, bf16[128,1536]{1,0:T(8,128)(2,1)S(1)}, u32[]{:S(2)}, u32[]{:S(2)}) collective-permute-start(bf16[128,1536]{1,0:T(8,128)(2,1)S(1)} %dynamic-slice_convert_fusion.3), channel_id=1, source_target_pairs={{0,16},{4,20},{8,24},{12,28},{16,0},{20,4},{24,8},{28,12},{1,17},{... | collective-permute-start | bytes 1179656 | tf_op jit(solution)/shard_map/ppermute | solution.py:35
  526.2 16.8 %collective-permute-start.59 = (bf16[192,1024]{1,0:T(8,128)(2,1)S(1)}, bf16[192,1024]{1,0:T(8,128)(2,1)S(1)}, u32[]{:S(2)}, u32[]{:S(2)}) collective-permute-start(bf16[192,1024]{1,0:T(8,128)(2,1)S(1)} %add_convert_fusion.5), channel_id=1, source_target_pairs={{0,16},{4,20},{8,24},{12,28},{16,0},{20,4},{24,8},{28,12},{1,17},{... | collective-permute-start | bytes 1179656 | tf_op jit(solution)/shard_map/ppermute | solution.py:35
  527.0 17.9 %collective-permute-start.64 = (bf16[192,1024]{1,0:T(8,128)(2,1)S(1)}, bf16[192,1024]{1,0:T(8,128)(2,1)S(1)}, u32[]{:S(2)}, u32[]{:S(2)}) collective-permute-start(bf16[192,1024]{1,0:T(8,128)(2,1)S(1)} %add_convert_fusion.4), channel_id=1, source_target_pairs={{0,8},{4,12},{8,0},{12,4},{16,24},{20,28},{24,16},{28,20},{1,9},{5... | collective-permute-start | bytes 1179656 | tf_op jit(solution)/shard_map/ppermute | solution.py:35
  534.6 16.8 %collective-permute-start.69 = (bf16[128,1536]{1,0:T(8,128)(2,1)S(1)}, bf16[128,1536]{1,0:T(8,128)(2,1)S(1)}, u32[]{:S(2)}, u32[]{:S(2)}) collective-permute-start(bf16[128,1536]{1,0:T(8,128)(2,1)S(1)} %add_convert_fusion.3), channel_id=1, source_target_pairs={{0,16},{4,20},{8,24},{12,28},{16,0},{20,4},{24,8},{28,12},{1,17},{... | collective-permute-start | bytes 1179656 | tf_op jit(solution)/shard_map/ppermute | solution.py:35
  543.2 20.0 %collective-permute-start.60 = (bf16[384,1024]{1,0:T(8,128)(2,1)S(1)}, bf16[384,1024]{1,0:T(8,128)(2,1)S(1)}, u32[]{:S(2)}, u32[]{:S(2)}) collective-permute-start(bf16[384,1024]{1,0:T(8,128)(2,1)S(1)} %maximum_select_fusion.9), channel_id=1, source_target_pairs={{0,8},{4,12},{8,0},{12,4},{16,24},{20,28},{24,16},{28,20},{1,9},{5... | collective-permute-start | bytes 2359304 | tf_op jit(solution)/shard_map/ppermute | solution.py:35
  545.2 19.8 %collective-permute-start.65 = (bf16[384,1024]{1,0:T(8,128)(2,1)S(1)}, bf16[384,1024]{1,0:T(8,128)(2,1)}, u32[]{:S(2)}, u32[]{:S(2)}) collective-permute-start(bf16[384,1024]{1,0:T(8,128)(2,1)S(1)} %maximum_select_fusion.10), channel_id=1, source_target_pairs={{0,16},{4,20},{8,24},{12,28},{16,0},{20,4},{24,8},{28,12},{1,17},{... | collective-permute-start | bytes 2359304 | tf_op jit(solution)/shard_map/ppermute | solution.py:35
  551.5 20.2 %collective-permute-start.70 = (bf16[256,1536]{1,0:T(8,128)(2,1)S(1)}, bf16[256,1536]{1,0:T(8,128)(2,1)}, u32[]{:S(2)}, u32[]{:S(2)}) collective-permute-start(bf16[256,1536]{1,0:T(8,128)(2,1)S(1)} %maximum_select_fusion.11), channel_id=1, source_target_pairs={{0,8},{4,12},{8,0},{12,4},{16,24},{20,28},{24,16},{28,20},{1,9},{5... | collective-permute-start | bytes 2359304 | tf_op jit(solution)/shard_map/ppermute | solution.py:35
  565.0 150.8 %collective-permute-start.61 = (bf16[768,1024]{1,0:T(8,128)(2,1)}, bf16[768,1024]{1,0:T(8,128)(2,1)}, u32[]{:S(2)}, u32[]{:S(2)}) collective-permute-start(bf16[768,1024]{1,0:T(8,128)(2,1)} %maximum_select_fusion.3), channel_id=1, source_target_pairs={{0,4},{4,0},{8,12},{12,8},{16,20},{20,16},{24,28},{28,24},{1,5},{5... | collective-permute-start | bytes 4718600 | tf_op jit(solution)/shard_map/ppermute | solution.py:35
  600.4 15.1 %collective-permute-start.29 = (bf16[1024,256]{1,0:T(8,128)(2,1)S(1)}, bf16[1024,256]{1,0:T(8,128)(2,1)}, u32[]{:S(2)}, u32[]{:S(2)}) collective-permute-start(bf16[1024,256]{1,0:T(8,128)(2,1)S(1)} %get-tuple-element.144), channel_id=1, source_target_pairs={{4,0},{8,4},{12,8},{16,12},{20,16},{24,20},{28,24},{5,1},{9,5},{13... | collective-permute-start | bytes 1572872 | tf_op jit(solution)/shard_map/ppermute | solution.py:30
  602.0 24.6 %collective-permute-start.30 = (bf16[1024,256]{1,0:T(8,128)(2,1)S(1)}, bf16[1024,256]{1,0:T(8,128)(2,1)}, u32[]{:S(2)}, u32[]{:S(2)}) collective-permute-start(bf16[1024,256]{1,0:T(8,128)(2,1)S(1)} %get-tuple-element.142), channel_id=1, source_target_pairs={{4,0},{8,4},{12,8},{16,12},{20,16},{24,20},{28,24},{5,1},{9,5},{13... | collective-permute-start | bytes 1572872 | tf_op jit(solution)/shard_map/ppermute | solution.py:30
  603.6 44.0 %collective-permute-start.31 = (bf16[1024,256]{1,0:T(8,128)(2,1)S(1)}, bf16[1024,256]{1,0:T(8,128)(2,1)}, u32[]{:S(2)}, u32[]{:S(2)}) collective-permute-start(bf16[1024,256]{1,0:T(8,128)(2,1)S(1)} %get-tuple-element.143), channel_id=1, source_target_pairs={{8,0},{12,4},{16,8},{20,12},{24,16},{28,20},{9,1},{13,5},{17,9},{2... | collective-permute-start | bytes 1572872 | tf_op jit(solution)/shard_map/ppermute | solution.py:30
  604.9 48.3 %collective-permute-start.32 = (bf16[1024,256]{1,0:T(8,128)(2,1)S(1)}, bf16[1024,256]{1,0:T(8,128)(2,1)}, u32[]{:S(2)}, u32[]{:S(2)}) collective-permute-start(bf16[1024,256]{1,0:T(8,128)(2,1)S(1)} %get-tuple-element.141), channel_id=1, source_target_pairs={{8,0},{12,4},{16,8},{20,12},{24,16},{28,20},{9,1},{13,5},{17,9},{2... | collective-permute-start | bytes 1572872 | tf_op jit(solution)/shard_map/ppermute | solution.py:30
  615.5 105.8 %collective-permute-start.66 = (bf16[768,1024]{1,0:T(8,128)(2,1)}, bf16[768,1024]{1,0:T(8,128)(2,1)}, u32[]{:S(2)}, u32[]{:S(2)}) collective-permute-start(bf16[768,1024]{1,0:T(8,128)(2,1)} %maximum_select_fusion.4), channel_id=1, source_target_pairs={{0,4},{4,0},{8,12},{12,8},{16,20},{20,16},{24,28},{28,24},{1,5},{5... | collective-permute-start | bytes 4718600 | tf_op jit(solution)/shard_map/ppermute | solution.py:35
  626.6 54.0 %collective-permute-start.37 = (bf16[768,384]{1,0:T(8,128)(2,1)}, bf16[768,384]{1,0:T(8,128)(2,1)}, u32[]{:S(2)}, u32[]{:S(2)}) collective-permute-start(bf16[768,384]{1,0:T(8,128)(2,1)} %fusion.38), channel_id=1, source_target_pairs={{0,4},{4,0},{8,12},{12,8},{16,20},{20,16},{24,28},{28,24},{1,5},{5... | collective-permute-start | bytes 1769480 | tf_op jit(solution)/shard_map/ppermute | solution.py:35
  668.9 14.4 %collective-permute-start.51 = (bf16[192,1536]{1,0:T(8,128)(2,1)S(1)}, bf16[192,1536]{1,0:T(8,128)(2,1)S(1)}, u32[]{:S(2)}, u32[]{:S(2)}) collective-permute-start(bf16[192,1536]{1,0:T(8,128)(2,1)S(1)} %convolution_convert_fusion.4), channel_id=1, source_target_pairs={{0,4},{4,0},{8,12},{12,8},{16,20},{20,16},{24,28},{28,24},{1,5},{5... | collective-permute-start | bytes 1769480 | tf_op jit(solution)/shard_map/ppermute | solution.py:35
  680.0 69.4 %collective-permute-start.71 = (bf16[512,1536]{1,0:T(8,128)(2,1)S(1)}, bf16[512,1536]{1,0:T(8,128)(2,1)S(1)}, u32[]{:S(2)}, u32[]{:S(2)}) collective-permute-start(bf16[512,1536]{1,0:T(8,128)(2,1)S(1)} %copy-done.21), channel_id=1, source_target_pairs={{0,4},{4,0},{8,12},{12,8},{16,20},{20,16},{24,28},{28,24},{1,5},{5... | collective-permute-start | bytes 4718600 | tf_op jit(solution)/shard_map/ppermute | solution.py:35
  680.6 30.8 %collective-permute-start.38 = (bf16[768,384]{1,0:T(8,128)(2,1)S(1)}, bf16[768,384]{1,0:T(8,128)(2,1)S(1)}, u32[]{:S(2)}, u32[]{:S(2)}) collective-permute-start(bf16[768,384]{1,0:T(8,128)(2,1)S(1)} %fusion.41), channel_id=1, source_target_pairs={{0,4},{4,0},{8,12},{12,8},{16,20},{20,16},{24,28},{28,24},{1,5},{5... | collective-permute-start | bytes 1769480 | tf_op jit(solution)/shard_map/ppermute | solution.py:35
  710.7 28.1 %collective-permute-start.34 = (bf16[256,1536]{1,0:T(8,128)(2,1)S(1)}, bf16[256,1536]{1,0:T(8,128)(2,1)S(1)}, u32[]{:S(2)}, u32[]{:S(2)}) collective-permute-start(bf16[256,1536]{1,0:T(8,128)(2,1)S(1)} %get-tuple-element.86), channel_id=1, source_target_pairs={{3,2},{7,6},{11,10},{15,14},{19,18},{23,22},{27,26},{31,30}} | collective-permute-start | bytes 2359304 | tf_op jit(solution)/shard_map/ppermute | solution.py:469
  711.4 28.7 %collective-permute-start.33 = (bf16[256,1536]{1,0:T(8,128)(2,1)S(1)}, bf16[256,1536]{1,0:T(8,128)(2,1)S(1)}, u32[]{:S(2)}, u32[]{:S(2)}) collective-permute-start(bf16[256,1536]{1,0:T(8,128)(2,1)S(1)} %get-tuple-element.85), channel_id=1, source_target_pairs={{0,1},{4,5},{8,9},{12,13},{16,17},{20,21},{24,25},{28,29}} | collective-permute-start | bytes 2359304 | tf_op jit(solution)/shard_map/ppermute | solution.py:468
  715.8 11.3 %collective-permute-start.43 = (bf16[192,384]{1,0:T(8,128)(2,1)S(1)}, bf16[192,384]{1,0:T(8,128)(2,1)S(1)}, u32[]{:S(2)}, u32[]{:S(2)}) collective-permute-start(bf16[192,384]{1,0:T(8,128)(2,1)S(1)} %add_convert_fusion.16), channel_id=1, source_target_pairs={{0,16},{4,20},{8,24},{12,28},{16,0},{20,4},{24,8},{28,12},{1,17},{... | collective-permute-start | bytes 442376 | tf_op jit(solution)/shard_map/ppermute | solution.py:35
  727.1 9.5 %collective-permute-start.46 = (bf16[384,384]{1,0:T(8,128)(2,1)S(1)}, bf16[384,384]{1,0:T(8,128)(2,1)S(1)}, u32[]{:S(2)}, u32[]{:S(2)}) collective-permute-start(bf16[384,384]{1,0:T(8,128)(2,1)S(1)} %dynamic-slice_convert_fusion.7), channel_id=1, source_target_pairs={{0,16},{4,20},{8,24},{12,28},{16,0},{20,4},{24,8},{28,12},{1,17},{... | collective-permute-start | bytes 884744 | tf_op jit(solution)/shard_map/ppermute | solution.py:35
  729.0 12.9 %collective-permute-start.44 = (bf16[384,384]{1,0:T(8,128)(2,1)S(1)}, bf16[384,384]{1,0:T(8,128)(2,1)S(1)}, u32[]{:S(2)}, u32[]{:S(2)}) collective-permute-start(bf16[384,384]{1,0:T(8,128)(2,1)S(1)} %maximum_select_fusion.15), channel_id=1, source_target_pairs={{0,8},{4,12},{8,0},{12,4},{16,24},{20,28},{24,16},{28,20},{1,9},{5... | collective-permute-start | bytes 884744 | tf_op jit(solution)/shard_map/ppermute | solution.py:35
  740.5 19.3 %collective-permute-start.35 = (bf16[256,1536]{1,0:T(8,128)(2,1)S(1)}, bf16[256,1536]{1,0:T(8,128)(2,1)S(1)}, u32[]{:S(2)}, u32[]{:S(2)}) collective-permute-start(bf16[256,1536]{1,0:T(8,128)(2,1)S(1)} %get-tuple-element.87), channel_id=1, source_target_pairs={{0,1},{1,2},{4,5},{5,6},{8,9},{9,10},{12,13},{13,14},{16,17},{17,1... | collective-permute-start | bytes 2359304 | tf_op jit(solution)/shard_map/ppermute | solution.py:468
  742.1 14.4 %collective-permute-start.45 = (bf16[768,384]{1,0:T(8,128)(2,1)S(1)}, bf16[768,384]{1,0:T(8,128)(2,1)S(1)}, u32[]{:S(2)}, u32[]{:S(2)}) collective-permute-start(bf16[768,384]{1,0:T(8,128)(2,1)S(1)} %maximum_select_fusion.12), channel_id=1, source_target_pairs={{0,4},{4,0},{8,12},{12,8},{16,20},{20,16},{24,28},{28,24},{1,5},{5... | collective-permute-start | bytes 1769480 | tf_op jit(solution)/shard_map/ppermute | solution.py:35
  745.5 12.6 %collective-permute-start.56 = (bf16[192,1536]{1,0:T(8,128)(2,1)S(1)}, bf16[192,1536]{1,0:T(8,128)(2,1)S(1)}, u32[]{:S(2)}, u32[]{:S(2)}) collective-permute-start(bf16[192,1536]{1,0:T(8,128)(2,1)S(1)} %maximum_select_fusion.14), channel_id=1, source_target_pairs={{0,4},{4,0},{8,12},{12,8},{16,20},{20,16},{24,28},{28,24},{1,5},{5... | collective-permute-start | bytes 1769480 | tf_op jit(solution)/shard_map/ppermute | solution.py:35
  756.4 22.4 %collective-permute-start.50 = (bf16[768,384]{1,0:T(8,128)(2,1)S(1)}, bf16[768,384]{1,0:T(8,128)(2,1)S(1)}, u32[]{:S(2)}, u32[]{:S(2)}) collective-permute-start(bf16[768,384]{1,0:T(8,128)(2,1)S(1)} %maximum_select_fusion.13), channel_id=1, source_target_pairs={{0,4},{4,0},{8,12},{12,8},{16,20},{20,16},{24,28},{28,24},{1,5},{5... | collective-permute-start | bytes 1769480 | tf_op jit(solution)/shard_map/ppermute | solution.py:35
  762.1 30.4 %collective-permute-start.40 = (bf16[256,1536]{1,0:T(8,128)(2,1)}, bf16[256,1536]{1,0:T(8,128)(2,1)}, u32[]{:S(2)}, u32[]{:S(2)}) collective-permute-start(bf16[256,1536]{1,0:T(8,128)(2,1)} %add_convert_fusion.1), channel_id=1, source_target_pairs={{1,0},{2,1},{3,2},{5,4},{6,5},{7,6},{9,8},{10,9},{11,10},{13,12},{... | collective-permute-start | bytes 2359304 | tf_op jit(solution)/shard_map/ppermute | solution.py:469
  763.4 30.3 %collective-permute-start.39 = (bf16[256,1536]{1,0:T(8,128)(2,1)}, bf16[256,1536]{1,0:T(8,128)(2,1)}, u32[]{:S(2)}, u32[]{:S(2)}) collective-permute-start(bf16[256,1536]{1,0:T(8,128)(2,1)} %add_convert_fusion.2), channel_id=1, source_target_pairs={{0,1},{1,2},{2,3},{4,5},{5,6},{6,7},{8,9},{9,10},{10,11},{12,13},{... | collective-permute-start | bytes 2359304 | tf_op jit(solution)/shard_map/ppermute | solution.py:468
  (123 other events, 1600.1 us)
Sparse Core Ops, SparseCore 0:
  12.1 66.1 all-gather.6
  175.1 71.8 all-gather.8
  249.1 66.0 all-gather.12
  334.9 46.1 all-gather.10
  430.6 38.8 all-gather.14
  492.0 35.8 all-gather.16
  574.9 57.9 reduce-scatter.1

commit v3 on v2

--- a/solution.py
+++ b/solution.py
@@ -232,7 +232,9 @@
     )(low, queries_joined, firsts, *arrays, *arrays)
 
 
-def attend_back_kernel(tiles, chunks, group, factor, scale, low_ref, query_ref, first_ref, *refs):
+def attend_back_kernel(
+    tiles, chunks, group, factor, scale, low_ref, slot_ref, query_ref, first_ref, *refs
+):
     mixed_ref, log_ref, cosine_ref, sine_ref = refs[:4]
     grad_refs = refs[4 : 4 + chunks]
     refs = refs[4 + chunks :]
@@ -303,7 +305,7 @@
 
 
 def attend_back(
-    queries_joined, windows, firsts, low, mixed, grads, logs, cosine, sine,
+    queries_joined, windows, firsts, low, slots, mixed, grads, logs, cosine, sine,
     kv_heads, group, rows, tile_rows,
 ):
     stretch = queries_joined.shape[0]
@@ -321,7 +323,7 @@
     table_spec = pl.BlockSpec((rows, LANES), lambda g, i, *s: (i, 0))
     total_spec = pl.BlockSpec((tiles * stretch, LANES), lambda g, i, *s: (0, g))
     grid_spec = pltpu.PrefetchScalarGridSpec(
-        num_scalar_prefetch=1,
+        num_scalar_prefetch=2,
         grid=(kv_heads, blocks),
         in_specs=[
             heads_spec,
@@ -331,7 +333,10 @@
             table_spec,
             table_spec,
         ]
-        + [pl.BlockSpec((rows // chunks, group * LANES), lambda g, i, *s: (i, g))] * chunks
+        + [
+            pl.BlockSpec((rows // chunks, group * LANES), lambda g, i, low, slot: (slot[i], g))
+        ]
+        * chunks
         + window_specs(stretch, key_columns)
         + window_specs(stretch, value_columns),
         out_specs=[heads_spec, total_spec, total_spec],
@@ -355,7 +360,7 @@
             flops=40 * LANES * work, bytes_accessed=16 * stretch * stretch, transcendentals=work
         ),
         name="attend_back",
-    )(low, queries_joined, firsts, mixed, logs, cosine, sine, *grads, *arrays, *arrays)
+    )(low, slots, queries_joined, firsts, mixed, logs, cosine, sine, *grads, *arrays, *arrays)
 
 
 def gather_back_kernel(kv_heads, parts, key_ref, value_ref, cosine_ref, sine_ref, *refs):
@@ -406,27 +411,35 @@
 
     def meet(self):
         got = exchange(self.sent, self.axis, 1 << self.order[0])
-        self.kept = self.times(0, False) + got.astype(f32)
-        return self.kept
+        self.value = self.times(0, False) + got.astype(f32)
+        self.down = list(self.order[1:])
+        self.up = list(reversed(self.order))
+        return self.value
+
+    def step(self):
+        if self.down:
+            place = self.down.pop(0)
+            bit = self.bit(place)
+            size = self.value.shape[0] // 2
+            sent = lax.dynamic_slice_in_dim(self.value, (1 - bit) * size, size, 0).astype(bf16)
+            got = exchange(sent, self.axis, 1 << place)
+            kept = lax.dynamic_slice_in_dim(self.value, bit * size, size, 0)
+            self.value = kept + got.astype(f32)
+            return self.value
+        place = self.up.pop(0)
+        whole = self.value.astype(bf16)
+        got = exchange(whole, self.axis, 1 << place)
+        self.value = jnp.where(
+            self.bit(place) == 1,
+            jnp.concatenate([got, whole], axis=0),
+            jnp.concatenate([whole, got], axis=0),
+        )
+        return self.value
 
     def finish(self):
-        axis, kept, size = self.axis, self.kept, self.size
-        for place in self.order[1:]:
-            bit = self.bit(place)
-            size //= 2
-            sent = lax.dynamic_slice_in_dim(kept, (1 - bit) * size, size, 0).astype(bf16)
-            got = exchange(sent, axis, 1 << place)
-            kept = lax.dynamic_slice_in_dim(kept, bit * size, size, 0) + got.astype(f32)
-        whole = kept.astype(bf16)
-        for place in reversed(self.order):
-            bit = self.bit(place)
-            got = exchange(whole, axis, 1 << place)
-            whole = jnp.where(
-                bit == 1,
-                jnp.concatenate([got, whole], axis=0),
-                jnp.concatenate([whole, got], axis=0),
-            )
-        return whole.astype(f32)
+        while self.up:
+            self.step()
+        return self.value.astype(f32)
 
 
 def sum_everywhere(value, axes):
@@ -445,31 +458,75 @@
     ).astype(f32)
 
 
-def chain_scatter(product, axis, fillers=()):
-    count = lax.axis_size(axis)
-    index = lax.axis_index(axis)
-    rows = product.shape[0] // count
-
-    def piece(offset):
-        start = lax.rem(index + offset, count) * rows
-        return lax.dynamic_slice_in_dim(product, start, rows, 0).astype(f32)
-
-    right = left = None
-    for step in range(1, count):
-        to_right = piece((count - step) % count)
-        to_left = piece(step % count)
-        if right is not None:
-            to_right = to_right + right.astype(f32)
-            to_left = to_left + left.astype(f32)
-        others = fillers[step - 2] if 0 <= step - 2 < len(fillers) else ()
-        to_right, to_left = lax.optimization_barrier(
-            (to_right.astype(bf16), to_left.astype(bf16)) + tuple(others)
-        )[:2]
-        right = lax.ppermute(to_right, axis, [(i, i + 1) for i in range(min(step, count - 1))])
-        left = lax.ppermute(
-            to_left, axis, [(i, i - 1) for i in range(max(count - step, 1), count)]
-        )
-    return piece(0) + right.astype(f32) + left.astype(f32)
+class ChainSum:
+
+    def __init__(self, piece, axis):
+        self.piece, self.axis = piece, axis
+        self.count = lax.axis_size(axis)
+        self.step = 0
+        self.right = self.left = None
+
+    def outgoing(self):
+        self.step += 1
+        to_right = self.piece((self.count - self.step) % self.count)
+        to_left = self.piece(self.step % self.count)
+        if self.right is not None:
+            to_right = to_right.astype(f32) + self.right.astype(f32)
+            to_left = to_left.astype(f32) + self.left.astype(f32)
+        return to_right.astype(bf16), to_left.astype(bf16)
+
+    def send(self, to_right, to_left):
+        count, step = self.count, self.step
+        self.right = lax.ppermute(
+            to_right, self.axis, [(i, i + 1) for i in range(min(step, count - 1))]
+        )
+        self.left = lax.ppermute(
+            to_left, self.axis, [(i, i - 1) for i in range(max(count - step, 1), count)]
+        )
+
+    def result(self):
+        return self.piece(0).astype(f32) + self.right.astype(f32) + self.left.astype(f32)
+
+
+class ChainGather:
+
+    def __init__(self, own, axis):
+        self.own, self.axis = own, axis
+        self.count = lax.axis_size(axis)
+        self.step = 0
+        self.from_left, self.from_right = [own], [own]
+
+    def outgoing(self):
+        self.step += 1
+        return self.from_left[-1], self.from_right[-1]
+
+    def send(self, to_right, to_left):
+        count, step = self.count, self.step
+        self.from_left.append(
+            lax.ppermute(to_right, self.axis, [(i, i + 1) for i in range(step - 1, count - 1)])
+        )
+        self.from_right.append(
+            lax.ppermute(to_left, self.axis, [(i, i - 1) for i in range(1, count - step + 1)])
+        )
+
+    def result(self):
+        others = [
+            self.from_right[d] + self.from_left[self.count - d] for d in range(1, self.count)
+        ]
+        return jnp.concatenate([self.own] + others, axis=0)
+
+
+def hop(chains, fillers=()):
+    values = [value for chain in chains for value in chain.outgoing()]
+    values = lax.optimization_barrier(tuple(values) + tuple(fillers))[: 2 * len(chains)]
+    for place, chain in enumerate(chains):
+        chain.send(values[2 * place], values[2 * place + 1])
+
+
+def run_chain(chain, fillers=()):
+    for step in range(lax.axis_size(chain.axis) - 1):
+        hop([chain], fillers[step - 1] if 0 < step <= len(fillers) else ())
+    return chain.result()
 
 
 def gather_rows(rows):
@@ -507,16 +564,28 @@
     places = list(range((lax.axis_size("dp") - 1).bit_length()))
     crossed = places[:1] + places[:0:-1]
 
+    here = lax.axis_index("tensor")
+    devices = lax.axis_size("tensor")
+    hops = devices - 1
+    slots = lax.rem(jnp.arange(devices, dtype=jnp.int32) + devices - here, devices)
+
     def own_parts(value):
         return [value[c * part_rows : (c + 1) * part_rows] for c in range(chunks)]
 
-    def whole_parts(value):
-        cut = value.reshape(blocks, chunks, part_rows, value.shape[1])
-        return [cut[:, c].reshape(blocks * part_rows, value.shape[1]) for c in range(chunks)]
-
-    def whole_order(parts):
-        cut = [part.reshape(blocks, 1, part_rows, part.shape[1]) for part in parts]
-        return jnp.concatenate(cut, axis=1).reshape(stretch, parts[0].shape[1])
+    def piece_of(value, c, d):
+        start = lax.rem(here + d, devices) * rows + c * part_rows
+        return lax.dynamic_slice_in_dim(value, start, part_rows, 0)
+
+    def turned_part(value, c):
+        return jnp.concatenate([piece_of(value, c, d) for d in range(devices)], axis=0)
+
+    def in_order(parts):
+        pieces = [
+            lax.dynamic_slice_in_dim(part, slots[t] * part_rows, part_rows, 0)
+            for t in range(devices)
+            for part in parts
+        ]
+        return jnp.concatenate(pieces, axis=0)
 
     normed_own, inv_rms_attn = normalize(block_input, attn_gain)
     attention_normed = gather_rows(normed_own)
@@ -542,94 +611,124 @@
     windows = windows + [(joined, heads)]
     attended, logs = attend(joined, windows, firsts, low, kv_heads, group, rows, tile_rows)
 
-    out_parts = whole_parts(out_low)
     mixed_product = jnp.dot(attended, w_out_spread, preferred_element_type=f32).astype(bf16)
-    residuals, inv_rms_mlps, normed_mlps, c_normed = [], [], [], []
-    for part, product in zip(own_parts(block_input), whole_parts(mixed_product)):
-        if c_normed:
-            product = after(product, c_normed[-1])
-        residual = part + chain_scatter(product, "tensor")
-        mlp_normed_own, inv_rms_mlp = normalize(residual, mlp_gain)
-        c_normed.append(mlp_normed_own)
-        residuals.append(residual)
-        inv_rms_mlps.append(inv_rms_mlp)
-        normed_mlps.append(gather_rows(mlp_normed_own))
-
-    hiddens, gate_grads, up_grads, residual_grads, residual_lows = [], [], [], [], []
-    own_lows = []
-    gate_pres = [jnp.dot(part, w_gate, preferred_element_type=f32) for part in normed_mlps]
-    up_projs = [jnp.dot(part, w_up, preferred_element_type=f32) for part in normed_mlps]
-    mlp_gain_part = 0.0
-    for c in range(chunks):
-        gate_pre, up_proj = gate_pres[c], up_projs[c]
+    inputs = own_parts(block_input)
+    cotangents = own_parts(out_grad)
+    residuals, inv_rms_mlps = {}, {}
+    normed_mlps, out_parts, hidden_grads, gate_pres, up_projs = {}, {}, {}, {}, {}
+    hiddens, gate_grads, up_grads = {}, {}, {}
+    residual_grads, residual_lows, gain_parts = {}, {}, {}
+    scatter_out, gather_mlp, scatter_mlp, gather_low = {}, {}, {}, {}
+    shared = []
+
+    def begin_scatter_out(c):
+        scatter_out[c] = ChainSum(lambda d: piece_of(mixed_product, c, d), "tensor")
+        return scatter_out[c]
+
+    def begin_gather_mlp(c):
+        residuals[c] = inputs[c] + scatter_out[c].result()
+        own, inv_rms_mlps[c] = normalize(residuals[c], mlp_gain)
+        gather_mlp[c] = ChainGather(own, "tensor")
+        return gather_mlp[c]
+
+    def back_product(c):
+        out_parts[c] = turned_part(out_low, c)
+        hidden_grads[c] = jnp.dot(out_parts[c], w_down.T, preferred_element_type=f32)
+        return (hidden_grads[c],)
+
+    def hidden_products(c):
+        normed_mlps[c] = gather_mlp[c].result()
+        gate_pres[c] = jnp.dot(normed_mlps[c], w_gate, preferred_element_type=f32)
+        up_projs[c] = jnp.dot(normed_mlps[c], w_up, preferred_element_type=f32)
+        return (gate_pres[c], up_projs[c])
+
+    def begin_scatter_mlp(c):
+        gate_pre, up_proj, hidden_grad = gate_pres[c], up_projs[c], hidden_grads[c]
         sigmoid_gate = jax.nn.sigmoid(gate_pre)
         silu_gate = gate_pre * sigmoid_gate
-        hiddens.append((silu_gate * up_proj).astype(bf16))
-        hidden_grad = jnp.dot(out_parts[c], w_down.T, preferred_element_type=f32)
-        gate_grad = (
+        hiddens[c] = (silu_gate * up_proj).astype(bf16)
+        gate_grads[c] = (
             hidden_grad * up_proj * sigmoid_gate * (1.0 + gate_pre * (1.0 - sigmoid_gate))
         ).astype(bf16)
-        up_grad = (hidden_grad * silu_gate).astype(bf16)
-        gate_grads.append(gate_grad)
-        up_grads.append(up_grad)
+        up_grads[c] = (hidden_grad * silu_gate).astype(bf16)
         product = (
-            jnp.dot(gate_grad, w_gate.T, preferred_element_type=f32)
-            + jnp.dot(up_grad, w_up.T, preferred_element_type=f32)
+            jnp.dot(gate_grads[c], w_gate.T, preferred_element_type=f32)
+            + jnp.dot(up_grads[c], w_up.T, preferred_element_type=f32)
         ).astype(bf16)
-        fillers = ()
-        if c + 1 < chunks:
-            product = after(product, c_normed[c + 1])
-            fillers = ((), (gate_pres[c + 1], up_projs[c + 1]))
-        else:
-            normed_joined = jnp.concatenate(normed_mlps, axis=0)
-            shared = [
-                SharedProduct(normed_joined, jnp.concatenate(gate_grads, axis=0), "dp", places),
-                SharedProduct(normed_joined, jnp.concatenate(up_grads, axis=0), "dp", crossed),
-                SharedProduct(
-                    jnp.concatenate(hiddens, axis=0), jnp.concatenate(out_parts, axis=0),
-                    "dp", places,
-                ),
-            ]
-            fillers = ([p.sent for p in shared], [p.meet() for p in shared])
-        if c > 0:
-            product = after(product, own_lows[-1])
-        mlp_normed_grad = chain_scatter(product, "tensor", fillers)
-        residual_part = normalize_back(residuals[c], inv_rms_mlps[c], mlp_gain, mlp_normed_grad)
-        residual_grad = own_parts(out_grad)[c] + residual_part
-        residual_grads.append(residual_grad)
-        own_lows.append(residual_grad.astype(bf16))
-        residual_lows.append(gather_rows(own_lows[-1]))
-        mlp_gain_part = mlp_gain_part + jnp.sum(
-            mlp_normed_grad * residuals[c] * inv_rms_mlps[c], axis=0, keepdims=True
-        )
-
-    grad_gate, grad_up, grad_down = [p.finish() for p in shared]
-    grad_mlp_gain = sum_everywhere(mlp_gain_part, ("tensor", "dp"))[0]
-
-    down_product = after(
-        whole_order(
-            [jnp.dot(h, w_down, preferred_element_type=f32).astype(bf16) for h in hiddens]
-        ),
-        *residual_lows,
-    )
+        scatter_mlp[c] = ChainSum(
+            lambda d: product[d * part_rows : (d + 1) * part_rows], "tensor"
+        )
+        return scatter_mlp[c]
+
+    def begin_gather_low(c):
+        normed_grad = scatter_mlp[c].result()
+        part = normalize_back(residuals[c], inv_rms_mlps[c], mlp_gain, normed_grad)
+        residual_grads[c] = cotangents[c] + part
+        gain_parts[c] = jnp.sum(
+            normed_grad * residuals[c] * inv_rms_mlps[c], axis=0, keepdims=True
+        )
+        gather_low[c] = ChainGather(residual_grads[c].astype(bf16), "tensor")
+        return gather_low[c]
+
+    def joined_parts(parts):
+        return jnp.concatenate([parts[c] for c in range(chunks)], axis=0)
+
+    def share_halves():
+        normed_joined = joined_parts(normed_mlps)
+        shared.append(SharedProduct(normed_joined, joined_parts(gate_grads), "dp", places))
+        shared.append(SharedProduct(normed_joined, joined_parts(up_grads), "dp", crossed))
+        shared.append(
+            SharedProduct(joined_parts(hiddens), joined_parts(out_parts), "dp", places)
+        )
+        return [p.sent for p in shared]
+
+    plan = [
+        (0, begin_scatter_out, 0),
+        (hops, begin_scatter_out, 1),
+        (hops, begin_gather_mlp, 0),
+        (2 * hops, begin_gather_mlp, 1),
+        (2 * hops + 2, begin_scatter_mlp, 0),
+        (3 * hops + 2, begin_scatter_mlp, 1),
+        (3 * hops + 2, begin_gather_low, 0),
+        (4 * hops + 2, begin_gather_low, 1),
+    ]
+    between = {
+        hops + 1: lambda: back_product(0),
+        hops + 2: lambda: back_product(1),
+        2 * hops + 1: lambda: hidden_products(0),
+        3 * hops + 1: lambda: hidden_products(1),
+        3 * hops + 3: share_halves,
+        3 * hops + 4: lambda: [p.meet() for p in shared],
+        5 * hops + 1: lambda: [p.step() for p in shared],
+    }
+    running = []
+    for moment in range(5 * hops + 2):
+        fillers = between[moment]() if moment in between else ()
+        running = [chain for chain in running if chain.step < hops]
+        running = running + [begin(c) for start, begin, c in plan if start == moment]
+        hop(running, fillers)
+    for c in range(chunks):
+        residual_lows[c] = gather_low[c].result()
+
+    grad_mlp_gain = sum_everywhere(gain_parts[0] + gain_parts[1], ("tensor", "dp"))[0]
+
+    down_product = in_order(
+        [
+            jnp.dot(hiddens[c], w_down, preferred_element_type=f32).astype(bf16)
+            for c in range(chunks)
+        ]
+    )
+    down_product, residual_lows = lax.optimization_barrier((down_product, residual_lows))
     block_scattered = scatter_sum(down_product)
-    block_output = jnp.concatenate(residuals, axis=0) + block_scattered
-
-    attended_plain = jnp.concatenate(
-        whole_parts(jnp.dot(attended, query_spread.T, preferred_element_type=bf16)), axis=0
-    )
-    out_shared = SharedProduct(
-        attended_plain, jnp.concatenate(residual_lows, axis=0), "dp", crossed
-    )
-    out_shared.meet()
-    grad_out = out_shared.finish()
+    block_output = joined_parts(residuals) + block_scattered
+
     attended_gradients = [
-        jnp.dot(low_rows, w_out_spread.T, preferred_element_type=f32).astype(bf16)
-        for low_rows in residual_lows
+        jnp.dot(residual_lows[c], w_out_spread.T, preferred_element_type=f32).astype(bf16)
+        for c in range(chunks)
     ]
     query_grad, key_totals, value_totals = attend_back(
-        joined, windows, firsts, low, attended, attended_gradients, logs, cosine, sine,
-        kv_heads, group, rows, tile_rows,
+        joined, windows, firsts, low, slots, attended, attended_gradients, logs, cosine,
+        sine, kv_heads, group, rows, tile_rows,
     )
     received = []
     for distance in range(1, reach + 1):
@@ -640,6 +739,16 @@
                 for total in (key_totals, value_totals)
             ]
         )
+    shared[2].step()
+    shared[2].value, received = lax.optimization_barrier((shared[2].value, received))
+    grad_gate, grad_up, grad_down = [p.finish() for p in shared]
+    attended_plain = jnp.dot(
+        after(attended, key_totals), query_spread.T, preferred_element_type=bf16
+    )
+    out_shared = SharedProduct(
+        jnp.concatenate([turned_part(attended_plain, c) for c in range(chunks)], axis=0),
+        joined_parts(residual_lows), "dp", crossed,
+    )
     key_value_grad = gather_back(
         key_totals, value_totals, received, cosine, sine, kv_heads, stretch, rows
     )
@@ -658,17 +767,21 @@
         )
         / attn_gain
     )
-    attn_normed_grad = chain_scatter(
-        attn_normed_part, "tensor",
-        (
-            [query_shared.sent, kv_shared.sent, attn_gain_part],
-            [query_shared.meet(), kv_shared.meet()],
+    small = (query_shared, kv_shared, out_shared)
+    attn_normed_grad = run_chain(
+        ChainSum(
+            lambda d: lax.dynamic_slice_in_dim(
+                attn_normed_part, lax.rem(here + d, devices) * rows, rows, 0
+            ),
+            "tensor",
         ),
+        ([p.sent for p in small] + [attn_gain_part], [p.meet() for p in small]),
     )
     input_part = normalize_back(block_input, inv_rms_attn, attn_gain, attn_normed_grad)
-    input_grad = jnp.concatenate(residual_grads, axis=0) + input_part
+    input_grad = joined_parts(residual_grads) + input_part
     grad_query = query_shared.finish()
     grad_key_value = kv_shared.finish()
+    grad_out = out_shared.finish()
     grad_key = grad_key_value[:, : kv_heads * HEAD_SIZE]
     grad_value = grad_key_value[:, kv_heads * HEAD_SIZE :]
 

time: 820 us -> 777 us (0.948)
  waiting for transfers between devices: 357 us -> 282 us
  starting transfers between devices: 175 us -> 216 us
  matrix products: 91.8 us -> 81.5 us
    all_gather x6 -> x2, waiting for transfers between devices: 142 us -> 52.3 us  [gather_rows(): return lax.all_gather(rows, 'tensor', axis=0, tiled=True)]
    ppermute x30 -> x54, starting transfers between devices: 103 us -> 131 us  [the longest x15 83.2 us: send(): lax.ppermute(to_right, self.axis, [(i, i + 1) for i in range(min(step, co...]
    ppermute x46, starting transfers between devices: 59.1 us -> 72.6 us  [exchange(): return lax.ppermute(value, axis, [(i, i ^ distance) for i in range(count)])]
    ppermute x46, waiting for transfers between devices: 99.7 us -> 109 us  [exchange(): return lax.ppermute(value, axis, [(i, i ^ distance) for i in range(count)])]
    ppermute x30 -> x54, waiting for transfers between devices: 76.6 us -> 85.1 us  [the longest x15 40.3 us: send(): lax.ppermute(to_right, self.axis, [(i, i + 1) for i in range(min(step, co...]
    unnamed x202 -> x170, local copies, waits for them, and re-layouts: 23.6 us -> 29.1 us
    convert_element_type x29 -> x26, other arithmetic: 36.7 us -> 35 us  [the longest x6 15.6 us: finish(): return self.value.astype(f32)]
  transfers between devices with their start and end apart: 89 -> 109, of which waited for: 44 -> 43; matrix products, arithmetic and copies ran while one was open for 20% -> 24% of each run, Pallas kernels for 3% -> 5%
where the time goes in v3:
time: 777 us; the launch traced here: 766 us
  waiting for transfers between devices  282 us (36%)
  starting transfers between devices  216 us (28%)
  other arithmetic  82.7 us (11%)
  matrix products  81.5 us (10%)
  Pallas kernels  45.5 us (6%)
  local copies, waits for them, and re-layouts  39.9 us (5%)
  between operations  18.9 us (2%)
    ppermute x46, waiting for transfers between devices, exchange(): return lax.ppermute(value, axis, [(i, i ^ distance) for i in range(count)])  109 us
    ppermute x15, starting transfers between devices, send(): lax.ppermute(to_right, self.axis, [(i, i + 1) for i in range(min(step, co...  83.2 us
    ppermute x46, starting transfers between devices, exchange(): return lax.ppermute(value, axis, [(i, i ^ distance) for i in range(count)])  72.6 us
    all_gather x2, waiting for transfers between devices, gather_rows(): return lax.all_gather(rows, 'tensor', axis=0, tiled=True)  52.3 us
    ppermute x15, waiting for transfers between devices, send(): lax.ppermute(to_right, self.axis, [(i, i + 1) for i in range(min(step, co...  40.3 us
    ppermute x6, waiting for transfers between devices, from_behind(): lax.ppermute(value, axis, [(source, source + steps) for source in range(l...  35.4 us
    unnamed x170, local copies, waits for them, and re-layouts  29.1 us
    ppermute x12, waiting for transfers between devices, send(): lax.ppermute(to_left, self.axis, [(i, i - 1) for i in range(1, count - st...  26.5 us
  transfers between devices with their start and end apart: 109, of which 43 were waited for; matrix products, arithmetic and copies ran while one was open for 24% of the time, Pallas kernels for 5%

profile of v3, /device:TPU:0, one launch (start us, length us, event | category | flops | bytes accessed | tf_op | source)
XLA Modules:
  0.0 766.3 jit_solution(9716442752339895899)
XLA Ops:
  19.6 6.3 fusion.3.weight_ref
  25.9 52.3 %all-gather.3.cloned.1.call-done.rows_ref = bf16[1024,1536]{1,0:T(8,128)(2,1)} async-done(((bf16[256,1536]{1,0:T(8,128)(2,1)}), bf16[1024,1536]{1,0:T(8,128)(2,1)}) %all-gather.3.cloned.1.call-update) | async-done | bytes 3145744 | tf_op jit(solution)/shard_map/all_gather | solution.py:533
  78.3 7.7 %project.1.query_ref.refs_2_.refs_5_.refs_8_.refs_11_ = bf16[1024,1024]{1,0:T(8,128)(2,1)} custom-call(bf16[1024,1536]{1,0:T(8,128)(2,1)} %all-gather.3.cloned.1.call-done.rows_ref, bf16[1536,1024]{1,0:T(8,128)(2,1)} %fusion.3.weight_ref, f32[1024,128]{1,0:T(8,128)} %get-tuple-element.252.cosine_ref.refs_2_, f32[1024,128]{1,0:T(8,128)} %get-tuple-element.251.sine_ref.refs_3_), custom_call_target="tpu_custom_call" | custom-call | flops 3221225472 | bytes 8388608 | tf_op jit(solution)/shard_map/project/pallas_call | solution.py:92
  88.2 4.4 collective-permute-start
  98.0 3.5 fusion.74
  101.6 13.8 %collective-permute-done.refs_0_.refs_3_.refs_6_.refs_9_ = bf16[1024,512]{1,0:T(8,128)(2,1)} collective-permute-done((bf16[1024,512]{1,0:T(8,128)(2,1)}, bf16[1024,512]{1,0:T(8,128)(2,1)}, u32[]{:S(2)}, u32[]{:S(2)}) %collective-permute-start) | collective-permute-done | bytes 1048608 | tf_op jit(solution)/shard_map/ppermute | solution.py:30
  115.5 13.4 %attend.1 = (bf16[1024,512]{1,0:T(8,128)(2,1)}, f32[2,4,1,512]{3,2,1,0:T(1,128)}) custom-call(s32[4]{0:T(128)} %get-tuple-element.270.low_ref, bf16[1024,1024]{1,0:T(8,128)(2,1)} %project.1.query_ref.refs_2_.refs_5_.refs_8_.refs_11_, s32[4,1,256]{2,1,0:T(1,128)} %bitcast.43, bf16[1024,512]{1,0:T(8,128)(2,1)} %collective-permute-done.refs_0_.refs_3_.refs_6_.refs_9_, ...), custom_call_target="tpu_custom_call" | custom-call | flops 8589934592 | bytes 8388608 | tf_op jit(solution)/shard_map/attend/pallas_call | solution.py:221
  128.8 3.5 convolution_convert_fusion
  138.5 13.4 %collective-permute-done.2 = bf16[128,1536]{1,0:T(8,128)(2,1)} collective-permute-done((bf16[128,1536]{1,0:T(8,128)(2,1)}, bf16[128,1536]{1,0:T(8,128)(2,1)}, u32[]{:S(2)}, u32[]{:S(2)}) %collective-permute-start.2) | collective-permute-done | bytes 393248 | tf_op jit(solution)/shard_map/ppermute | solution.py:480
  153.3 4.4 collective-permute-start.4
  158.4 12.9 %collective-permute-done.4 = bf16[128,1536]{1,0:T(8,128)(2,1)S(1)} collective-permute-done((bf16[128,1536]{1,0:T(8,128)(2,1)S(1)}, bf16[128,1536]{1,0:T(8,128)(2,1)S(1)}, u32[]{:S(2)}, u32[]{:S(2)}) %collective-permute-start.4) | collective-permute-done | bytes 393248 | tf_op jit(solution)/shard_map/ppermute | solution.py:480
  176.2 5.8 collective-permute-start.6
  182.0 3.4 collective-permute-done.7
  192.0 6.7 collective-permute-start.8
  202.2 3.5 collective-permute-done.8
  211.5 5.1 fusion.18
  216.6 4.5 collective-permute-start.12
  236.9 7.0 collective-permute-start.16
  255.0 6.4 collective-permute-done.19
  265.4 4.6 collective-permute-start.21
  271.8 3.9 multiply_convert_fusion.3
  281.5 8.3 %collective-permute-done.23 = bf16[128,1536]{1,0:T(8,128)(2,1)S(1)} collective-permute-done((bf16[128,1536]{1,0:T(8,128)(2,1)S(1)}, bf16[128,1536]{1,0:T(8,128)(2,1)S(1)}, u32[]{:S(2)}, u32[]{:S(2)}) %collective-permute-start.23) | collective-permute-done | bytes 393248 | tf_op jit(solution)/shard_map/ppermute | solution.py:509
  295.3 4.6 collective-permute-start.26
  304.9 3.9 multiply_convert_fusion
  317.7 5.8 collective-permute-start.40
  333.3 4.9 collective-permute-start.30
  338.3 7.7 %collective-permute-done.31 = bf16[128,1536]{1,0:T(8,128)(2,1)S(1)} collective-permute-done((bf16[128,1536]{1,0:T(8,128)(2,1)S(1)}, bf16[128,1536]{1,0:T(8,128)(2,1)S(1)}, u32[]{:S(2)}, u32[]{:S(2)}) %collective-permute-start.31) | collective-permute-done | bytes 393248 | tf_op jit(solution)/shard_map/ppermute | solution.py:483
  349.6 4.4 collective-permute-start.33
  356.9 6.6 collective-permute-done.33
  364.9 5.6 collective-permute-done.35
  370.5 6.1 collective-permute-done.32
  377.3 4.3 collective-permute-start.36
  382.3 3.5 convert_add_fusion.2
  388.5 3.6 convert_add_fusion
  392.1 3.5 convert_add_fusion.1
  398.4 7.5 collective-permute-start.45
  411.3 7.5 collective-permute-start.51
  424.5 3.4 collective-permute-start.102
  431.9 3.7 collective-permute-start.48
  443.1 15.2 %collective-permute-done.105 = f32[1,1536]{1,0:T(1,128)S(1)} collective-permute-done((f32[1,1536]{1,0:T(1,128)S(1)}, f32[1,1536]{1,0:T(1,128)S(1)}, u32[]{:S(2)}, u32[]{:S(2)}) %collective-permute-start.105) | collective-permute-done | bytes 6176 | tf_op jit(solution)/shard_map/ppermute | solution.py:35
  465.3 13.4 %collective-permute-done.53 = bf16[256,1536]{1,0:T(8,128)(2,1)S(1)} collective-permute-done((bf16[256,1536]{1,0:T(8,128)(2,1)S(1)}, bf16[256,1536]{1,0:T(8,128)(2,1)S(1)}, u32[]{:S(2)}, u32[]{:S(2)}) %collective-permute-start.53) | collective-permute-done | bytes 786464 | tf_op jit(solution)/shard_map/ppermute | solution.py:35
  486.1 4.6 collective-permute-done.56
  496.1 20.0 %attend_back.1 = (bf16[1024,512]{1,0:T(8,128)(2,1)}, f32[3072,256]{1,0:T(8,128)}, f32[3072,256]{1,0:T(8,128)}) custom-call(s32[4]{0:T(128)} %get-tuple-element.270.low_ref, s32[4]{0:T(128)} %copy-done.50, bf16[1024,1024]{1,0:T(8,128)(2,1)} %project.1.query_ref.refs_2_.refs_5_.refs_8_.refs_11_, s32[4,1,256]{2,1,0:T(1,128)} %bitcast.44, ...), custom_call_target="tpu_custom_call" | custom-call | flops 21474836480 | bytes 16777216 | tf_op jit(solution)/shard_map/attend_back/pallas_call | solution.py:351
  516.1 3.2 convert.8
  536.2 18.8 %collective-permute-start.90 = (bf16[192,1024]{1,0:T(8,128)(2,1)}, bf16[192,1024]{1,0:T(8,128)(2,1)}, u32[]{:S(2)}, u32[]{:S(2)}) collective-permute-start(bf16[192,1024]{1,0:T(8,128)(2,1)} %add_convert_fusion.3), channel_id=1, source_target_pairs={{0,8},{4,12},{8,0},{12,4},{16,24},{20,28},{24,16},{28,20},{1,9},{5... | collective-permute-start | bytes 1179656 | tf_op jit(solution)/shard_map/ppermute | solution.py:35
  556.6 11.1 %collective-permute-done.59.refs_2_ = bf16[1024,256]{1,0:T(8,128)(2,1)} collective-permute-done((bf16[1024,256]{1,0:T(8,128)(2,1)S(1)}, bf16[1024,256]{1,0:T(8,128)(2,1)}, u32[]{:S(2)}, u32[]{:S(2)}) %collective-permute-start.59) | collective-permute-done | bytes 524320 | tf_op jit(solution)/shard_map/ppermute | solution.py:30
  567.7 10.5 %collective-permute-done.60.refs_3_ = bf16[1024,256]{1,0:T(8,128)(2,1)} collective-permute-done((bf16[1024,256]{1,0:T(8,128)(2,1)S(1)}, bf16[1024,256]{1,0:T(8,128)(2,1)}, u32[]{:S(2)}, u32[]{:S(2)}) %collective-permute-start.60) | collective-permute-done | bytes 524320 | tf_op jit(solution)/shard_map/ppermute | solution.py:30
  578.2 4.4 gather_back.1
  582.6 3.7 fusion.15
  607.0 4.0 collective-permute-done.100
  612.4 3.3 collective-permute-start.61
  623.5 6.4 collective-permute-done.80
  630.9 7.1 collective-permute-done.70
  638.9 5.5 collective-permute-done.71
  650.4 7.1 collective-permute-done.75
  658.5 4.8 collective-permute-done.82
  665.5 4.5 collective-permute-done.76
  673.1 17.5 %collective-permute-done.73 = bf16[384,384]{1,0:T(8,128)(2,1)S(1)} collective-permute-done((bf16[384,384]{1,0:T(8,128)(2,1)S(1)}, bf16[384,384]{1,0:T(8,128)(2,1)S(1)}, u32[]{:S(2)}, u32[]{:S(2)}) %collective-permute-start.73) | collective-permute-done | bytes 294944 | tf_op jit(solution)/shard_map/ppermute | solution.py:35
  695.1 6.7 collective-permute-done.78
  710.0 20.0 %collective-permute-start.68 = (bf16[256,1536]{1,0:T(8,128)(2,1)}, bf16[256,1536]{1,0:T(8,128)(2,1)}, u32[]{:S(2)}, u32[]{:S(2)}) collective-permute-start(bf16[256,1536]{1,0:T(8,128)(2,1)} %add_convert_fusion.2), channel_id=1, source_target_pairs={{0,1},{1,2},{2,3},{4,5},{5,6},{6,7},{8,9},{9,10},{10,11},{12,13},{... | collective-permute-start | bytes 2359304 | tf_op jit(solution)/shard_map/ppermute | solution.py:480
  730.1 3.5 fusion
  733.5 3.5 fusion.1
  747.9 3.3 maximum_add_fusion.1
  751.3 5.0 fusion.2
  (493 shorter events, 258.9 us)
Async XLA Ops:
  7.2 71.1 %all-gather.3.cloned.1.call-start = ((), (), s32[]{:S(2)}) async-start(), calls=%async_computation.1 | async-start | bytes 3932160 | tf_op jit(solution)/shard_map/all_gather | solution.py:533
  11.9 196.1 %all-gather.5.cloned.1.call-start = ((), (), s32[]{:S(2)}) async-start(), calls=%async_computation.2 | async-start | bytes 3932160 | tf_op jit(solution)/shard_map/all_gather | solution.py:533
  88.2 27.2 %collective-permute-start = (bf16[1024,512]{1,0:T(8,128)(2,1)}, bf16[1024,512]{1,0:T(8,128)(2,1)}, u32[]{:S(2)}, u32[]{:S(2)}) collective-permute-start(bf16[1024,512]{1,0:T(8,128)(2,1)} %slice.114), channel_id=1, source_target_pairs={{0,8},{4,12},{8,16},{12,20},{16,24},{20,28},{1,9},{5,13},{9,17},{1... | collective-permute-start | bytes 3145736 | tf_op jit(solution)/shard_map/ppermute | solution.py:30
  92.6 22.8 %collective-permute-start.1 = (bf16[1024,512]{1,0:T(8,128)(2,1)}, bf16[1024,512]{1,0:T(8,128)(2,1)}, u32[]{:S(2)}, u32[]{:S(2)}) collective-permute-start(bf16[1024,512]{1,0:T(8,128)(2,1)} %slice.114), channel_id=1, source_target_pairs={{0,4},{4,8},{8,12},{12,16},{16,20},{20,24},{24,28},{1,5},{5,9},{9,... | collective-permute-start | bytes 3145736 | tf_op jit(solution)/shard_map/ppermute | solution.py:30
  101.6 654.7 %reduce-scatter.2.cloned.1.call-start = ((), (), s32[]{:S(2)}) async-start(), calls=%async_computation.3 | async-start | bytes 3932160 | tf_op jit(solution)/shard_map/reduce_scatter | solution.py:456
  136.5 15.4 %collective-permute-start.2 = (bf16[128,1536]{1,0:T(8,128)(2,1)}, bf16[128,1536]{1,0:T(8,128)(2,1)}, u32[]{:S(2)}, u32[]{:S(2)}) collective-permute-start(bf16[128,1536]{1,0:T(8,128)(2,1)} %get-tuple-element.81), channel_id=1, source_target_pairs={{0,1},{4,5},{8,9},{12,13},{16,17},{20,21},{24,25},{28,29}} | collective-permute-start | bytes 1179656 | tf_op jit(solution)/shard_map/ppermute | solution.py:480
  153.3 18.0 %collective-permute-start.4 = (bf16[128,1536]{1,0:T(8,128)(2,1)S(1)}, bf16[128,1536]{1,0:T(8,128)(2,1)S(1)}, u32[]{:S(2)}, u32[]{:S(2)}) collective-permute-start(bf16[128,1536]{1,0:T(8,128)(2,1)S(1)} %get-tuple-element.83), channel_id=1, source_target_pairs={{0,1},{1,2},{4,5},{5,6},{8,9},{9,10},{12,13},{13,14},{16,17},{17,1... | collective-permute-start | bytes 1179656 | tf_op jit(solution)/shard_map/ppermute | solution.py:480
  157.7 15.4 %collective-permute-start.5 = (bf16[128,1536]{1,0:T(8,128)(2,1)S(1)}, bf16[128,1536]{1,0:T(8,128)(2,1)S(1)}, u32[]{:S(2)}, u32[]{:S(2)}) collective-permute-start(bf16[128,1536]{1,0:T(8,128)(2,1)S(1)} %get-tuple-element.84), channel_id=1, source_target_pairs={{2,1},{3,2},{6,5},{7,6},{10,9},{11,10},{14,13},{15,14},{18,17},{19... | collective-permute-start | bytes 1179656 | tf_op jit(solution)/shard_map/ppermute | solution.py:483
  198.7 17.9 %collective-permute-start.10 = (bf16[128,1536]{1,0:T(8,128)(2,1)}, bf16[128,1536]{1,0:T(8,128)(2,1)}, u32[]{:S(2)}, u32[]{:S(2)}) collective-permute-start(bf16[128,1536]{1,0:T(8,128)(2,1)} %get-tuple-element.90), channel_id=1, source_target_pairs={{0,1},{1,2},{2,3},{4,5},{5,6},{6,7},{8,9},{9,10},{10,11},{12,13},{... | collective-permute-start | bytes 1179656 | tf_op jit(solution)/shard_map/ppermute | solution.py:506
  200.7 15.8 %collective-permute-start.11 = (bf16[128,1536]{1,0:T(8,128)(2,1)}, bf16[128,1536]{1,0:T(8,128)(2,1)}, u32[]{:S(2)}, u32[]{:S(2)}) collective-permute-start(bf16[128,1536]{1,0:T(8,128)(2,1)} %get-tuple-element.90), channel_id=1, source_target_pairs={{1,0},{2,1},{3,2},{5,4},{6,5},{7,6},{9,8},{10,9},{11,10},{13,12},{... | collective-permute-start | bytes 1179656 | tf_op jit(solution)/shard_map/ppermute | solution.py:509
  235.6 14.4 %collective-permute-start.17 = (bf16[128,1536]{1,0:T(8,128)(2,1)}, bf16[128,1536]{1,0:T(8,128)(2,1)S(1)}, u32[]{:S(2)}, u32[]{:S(2)}) collective-permute-start(bf16[128,1536]{1,0:T(8,128)(2,1)} %add_convert_fusion.9), channel_id=1, source_target_pairs={{1,0},{2,1},{3,2},{5,4},{6,5},{7,6},{9,8},{10,9},{11,10},{13,12},{... | collective-permute-start | bytes 1179656 | tf_op jit(solution)/shard_map/ppermute | solution.py:483
  264.1 15.3 %collective-permute-start.20 = (bf16[128,1536]{1,0:T(8,128)(2,1)S(1)}, bf16[128,1536]{1,0:T(8,128)(2,1)S(1)}, u32[]{:S(2)}, u32[]{:S(2)}) collective-permute-start(bf16[128,1536]{1,0:T(8,128)(2,1)S(1)} %get-tuple-element.101), channel_id=1, source_target_pairs={{1,0},{2,1},{3,2},{5,4},{6,5},{7,6},{9,8},{10,9},{11,10},{13,12},{... | collective-permute-start | bytes 1179656 | tf_op jit(solution)/shard_map/ppermute | solution.py:509
  265.4 14.0 %collective-permute-start.21 = (bf16[128,1536]{1,0:T(8,128)(2,1)S(1)}, bf16[128,1536]{1,0:T(8,128)(2,1)S(1)}, u32[]{:S(2)}, u32[]{:S(2)}) collective-permute-start(bf16[128,1536]{1,0:T(8,128)(2,1)S(1)} %get-tuple-element.101), channel_id=1, source_target_pairs={{0,1},{1,2},{2,3},{4,5},{5,6},{6,7},{8,9},{9,10},{10,11},{12,13},{... | collective-permute-start | bytes 1179656 | tf_op jit(solution)/shard_map/ppermute | solution.py:506
  294.6 17.8 %collective-permute-start.27 = (bf16[128,1536]{1,0:T(8,128)(2,1)S(1)}, bf16[128,1536]{1,0:T(8,128)(2,1)S(1)}, u32[]{:S(2)}, u32[]{:S(2)}) collective-permute-start(bf16[128,1536]{1,0:T(8,128)(2,1)S(1)} %get-tuple-element.107), channel_id=1, source_target_pairs={{3,2},{7,6},{11,10},{15,14},{19,18},{23,22},{27,26},{31,30}} | collective-permute-start | bytes 1179656 | tf_op jit(solution)/shard_map/ppermute | solution.py:483
  295.3 17.1 %collective-permute-start.26 = (bf16[128,1536]{1,0:T(8,128)(2,1)S(1)}, bf16[128,1536]{1,0:T(8,128)(2,1)S(1)}, u32[]{:S(2)}, u32[]{:S(2)}) collective-permute-start(bf16[128,1536]{1,0:T(8,128)(2,1)S(1)} %get-tuple-element.106), channel_id=1, source_target_pairs={{0,1},{4,5},{8,9},{12,13},{16,17},{20,21},{24,25},{28,29}} | collective-permute-start | bytes 1179656 | tf_op jit(solution)/shard_map/ppermute | solution.py:480
  312.6 19.0 %collective-permute-start.29 = (bf16[128,1536]{1,0:T(8,128)(2,1)S(1)}, bf16[128,1536]{1,0:T(8,128)(2,1)S(1)}, u32[]{:S(2)}, u32[]{:S(2)}) collective-permute-start(bf16[128,1536]{1,0:T(8,128)(2,1)S(1)} %get-tuple-element.109), channel_id=1, source_target_pairs={{2,1},{3,2},{6,5},{7,6},{10,9},{11,10},{14,13},{15,14},{18,17},{19... | collective-permute-start | bytes 1179656 | tf_op jit(solution)/shard_map/ppermute | solution.py:483
  313.3 18.4 %collective-permute-start.28 = (bf16[128,1536]{1,0:T(8,128)(2,1)S(1)}, bf16[128,1536]{1,0:T(8,128)(2,1)S(1)}, u32[]{:S(2)}, u32[]{:S(2)}) collective-permute-start(bf16[128,1536]{1,0:T(8,128)(2,1)S(1)} %get-tuple-element.108), channel_id=1, source_target_pairs={{0,1},{1,2},{4,5},{5,6},{8,9},{9,10},{12,13},{13,14},{16,17},{17,1... | collective-permute-start | bytes 1179656 | tf_op jit(solution)/shard_map/ppermute | solution.py:480
  317.7 64.0 %collective-permute-start.40 = (bf16[768,1024]{1,0:T(8,128)(2,1)S(1)}, bf16[768,1024]{1,0:T(8,128)(2,1)S(1)}, u32[]{:S(2)}, u32[]{:S(2)}) collective-permute-start(bf16[768,1024]{1,0:T(8,128)(2,1)S(1)} %convolution_convert_fusion.6), channel_id=1, source_target_pairs={{0,4},{4,0},{8,12},{12,8},{16,20},{20,16},{24,28},{28,24},{1,5},{5... | collective-permute-start | bytes 4718600 | tf_op jit(solution)/shard_map/ppermute | solution.py:35
  325.4 63.1 %collective-permute-start.42 = (bf16[512,1536]{1,0:T(8,128)(2,1)S(1)}, bf16[512,1536]{1,0:T(8,128)(2,1)S(1)}, u32[]{:S(2)}, u32[]{:S(2)}) collective-permute-start(bf16[512,1536]{1,0:T(8,128)(2,1)S(1)} %convolution_convert_fusion.1), channel_id=1, source_target_pairs={{0,4},{4,0},{8,12},{12,8},{16,20},{20,16},{24,28},{28,24},{1,5},{5... | collective-permute-start | bytes 4718600 | tf_op jit(solution)/shard_map/ppermute | solution.py:35
  331.9 14.1 %collective-permute-start.31 = (bf16[128,1536]{1,0:T(8,128)(2,1)S(1)}, bf16[128,1536]{1,0:T(8,128)(2,1)S(1)}, u32[]{:S(2)}, u32[]{:S(2)}) collective-permute-start(bf16[128,1536]{1,0:T(8,128)(2,1)S(1)} %get-tuple-element.111), channel_id=1, source_target_pairs={{1,0},{2,1},{3,2},{5,4},{6,5},{7,6},{9,8},{10,9},{11,10},{13,12},{... | collective-permute-start | bytes 1179656 | tf_op jit(solution)/shard_map/ppermute | solution.py:483
  333.3 13.9 %collective-permute-start.30 = (bf16[128,1536]{1,0:T(8,128)(2,1)S(1)}, bf16[128,1536]{1,0:T(8,128)(2,1)S(1)}, u32[]{:S(2)}, u32[]{:S(2)}) collective-permute-start(bf16[128,1536]{1,0:T(8,128)(2,1)S(1)} %get-tuple-element.110), channel_id=1, source_target_pairs={{0,1},{1,2},{2,3},{4,5},{5,6},{6,7},{8,9},{9,10},{10,11},{12,13},{... | collective-permute-start | bytes 1179656 | tf_op jit(solution)/shard_map/ppermute | solution.py:480
  355.6 36.5 %collective-permute-start.41 = (bf16[768,1024]{1,0:T(8,128)(2,1)S(1)}, bf16[768,1024]{1,0:T(8,128)(2,1)S(1)}, u32[]{:S(2)}, u32[]{:S(2)}) collective-permute-start(bf16[768,1024]{1,0:T(8,128)(2,1)S(1)} %convolution_convert_fusion.5), channel_id=1, source_target_pairs={{0,4},{4,0},{8,12},{12,8},{16,20},{20,16},{24,28},{28,24},{1,5},{5... | collective-permute-start | bytes 4718600 | tf_op jit(solution)/shard_map/ppermute | solution.py:35
  355.6 15.0 %collective-permute-start.35 = (bf16[128,1536]{1,0:T(8,128)(2,1)S(1)}, bf16[128,1536]{1,0:T(8,128)(2,1)S(1)}, u32[]{:S(2)}, u32[]{:S(2)}) collective-permute-start(bf16[128,1536]{1,0:T(8,128)(2,1)S(1)} %get-tuple-element.112), channel_id=1, source_target_pairs={{0,1},{1,2},{2,3},{4,5},{5,6},{6,7},{8,9},{9,10},{10,11},{12,13},{... | collective-permute-start | bytes 1179656 | tf_op jit(solution)/shard_map/ppermute | solution.py:506
  381.6 14.0 %collective-permute-start.38 = (bf16[128,1536]{1,0:T(8,128)(2,1)S(1)}, bf16[128,1536]{1,0:T(8,128)(2,1)S(1)}, u32[]{:S(2)}, u32[]{:S(2)}) collective-permute-start(bf16[128,1536]{1,0:T(8,128)(2,1)S(1)} %collective-permute-done.35), channel_id=1, source_target_pairs={{1,2},{2,3},{5,6},{6,7},{9,10},{10,11},{13,14},{14,15},{17,18},{18... | collective-permute-start | bytes 1179656 | tf_op jit(solution)/shard_map/ppermute | solution.py:506
  397.1 21.7 %collective-permute-start.46 = (bf16[128,1536]{1,0:T(8,128)(2,1)}, bf16[128,1536]{1,0:T(8,128)(2,1)S(1)}, u32[]{:S(2)}, u32[]{:S(2)}) collective-permute-start(bf16[128,1536]{1,0:T(8,128)(2,1)} %get-tuple-element.123), channel_id=1, source_target_pairs={{1,0},{2,1},{3,2},{5,4},{6,5},{7,6},{9,8},{10,9},{11,10},{13,12},{... | collective-permute-start | bytes 1179656 | tf_op jit(solution)/shard_map/ppermute | solution.py:483
  398.4 20.4 %collective-permute-start.45 = (bf16[128,1536]{1,0:T(8,128)(2,1)}, bf16[128,1536]{1,0:T(8,128)(2,1)S(1)}, u32[]{:S(2)}, u32[]{:S(2)}) collective-permute-start(bf16[128,1536]{1,0:T(8,128)(2,1)} %get-tuple-element.122), channel_id=1, source_target_pairs={{0,1},{1,2},{2,3},{4,5},{5,6},{6,7},{8,9},{9,10},{10,11},{12,13},{... | collective-permute-start | bytes 1179656 | tf_op jit(solution)/shard_map/ppermute | solution.py:480
  407.5 29.5 %collective-permute-start.44 = (bf16[128,1536]{1,0:T(8,128)(2,1)}, bf16[128,1536]{1,0:T(8,128)(2,1)S(1)}, u32[]{:S(2)}, u32[]{:S(2)}) collective-permute-start(bf16[128,1536]{1,0:T(8,128)(2,1)} %copy-done.41), channel_id=1, source_target_pairs={{1,0},{5,4},{9,8},{13,12},{17,16},{21,20},{25,24},{29,28}} | collective-permute-start | bytes 1179656 | tf_op jit(solution)/shard_map/ppermute | solution.py:509
  409.0 29.7 %collective-permute-start.43 = (bf16[128,1536]{1,0:T(8,128)(2,1)}, bf16[128,1536]{1,0:T(8,128)(2,1)S(1)}, u32[]{:S(2)}, u32[]{:S(2)}) collective-permute-start(bf16[128,1536]{1,0:T(8,128)(2,1)} %copy-done.39), channel_id=1, source_target_pairs={{2,3},{6,7},{10,11},{14,15},{18,19},{22,23},{26,27},{30,31}} | collective-permute-start | bytes 1179656 | tf_op jit(solution)/shard_map/ppermute | solution.py:506
  411.3 50.8 %collective-permute-start.51 = (bf16[384,1024]{1,0:T(8,128)(2,1)S(1)}, bf16[384,1024]{1,0:T(8,128)(2,1)S(1)}, u32[]{:S(2)}, u32[]{:S(2)}) collective-permute-start(bf16[384,1024]{1,0:T(8,128)(2,1)S(1)} %dynamic-slice_convert_fusion.2), channel_id=1, source_target_pairs={{0,8},{4,12},{8,0},{12,4},{16,24},{20,28},{24,16},{28,20},{1,9},{5... | collective-permute-start | bytes 2359304 | tf_op jit(solution)/shard_map/ppermute | solution.py:35
  431.9 28.2 %collective-permute-start.48 = (bf16[128,1536]{1,0:T(8,128)(2,1)S(1)}, bf16[128,1536]{1,0:T(8,128)(2,1)S(1)}, u32[]{:S(2)}, u32[]{:S(2)}) collective-permute-start(bf16[128,1536]{1,0:T(8,128)(2,1)S(1)} %get-tuple-element.124), channel_id=1, source_target_pairs={{0,1},{1,2},{2,3},{4,5},{5,6},{6,7},{8,9},{9,10},{10,11},{12,13},{... | collective-permute-start | bytes 1179656 | tf_op jit(solution)/shard_map/ppermute | solution.py:506
  435.6 24.5 %collective-permute-start.47 = (bf16[128,1536]{1,0:T(8,128)(2,1)S(1)}, bf16[128,1536]{1,0:T(8,128)(2,1)S(1)}, u32[]{:S(2)}, u32[]{:S(2)}) collective-permute-start(bf16[128,1536]{1,0:T(8,128)(2,1)S(1)} %get-tuple-element.124), channel_id=1, source_target_pairs={{1,0},{2,1},{3,2},{5,4},{6,5},{7,6},{9,8},{10,9},{11,10},{13,12},{... | collective-permute-start | bytes 1179656 | tf_op jit(solution)/shard_map/ppermute | solution.py:509
  438.8 25.5 %collective-permute-start.52 = (bf16[384,1024]{1,0:T(8,128)(2,1)S(1)}, bf16[384,1024]{1,0:T(8,128)(2,1)S(1)}, u32[]{:S(2)}, u32[]{:S(2)}) collective-permute-start(bf16[384,1024]{1,0:T(8,128)(2,1)S(1)} %dynamic-slice_convert_fusion.1), channel_id=1, source_target_pairs={{0,16},{4,20},{8,24},{12,28},{16,0},{20,4},{24,8},{28,12},{1,17},{... | collective-permute-start | bytes 2359304 | tf_op jit(solution)/shard_map/ppermute | solution.py:35
  440.7 17.7 %collective-permute-start.105 = (f32[1,1536]{1,0:T(1,128)S(1)}, f32[1,1536]{1,0:T(1,128)S(1)}, u32[]{:S(2)}, u32[]{:S(2)}) collective-permute-start(f32[1,1536]{1,0:T(1,128)S(1)} %add.759), channel_id=1, source_target_pairs={{0,16},{4,20},{8,24},{12,28},{16,0},{20,4},{24,8},{28,12},{1,17},{... | collective-permute-start | bytes 18440 | tf_op jit(solution)/shard_map/ppermute | solution.py:35
  458.3 20.4 %collective-permute-start.53 = (bf16[256,1536]{1,0:T(8,128)(2,1)S(1)}, bf16[256,1536]{1,0:T(8,128)(2,1)S(1)}, u32[]{:S(2)}, u32[]{:S(2)}) collective-permute-start(bf16[256,1536]{1,0:T(8,128)(2,1)S(1)} %dynamic-slice_convert_fusion), channel_id=1, source_target_pairs={{0,8},{4,12},{8,0},{12,4},{16,24},{20,28},{24,16},{28,20},{1,9},{5... | collective-permute-start | bytes 2359304 | tf_op jit(solution)/shard_map/ppermute | solution.py:35
  460.1 20.5 %collective-permute-start.49 = (bf16[128,1536]{1,0:T(8,128)(2,1)S(1)}, bf16[128,1536]{1,0:T(8,128)(2,1)S(1)}, u32[]{:S(2)}, u32[]{:S(2)}) collective-permute-start(bf16[128,1536]{1,0:T(8,128)(2,1)S(1)} %collective-permute-done.48), channel_id=1, source_target_pairs={{1,2},{2,3},{5,6},{6,7},{9,10},{10,11},{13,14},{14,15},{17,18},{18... | collective-permute-start | bytes 1179656 | tf_op jit(solution)/shard_map/ppermute | solution.py:506
  460.8 19.8 %collective-permute-start.50 = (bf16[128,1536]{1,0:T(8,128)(2,1)S(1)}, bf16[128,1536]{1,0:T(8,128)(2,1)S(1)}, u32[]{:S(2)}, u32[]{:S(2)}) collective-permute-start(bf16[128,1536]{1,0:T(8,128)(2,1)S(1)} %collective-permute-done.47), channel_id=1, source_target_pairs={{1,0},{2,1},{5,4},{6,5},{9,8},{10,9},{13,12},{14,13},{17,16},{18,1... | collective-permute-start | bytes 1179656 | tf_op jit(solution)/shard_map/ppermute | solution.py:509
  462.5 20.1 %collective-permute-start.85 = (bf16[192,1024]{1,0:T(8,128)(2,1)S(1)}, bf16[192,1024]{1,0:T(8,128)(2,1)S(1)}, u32[]{:S(2)}, u32[]{:S(2)}) collective-permute-start(bf16[192,1024]{1,0:T(8,128)(2,1)S(1)} %dynamic-slice_convert_fusion.4), channel_id=1, source_target_pairs={{0,16},{4,20},{8,24},{12,28},{16,0},{20,4},{24,8},{28,12},{1,17},{... | collective-permute-start | bytes 1179656 | tf_op jit(solution)/shard_map/ppermute | solution.py:35
  464.6 20.7 %collective-permute-start.89 = (bf16[192,1024]{1,0:T(8,128)(2,1)S(1)}, bf16[192,1024]{1,0:T(8,128)(2,1)S(1)}, u32[]{:S(2)}, u32[]{:S(2)}) collective-permute-start(bf16[192,1024]{1,0:T(8,128)(2,1)S(1)} %dynamic-slice_convert_fusion.3), channel_id=1, source_target_pairs={{0,8},{4,12},{8,0},{12,4},{16,24},{20,28},{24,16},{28,20},{1,9},{5... | collective-permute-start | bytes 1179656 | tf_op jit(solution)/shard_map/ppermute | solution.py:35
  483.5 107.4 %collective-permute-start.86 = (bf16[192,1024]{1,0:T(8,128)(2,1)}, bf16[192,1024]{1,0:T(8,128)(2,1)}, u32[]{:S(2)}, u32[]{:S(2)}) collective-permute-start(bf16[192,1024]{1,0:T(8,128)(2,1)} %add_convert_fusion.4), channel_id=1, source_target_pairs={{0,16},{4,20},{8,24},{12,28},{16,0},{20,4},{24,8},{28,12},{1,17},{... | collective-permute-start | bytes 1179656 | tf_op jit(solution)/shard_map/ppermute | solution.py:35
  520.6 15.6 %collective-permute-start.57 = (bf16[1024,256]{1,0:T(8,128)(2,1)S(1)}, bf16[1024,256]{1,0:T(8,128)(2,1)}, u32[]{:S(2)}, u32[]{:S(2)}) collective-permute-start(bf16[1024,256]{1,0:T(8,128)(2,1)S(1)} %get-tuple-element.238), channel_id=1, source_target_pairs={{4,0},{8,4},{12,8},{16,12},{20,16},{24,20},{28,24},{5,1},{9,5},{13... | collective-permute-start | bytes 1572872 | tf_op jit(solution)/shard_map/ppermute | solution.py:30
  524.3 30.6 %collective-permute-start.58 = (bf16[1024,256]{1,0:T(8,128)(2,1)S(1)}, bf16[1024,256]{1,0:T(8,128)(2,1)}, u32[]{:S(2)}, u32[]{:S(2)}) collective-permute-start(bf16[1024,256]{1,0:T(8,128)(2,1)S(1)} %get-tuple-element.236), channel_id=1, source_target_pairs={{4,0},{8,4},{12,8},{16,12},{20,16},{24,20},{28,24},{5,1},{9,5},{13... | collective-permute-start | bytes 1572872 | tf_op jit(solution)/shard_map/ppermute | solution.py:30
  525.7 42.0 %collective-permute-start.59 = (bf16[1024,256]{1,0:T(8,128)(2,1)S(1)}, bf16[1024,256]{1,0:T(8,128)(2,1)}, u32[]{:S(2)}, u32[]{:S(2)}) collective-permute-start(bf16[1024,256]{1,0:T(8,128)(2,1)S(1)} %get-tuple-element.237), channel_id=1, source_target_pairs={{8,0},{12,4},{16,8},{20,12},{24,16},{28,20},{9,1},{13,5},{17,9},{2... | collective-permute-start | bytes 1572872 | tf_op jit(solution)/shard_map/ppermute | solution.py:30
  527.0 51.2 %collective-permute-start.60 = (bf16[1024,256]{1,0:T(8,128)(2,1)S(1)}, bf16[1024,256]{1,0:T(8,128)(2,1)}, u32[]{:S(2)}, u32[]{:S(2)}) collective-permute-start(bf16[1024,256]{1,0:T(8,128)(2,1)S(1)} %get-tuple-element.235), channel_id=1, source_target_pairs={{8,0},{12,4},{16,8},{20,12},{24,16},{28,20},{9,1},{13,5},{17,9},{2... | collective-permute-start | bytes 1572872 | tf_op jit(solution)/shard_map/ppermute | solution.py:30
  536.2 61.0 %collective-permute-start.90 = (bf16[192,1024]{1,0:T(8,128)(2,1)}, bf16[192,1024]{1,0:T(8,128)(2,1)}, u32[]{:S(2)}, u32[]{:S(2)}) collective-permute-start(bf16[192,1024]{1,0:T(8,128)(2,1)} %add_convert_fusion.3), channel_id=1, source_target_pairs={{0,8},{4,12},{8,0},{12,4},{16,24},{20,28},{24,16},{28,20},{1,9},{5... | collective-permute-start | bytes 1179656 | tf_op jit(solution)/shard_map/ppermute | solution.py:35
  555.0 57.4 %collective-permute-start.65 = (bf16[768,384]{1,0:T(8,128)(2,1)}, bf16[768,384]{1,0:T(8,128)(2,1)}, u32[]{:S(2)}, u32[]{:S(2)}) collective-permute-start(bf16[768,384]{1,0:T(8,128)(2,1)} %fusion.47), channel_id=1, source_target_pairs={{0,4},{4,0},{8,12},{12,8},{16,20},{20,16},{24,28},{28,24},{1,5},{5... | collective-permute-start | bytes 1769480 | tf_op jit(solution)/shard_map/ppermute | solution.py:35
  567.7 50.1 %collective-permute-start.67 = (bf16[192,1536]{1,0:T(8,128)(2,1)}, bf16[192,1536]{1,0:T(8,128)(2,1)}, u32[]{:S(2)}, u32[]{:S(2)}) collective-permute-start(bf16[192,1536]{1,0:T(8,128)(2,1)} %convolution_convert_fusion.4), channel_id=1, source_target_pairs={{0,4},{4,0},{8,12},{12,8},{16,20},{20,16},{24,28},{28,24},{1,5},{5... | collective-permute-start | bytes 1769480 | tf_op jit(solution)/shard_map/ppermute | solution.py:35
  592.7 27.3 %collective-permute-start.87 = (bf16[384,1024]{1,0:T(8,128)(2,1)S(1)}, bf16[384,1024]{1,0:T(8,128)(2,1)S(1)}, u32[]{:S(2)}, u32[]{:S(2)}) collective-permute-start(bf16[384,1024]{1,0:T(8,128)(2,1)S(1)} %maximum_select_fusion.9), channel_id=1, source_target_pairs={{0,8},{4,12},{8,0},{12,4},{16,24},{20,28},{24,16},{28,20},{1,9},{5... | collective-permute-start | bytes 2359304 | tf_op jit(solution)/shard_map/ppermute | solution.py:35
  598.9 21.9 %collective-permute-start.91 = (bf16[384,1024]{1,0:T(8,128)(2,1)S(1)}, bf16[384,1024]{1,0:T(8,128)(2,1)S(1)}, u32[]{:S(2)}, u32[]{:S(2)}) collective-permute-start(bf16[384,1024]{1,0:T(8,128)(2,1)S(1)} %maximum_select_fusion.10), channel_id=1, source_target_pairs={{0,16},{4,20},{8,24},{12,28},{16,0},{20,4},{24,8},{28,12},{1,17},{... | collective-permute-start | bytes 2359304 | tf_op jit(solution)/shard_map/ppermute | solution.py:35
  611.1 59.8 %collective-permute-start.62 = (bf16[256,1536]{1,0:T(8,128)(2,1)S(1)}, bf16[256,1536]{1,0:T(8,128)(2,1)S(1)}, u32[]{:S(2)}, u32[]{:S(2)}) collective-permute-start(bf16[256,1536]{1,0:T(8,128)(2,1)S(1)} %get-tuple-element.142), channel_id=1, source_target_pairs={{3,2},{7,6},{11,10},{15,14},{19,18},{23,22},{27,26},{31,30}} | collective-permute-start | bytes 2359304 | tf_op jit(solution)/shard_map/ppermute | solution.py:483
  612.4 59.1 %collective-permute-start.61 = (bf16[256,1536]{1,0:T(8,128)(2,1)S(1)}, bf16[256,1536]{1,0:T(8,128)(2,1)S(1)}, u32[]{:S(2)}, u32[]{:S(2)}) collective-permute-start(bf16[256,1536]{1,0:T(8,128)(2,1)S(1)} %get-tuple-element.141), channel_id=1, source_target_pairs={{0,1},{4,5},{8,9},{12,13},{16,17},{20,21},{24,25},{28,29}} | collective-permute-start | bytes 2359304 | tf_op jit(solution)/shard_map/ppermute | solution.py:480
  617.9 27.5 %collective-permute-start.66 = (bf16[768,384]{1,0:T(8,128)(2,1)S(1)}, bf16[768,384]{1,0:T(8,128)(2,1)S(1)}, u32[]{:S(2)}, u32[]{:S(2)}) collective-permute-start(bf16[768,384]{1,0:T(8,128)(2,1)S(1)} %fusion.50), channel_id=1, source_target_pairs={{0,4},{4,0},{8,12},{12,8},{16,20},{20,16},{24,28},{28,24},{1,5},{5... | collective-permute-start | bytes 1769480 | tf_op jit(solution)/shard_map/ppermute | solution.py:35
  620.8 17.3 %collective-permute-start.93 = (bf16[128,1536]{1,0:T(8,128)(2,1)S(1)}, bf16[128,1536]{1,0:T(8,128)(2,1)S(1)}, u32[]{:S(2)}, u32[]{:S(2)}) collective-permute-start(bf16[128,1536]{1,0:T(8,128)(2,1)S(1)} %convert_add_fusion.19), channel_id=1, source_target_pairs={{0,16},{4,20},{8,24},{12,28},{16,0},{20,4},{24,8},{28,12},{1,17},{... | collective-permute-start | bytes 1179656 | tf_op jit(solution)/shard_map/ppermute | solution.py:35
  638.0 72.1 %collective-permute-start.88 = (bf16[768,1024]{1,0:T(8,128)(2,1)S(1)}, bf16[768,1024]{1,0:T(8,128)(2,1)S(1)}, u32[]{:S(2)}, u32[]{:S(2)}) collective-permute-start(bf16[768,1024]{1,0:T(8,128)(2,1)S(1)} %maximum_select_fusion.3), channel_id=1, source_target_pairs={{0,4},{4,0},{8,12},{12,8},{16,20},{20,16},{24,28},{28,24},{1,5},{5... | collective-permute-start | bytes 4718600 | tf_op jit(solution)/shard_map/ppermute | solution.py:35
  645.3 18.9 %collective-permute-start.72 = (bf16[192,384]{1,0:T(8,128)(2,1)S(1)}, bf16[192,384]{1,0:T(8,128)(2,1)S(1)}, u32[]{:S(2)}, u32[]{:S(2)}) collective-permute-start(bf16[192,384]{1,0:T(8,128)(2,1)S(1)} %add_convert_fusion.15), channel_id=1, source_target_pairs={{0,16},{4,20},{8,24},{12,28},{16,0},{20,4},{24,8},{28,12},{1,17},{... | collective-permute-start | bytes 442376 | tf_op jit(solution)/shard_map/ppermute | solution.py:35
  664.2 28.8 %collective-permute-start.94 = (bf16[256,1536]{1,0:T(8,128)(2,1)S(1)}, bf16[256,1536]{1,0:T(8,128)(2,1)S(1)}, u32[]{:S(2)}, u32[]{:S(2)}) collective-permute-start(bf16[256,1536]{1,0:T(8,128)(2,1)S(1)} %maximum_select_fusion.11), channel_id=1, source_target_pairs={{0,8},{4,12},{8,0},{12,4},{16,24},{20,28},{24,16},{28,20},{1,9},{5... | collective-permute-start | bytes 2359304 | tf_op jit(solution)/shard_map/ppermute | solution.py:35
  670.0 20.6 %collective-permute-start.73 = (bf16[384,384]{1,0:T(8,128)(2,1)S(1)}, bf16[384,384]{1,0:T(8,128)(2,1)S(1)}, u32[]{:S(2)}, u32[]{:S(2)}) collective-permute-start(bf16[384,384]{1,0:T(8,128)(2,1)S(1)} %maximum_select_fusion.15), channel_id=1, source_target_pairs={{0,8},{4,12},{8,0},{12,4},{16,24},{20,28},{24,16},{28,20},{1,9},{5... | collective-permute-start | bytes 884744 | tf_op jit(solution)/shard_map/ppermute | solution.py:35
  670.9 21.4 %collective-permute-start.83 = (bf16[96,1536]{1,0:T(8,128)(2,1)S(1)}, bf16[96,1536]{1,0:T(8,128)(2,1)S(1)}, u32[]{:S(2)}, u32[]{:S(2)}) collective-permute-start(bf16[96,1536]{1,0:T(8,128)(2,1)S(1)} %maximum_select_fusion.17), channel_id=1, source_target_pairs={{0,16},{4,20},{8,24},{12,28},{16,0},{20,4},{24,8},{28,12},{1,17},{... | collective-permute-start | bytes 884744 | tf_op jit(solution)/shard_map/ppermute | solution.py:35
  671.5 20.6 %collective-permute-start.77 = (bf16[192,384]{1,0:T(8,128)(2,1)S(1)}, bf16[192,384]{1,0:T(8,128)(2,1)S(1)}, u32[]{:S(2)}, u32[]{:S(2)}) collective-permute-start(bf16[192,384]{1,0:T(8,128)(2,1)S(1)} %add_convert_fusion.14), channel_id=1, source_target_pairs={{0,8},{4,12},{8,0},{12,4},{16,24},{20,28},{24,16},{28,20},{1,9},{5... | collective-permute-start | bytes 442376 | tf_op jit(solution)/shard_map/ppermute | solution.py:35
  690.6 16.0 %collective-permute-start.63 = (bf16[256,1536]{1,0:T(8,128)(2,1)S(1)}, bf16[256,1536]{1,0:T(8,128)(2,1)S(1)}, u32[]{:S(2)}, u32[]{:S(2)}) collective-permute-start(bf16[256,1536]{1,0:T(8,128)(2,1)S(1)} %get-tuple-element.144), channel_id=1, source_target_pairs={{0,1},{1,2},{4,5},{5,6},{8,9},{9,10},{12,13},{13,14},{16,17},{17,1... | collective-permute-start | bytes 2359304 | tf_op jit(solution)/shard_map/ppermute | solution.py:480
  701.8 31.8 %collective-permute-start.92 = (bf16[768,1024]{1,0:T(8,128)(2,1)S(1)}, bf16[768,1024]{1,0:T(8,128)(2,1)S(1)}, u32[]{:S(2)}, u32[]{:S(2)}) collective-permute-start(bf16[768,1024]{1,0:T(8,128)(2,1)S(1)} %maximum_select_fusion.4), channel_id=1, source_target_pairs={{0,4},{4,0},{8,12},{12,8},{16,20},{20,16},{24,28},{28,24},{1,5},{5... | collective-permute-start | bytes 4718600 | tf_op jit(solution)/shard_map/ppermute | solution.py:35
  704.4 46.9 %collective-permute-start.95 = (bf16[512,1536]{1,0:T(8,128)(2,1)}, bf16[512,1536]{1,0:T(8,128)(2,1)}, u32[]{:S(2)}, u32[]{:S(2)}) collective-permute-start(bf16[512,1536]{1,0:T(8,128)(2,1)} %maximum_select_fusion.5), channel_id=1, source_target_pairs={{0,4},{4,0},{8,12},{12,8},{16,20},{20,16},{24,28},{28,24},{1,5},{5... | collective-permute-start | bytes 4718600 | tf_op jit(solution)/shard_map/ppermute | solution.py:35
  706.6 30.4 %collective-permute-start.79 = (bf16[768,384]{1,0:T(8,128)(2,1)S(1)}, bf16[768,384]{1,0:T(8,128)(2,1)S(1)}, u32[]{:S(2)}, u32[]{:S(2)}) collective-permute-start(bf16[768,384]{1,0:T(8,128)(2,1)S(1)} %maximum_select_fusion.13), channel_id=1, source_target_pairs={{0,4},{4,0},{8,12},{12,8},{16,20},{20,16},{24,28},{28,24},{1,5},{5... | collective-permute-start | bytes 1769480 | tf_op jit(solution)/shard_map/ppermute | solution.py:35
  708.7 35.9 %collective-permute-start.69 = (bf16[256,1536]{1,0:T(8,128)(2,1)}, bf16[256,1536]{1,0:T(8,128)(2,1)}, u32[]{:S(2)}, u32[]{:S(2)}) collective-permute-start(bf16[256,1536]{1,0:T(8,128)(2,1)} %add_convert_fusion.1), channel_id=1, source_target_pairs={{1,0},{2,1},{3,2},{5,4},{6,5},{7,6},{9,8},{10,9},{11,10},{13,12},{... | collective-permute-start | bytes 2359304 | tf_op jit(solution)/shard_map/ppermute | solution.py:483
  710.0 35.7 %collective-permute-start.68 = (bf16[256,1536]{1,0:T(8,128)(2,1)}, bf16[256,1536]{1,0:T(8,128)(2,1)}, u32[]{:S(2)}, u32[]{:S(2)}) collective-permute-start(bf16[256,1536]{1,0:T(8,128)(2,1)} %add_convert_fusion.2), channel_id=1, source_target_pairs={{0,1},{1,2},{2,3},{4,5},{5,6},{6,7},{8,9},{9,10},{10,11},{12,13},{... | collective-permute-start | bytes 2359304 | tf_op jit(solution)/shard_map/ppermute | solution.py:480
  (117 other events, 1525.3 us)
Sparse Core Ops, SparseCore 0:
  12.1 66.1 all-gather.2
  101.7 65.4 all-gather.4
  519.4 76.0 reduce-scatter.1

commit v4 on v1

--- a/solution.py
+++ b/solution.py
@@ -8,8 +8,7 @@
 from jax.experimental.pallas import tpu as pltpu
 from jax.sharding import PartitionSpec as P
 
-QUERY_HEADS = 16
-KEY_VALUE_HEADS = 8
+
 HEAD_SIZE = 96
 LONGEST_DOCUMENT = 2048
 
@@ -17,6 +16,7 @@
 HALF_LANES = LANES // 2
 FAR = -1e30
 
+
 epsilon = 1e-05
 rope_base = 100000.0
 
@@ -25,6 +25,8 @@
 
 
 def from_behind(value, axis, steps):
+    if steps == 0:
+        return value
     count = lax.axis_size(axis)
     leading, last = (max(0, -steps), min(count, count - steps))
     return lax.ppermute(value, axis, [(source, source + steps) for source in range(leading, last)])
@@ -45,13 +47,16 @@
     return (jnp.cos(angles), jnp.sin(angles) * sign[None, :])
 
 
-def spread_matrix(heads, dtype=bf16):
+def spread_matrix(heads, gap_after=0, gap=0, dtype=bf16):
     half_size = HEAD_SIZE // 2
     rows = jnp.arange(heads * HEAD_SIZE, dtype=jnp.int32)
     inner = rows % HEAD_SIZE
     lane = (rows // HEAD_SIZE) * LANES + jnp.where(
         inner < half_size, inner, inner - half_size + HALF_LANES
     )
+    if gap:
+        cut = gap_after * HEAD_SIZE
+        lane = jnp.concatenate([lane[:cut], jnp.full((gap,), -1, jnp.int32), lane[cut:]])
     columns = jnp.arange(heads * LANES, dtype=jnp.int32)
     return (lane[:, None] == columns[None, :]).astype(dtype)
 
@@ -75,18 +80,21 @@
     return value * cosine - pltpu.roll(value, HALF_LANES, 1) * sine
 
 
-def project_kernel(rotated, rows_ref, weight_ref, cosine_ref, sine_ref, out_ref):
+def project_kernel(rotated, rows_ref, weight_ref, cosine_ref, sine_ref, *out_refs):
     product = jnp.dot(rows_ref[...], weight_ref[...], preferred_element_type=f32)
     cosine = cosine_ref[...]
     sine = sine_ref[...]
-    for head in range(out_ref.shape[1] // LANES):
-        part = product[:, head * LANES : (head + 1) * LANES]
-        if head < rotated:
-            part = turn(part, cosine, sine)
-        out_ref[:, head * LANES : (head + 1) * LANES] = part.astype(bf16)
-
-
-def project(rows, weight, cosine, sine, rotated, block):
+    head = 0
+    for out_ref in out_refs:
+        for place in range(out_ref.shape[1] // LANES):
+            part = product[:, head * LANES : (head + 1) * LANES]
+            if head < rotated:
+                part = turn(part, cosine, sine)
+            out_ref[:, place * LANES : (place + 1) * LANES] = part.astype(bf16)
+            head += 1
+
+
+def project(rows, weight, cosine, sine, rotated, widths, block):
     count, depth = rows.shape
     width = weight.shape[1]
     return pl.pallas_call(
@@ -98,8 +106,8 @@
             pl.BlockSpec((block, LANES), lambda i: (i, 0)),
             pl.BlockSpec((block, LANES), lambda i: (i, 0)),
         ],
-        out_specs=pl.BlockSpec((block, width), lambda i: (i, 0)),
-        out_shape=jax.ShapeDtypeStruct((count, width), bf16),
+        out_specs=[pl.BlockSpec((block, part), lambda i: (i, 0)) for part in widths],
+        out_shape=[jax.ShapeDtypeStruct((count, part), bf16) for part in widths],
         cost_estimate=pl.CostEstimate(
             flops=2 * count * depth * width,
             bytes_accessed=2 * (count * depth + depth * width + count * width),
@@ -180,7 +188,7 @@
     log_ref[0, 0] = top[...] * factor + jnp.log2(total[...])
 
 
-def window_specs(tiles, stretch, first_column):
+def window_specs(stretch, first_column):
     return [
         pl.BlockSpec((stretch, LANES), lambda g, i, *s, c=c: (0, c + g)) for c in first_column
     ]
@@ -203,8 +211,8 @@
             pl.BlockSpec((rows, group * LANES), lambda g, i, *s: (i, g)),
             pl.BlockSpec((1, 1, rows), lambda g, i, *s: (i, 0, 0)),
         ]
-        + window_specs(tiles, stretch, key_columns)
-        + window_specs(tiles, stretch, value_columns),
+        + window_specs(stretch, key_columns)
+        + window_specs(stretch, value_columns),
         out_specs=[
             pl.BlockSpec((rows, group * LANES), lambda g, i, *s: (i, g)),
             pl.BlockSpec((1, 1, 1, pairs), lambda g, i, *s: (g, i, 0, 0)),
@@ -232,19 +240,26 @@
     )(low, queries_joined, firsts, *arrays, *arrays)
 
 
-def attend_back_kernel(tiles, group, factor, scale, low_ref, query_ref, first_ref, *refs):
-    mixed_ref, grad_ref, log_ref, cosine_ref, sine_ref = refs[:5]
-    keys = refs[5 : 5 + tiles]
-    values = refs[5 + tiles : 5 + 2 * tiles]
+def attend_back_kernel(
+    tiles, chunks, group, factor, scale, low_ref, slot_ref, query_ref, first_ref, *refs
+):
+    mixed_ref, log_ref, cosine_ref, sine_ref = refs[:4]
+    grad_refs = refs[4 : 4 + chunks]
+    refs = refs[4 + chunks :]
+    keys = refs[:tiles]
+    values = refs[tiles : 2 * tiles]
     (
         query_out,
+        key_own,
+        value_own,
+        earlier_out,
         key_out,
         value_out,
         key_window,
         value_window,
         key_turned,
         query_total,
-    ) = refs[5 + 2 * tiles :]
+    ) = refs[2 * tiles :]
     query_block = pl.program_id(1)
     rows = query_ref.shape[0]
     stretch = keys[0].shape[0]
@@ -264,7 +279,9 @@
 
     offset = (tiles - 1) * stretch
     query = pair_rows(query_ref, group)
-    grad = pair_rows(grad_ref, group)
+    grad = jnp.concatenate(
+        [ref[:, h * LANES : (h + 1) * LANES] for h in range(group) for ref in grad_refs], axis=0
+    )
     mixed = pair_rows(mixed_ref, group)
     inner = jnp.sum((grad.astype(f32) * mixed.astype(f32)).T, axis=0, keepdims=True)
     log_total = log_ref[0, 0]
@@ -297,9 +314,18 @@
             part, cosine_ref[...], sine_ref[...]
         ).astype(bf16)
 
+    @pl.when(query_block == pl.num_programs(1) - 1)
+    def _():
+        for tile in range(tiles - 1):
+            at = pl.ds(tile * stretch, stretch)
+            earlier_out[tile, 0] = key_out[at, :].astype(bf16)
+            earlier_out[tile, 1] = value_out[at, :].astype(bf16)
+        key_own[...] = key_out[pl.ds(offset, stretch), :]
+        value_own[...] = value_out[pl.ds(offset, stretch), :]
+
 
 def attend_back(
-    queries_joined, windows, firsts, low, mixed, grads, logs, cosine, sine,
+    queries_joined, windows, firsts, low, slots, mixed, grads, logs, cosine, sine,
     kv_heads, group, rows, tile_rows,
 ):
     stretch = queries_joined.shape[0]
@@ -307,6 +333,7 @@
     blocks = stretch // rows
     pairs = group * rows
     window_tiles = tiles * stretch // tile_rows
+    chunks = len(grads)
     scale = HEAD_SIZE ** (-0.5)
     factor = scale * math.log2(math.e)
     key_columns = [at for _, at in windows]
@@ -314,23 +341,29 @@
     arrays = [a for a, _ in windows]
     heads_spec = pl.BlockSpec((rows, group * LANES), lambda g, i, *s: (i, g))
     table_spec = pl.BlockSpec((rows, LANES), lambda g, i, *s: (i, 0))
-    total_spec = pl.BlockSpec((tiles * stretch, LANES), lambda g, i, *s: (0, g))
+    own_spec = pl.BlockSpec((stretch, LANES), lambda g, i, *s: (0, g))
+    earlier_spec = pl.BlockSpec((tiles - 1, 2, stretch, LANES), lambda g, i, *s: (0, 0, 0, g))
     grid_spec = pltpu.PrefetchScalarGridSpec(
-        num_scalar_prefetch=1,
+        num_scalar_prefetch=2,
         grid=(kv_heads, blocks),
         in_specs=[
             heads_spec,
             pl.BlockSpec((1, 1, rows), lambda g, i, *s: (i, 0, 0)),
             heads_spec,
-            heads_spec,
             pl.BlockSpec((1, 1, 1, pairs), lambda g, i, *s: (g, i, 0, 0)),
             table_spec,
             table_spec,
         ]
-        + window_specs(tiles, stretch, key_columns)
-        + window_specs(tiles, stretch, value_columns),
-        out_specs=[heads_spec, total_spec, total_spec],
+        + [
+            pl.BlockSpec((rows // chunks, group * LANES), lambda g, i, low, slot: (slot[i], g))
+        ]
+        * chunks
+        + window_specs(stretch, key_columns)
+        + window_specs(stretch, value_columns),
+        out_specs=[heads_spec, own_spec, own_spec, earlier_spec],
         scratch_shapes=[
+            pltpu.VMEM((tiles * stretch, LANES), f32),
+            pltpu.VMEM((tiles * stretch, LANES), f32),
             pltpu.VMEM((window_tiles, tile_rows, LANES), bf16),
             pltpu.VMEM((window_tiles, tile_rows, LANES), bf16),
             pltpu.VMEM((window_tiles, LANES, tile_rows), bf16),
@@ -339,81 +372,96 @@
     )
     work = stretch * stretch * kv_heads * group
     return pl.pallas_call(
-        functools.partial(attend_back_kernel, tiles, group, factor, scale),
+        functools.partial(attend_back_kernel, tiles, chunks, group, factor, scale),
         grid_spec=grid_spec,
         out_shape=[
             jax.ShapeDtypeStruct((stretch, kv_heads * group * LANES), bf16),
-            jax.ShapeDtypeStruct((tiles * stretch, kv_heads * LANES), f32),
-            jax.ShapeDtypeStruct((tiles * stretch, kv_heads * LANES), f32),
+            jax.ShapeDtypeStruct((stretch, kv_heads * LANES), f32),
+            jax.ShapeDtypeStruct((stretch, kv_heads * LANES), f32),
+            jax.ShapeDtypeStruct((tiles - 1, 2, stretch, kv_heads * LANES), bf16),
         ],
         cost_estimate=pl.CostEstimate(
             flops=40 * LANES * work, bytes_accessed=16 * stretch * stretch, transcendentals=work
         ),
         name="attend_back",
-    )(low, queries_joined, firsts, mixed, grads, logs, cosine, sine, *arrays, *arrays)
+    )(low, slots, queries_joined, firsts, mixed, logs, cosine, sine, *grads, *arrays, *arrays)
 
 
 def gather_back_kernel(kv_heads, parts, key_ref, value_ref, cosine_ref, sine_ref, *refs):
-    out_ref = refs[2 * parts]
+    out_ref = refs[parts]
     for head in range(kv_heads):
         at = pl.ds(head * LANES, LANES)
         key = key_ref[:, at]
         value = value_ref[:, at]
         for part in range(parts):
-            key = key + refs[2 * part][:, at].astype(f32)
-            value = value + refs[2 * part + 1][:, at].astype(f32)
+            key = key + refs[part][0, :, at].astype(f32)
+            value = value + refs[part][1, :, at].astype(f32)
         out_ref[:, at] = turn_back(key, cosine_ref[...], sine_ref[...]).astype(bf16)
         out_ref[:, pl.ds((kv_heads + head) * LANES, LANES)] = value.astype(bf16)
 
 
 def gather_back(key_totals, value_totals, received, cosine, sine, kv_heads, stretch, block):
-    skipped = key_totals.shape[0] // block - stretch // block
     width = kv_heads * LANES
-    own = pl.BlockSpec((block, width), lambda i: (i + skipped, 0))
-    other = pl.BlockSpec((block, width), lambda i: (i, 0))
+    own = pl.BlockSpec((block, width), lambda i: (i, 0))
+    other = pl.BlockSpec((2, block, width), lambda i: (0, i, 0))
     table = pl.BlockSpec((block, LANES), lambda i: (i, 0))
-    flat = [array for pair in received for array in pair]
     return pl.pallas_call(
         functools.partial(gather_back_kernel, kv_heads, len(received)),
         grid=(stretch // block,),
-        in_specs=[own, own, table, table] + [other] * len(flat),
+        in_specs=[own, own, table, table] + [other] * len(received),
         out_specs=pl.BlockSpec((block, 2 * width), lambda i: (i, 0)),
         out_shape=jax.ShapeDtypeStruct((stretch, 2 * width), bf16),
         name="gather_back",
-    )(key_totals, value_totals, cosine, sine, *flat)
-
-
-def product_over(left, right, axis, order):
-    count = lax.axis_size(axis)
-    index = lax.axis_index(axis)
-    size = left.shape[1] // 2
-
-    def times(offset):
-        part = lax.dynamic_slice_in_dim(left, offset, size, 1)
-        return jnp.dot(part.T, right, preferred_element_type=f32)
-
-    kept = None
-    for place in order:
-        bit = (index >> place) & 1
-        if kept is None:
-            sent = times((1 - bit) * size).astype(bf16)
-            got = exchange(sent, axis, 1 << place)
-            kept = times(bit * size) + got.astype(f32)
-        else:
-            size //= 2
-            sent = lax.dynamic_slice_in_dim(kept, (1 - bit) * size, size, 0).astype(bf16)
-            got = exchange(sent, axis, 1 << place)
-            kept = lax.dynamic_slice_in_dim(kept, bit * size, size, 0) + got.astype(f32)
-    whole = kept.astype(bf16)
-    for place in reversed(order):
-        bit = (index >> place) & 1
-        got = exchange(whole, axis, 1 << place)
-        whole = jnp.where(
-            bit == 1,
+    )(key_totals, value_totals, cosine, sine, *received)
+
+
+class SharedProduct:
+
+    def __init__(self, left, right, axis, order):
+        self.left, self.right, self.axis, self.order = left, right, axis, order
+        self.size = left.shape[1] // 2
+        self.sent = self.times(0, True).astype(bf16)
+
+    def bit(self, place):
+        return (lax.axis_index(self.axis) >> place) & 1
+
+    def times(self, place, other):
+        bit = self.bit(self.order[place])
+        offset = ((1 - bit) if other else bit) * self.size
+        part = lax.dynamic_slice_in_dim(self.left, offset, self.size, 1)
+        return jnp.dot(part.T, self.right, preferred_element_type=f32)
+
+    def meet(self):
+        got = exchange(self.sent, self.axis, 1 << self.order[0])
+        self.value = self.times(0, False) + got.astype(f32)
+        self.down = list(self.order[1:])
+        self.up = list(reversed(self.order))
+        return self.value
+
+    def step(self):
+        if self.down:
+            place = self.down.pop(0)
+            bit = self.bit(place)
+            size = self.value.shape[0] // 2
+            sent = lax.dynamic_slice_in_dim(self.value, (1 - bit) * size, size, 0).astype(bf16)
+            got = exchange(sent, self.axis, 1 << place)
+            kept = lax.dynamic_slice_in_dim(self.value, bit * size, size, 0)
+            self.value = kept + got.astype(f32)
+            return self.value
+        place = self.up.pop(0)
+        whole = self.value.astype(bf16)
+        got = exchange(whole, self.axis, 1 << place)
+        self.value = jnp.where(
+            self.bit(place) == 1,
             jnp.concatenate([got, whole], axis=0),
             jnp.concatenate([whole, got], axis=0),
         )
-    return whole.astype(f32)
+        return self.value
+
+    def finish(self):
+        while self.up:
+            self.step()
+        return self.value
 
 
 def sum_everywhere(value, axes):
@@ -426,18 +474,12 @@
     return value
 
 
-def scatter_sum(product):
-    return lax.psum_scatter(
-        product.astype(bf16), "tensor", scatter_dimension=0, tiled=True
-    ).astype(f32)
+def scatter_low(product):
+    return lax.psum_scatter(product.astype(bf16), "tensor", scatter_dimension=0, tiled=True)
 
 
 def gather_rows(rows):
     return lax.all_gather(rows, "tensor", axis=0, tiled=True)
-
-
-def after(value, *others):
-    return lax.optimization_barrier((value,) + others)[0]
 
 
 def per_device(
@@ -464,113 +506,145 @@
     blocks = stretch // rows
     places = list(range((lax.axis_size("dp") - 1).bit_length()))
     crossed = places[:1] + places[:0:-1]
+    tied = lax.optimization_barrier
 
     normed_own, inv_rms_attn = normalize(block_input, attn_gain)
     attention_normed = gather_rows(normed_own)
-    out_low = gather_rows(after(out_grad.astype(bf16), attention_normed))
+    out_low = gather_rows(out_grad.astype(bf16))
 
     query_spread = spread_matrix(heads)
-    kv_spread = spread_matrix(2 * kv_heads)
+    gap = -kv_heads * HEAD_SIZE % LANES
+    kv_spread = spread_matrix(2 * kv_heads, kv_heads, gap)
     all_spread = spread_matrix(heads + 2 * kv_heads)
     w_joined = jnp.dot(
         jnp.concatenate([w_query, key_weight, value_weight], axis=1), all_spread,
         preferred_element_type=bf16,
     )
     w_out_spread = jnp.dot(query_spread.T, w_out, preferred_element_type=bf16)
+    w_pair = jnp.concatenate([w_gate, w_up], axis=1)
     cosine, sine = rope_tables(positions)
     local = jnp.arange(stretch, dtype=jnp.int32)
     window_first = reach * stretch + local - positions
     firsts = window_first.reshape(blocks, 1, rows)
     low = jnp.min(window_first.reshape(blocks, rows), axis=1) // tile_rows
 
-    joined = project(attention_normed, w_joined, cosine, sine, heads + kv_heads, rows)
-    key_value = joined[:, heads * LANES :]
-    windows = [(from_behind(key_value, "dp", d), 0) for d in range(reach, 0, -1)]
-    windows = windows + [(joined, heads)]
-    attended, logs = attend(joined, windows, firsts, low, kv_heads, group, rows, tile_rows)
-
-    residual = block_input + scatter_sum(
-        jnp.dot(attended, w_out_spread, preferred_element_type=f32)
-    )
+    queries, key_value = project(
+        attention_normed, w_joined, cosine, sine, heads + kv_heads,
+        (heads * LANES, 2 * kv_heads * LANES), rows,
+    )
+    windows = [(from_behind(key_value, "dp", d), 0) for d in range(reach, -1, -1)]
+    attended, logs = attend(queries, windows, firsts, low, kv_heads, group, rows, tile_rows)
+    hidden_grad = jnp.dot(out_low, w_down.T, preferred_element_type=f32)
+    mixed = scatter_low(jnp.dot(attended, w_out_spread, preferred_element_type=f32))
+    mixed, hidden_grad = tied((mixed, hidden_grad))
+    residual = block_input + mixed.astype(f32)
     mlp_normed_own, inv_rms_mlp = normalize(residual, mlp_gain)
     normed_mlp = gather_rows(mlp_normed_own)
-    gate_pre = jnp.dot(normed_mlp, w_gate, preferred_element_type=f32)
-    up_proj = jnp.dot(normed_mlp, w_up, preferred_element_type=f32)
+
+    width = w_gate.shape[1]
+    pre = jnp.dot(normed_mlp, w_pair, preferred_element_type=f32)
+    gate_pre, up_proj = pre[:, :width], pre[:, width:]
     sigmoid_gate = jax.nn.sigmoid(gate_pre)
     silu_gate = gate_pre * sigmoid_gate
     hidden = (silu_gate * up_proj).astype(bf16)
-    hidden_grad = jnp.dot(out_low, w_down.T, preferred_element_type=f32)
-    gate_grad = (
-        hidden_grad * up_proj * sigmoid_gate * (1.0 + gate_pre * (1.0 - sigmoid_gate))
-    ).astype(bf16)
-    up_grad = (hidden_grad * silu_gate).astype(bf16)
-    mlp_normed_grad = scatter_sum(
-        jnp.dot(gate_grad, w_gate.T, preferred_element_type=f32)
-        + jnp.dot(up_grad, w_up.T, preferred_element_type=f32)
-    )
+    gate_grad = hidden_grad * up_proj * sigmoid_gate * (1.0 + gate_pre * (1.0 - sigmoid_gate))
+    up_grad = hidden_grad * silu_gate
+    pair_grad = jnp.concatenate([gate_grad.astype(bf16), up_grad.astype(bf16)], axis=1)
+    mlp_scattered = scatter_low(jnp.dot(pair_grad, w_pair.T, preferred_element_type=f32))
+    down_product = jnp.dot(hidden, w_down, preferred_element_type=f32).astype(bf16)
+    pair_shared = SharedProduct(normed_mlp, pair_grad, "dp", places)
+    down_shared = SharedProduct(hidden, out_low, "dp", crossed)
+    wide = (pair_shared, down_shared)
+    for shared in wide:
+        shared.meet()
+        shared.step()
+    mlp_scattered, down_product, pair_shared.value, down_shared.value = tied(
+        (mlp_scattered, down_product, pair_shared.value, down_shared.value)
+    )
+    mlp_normed_grad = mlp_scattered.astype(f32)
     residual_part = normalize_back(residual, inv_rms_mlp, mlp_gain, mlp_normed_grad)
     residual_grad = out_grad + residual_part
     residual_low = gather_rows(residual_grad.astype(bf16))
-
-    down_product = after(
-        jnp.dot(hidden, w_down, preferred_element_type=f32).astype(bf16), residual_low
-    )
-    block_output = residual + scatter_sum(down_product)
-
-    grad_gate = product_over(normed_mlp, gate_grad, "dp", places)
-    grad_up = product_over(normed_mlp, up_grad, "dp", crossed)
-    grad_down = product_over(hidden, out_low, "dp", places)
-
     attended_plain = jnp.dot(attended, query_spread.T, preferred_element_type=bf16)
-    grad_out = product_over(attended_plain, residual_low, "dp", crossed)
+    for shared in wide:
+        for _ in range(len(places) - 1):
+            shared.step()
+    residual_low, down_product, pair_shared.value, down_shared.value = tied(
+        (residual_low, down_product, pair_shared.value, down_shared.value)
+    )
+    block_scattered = lax.psum_scatter(
+        down_product, "tensor", scatter_dimension=0, tiled=True
+    )
+    block_output = residual + block_scattered.astype(f32)
+
     attended_gradient = jnp.dot(residual_low, w_out_spread.T, preferred_element_type=f32).astype(
         bf16
     )
-    query_grad, key_totals, value_totals = attend_back(
-        joined, windows, firsts, low, attended, attended_gradient, logs, cosine, sine,
-        kv_heads, group, rows, tile_rows,
-    )
-    received = []
-    for distance in range(1, reach + 1):
-        begin = (reach - distance) * stretch
-        received.append(
-            [
-                from_behind(total[begin : begin + stretch].astype(bf16), "dp", -distance)
-                for total in (key_totals, value_totals)
-            ]
+    slots = jnp.arange(blocks, dtype=jnp.int32)
+    query_grad, key_own, value_own, earlier = attend_back(
+        queries, windows, firsts, low, slots, attended, [attended_gradient], logs, cosine,
+        sine, kv_heads, group, rows, tile_rows,
+    )
+    for shared in wide:
+        while len(shared.up) > 1:
+            shared.step()
+    earlier, pair_shared.value, down_shared.value, attended_plain = tied(
+        (earlier, pair_shared.value, down_shared.value, attended_plain)
+    )
+    received = [
+        from_behind(earlier[reach - d], "dp", -d) for d in range(1, reach + 1)
+    ]
+    out_shared = SharedProduct(attended_plain, residual_low, "dp", crossed)
+    out_shared.meet()
+    key_value_grad = gather_back(
+        key_own, value_own, received, cosine, sine, kv_heads, stretch, rows
+    )
+    split = heads * LANES
+    attn_normed_part = (
+        jnp.dot(query_grad, w_joined[:, :split].T, preferred_element_type=f32)
+        + jnp.dot(key_value_grad, w_joined[:, split:].T, preferred_element_type=f32)
+    ).astype(bf16)
+    attn_scattered = lax.psum_scatter(attn_normed_part, "tensor", scatter_dimension=0, tiled=True)
+    query_plain = jnp.dot(query_grad, query_spread.T, preferred_element_type=bf16)
+    kv_plain = jnp.dot(key_value_grad, kv_spread.T, preferred_element_type=bf16)
+    joined_shared = SharedProduct(
+        attention_normed, jnp.concatenate([query_plain, kv_plain], axis=1), "dp", places
+    )
+    joined_shared.meet()
+    grad_joined = joined_shared.finish()
+    grad_pair = pair_shared.finish()
+    grad_down = down_shared.finish()
+    grad_out = out_shared.finish()
+    attn_gain_part = (
+        jnp.sum(
+            attn_normed_part.astype(f32) * attention_normed.astype(f32), axis=0, keepdims=True
         )
-    key_value_grad = gather_back(
-        key_totals, value_totals, received, cosine, sine, kv_heads, stretch, rows
-    )
-    split = heads * LANES
-    attn_normed_part = jnp.dot(
-        query_grad, w_joined[:, :split].T, preferred_element_type=f32
-    ) + jnp.dot(key_value_grad, w_joined[:, split:].T, preferred_element_type=f32)
-    attn_normed_grad = scatter_sum(attn_normed_part)
+        / attn_gain
+    )
+    mlp_gain_part = jnp.sum(mlp_normed_grad * residual * inv_rms_mlp, axis=0, keepdims=True)
+    gains = sum_everywhere(
+        jnp.concatenate([attn_gain_part, mlp_gain_part], axis=0), ("tensor", "dp")
+    )
+    grad_attn_gain, grad_mlp_gain = gains[0], gains[1]
+
+    attn_normed_grad = attn_scattered.astype(f32)
     input_part = normalize_back(block_input, inv_rms_attn, attn_gain, attn_normed_grad)
     input_grad = residual_grad + input_part
-
-    query_plain = jnp.dot(query_grad, query_spread.T, preferred_element_type=bf16)
-    kv_plain = jnp.dot(key_value_grad, kv_spread.T, preferred_element_type=bf16)
-    grad_query = product_over(attention_normed, query_plain, "dp", places)
-    grad_key_value = product_over(attention_normed, kv_plain, "dp", crossed)
-    grad_key = grad_key_value[:, : kv_heads * HEAD_SIZE]
-    grad_value = grad_key_value[:, kv_heads * HEAD_SIZE :]
-
-    mlp_gain_part = jnp.sum(mlp_normed_grad * residual * inv_rms_mlp, axis=0, keepdims=True)
-    attn_gain_part = jnp.sum(attn_normed_grad * block_input * inv_rms_attn, axis=0, keepdims=True)
-    grad_mlp_gain = sum_everywhere(mlp_gain_part, ("tensor", "dp"))[0]
-    grad_attn_gain = sum_everywhere(attn_gain_part, ("tensor", "dp"))[0]
+    query_width = w_query.shape[1]
+    kv_width = key_weight.shape[1]
+    grad_query = grad_joined[:, :query_width].astype(f32)
+    grad_key = grad_joined[:, query_width : query_width + kv_width].astype(f32)
+    grad_value = grad_joined[:, query_width + kv_width + gap :].astype(f32)
     return (
         block_output,
         input_grad,
         grad_query,
         grad_key,
         grad_value,
-        grad_out,
-        grad_gate,
-        grad_up,
-        grad_down,
+        grad_out.astype(f32),
+        grad_pair[:, :width].astype(f32),
+        grad_pair[:, width:].astype(f32),
+        grad_down.astype(f32),
         grad_attn_gain,
         grad_mlp_gain,
     )
@@ -604,6 +678,7 @@
         P(),
         P(),
     )
+
     return jax.shard_map(
         per_device, mesh=mesh, in_specs=in_specs, out_specs=out_specs, check_vma=False
     )

time: 785 us -> 664 us (0.85); the launches traced: 784 us -> 655 us
  waiting for transfers between devices: 443 us -> 312 us
  local copies, waits for them, and re-layouts: 24 us -> 32.8 us
  starting transfers between devices: 80 us -> 72 us
    reduce_scatter x4, waiting for transfers between devices: 144 us -> 65.5 us  [the longest x2 65.4 us: scatter_low(): lax.psum_scatter(product.astype(bf16), 'tensor', scatter_dimension=0, til...]
    all_gather x4, waiting for transfers between devices: 193 us -> 135 us  [gather_rows(): return lax.all_gather(rows, 'tensor', axis=0, tiled=True)]
    ppermute x46 -> x29, waiting for transfers between devices: 53 us -> 94.8 us  [exchange(): return lax.ppermute(value, axis, [(i, i ^ distance) for i in range(count)])]
    ppermute x6 -> x4, waiting for transfers between devices: 53.1 us -> 16.4 us  [from_behind(): lax.ppermute(value, axis, [(source, source + steps) for source in range(l...]
    unnamed x100 -> x98, local copies, waits for them, and re-layouts: 13.8 us -> 20.5 us
    ppermute x46 -> x29, starting transfers between devices: 67 us -> 61.5 us  [exchange(): return lax.ppermute(value, axis, [(i, i ^ distance) for i in range(count)])]
    select_n x12 -> x10, other arithmetic: 14.5 us -> 19.6 us  [step(): jnp.where(self.bit(place) == 1, jnp.concatenate([got, whole], axis=0), jn...]
    dot_general x16 -> x10, matrix products: 57.9 us -> 53 us  [the longest x8 33.3 us: times(): return jnp.dot(part.T, self.right, preferred_element_type=f32)]
  transfers between devices with their start and end apart: 60 -> 41, of which waited for: 28 -> 22; matrix products, arithmetic and copies ran while one was open for 20% -> 26% of each run, Pallas kernels for 3% -> 7%
where the time goes in v4:
time: 664 us; the launch traced here: 655 us
  waiting for transfers between devices  312 us (47%)
  matrix products  99.8 us (15%)
  other arithmetic  78.8 us (12%)
  starting transfers between devices  72 us (11%)
  Pallas kernels  45.1 us (7%)
  local copies, waits for them, and re-layouts  32.8 us (5%)
  between operations  15.1 us (2%)
    all_gather x4, waiting for transfers between devices, gather_rows(): return lax.all_gather(rows, 'tensor', axis=0, tiled=True)  135 us
    ppermute x29, waiting for transfers between devices, exchange(): return lax.ppermute(value, axis, [(i, i ^ distance) for i in range(count)])  94.8 us
    reduce_scatter x2, waiting for transfers between devices, scatter_low(): lax.psum_scatter(product.astype(bf16), 'tensor', scatter_dimension=0, til...  65.4 us
    ppermute x29, starting transfers between devices, exchange(): return lax.ppermute(value, axis, [(i, i ^ distance) for i in range(count)])  61.5 us
    dot_general x8, matrix products, times(): return jnp.dot(part.T, self.right, preferred_element_type=f32)  33.3 us
    unnamed x98, local copies, waits for them, and re-layouts  20.5 us
    pallas_call x1, Pallas kernels, attend_back(): pl.pallas_call(functools.partial(attend_back_kernel, tiles, chunks, group...  20 us
    select_n x10, other arithmetic, step(): jnp.where(self.bit(place) == 1, jnp.concatenate([got, whole], axis=0), jn...  19.6 us
  transfers between devices with their start and end apart: 41, of which 22 were waited for; matrix products, arithmetic and copies ran while one was open for 26% of the time, Pallas kernels for 7%

profile of v4, /device:TPU:0, one launch (start us, length us, event | category | flops | bytes accessed | tf_op | source)
XLA Modules:
  0.0 655.1 jit_solution(1756115232285395374)
XLA Ops:
  11.9 2.4 convert_element_type.168
  19.0 3.1 fusion.39
  22.0 6.4 fusion.2.weight_ref
  28.4 49.8 %all-gather.5.cloned.1.call-done.rows_ref = bf16[1024,1536]{1,0:T(8,128)(2,1)} async-done(((bf16[256,1536]{1,0:T(8,128)(2,1)}), bf16[1024,1536]{1,0:T(8,128)(2,1)}) %all-gather.5.cloned.1.call-update) | async-done | bytes 3145744 | tf_op jit(solution)/shard_map/all_gather | solution.py:482
  78.2 7.5 %project.1 = (bf16[1024,512]{1,0:T(8,128)(2,1)}, bf16[1024,512]{1,0:T(8,128)(2,1)}) custom-call(bf16[1024,1536]{1,0:T(8,128)(2,1)} %all-gather.5.cloned.1.call-done.rows_ref, bf16[1536,1024]{1,0:T(8,128)(2,1)} %fusion.2.weight_ref, f32[1024,128]{1,0:T(8,128)} %get-tuple-element.95.cosine_ref.refs_2_, f32[1024,128]{1,0:T(8,128)} %get-tuple-element.94.sine_ref.refs_3_), custom_call_target="tpu_custom_call" | custom-call | flops 3221225472 | bytes 8388608 | tf_op jit(solution)/shard_map/project/pallas_call | solution.py:100
  85.7 4.4 collective-permute-start
  93.1 3.5 fusion.38
  96.6 16.4 %collective-permute-done.refs_0_.refs_3_.refs_5_.refs_8_ = bf16[1024,512]{1,0:T(8,128)(2,1)} collective-permute-done((bf16[1024,512]{1,0:T(8,128)(2,1)}, bf16[1024,512]{1,0:T(8,128)(2,1)}, u32[]{:S(2)}, u32[]{:S(2)}) %collective-permute-start) | collective-permute-done | bytes 1048608 | tf_op jit(solution)/shard_map/ppermute | solution.py:32
  113.0 13.2 %attend.1 = (bf16[1024,512]{1,0:T(8,128)(2,1)}, f32[2,4,1,512]{3,2,1,0:T(1,128)}) custom-call(s32[4]{0:T(128)} %and_select_fusion.low_ref, bf16[1024,512]{1,0:T(8,128)(2,1)} %get-tuple-element.33.query_ref, s32[4,1,256]{2,1,0:T(1,128)} %bitcast.26, bf16[1024,512]{1,0:T(8,128)(2,1)} %collective-permute-done.refs_0_.refs_3_.refs_5_.refs_8_, ...), custom_call_target="tpu_custom_call" | custom-call | flops 8589934592 | bytes 8388608 | tf_op jit(solution)/shard_map/attend/pallas_call | solution.py:229
  126.2 5.2 convolution_convert_fusion.1
  131.4 11.0 %all-gather.7.cloned.1.call-done = bf16[1024,1536]{1,0:T(8,128)(2,1)} async-done(((bf16[256,1536]{1,0:T(8,128)(2,1)}), bf16[1024,1536]{1,0:T(8,128)(2,1)}) %all-gather.7.cloned.1.call-update) | async-done | bytes 3145744 | tf_op jit(solution)/shard_map/all_gather | solution.py:482
  142.5 6.9 %fusion.86 = f32[1024,1024]{1,0:T(8,128)} fusion(bf16[1024,1536]{1,0:T(8,128)(2,1)} %all-gather.7.cloned.1.call-done, bf16[1024,1536]{1,0:T(8,128)(2,1)S(1)} %copy-done), kind=kOutput, calls=%fused_computation.178 | convolution fusion | flops 3221225472 | bytes 10485760 | tf_op jit(solution)/shard_map/dot_general | solution.py:537
  149.3 62.3 %reduce-scatter.5.cloned.1.call-done = bf16[256,1536]{1,0:T(8,128)(2,1)} async-done(((bf16[1024,1536]{1,0:T(8,128)(2,1)}), bf16[256,1536]{1,0:T(8,128)(2,1)}) %reduce-scatter.5.cloned.1.call-update) | async-done | bytes 786448 | tf_op jit(solution)/shard_map/reduce_scatter | solution.py:478
  216.0 4.0 constant_dynamic-update-slice_fusion.1
  222.0 57.3 %all-gather.9.cloned.1.call-done = bf16[1024,1536]{1,0:T(8,128)(2,1)} async-done(((bf16[256,1536]{1,0:T(8,128)(2,1)}), bf16[1024,1536]{1,0:T(8,128)(2,1)}) %all-gather.9.cloned.1.call-update) | async-done | bytes 3145744 | tf_op jit(solution)/shard_map/all_gather | solution.py:482
  279.3 9.8 %fusion.87 = f32[1024,2048]{1,0:T(8,128)S(1)} fusion(bf16[1024,1536]{1,0:T(8,128)(2,1)} %all-gather.9.cloned.1.call-done, bf16[1536,2048]{1,0:T(8,128)(2,1)} %constant_dynamic-update-slice_fusion), kind=kOutput, calls=%fused_computation.179 | convolution fusion | flops 6442450944 | bytes 17825792 | tf_op jit(solution)/shard_map/dot_general | solution.py:545
  289.1 3.9 multiply_convert_fusion.2
  293.0 5.0 convolution_convert_fusion.3
  298.1 9.9 %convolution_convert_fusion = bf16[1024,1536]{1,0:T(8,128)(2,1)} fusion(bf16[1536,2048]{1,0:T(8,128)(2,1)} %constant_dynamic-update-slice_fusion, bf16[1024,1024]{1,0:T(8,128)(2,1)S(1)} %get-tuple-element.86, bf16[1024,1024]{1,0:T(8,128)(2,1)S(1)} %get-tuple-element.85), kind=kOutput, calls=%fused_computation.10 | convolution fusion | flops 6452412416 | bytes 13631488 | tf_op jit(solution)/shard_map/dot_general | solution.py:553
  308.3 5.2 convolution_convert_fusion.4
  314.0 7.4 %convert_add_fusion = f32[768,2048]{1,0:T(8,128)S(1)} fusion(bf16[768,2048]{1,0:T(8,128)(2,1)} %collective-permute-done.2, bf16[1024,1536]{1,0:T(8,128)(2,1)} %all-gather.9.cloned.1.call-done, s32[]{:T(128)S(6)} %select_n.258, bf16[1024,1024]{1,0:T(8,128)(2,1)} %copy-done.28, bf16[1024,1024]{1,0:T(8,128)(2,1)} %copy-done.27), kind=kOutput, calls=%fused_computation.3 | convolution fusion | flops 3232759808 | bytes 15204356 | tf_op jit(solution)/shard_map/dot_general | solution.py:432
  325.6 3.3 convert_add_fusion.1
  333.1 6.4 convolution_convert_fusion.2
  339.5 11.9 %collective-permute-done.5 = bf16[256,1536]{1,0:T(8,128)(2,1)} collective-permute-done((bf16[256,1536]{1,0:T(8,128)(2,1)}, bf16[256,1536]{1,0:T(8,128)(2,1)}, u32[]{:S(2)}, u32[]{:S(2)}) %collective-permute-start.5) | collective-permute-done | bytes 786464 | tf_op jit(solution)/shard_map/ppermute | solution.py:37
  351.4 3.0 convert_add_fusion.5
  354.4 5.1 collective-permute-done.3
  359.5 4.8 convert_add_fusion.2
  364.2 3.2 reduce-scatter.7.cloned.1.call-done
  371.4 2.4 dynamic-slice_convert_fusion.1
  376.9 16.1 %collective-permute-done.6 = bf16[192,2048]{1,0:T(8,128)(2,1)} collective-permute-done((bf16[192,2048]{1,0:T(8,128)(2,1)}, bf16[192,2048]{1,0:T(8,128)(2,1)}, u32[]{:S(2)}, u32[]{:S(2)}) %collective-permute-start.6) | collective-permute-done | bytes 786464 | tf_op jit(solution)/shard_map/ppermute | solution.py:37
  393.0 2.7 add_convert_fusion.1
  398.9 3.0 fusion.37
  401.8 4.9 collective-permute-done.9
  406.9 7.2 %collective-permute-done.7 = bf16[192,2048]{1,0:T(8,128)(2,1)} collective-permute-done((bf16[192,2048]{1,0:T(8,128)(2,1)}, bf16[192,2048]{1,0:T(8,128)(2,1)}, u32[]{:S(2)}, u32[]{:S(2)}) %collective-permute-start.7) | collective-permute-done | bytes 786464 | tf_op jit(solution)/shard_map/ppermute | solution.py:37
  414.1 3.7 maximum_select_fusion.4
  417.8 16.7 %all-gather.11.cloned.1.call-done = bf16[1024,1536]{1,0:T(8,128)(2,1)} async-done(((bf16[256,1536]{1,0:T(8,128)(2,1)}), bf16[1024,1536]{1,0:T(8,128)(2,1)}) %all-gather.11.cloned.1.call-update) | async-done | bytes 3145744 | tf_op jit(solution)/shard_map/all_gather | solution.py:482
  437.4 5.1 convolution_convert_fusion.7.refs_4_
  443.1 20.0 %attend_back.1 = (bf16[1024,512]{1,0:T(8,128)(2,1)}, f32[1024,256]{1,0:T(8,128)}, f32[1024,256]{1,0:T(8,128)}, bf16[2,2,1024,256]{3,2,1,0:T(8,128)(2,1)}) custom-call(s32[4]{0:T(128)} %and_select_fusion.low_ref, s32[4]{0:T(128)} %iota.50.slot_ref, bf16[1024,512]{1,0:T(8,128)(2,1)} %get-tuple-element.33.query_ref, s32[4,1,256]{2,1,0:T(1,128)} %bitcast.27, ...), custom_call_target="tpu_custom_call" | custom-call | flops 21474836480 | bytes 16777216 | tf_op jit(solution)/shard_map/attend_back/pallas_call | solution.py:374
  463.1 2.3 maximum_select_fusion.5
  465.5 6.5 collective-permute-done.10
  472.0 5.0 maximum_select_fusion.1
  478.7 7.3 %collective-permute-start.20 = (bf16[192,1536]{1,0:T(8,128)(2,1)}, bf16[192,1536]{1,0:T(8,128)(2,1)}, u32[]{:S(2)}, u32[]{:S(2)}) collective-permute-start(bf16[192,1536]{1,0:T(8,128)(2,1)} %convolution_convert_fusion.5), channel_id=1, source_target_pairs={{0,4},{4,0},{8,12},{12,8},{16,20},{20,16},{24,28},{28,24},{1,5},{5... | collective-permute-start | bytes 1769480 | tf_op jit(solution)/shard_map/ppermute | solution.py:37
  486.0 3.2 slice_bitcast_fusion
  495.0 4.4 collective-permute-start.21
  499.5 2.8 fusion.36
  502.9 3.9 collective-permute-done.21
  508.7 30.7 %collective-permute-start.22 = (bf16[48,1536]{1,0:T(8,128)(2,1)S(1)}, bf16[48,1536]{1,0:T(8,128)(2,1)S(1)}, u32[]{:S(2)}, u32[]{:S(2)}) collective-permute-start(bf16[48,1536]{1,0:T(8,128)(2,1)S(1)} %dynamic-slice_convert_fusion.7), channel_id=1, source_target_pairs={{0,8},{4,12},{8,0},{12,4},{16,24},{20,28},{24,16},{28,20},{1,9},{5... | collective-permute-start | bytes 442376 | tf_op jit(solution)/shard_map/ppermute | solution.py:37
  539.4 4.4 gather_back.1
  545.8 4.3 convolution_convert_fusion.6
  552.3 3.6 multiply_reduce_fusion
  556.2 3.5 collective-permute-done.28
  560.9 4.4 convert_add_fusion.3
  571.0 11.6 %collective-permute-done.31 = f32[2,1536]{1,0:T(2,128)S(1)} collective-permute-done((f32[2,1536]{1,0:T(2,128)S(1)}, f32[2,1536]{1,0:T(2,128)S(1)}, u32[]{:S(2)}, u32[]{:S(2)}) %collective-permute-start.31) | collective-permute-done | bytes 12320 | tf_op jit(solution)/shard_map/ppermute | solution.py:37
  582.7 3.8 collective-permute-done.32
  591.2 5.3 collective-permute-done.24
  596.7 5.8 collective-permute-done.16
  602.8 4.4 fusion.1
  611.8 5.1 maximum_select_fusion
  616.9 6.1 collective-permute-done.18
  623.4 6.3 slice_convert_fusion
  629.8 2.6 convert_add_fusion.4
  636.9 3.0 copy.28
  640.0 3.1 slice_convert_fusion.3
  644.9 3.2 subtract_add_fusion
  (221 shorter events, 79.4 us)
Async XLA Ops:
  7.2 135.3 %copy-start = (bf16[1024,1536]{1,0:T(8,128)(2,1)S(1)}, bf16[1024,1536]{1,0:T(8,128)(2,1)}, u32[]{:S(2)}) copy-start(bf16[1024,1536]{1,0:T(8,128)(2,1)} %param.22) | copy-start | bytes 9437188
  7.2 71.0 %all-gather.5.cloned.1.call-start = ((), (), s32[]{:S(2)}) async-start(), calls=%async_computation.4 | async-start | bytes 3932160 | tf_op jit(solution)/shard_map/all_gather | solution.py:482
  11.9 7.1 %copy-start.42 = (s32[1024]{0:T(1024)S(1)}, s32[1024]{0:T(1024)}, u32[]{:S(2)}) copy-start(s32[1024]{0:T(1024)} %param.13) | copy-start | bytes 12292
  11.9 130.6 %all-gather.7.cloned.1.call-start = ((), (), s32[]{:S(2)}) async-start(), calls=%async_computation.6 | async-start | bytes 3932160 | tf_op jit(solution)/shard_map/all_gather | solution.py:482
  14.3 197.3 %reduce-scatter.5.cloned.1.call-start = ((), (), s32[]{:S(2)}) async-start(), calls=%async_computation.5 | async-start | bytes 3932160 | tf_op jit(solution)/shard_map/reduce_scatter | solution.py:478
  19.0 73.5 %copy-start.39 = (s32[1024]{0:T(1024)}, s32[1024]{0:T(1024)S(1)}, u32[]{:S(2)}) copy-start(s32[1024]{0:T(1024)S(1)} %get-tuple-element.97) | copy-start | bytes 12292
  85.7 27.2 %collective-permute-start = (bf16[1024,512]{1,0:T(8,128)(2,1)}, bf16[1024,512]{1,0:T(8,128)(2,1)}, u32[]{:S(2)}, u32[]{:S(2)}) collective-permute-start(bf16[1024,512]{1,0:T(8,128)(2,1)} %get-tuple-element.34.refs_2_.refs_5_.refs_7_.refs_10_), channel_id=1, source_target_pairs={{0,8},{4,12},{8,16},{12,20},{16,24},{20,28},{1,9},{5,13},{9,17},{1... | collective-permute-start | bytes 3145736 | tf_op jit(solution)/shard_map/ppermute | solution.py:32
  90.1 22.8 %collective-permute-start.1 = (bf16[1024,512]{1,0:T(8,128)(2,1)}, bf16[1024,512]{1,0:T(8,128)(2,1)}, u32[]{:S(2)}, u32[]{:S(2)}) collective-permute-start(bf16[1024,512]{1,0:T(8,128)(2,1)} %get-tuple-element.34.refs_2_.refs_5_.refs_7_.refs_10_), channel_id=1, source_target_pairs={{0,4},{4,8},{8,12},{12,16},{16,20},{20,24},{24,28},{1,5},{5,9},{9,... | collective-permute-start | bytes 3145736 | tf_op jit(solution)/shard_map/ppermute | solution.py:32
  131.4 147.9 %all-gather.9.cloned.1.call-start = ((), (), s32[]{:S(2)}) async-start(), calls=%async_computation.7 | async-start | bytes 3932160 | tf_op jit(solution)/shard_map/all_gather | solution.py:482
  149.3 65.3 %copy-start.38 = (f32[1536]{0:T(1024)S(1)}, f32[1536]{0:T(1024)}, u32[]{:S(2)}) copy-start(f32[1536]{0:T(1024)} %param.19) | copy-start | bytes 18436
  215.8 151.7 %reduce-scatter.7.cloned.1.call-start = ((), (), s32[]{:S(2)}) async-start(), calls=%async_computation.8 | async-start | bytes 3932160 | tf_op jit(solution)/shard_map/reduce_scatter | solution.py:478
  279.3 9.9 %copy-start.18 = (f32[1024,1024]{1,0:T(8,128)S(1)}, f32[1024,1024]{1,0:T(8,128)}, u32[]{:S(2)}) copy-start(f32[1024,1024]{1,0:T(8,128)} %fusion.86) | copy-start | bytes 12582916
  293.0 5.1 copy-start.27
  293.0 5.1 copy-start.28
  298.1 15.9 %collective-permute-start.2 = (bf16[768,2048]{1,0:T(8,128)(2,1)}, bf16[768,2048]{1,0:T(8,128)(2,1)}, u32[]{:S(2)}, u32[]{:S(2)}) collective-permute-start(bf16[768,2048]{1,0:T(8,128)(2,1)} %convolution_convert_fusion.3), channel_id=1, source_target_pairs={{0,4},{4,0},{8,12},{12,8},{16,20},{20,16},{24,28},{28,24},{1,5},{5... | collective-permute-start | bytes 9437192 | tf_op jit(solution)/shard_map/ppermute | solution.py:37
  308.1 126.4 %all-gather.11.cloned.1.call-start = ((), (), s32[]{:S(2)}) async-start(), calls=%async_computation.9 | async-start | bytes 3932160 | tf_op jit(solution)/shard_map/all_gather | solution.py:482
  313.5 10.8 %collective-permute-start.4 = (bf16[512,1536]{1,0:T(8,128)(2,1)}, bf16[512,1536]{1,0:T(8,128)(2,1)}, u32[]{:S(2)}, u32[]{:S(2)}) collective-permute-start(bf16[512,1536]{1,0:T(8,128)(2,1)} %convolution_convert_fusion.4), channel_id=1, source_target_pairs={{0,4},{4,0},{8,12},{12,8},{16,20},{20,16},{24,28},{28,24},{1,5},{5... | collective-permute-start | bytes 4718600 | tf_op jit(solution)/shard_map/ppermute | solution.py:37
  314.0 10.3 %copy-start.17 = (bf16[1024,1024]{1,0:T(8,128)(2,1)S(1)}, bf16[1024,1024]{1,0:T(8,128)(2,1)}, u32[]{:S(2)}) copy-start(bf16[1024,1024]{1,0:T(8,128)(2,1)} %get-tuple-element.87) | copy-start | bytes 6291460
  321.4 7.5 %copy-start.21 = (f32[768,2048]{1,0:T(8,128)}, f32[768,2048]{1,0:T(8,128)S(1)}, u32[]{:S(2)}) copy-start(f32[768,2048]{1,0:T(8,128)S(1)} %convert_add_fusion) | copy-start | bytes 18874372
  322.8 36.6 %collective-permute-start.3 = (bf16[384,2048]{1,0:T(8,128)(2,1)}, bf16[384,2048]{1,0:T(8,128)(2,1)}, u32[]{:S(2)}, u32[]{:S(2)}) collective-permute-start(bf16[384,2048]{1,0:T(8,128)(2,1)} %dynamic-slice_convert_fusion), channel_id=1, source_target_pairs={{0,8},{4,12},{8,0},{12,4},{16,24},{20,28},{24,16},{28,20},{1,9},{5... | collective-permute-start | bytes 4718600 | tf_op jit(solution)/shard_map/ppermute | solution.py:37
  331.6 19.8 %collective-permute-start.5 = (bf16[256,1536]{1,0:T(8,128)(2,1)}, bf16[256,1536]{1,0:T(8,128)(2,1)}, u32[]{:S(2)}, u32[]{:S(2)}) collective-permute-start(bf16[256,1536]{1,0:T(8,128)(2,1)} %dynamic-slice_convert_fusion.2), channel_id=1, source_target_pairs={{0,16},{4,20},{8,24},{12,28},{16,0},{20,4},{24,8},{28,12},{1,17},{... | collective-permute-start | bytes 2359304 | tf_op jit(solution)/shard_map/ppermute | solution.py:37
  354.4 13.0 %copy-start.5 = (f32[256,1536]{1,0:T(8,128)S(1)}, f32[256,1536]{1,0:T(8,128)}, u32[]{:S(2)}) copy-start(f32[256,1536]{1,0:T(8,128)} %copy-done.4) | copy-start | bytes 4718596
  364.2 4.8 copy-start.12
  371.0 258.8 %reduce-scatter.9.cloned.1.call-start = ((), (), s32[]{:S(2)}) async-start(), calls=%async_computation.10 | async-start | bytes 3932160 | tf_op jit(solution)/shard_map/reduce_scatter | solution.py:575
  373.8 19.2 %collective-permute-start.6 = (bf16[192,2048]{1,0:T(8,128)(2,1)}, bf16[192,2048]{1,0:T(8,128)(2,1)}, u32[]{:S(2)}, u32[]{:S(2)}) collective-permute-start(bf16[192,2048]{1,0:T(8,128)(2,1)} %dynamic-slice_convert_fusion.1), channel_id=1, source_target_pairs={{0,16},{4,20},{8,24},{12,28},{16,0},{20,4},{24,8},{28,12},{1,17},{... | collective-permute-start | bytes 2359304 | tf_op jit(solution)/shard_map/ppermute | solution.py:37
  375.4 21.9 %collective-permute-start.8 = (bf16[128,1536]{1,0:T(8,128)(2,1)S(1)}, bf16[128,1536]{1,0:T(8,128)(2,1)S(1)}, u32[]{:S(2)}, u32[]{:S(2)}) collective-permute-start(bf16[128,1536]{1,0:T(8,128)(2,1)S(1)} %dynamic-slice_convert_fusion.5), channel_id=1, source_target_pairs={{0,8},{4,12},{8,0},{12,4},{16,24},{20,28},{24,16},{28,20},{1,9},{5... | collective-permute-start | bytes 1179656 | tf_op jit(solution)/shard_map/ppermute | solution.py:37
  395.8 18.3 %collective-permute-start.7 = (bf16[192,2048]{1,0:T(8,128)(2,1)}, bf16[192,2048]{1,0:T(8,128)(2,1)}, u32[]{:S(2)}, u32[]{:S(2)}) collective-permute-start(bf16[192,2048]{1,0:T(8,128)(2,1)} %add_convert_fusion.1), channel_id=1, source_target_pairs={{0,16},{4,20},{8,24},{12,28},{16,0},{20,4},{24,8},{28,12},{1,17},{... | collective-permute-start | bytes 2359304 | tf_op jit(solution)/shard_map/ppermute | solution.py:37
  397.3 9.4 %collective-permute-start.9 = (bf16[128,1536]{1,0:T(8,128)(2,1)S(1)}, bf16[128,1536]{1,0:T(8,128)(2,1)S(1)}, u32[]{:S(2)}, u32[]{:S(2)}) collective-permute-start(bf16[128,1536]{1,0:T(8,128)(2,1)S(1)} %add_convert_fusion.3), channel_id=1, source_target_pairs={{0,8},{4,12},{8,0},{12,4},{16,24},{20,28},{24,16},{28,20},{1,9},{5... | collective-permute-start | bytes 1179656 | tf_op jit(solution)/shard_map/ppermute | solution.py:37
  406.9 35.7 %copy-start.25 = (bf16[256,1536]{1,0:T(8,128)(2,1)}, bf16[256,1536]{1,0:T(8,128)(2,1)S(1)}, u32[]{:S(2)}) copy-start(bf16[256,1536]{1,0:T(8,128)(2,1)S(1)} %maximum_select_fusion.8) | copy-start | bytes 2359300
  434.5 28.6 %collective-permute-start.11 = (bf16[256,1536]{1,0:T(8,128)(2,1)S(1)}, bf16[256,1536]{1,0:T(8,128)(2,1)}, u32[]{:S(2)}, u32[]{:S(2)}) collective-permute-start(bf16[256,1536]{1,0:T(8,128)(2,1)S(1)} %maximum_select_fusion.8), channel_id=1, source_target_pairs={{0,16},{4,20},{8,24},{12,28},{16,0},{20,4},{24,8},{28,12},{1,17},{... | collective-permute-start | bytes 2359304 | tf_op jit(solution)/shard_map/ppermute | solution.py:37
  436.0 36.0 %collective-permute-start.10 = (bf16[384,2048]{1,0:T(8,128)(2,1)}, bf16[384,2048]{1,0:T(8,128)(2,1)}, u32[]{:S(2)}, u32[]{:S(2)}) collective-permute-start(bf16[384,2048]{1,0:T(8,128)(2,1)} %maximum_select_fusion.4), channel_id=1, source_target_pairs={{0,8},{4,12},{8,0},{12,4},{16,24},{20,28},{24,16},{28,20},{1,9},{5... | collective-permute-start | bytes 4718600 | tf_op jit(solution)/shard_map/ppermute | solution.py:37
  442.6 200.4 %reduce-scatter.11.cloned.1.call-start = ((), (), s32[]{:S(2)}) async-start(), calls=%async_computation.11 | async-start | bytes 3932160 | tf_op jit(solution)/shard_map/reduce_scatter | solution.py:607
  465.5 11.5 %copy-start.7 = (bf16[1024,1536]{1,0:T(8,128)(2,1)S(1)}, bf16[1024,1536]{1,0:T(8,128)(2,1)}, u32[]{:S(2)}) copy-start(bf16[1024,1536]{1,0:T(8,128)(2,1)} %all-gather.11.cloned.1.call-done) | copy-start | bytes 9437188
  465.5 11.5 %copy-start.32 = (bf16[1024,384]{1,0:T(8,128)(2,1)S(1)}, bf16[1024,384]{1,0:T(8,128)(2,1)}, u32[]{:S(2)}) copy-start(bf16[1024,384]{1,0:T(8,128)(2,1)} %fusion.37) | copy-start | bytes 2359300
  478.7 13.3 %collective-permute-start.20 = (bf16[192,1536]{1,0:T(8,128)(2,1)}, bf16[192,1536]{1,0:T(8,128)(2,1)}, u32[]{:S(2)}, u32[]{:S(2)}) collective-permute-start(bf16[192,1536]{1,0:T(8,128)(2,1)} %convolution_convert_fusion.5), channel_id=1, source_target_pairs={{0,4},{4,0},{8,12},{12,8},{16,20},{20,16},{24,28},{28,24},{1,5},{5... | collective-permute-start | bytes 1769480 | tf_op jit(solution)/shard_map/ppermute | solution.py:37
  486.0 6.0 copy-start.8
  486.0 6.1 copy-start.33
  489.2 50.1 %collective-permute-start.12 = (bf16[2,1024,256]{2,1,0:T(8,128)(2,1)}, bf16[2,1024,256]{2,1,0:T(8,128)(2,1)}, u32[]{:S(2)}, u32[]{:S(2)}) collective-permute-start(bf16[2,1024,256]{2,1,0:T(8,128)(2,1)} %get-tuple-element.93), channel_id=1, source_target_pairs={{4,0},{8,4},{12,8},{16,12},{20,16},{24,20},{28,24},{5,1},{9,5},{13... | collective-permute-start | bytes 3145736 | tf_op jit(solution)/shard_map/ppermute | solution.py:32
  490.5 48.8 %collective-permute-start.13 = (bf16[2,1024,256]{2,1,0:T(8,128)(2,1)}, bf16[2,1024,256]{2,1,0:T(8,128)(2,1)}, u32[]{:S(2)}, u32[]{:S(2)}) collective-permute-start(bf16[2,1024,256]{2,1,0:T(8,128)(2,1)} %get-tuple-element.92), channel_id=1, source_target_pairs={{8,0},{12,4},{16,8},{20,12},{24,16},{28,20},{9,1},{13,5},{17,9},{2... | collective-permute-start | bytes 3145736 | tf_op jit(solution)/shard_map/ppermute | solution.py:32
  495.0 11.8 %collective-permute-start.21 = (bf16[96,1536]{1,0:T(8,128)(2,1)S(1)}, bf16[96,1536]{1,0:T(8,128)(2,1)}, u32[]{:S(2)}, u32[]{:S(2)}) collective-permute-start(bf16[96,1536]{1,0:T(8,128)(2,1)S(1)} %dynamic-slice_convert_fusion.6), channel_id=1, source_target_pairs={{0,16},{4,20},{8,24},{12,28},{16,0},{20,4},{24,8},{28,12},{1,17},{... | collective-permute-start | bytes 884744 | tf_op jit(solution)/shard_map/ppermute | solution.py:37
  499.5 7.3 %copy-start.20 = (f32[192,1536]{1,0:T(8,128)S(1)}, f32[192,1536]{1,0:T(8,128)}, u32[]{:S(2)}) copy-start(f32[192,1536]{1,0:T(8,128)} %copy-done.19) | copy-start | bytes 3538948
  502.4 100.5 %collective-permute-start.27 = (bf16[512,1536]{1,0:T(8,128)(2,1)S(1)}, bf16[512,1536]{1,0:T(8,128)(2,1)}, u32[]{:S(2)}, u32[]{:S(2)}) collective-permute-start(bf16[512,1536]{1,0:T(8,128)(2,1)S(1)} %maximum_select_fusion.5), channel_id=1, source_target_pairs={{0,4},{4,0},{8,12},{12,8},{16,20},{20,16},{24,28},{28,24},{1,5},{5... | collective-permute-start | bytes 4718600 | tf_op jit(solution)/shard_map/ppermute | solution.py:37
  502.4 109.4 %collective-permute-start.26 = (bf16[768,2048]{1,0:T(8,128)(2,1)}, bf16[768,2048]{1,0:T(8,128)(2,1)}, u32[]{:S(2)}, u32[]{:S(2)}) collective-permute-start(bf16[768,2048]{1,0:T(8,128)(2,1)} %maximum_select_fusion.1), channel_id=1, source_target_pairs={{0,4},{4,0},{8,12},{12,8},{16,20},{20,16},{24,28},{28,24},{1,5},{5... | collective-permute-start | bytes 9437192 | tf_op jit(solution)/shard_map/ppermute | solution.py:37
  508.7 47.4 %collective-permute-start.22 = (bf16[48,1536]{1,0:T(8,128)(2,1)S(1)}, bf16[48,1536]{1,0:T(8,128)(2,1)S(1)}, u32[]{:S(2)}, u32[]{:S(2)}) collective-permute-start(bf16[48,1536]{1,0:T(8,128)(2,1)S(1)} %dynamic-slice_convert_fusion.7), channel_id=1, source_target_pairs={{0,8},{4,12},{8,0},{12,4},{16,24},{20,28},{24,16},{28,20},{1,9},{5... | collective-permute-start | bytes 442376 | tf_op jit(solution)/shard_map/ppermute | solution.py:37
  545.7 4.4 copy-start.35
  545.8 4.4 copy-start.36
  550.1 10.8 %collective-permute-start.14 = (bf16[768,832]{0,1:T(8,128)(2,1)}, bf16[768,832]{0,1:T(8,128)(2,1)}, u32[]{:S(2)}, u32[]{:S(2)}) collective-permute-start(bf16[768,832]{0,1:T(8,128)(2,1)} %convolution_convert_fusion.6), channel_id=1, source_target_pairs={{0,4},{4,0},{8,12},{12,8},{16,20},{20,16},{24,28},{28,24},{1,5},{5... | collective-permute-start | bytes 3833864 | tf_op jit(solution)/shard_map/ppermute | solution.py:37
  556.0 3.8 collective-permute-start.28
  556.1 30.4 %collective-permute-start.23 = (bf16[48,1536]{1,0:T(8,128)(2,1)S(1)}, bf16[48,1536]{1,0:T(8,128)(2,1)S(1)}, u32[]{:S(2)}, u32[]{:S(2)}) collective-permute-start(bf16[48,1536]{1,0:T(8,128)(2,1)S(1)} %add_convert_fusion.4), channel_id=1, source_target_pairs={{0,8},{4,12},{8,0},{12,4},{16,24},{20,28},{24,16},{28,20},{1,9},{5... | collective-permute-start | bytes 442376 | tf_op jit(solution)/shard_map/ppermute | solution.py:37
  559.7 7.9 %collective-permute-start.29 = (f32[2,1536]{1,0:T(2,128)S(1)}, f32[2,1536]{1,0:T(2,128)S(1)}, u32[]{:S(2)}, u32[]{:S(2)}) collective-permute-start(f32[2,1536]{1,0:T(2,128)S(1)} %fusion.81), channel_id=1, source_target_pairs={{0,2},{1,3},{2,0},{3,1},{4,6},{5,7},{6,4},{7,5},{8,10},{9,11},{10,... | collective-permute-start | bytes 36872 | tf_op jit(solution)/shard_map/ppermute | solution.py:37
  567.6 19.0 %collective-permute-start.15 = (bf16[384,832]{0,1:T(8,128)(2,1)}, bf16[384,832]{0,1:T(8,128)(2,1)}, u32[]{:S(2)}, u32[]{:S(2)}) collective-permute-start(bf16[384,832]{0,1:T(8,128)(2,1)} %dynamic-slice_convert_fusion.3), channel_id=1, source_target_pairs={{0,8},{4,12},{8,0},{12,4},{16,24},{20,28},{24,16},{28,20},{1,9},{5... | collective-permute-start | bytes 1916936 | tf_op jit(solution)/shard_map/ppermute | solution.py:37
  567.6 1.2 collective-permute-start.30
  568.9 13.7 %collective-permute-start.31 = (f32[2,1536]{1,0:T(2,128)S(1)}, f32[2,1536]{1,0:T(2,128)S(1)}, u32[]{:S(2)}, u32[]{:S(2)}) collective-permute-start(f32[2,1536]{1,0:T(2,128)S(1)} %add.321), channel_id=1, source_target_pairs={{0,8},{4,12},{8,0},{12,4},{16,24},{20,28},{24,16},{28,20},{1,9},{5... | collective-permute-start | bytes 36872 | tf_op jit(solution)/shard_map/ppermute | solution.py:37
  582.6 3.9 collective-permute-start.32
  586.5 9.9 %collective-permute-start.24 = (bf16[96,1536]{1,0:T(8,128)(2,1)S(1)}, bf16[96,1536]{1,0:T(8,128)(2,1)S(1)}, u32[]{:S(2)}, u32[]{:S(2)}) collective-permute-start(bf16[96,1536]{1,0:T(8,128)(2,1)S(1)} %maximum_select_fusion.11), channel_id=1, source_target_pairs={{0,16},{4,20},{8,24},{12,28},{16,0},{20,4},{24,8},{28,12},{1,17},{... | collective-permute-start | bytes 884744 | tf_op jit(solution)/shard_map/ppermute | solution.py:37
  588.5 14.0 %collective-permute-start.16 = (bf16[192,832]{0,1:T(8,128)(2,1)S(1)}, bf16[192,832]{0,1:T(8,128)(2,1)S(1)}, u32[]{:S(2)}, u32[]{:S(2)}) collective-permute-start(bf16[192,832]{0,1:T(8,128)(2,1)S(1)} %dynamic-slice_convert_fusion.4), channel_id=1, source_target_pairs={{0,16},{4,20},{8,24},{12,28},{16,0},{20,4},{24,8},{28,12},{1,17},{... | collective-permute-start | bytes 958472 | tf_op jit(solution)/shard_map/ppermute | solution.py:37
  596.6 10.7 %collective-permute-start.25 = (bf16[192,1536]{1,0:T(8,128)(2,1)S(1)}, bf16[192,1536]{1,0:T(8,128)(2,1)S(1)}, u32[]{:S(2)}, u32[]{:S(2)}) collective-permute-start(bf16[192,1536]{1,0:T(8,128)(2,1)S(1)} %maximum_select_fusion.10), channel_id=1, source_target_pairs={{0,4},{4,0},{8,12},{12,8},{16,20},{20,16},{24,28},{28,24},{1,5},{5... | collective-permute-start | bytes 1769480 | tf_op jit(solution)/shard_map/ppermute | solution.py:37
  602.7 8.2 %collective-permute-start.17 = (bf16[192,832]{0,1:T(8,128)(2,1)S(1)}, bf16[192,832]{0,1:T(8,128)(2,1)S(1)}, u32[]{:S(2)}, u32[]{:S(2)}) collective-permute-start(bf16[192,832]{0,1:T(8,128)(2,1)S(1)} %add_convert_fusion.2), channel_id=1, source_target_pairs={{0,16},{4,20},{8,24},{12,28},{16,0},{20,4},{24,8},{28,12},{1,17},{... | collective-permute-start | bytes 958472 | tf_op jit(solution)/shard_map/ppermute | solution.py:37
  607.3 4.5 copy-start.6
  611.5 11.5 %collective-permute-start.18 = (bf16[384,832]{0,1:T(8,128)(2,1)S(1)}, bf16[384,832]{0,1:T(8,128)(2,1)S(1)}, u32[]{:S(2)}, u32[]{:S(2)}) collective-permute-start(bf16[384,832]{0,1:T(8,128)(2,1)S(1)} %maximum_select_fusion.9), channel_id=1, source_target_pairs={{0,8},{4,12},{8,0},{12,4},{16,24},{20,28},{24,16},{28,20},{1,9},{5... | collective-permute-start | bytes 1916936 | tf_op jit(solution)/shard_map/ppermute | solution.py:37
  623.3 6.4 copy-start.14
  623.3 9.0 %collective-permute-start.19 = (bf16[768,832]{0,1:T(8,128)(2,1)S(1)}, bf16[768,832]{0,1:T(8,128)(2,1)}, u32[]{:S(2)}, u32[]{:S(2)}) collective-permute-start(bf16[768,832]{0,1:T(8,128)(2,1)S(1)} %maximum_select_fusion.6), channel_id=1, source_target_pairs={{0,4},{4,0},{8,12},{12,8},{16,20},{20,16},{24,28},{28,24},{1,5},{5... | collective-permute-start | bytes 3833864 | tf_op jit(solution)/shard_map/ppermute | solution.py:37
  640.0 4.7 copy-start.41
  640.0 4.7 copy-start.43
  (24 other events, 60.4 us)
Sparse Core Ops, SparseCore 0:
  12.0 66.1 all-gather.4
  80.4 62.0 all-gather.6
  145.4 66.2 reduce-scatter.4
  215.9 63.3 all-gather.8
  308.2 59.1 reduce-scatter.6
  371.1 63.3 all-gather.10
  442.7 57.2 reduce-scatter.8
  556.3 60.0 reduce-scatter.10

commit v5 on v4

--- a/solution.py
+++ b/solution.py
@@ -448,20 +448,34 @@
             kept = lax.dynamic_slice_in_dim(self.value, bit * size, size, 0)
             self.value = kept + got.astype(f32)
             return self.value
-        place = self.up.pop(0)
-        whole = self.value.astype(bf16)
-        got = exchange(whole, self.axis, 1 << place)
-        self.value = jnp.where(
-            self.bit(place) == 1,
+        self.begin_up()
+        return self.end_up()
+
+    def begin_up(self):
+        self.place = self.up.pop(0)
+        self.value = self.value.astype(bf16)
+        self.got = exchange(self.value, self.axis, 1 << self.place)
+
+    def end_up(self):
+        self.value = self.joined(self.value, self.got)
+        return self.value
+
+    def joined(self, whole, got):
+        return jnp.where(
+            self.bit(self.place) == 1,
             jnp.concatenate([got, whole], axis=0),
             jnp.concatenate([whole, got], axis=0),
         )
-        return self.value
-
-    def finish(self):
-        while self.up:
+
+    def finish(self, *spans):
+        while len(self.up) > 1:
             self.step()
-        return self.value
+        if self.up:
+            self.begin_up()
+        return [
+            self.joined(self.value[:, a:b], self.got[:, a:b]).astype(f32)
+            for a, b in spans
+        ]
 
 
 def sum_everywhere(value, axes):
@@ -509,8 +523,9 @@
     tied = lax.optimization_barrier
 
     normed_own, inv_rms_attn = normalize(block_input, attn_gain)
+    normed_own, out_own = tied((normed_own, out_grad.astype(bf16)))
     attention_normed = gather_rows(normed_own)
-    out_low = gather_rows(out_grad.astype(bf16))
+    out_low = gather_rows(out_own)
 
     query_spread = spread_matrix(heads)
     gap = -kv_heads * HEAD_SIZE % LANES
@@ -550,7 +565,9 @@
     gate_grad = hidden_grad * up_proj * sigmoid_gate * (1.0 + gate_pre * (1.0 - sigmoid_gate))
     up_grad = hidden_grad * silu_gate
     pair_grad = jnp.concatenate([gate_grad.astype(bf16), up_grad.astype(bf16)], axis=1)
-    mlp_scattered = scatter_low(jnp.dot(pair_grad, w_pair.T, preferred_element_type=f32))
+    mlp_product = jnp.dot(pair_grad, w_pair.T, preferred_element_type=f32).astype(bf16)
+    mlp_product, pair_grad, hidden = tied((mlp_product, pair_grad, hidden))
+    mlp_scattered = scatter_low(mlp_product)
     down_product = jnp.dot(hidden, w_down, preferred_element_type=f32).astype(bf16)
     pair_shared = SharedProduct(normed_mlp, pair_grad, "dp", places)
     down_shared = SharedProduct(hidden, out_low, "dp", crossed)
@@ -586,16 +603,24 @@
         sine, kv_heads, group, rows, tile_rows,
     )
     for shared in wide:
-        while len(shared.up) > 1:
+        while len(shared.up) > 2:
             shared.step()
-    earlier, pair_shared.value, down_shared.value, attended_plain = tied(
-        (earlier, pair_shared.value, down_shared.value, attended_plain)
-    )
+        shared.begin_up()
+    earlier, pair_shared.got, down_shared.got, attended_plain = tied(
+        (earlier, pair_shared.got, down_shared.got, attended_plain)
+    )
+    for shared in wide:
+        shared.end_up()
     received = [
         from_behind(earlier[reach - d], "dp", -d) for d in range(1, reach + 1)
     ]
     out_shared = SharedProduct(attended_plain, residual_low, "dp", crossed)
     out_shared.meet()
+    for shared in wide:
+        shared.begin_up()
+    received, pair_shared.got, down_shared.got, out_shared.value = tied(
+        (received, pair_shared.got, down_shared.got, out_shared.value)
+    )
     key_value_grad = gather_back(
         key_own, value_own, received, cosine, sine, kv_heads, stretch, rows
     )
@@ -611,10 +636,17 @@
         attention_normed, jnp.concatenate([query_plain, kv_plain], axis=1), "dp", places
     )
     joined_shared.meet()
-    grad_joined = joined_shared.finish()
-    grad_pair = pair_shared.finish()
-    grad_down = down_shared.finish()
-    grad_out = out_shared.finish()
+    query_width = w_query.shape[1]
+    kv_width = key_weight.shape[1]
+    value_from = query_width + kv_width + gap
+    grad_query, grad_key, grad_value = joined_shared.finish(
+        (0, query_width),
+        (query_width, query_width + kv_width),
+        (value_from, value_from + kv_width),
+    )
+    grad_gate, grad_up = pair_shared.finish((0, width), (width, 2 * width))
+    (grad_down,) = down_shared.finish((0, out_grad.shape[1]))
+    (grad_out,) = out_shared.finish((0, out_grad.shape[1]))
     attn_gain_part = (
         jnp.sum(
             attn_normed_part.astype(f32) * attention_normed.astype(f32), axis=0, keepdims=True
@@ -630,21 +662,16 @@
     attn_normed_grad = attn_scattered.astype(f32)
     input_part = normalize_back(block_input, inv_rms_attn, attn_gain, attn_normed_grad)
     input_grad = residual_grad + input_part
-    query_width = w_query.shape[1]
-    kv_width = key_weight.shape[1]
-    grad_query = grad_joined[:, :query_width].astype(f32)
-    grad_key = grad_joined[:, query_width : query_width + kv_width].astype(f32)
-    grad_value = grad_joined[:, query_width + kv_width + gap :].astype(f32)
     return (
         block_output,
         input_grad,
         grad_query,
         grad_key,
         grad_value,
-        grad_out.astype(f32),
-        grad_pair[:, :width].astype(f32),
-        grad_pair[:, width:].astype(f32),
-        grad_down.astype(f32),
+        grad_out,
+        grad_gate,
+        grad_up,
+        grad_down,
         grad_attn_gain,
         grad_mlp_gain,
     )

time: 664 us -> 653 us (0.983)
  starting transfers between devices: 72 us -> 40.9 us
  waiting for transfers between devices: 312 us -> 339 us
  other arithmetic: 78.8 us -> 69.1 us
    ppermute x29, starting transfers between devices: 61.5 us -> 30.2 us  [exchange(): return lax.ppermute(value, axis, [(i, i ^ distance) for i in range(count)])]
    ppermute x4, waiting for transfers between devices: 16.4 us -> 44 us  [from_behind(): lax.ppermute(value, axis, [(source, source + steps) for source in range(l...]
    slice x0 -> x6, local copies, waits for them, and re-layouts: none -> 10.8 us  [the longest x3 6.3 us: finish(): self.value[:, a:b]]
    select_n x10 -> x8, other arithmetic: 19.6 us -> 12.2 us  [joined(): jnp.where(self.bit(self.place) == 1, jnp.concatenate([got, whole], axis=0...]
    unnamed x98 -> x92, local copies, waits for them, and re-layouts: 20.5 us -> 15.6 us
    convert_element_type x10 -> x12, other arithmetic: 23 us -> 18.8 us  [the longest x7 14.7 us: finish(): self.joined(self.value[:, a:b], self.got[:, a:b]).astype(f32)]
  transfers between devices with their start and end apart: 41 -> 41, of which waited for: 22 -> 19; matrix products, arithmetic and copies ran while one was open for 26% -> 22% of each run, Pallas kernels for 7% -> 7%
where the time goes in v5:
time: 653 us; the launch traced here: 644 us
  waiting for transfers between devices  339 us (52%)
  matrix products  98.7 us (15%)
  other arithmetic  69.1 us (11%)
  Pallas kernels  45.2 us (7%)
  starting transfers between devices  40.9 us (6%)
  local copies, waits for them, and re-layouts  36.2 us (6%)
  between operations  15.1 us (2%)
    all_gather x4, waiting for transfers between devices, gather_rows(): return lax.all_gather(rows, 'tensor', axis=0, tiled=True)  138 us
    ppermute x29, waiting for transfers between devices, exchange(): return lax.ppermute(value, axis, [(i, i ^ distance) for i in range(count)])  91 us
    reduce_scatter x2, waiting for transfers between devices, scatter_low(): lax.psum_scatter(product.astype(bf16), 'tensor', scatter_dimension=0, til...  65.6 us
    ppermute x4, waiting for transfers between devices, from_behind(): lax.ppermute(value, axis, [(source, source + steps) for source in range(l...  44 us
    dot_general x8, matrix products, times(): return jnp.dot(part.T, self.right, preferred_element_type=f32)  32.7 us
    ppermute x29, starting transfers between devices, exchange(): return lax.ppermute(value, axis, [(i, i ^ distance) for i in range(count)])  30.2 us
    pallas_call x1, Pallas kernels, attend_back(): pl.pallas_call(functools.partial(attend_back_kernel, tiles, chunks, group...  20 us
    unnamed x92, local copies, waits for them, and re-layouts  15.6 us
  transfers between devices with their start and end apart: 41, of which 19 were waited for; matrix products, arithmetic and copies ran while one was open for 22% of the time, Pallas kernels for 7%

profile of v5, /device:TPU:0, one launch (start us, length us, event | category | flops | bytes accessed | tf_op | source)
XLA Modules:
  0.0 644.2 jit_solution(5361166433231255300)
XLA Ops:
  10.6 2.5 multiply_convert_fusion.4
  13.9 2.2 copy.26
  16.1 2.2 copy.27
  18.5 3.1 fusion.44
  21.6 6.4 fusion.4.weight_ref
  28.0 51.4 %all-gather.5.cloned.1.call-done.rows_ref = bf16[1024,1536]{1,0:T(8,128)(2,1)} async-done(((bf16[256,1536]{1,0:T(8,128)(2,1)}), bf16[1024,1536]{1,0:T(8,128)(2,1)}) %all-gather.5.cloned.1.call-update) | async-done | bytes 3145744 | tf_op jit(solution)/shard_map/all_gather | solution.py:496
  79.4 7.5 %project.1 = (bf16[1024,512]{1,0:T(8,128)(2,1)}, bf16[1024,512]{1,0:T(8,128)(2,1)}) custom-call(bf16[1024,1536]{1,0:T(8,128)(2,1)} %all-gather.5.cloned.1.call-done.rows_ref, bf16[1536,1024]{1,0:T(8,128)(2,1)} %fusion.4.weight_ref, f32[1024,128]{1,0:T(8,128)} %get-tuple-element.119.cosine_ref.refs_2_, f32[1024,128]{1,0:T(8,128)} %get-tuple-element.118.sine_ref.refs_3_), custom_call_target="tpu_custom_call" | custom-call | flops 3221225472 | bytes 8388608 | tf_op jit(solution)/shard_map/project/pallas_call | solution.py:100
  86.9 4.4 collective-permute-start
  91.3 2.3 collective-permute-start.1
  94.3 3.5 fusion.41
  97.8 16.3 %collective-permute-done.refs_0_.refs_3_.refs_5_.refs_8_ = bf16[1024,512]{1,0:T(8,128)(2,1)} collective-permute-done((bf16[1024,512]{1,0:T(8,128)(2,1)}, bf16[1024,512]{1,0:T(8,128)(2,1)}, u32[]{:S(2)}, u32[]{:S(2)}) %collective-permute-start) | collective-permute-done | bytes 1048608 | tf_op jit(solution)/shard_map/ppermute | solution.py:32
  114.2 13.2 %attend.1 = (bf16[1024,512]{1,0:T(8,128)(2,1)}, f32[2,4,1,512]{3,2,1,0:T(1,128)}) custom-call(s32[4]{0:T(128)} %and_select_fusion.low_ref, bf16[1024,512]{1,0:T(8,128)(2,1)} %get-tuple-element.44.query_ref, s32[4,1,256]{2,1,0:T(1,128)} %bitcast.28, bf16[1024,512]{1,0:T(8,128)(2,1)} %collective-permute-done.refs_0_.refs_3_.refs_5_.refs_8_, ...), custom_call_target="tpu_custom_call" | custom-call | flops 8589934592 | bytes 8388608 | tf_op jit(solution)/shard_map/attend/pallas_call | solution.py:229
  127.3 5.2 convolution_convert_fusion.1
  132.6 11.1 %all-gather.7.cloned.1.call-done = bf16[1024,1536]{1,0:T(8,128)(2,1)} async-done(((bf16[256,1536]{1,0:T(8,128)(2,1)}), bf16[1024,1536]{1,0:T(8,128)(2,1)}) %all-gather.7.cloned.1.call-update) | async-done | bytes 3145744 | tf_op jit(solution)/shard_map/all_gather | solution.py:496
  143.7 6.9 %fusion.89 = f32[1024,1024]{1,0:T(8,128)} fusion(bf16[1024,1536]{1,0:T(8,128)(2,1)} %all-gather.7.cloned.1.call-done, bf16[1024,1536]{1,0:T(8,128)(2,1)S(1)} %copy-done), kind=kOutput, calls=%fused_computation.181 | convolution fusion | flops 3221225472 | bytes 10485760 | tf_op jit(solution)/shard_map/dot_general | solution.py:552
  150.5 62.3 %reduce-scatter.5.cloned.1.call-done = bf16[256,1536]{1,0:T(8,128)(2,1)} async-done(((bf16[1024,1536]{1,0:T(8,128)(2,1)}), bf16[256,1536]{1,0:T(8,128)(2,1)}) %reduce-scatter.5.cloned.1.call-update) | async-done | bytes 786448 | tf_op jit(solution)/shard_map/reduce_scatter | solution.py:492
  217.2 4.0 constant_dynamic-update-slice_fusion.1
  221.2 2.0 constant_dynamic-update-slice_fusion
  223.2 57.3 %all-gather.9.cloned.1.call-done = bf16[1024,1536]{1,0:T(8,128)(2,1)} async-done(((bf16[256,1536]{1,0:T(8,128)(2,1)}), bf16[1024,1536]{1,0:T(8,128)(2,1)}) %all-gather.9.cloned.1.call-update) | async-done | bytes 3145744 | tf_op jit(solution)/shard_map/all_gather | solution.py:496
  280.4 9.8 %fusion.90 = f32[1024,2048]{1,0:T(8,128)S(1)} fusion(bf16[1024,1536]{1,0:T(8,128)(2,1)} %all-gather.9.cloned.1.call-done, bf16[1536,2048]{1,0:T(8,128)(2,1)} %constant_dynamic-update-slice_fusion), kind=kOutput, calls=%fused_computation.182 | convolution fusion | flops 6442450944 | bytes 17825792 | tf_op jit(solution)/shard_map/dot_general | solution.py:560
  290.3 3.9 multiply_convert_fusion.2
  294.2 2.4 pad_maximum_fusion
  296.6 10.1 %convolution_convert_fusion = bf16[1024,1536]{1,0:T(8,128)(2,1)} fusion(bf16[1536,2048]{1,0:T(8,128)(2,1)} %constant_dynamic-update-slice_fusion, bf16[1024,1024]{1,0:T(8,128)(2,1)S(1)} %get-tuple-element.106, bf16[1024,1024]{1,0:T(8,128)(2,1)S(1)} %get-tuple-element.105), kind=kOutput, calls=%fused_computation.9 | convolution fusion | flops 6452412416 | bytes 13631488 | tf_op jit(solution)/shard_map/dot_general | solution.py:568
  306.7 7.8 %convolution_convert_fusion.3 = bf16[768,2048]{1,0:T(8,128)(2,1)} fusion(bf16[1024,2048]{1,0:T(8,128)(2,1)} %pad_maximum_fusion, bf16[1024,1536]{1,0:T(8,128)(2,1)} %all-gather.9.cloned.1.call-done, s32[]{:T(128)S(6)} %select_n.275), kind=kOutput, calls=%fused_computation.12 | convolution fusion | flops 3222798336 | bytes 8912900 | tf_op jit(solution)/shard_map/dot_general | solution.py:432
  314.8 5.2 convolution_convert_fusion.4
  320.5 7.2 %convert_add_fusion = f32[768,2048]{1,0:T(8,128)S(1)} fusion(bf16[768,2048]{1,0:T(8,128)(2,1)} %collective-permute-done.2, bf16[1024,2048]{1,0:T(8,128)(2,1)} %pad_maximum_fusion, bf16[1024,1536]{1,0:T(8,128)(2,1)} %all-gather.9.cloned.1.call-done, s32[]{:T(128)S(6)} %select_n.274), kind=kOutput, calls=%fused_computation.2 | convolution fusion | flops 3224371200 | bytes 15204356 | tf_op jit(solution)/shard_map/dot_general | solution.py:432
  332.0 3.3 convert_add_fusion.1
  338.7 6.4 convolution_convert_fusion.2
  345.1 12.0 %collective-permute-done.5 = bf16[256,1536]{1,0:T(8,128)(2,1)} collective-permute-done((bf16[256,1536]{1,0:T(8,128)(2,1)}, bf16[256,1536]{1,0:T(8,128)(2,1)}, u32[]{:S(2)}, u32[]{:S(2)}) %collective-permute-start.5) | collective-permute-done | bytes 786464 | tf_op jit(solution)/shard_map/ppermute | solution.py:37
  357.1 3.0 convert_add_fusion.5
  360.1 5.8 collective-permute-done.3
  365.9 4.7 convert_add_fusion.2
  370.6 3.3 reduce-scatter.7.cloned.1.call-done
  377.9 2.4 dynamic-slice_convert_fusion.1
  383.4 16.1 %collective-permute-done.6 = bf16[192,2048]{1,0:T(8,128)(2,1)} collective-permute-done((bf16[192,2048]{1,0:T(8,128)(2,1)}, bf16[192,2048]{1,0:T(8,128)(2,1)}, u32[]{:S(2)}, u32[]{:S(2)}) %collective-permute-start.6) | collective-permute-done | bytes 786464 | tf_op jit(solution)/shard_map/ppermute | solution.py:37
  399.5 2.7 add_convert_fusion.1
  405.4 3.0 fusion.40
  408.4 4.9 collective-permute-done.9
  414.3 6.3 collective-permute-done.7
  420.6 2.6 maximum_select_fusion.4
  423.2 17.8 %all-gather.11.cloned.1.call-done = bf16[1024,1536]{1,0:T(8,128)(2,1)} async-done(((bf16[256,1536]{1,0:T(8,128)(2,1)}), bf16[1024,1536]{1,0:T(8,128)(2,1)}) %all-gather.11.cloned.1.call-update) | async-done | bytes 3145744 | tf_op jit(solution)/shard_map/all_gather | solution.py:496
  441.0 5.1 convolution_convert_fusion.7.refs_4_
  449.7 20.0 %attend_back.1 = (bf16[1024,512]{1,0:T(8,128)(2,1)}, f32[1024,256]{1,0:T(8,128)}, f32[1024,256]{1,0:T(8,128)}, bf16[2,2,1024,256]{3,2,1,0:T(8,128)(2,1)}) custom-call(s32[4]{0:T(128)} %and_select_fusion.low_ref, s32[4]{0:T(128)} %iota.50.slot_ref, bf16[1024,512]{1,0:T(8,128)(2,1)} %get-tuple-element.44.query_ref, s32[4,1,256]{2,1,0:T(1,128)} %bitcast.29, ...), custom_call_target="tpu_custom_call" | custom-call | flops 21474836480 | bytes 16777216 | tf_op jit(solution)/shard_map/attend_back/pallas_call | solution.py:374
  469.7 12.5 %collective-permute-done.10 = bf16[384,2048]{1,0:T(8,128)(2,1)} collective-permute-done((bf16[384,2048]{1,0:T(8,128)(2,1)S(1)}, bf16[384,2048]{1,0:T(8,128)(2,1)}, u32[]{:S(2)}, u32[]{:S(2)}) %collective-permute-start.10) | collective-permute-done | bytes 1572896 | tf_op jit(solution)/shard_map/ppermute | solution.py:37
  482.2 4.2 maximum_select_fusion
  487.7 2.3 maximum_select_fusion.5
  496.8 3.4 fusion.84
  502.1 27.7 %collective-permute-done.13.refs_1_ = bf16[2,1024,256]{2,1,0:T(8,128)(2,1)S(1)} collective-permute-done((bf16[2,1024,256]{2,1,0:T(8,128)(2,1)S(1)}, bf16[2,1024,256]{2,1,0:T(8,128)(2,1)S(1)}, u32[]{:S(2)}, u32[]{:S(2)}) %collective-permute-start.13) | collective-permute-done | bytes 1048608 | tf_op jit(solution)/shard_map/ppermute | solution.py:32
  531.4 4.5 gather_back.1
  535.9 3.7 fusion.17
  539.9 3.7 multiply_reduce_fusion
  546.1 2.6 convolution_convert_fusion.6
  550.4 3.1 fusion.3
  553.8 3.8 convert_add_fusion.3
  560.9 14.1 %collective-permute-done.18 = bf16[384,832]{0,1:T(8,128)(2,1)S(1)} collective-permute-done((bf16[384,832]{0,1:T(8,128)(2,1)S(1)}, bf16[384,832]{0,1:T(8,128)(2,1)S(1)}, u32[]{:S(2)}, u32[]{:S(2)}) %collective-permute-start.18) | collective-permute-done | bytes 639008 | tf_op jit(solution)/shard_map/ppermute | solution.py:37
  579.4 7.2 %collective-permute-done.19 = bf16[192,832]{0,1:T(8,128)(2,1)S(1)} collective-permute-done((bf16[192,832]{0,1:T(8,128)(2,1)S(1)}, bf16[192,832]{0,1:T(8,128)(2,1)S(1)}, u32[]{:S(2)}, u32[]{:S(2)}) %collective-permute-start.19) | collective-permute-done | bytes 319520 | tf_op jit(solution)/shard_map/ppermute | solution.py:37
  588.7 2.2 fusion.83
  592.9 6.8 %collective-permute-done.20 = bf16[192,832]{0,1:T(8,128)(2,1)S(1)} collective-permute-done((bf16[192,832]{0,1:T(8,128)(2,1)S(1)}, bf16[192,832]{0,1:T(8,128)(2,1)S(1)}, u32[]{:S(2)}, u32[]{:S(2)}) %collective-permute-start.20) | collective-permute-done | bytes 319520 | tf_op jit(solution)/shard_map/ppermute | solution.py:37
  601.7 3.5 fusion.2
  607.2 5.0 collective-permute-done.21
  613.5 3.7 fusion.1
  619.5 2.5 convert_add_fusion.4
  626.4 2.0 copy.28
  633.5 3.6 subtract_add_fusion
  (222 shorter events, 77.7 us)
Async XLA Ops:
  7.2 136.5 %copy-start = (bf16[1024,1536]{1,0:T(8,128)(2,1)S(1)}, bf16[1024,1536]{1,0:T(8,128)(2,1)}, u32[]{:S(2)}) copy-start(bf16[1024,1536]{1,0:T(8,128)(2,1)} %param.22) | copy-start | bytes 9437188
  7.2 72.2 %all-gather.5.cloned.1.call-start = ((), (), s32[]{:S(2)}) async-start(), calls=%async_computation.4 | async-start | bytes 3932160 | tf_op jit(solution)/shard_map/all_gather | solution.py:496
  13.1 5.4 copy-start.40
  13.1 130.6 %all-gather.7.cloned.1.call-start = ((), (), s32[]{:S(2)}) async-start(), calls=%async_computation.6 | async-start | bytes 3932160 | tf_op jit(solution)/shard_map/all_gather | solution.py:496
  13.8 199.0 %reduce-scatter.5.cloned.1.call-start = ((), (), s32[]{:S(2)}) async-start(), calls=%async_computation.5 | async-start | bytes 3932160 | tf_op jit(solution)/shard_map/reduce_scatter | solution.py:492
  18.4 75.1 %copy-start.35 = (s32[1024]{0:T(1024)}, s32[1024]{0:T(1024)S(1)}, u32[]{:S(2)}) copy-start(s32[1024]{0:T(1024)S(1)} %get-tuple-element.121) | copy-start | bytes 12292
  86.9 27.2 %collective-permute-start = (bf16[1024,512]{1,0:T(8,128)(2,1)}, bf16[1024,512]{1,0:T(8,128)(2,1)}, u32[]{:S(2)}, u32[]{:S(2)}) collective-permute-start(bf16[1024,512]{1,0:T(8,128)(2,1)} %get-tuple-element.45.refs_2_.refs_5_.refs_7_.refs_10_), channel_id=1, source_target_pairs={{0,8},{4,12},{8,16},{12,20},{16,24},{20,28},{1,9},{5,13},{9,17},{1... | collective-permute-start | bytes 3145736 | tf_op jit(solution)/shard_map/ppermute | solution.py:32
  91.3 22.9 %collective-permute-start.1 = (bf16[1024,512]{1,0:T(8,128)(2,1)}, bf16[1024,512]{1,0:T(8,128)(2,1)}, u32[]{:S(2)}, u32[]{:S(2)}) collective-permute-start(bf16[1024,512]{1,0:T(8,128)(2,1)} %get-tuple-element.45.refs_2_.refs_5_.refs_7_.refs_10_), channel_id=1, source_target_pairs={{0,4},{4,8},{8,12},{12,16},{16,20},{20,24},{24,28},{1,5},{5,9},{9,... | collective-permute-start | bytes 3145736 | tf_op jit(solution)/shard_map/ppermute | solution.py:32
  132.6 147.9 %all-gather.9.cloned.1.call-start = ((), (), s32[]{:S(2)}) async-start(), calls=%async_computation.7 | async-start | bytes 3932160 | tf_op jit(solution)/shard_map/all_gather | solution.py:496
  150.5 65.3 %copy-start.34 = (f32[1536]{0:T(1024)S(1)}, f32[1536]{0:T(1024)}, u32[]{:S(2)}) copy-start(f32[1536]{0:T(1024)} %param.19) | copy-start | bytes 18436
  216.9 157.0 %reduce-scatter.7.cloned.1.call-start = ((), (), s32[]{:S(2)}) async-start(), calls=%async_computation.8 | async-start | bytes 3932160 | tf_op jit(solution)/shard_map/reduce_scatter | solution.py:492
  217.2 4.0 copy-start.18
  280.4 9.9 %copy-start.16 = (f32[1024,1024]{1,0:T(8,128)S(1)}, f32[1024,1024]{1,0:T(8,128)}, u32[]{:S(2)}) copy-start(f32[1024,1024]{1,0:T(8,128)} %fusion.89) | copy-start | bytes 12582916
  314.5 6.0 collective-permute-start.2
  314.6 126.4 %all-gather.11.cloned.1.call-start = ((), (), s32[]{:S(2)}) async-start(), calls=%async_computation.9 | async-start | bytes 3932160 | tf_op jit(solution)/shard_map/all_gather | solution.py:496
  320.0 10.7 %collective-permute-start.4 = (bf16[512,1536]{1,0:T(8,128)(2,1)}, bf16[512,1536]{1,0:T(8,128)(2,1)}, u32[]{:S(2)}, u32[]{:S(2)}) collective-permute-start(bf16[512,1536]{1,0:T(8,128)(2,1)} %convolution_convert_fusion.4), channel_id=1, source_target_pairs={{0,4},{4,0},{8,12},{12,8},{16,20},{20,16},{24,28},{28,24},{1,5},{5... | collective-permute-start | bytes 4718600 | tf_op jit(solution)/shard_map/ppermute | solution.py:37
  320.5 10.1 %copy-start.15 = (bf16[1024,1024]{1,0:T(8,128)(2,1)S(1)}, bf16[1024,1024]{1,0:T(8,128)(2,1)}, u32[]{:S(2)}) copy-start(bf16[1024,1024]{1,0:T(8,128)(2,1)} %get-tuple-element.51) | copy-start | bytes 6291460
  327.8 7.5 %copy-start.5 = (f32[768,2048]{1,0:T(8,128)}, f32[768,2048]{1,0:T(8,128)S(1)}, u32[]{:S(2)}) copy-start(f32[768,2048]{1,0:T(8,128)S(1)} %convert_add_fusion) | copy-start | bytes 18874372
  327.8 4.2 copy-start.8
  329.2 36.8 %collective-permute-start.3 = (bf16[384,2048]{1,0:T(8,128)(2,1)}, bf16[384,2048]{1,0:T(8,128)(2,1)}, u32[]{:S(2)}, u32[]{:S(2)}) collective-permute-start(bf16[384,2048]{1,0:T(8,128)(2,1)} %dynamic-slice_convert_fusion), channel_id=1, source_target_pairs={{0,8},{4,12},{8,0},{12,4},{16,24},{20,28},{24,16},{28,20},{1,9},{5... | collective-permute-start | bytes 4718600 | tf_op jit(solution)/shard_map/ppermute | solution.py:37
  337.2 19.9 %collective-permute-start.5 = (bf16[256,1536]{1,0:T(8,128)(2,1)}, bf16[256,1536]{1,0:T(8,128)(2,1)}, u32[]{:S(2)}, u32[]{:S(2)}) collective-permute-start(bf16[256,1536]{1,0:T(8,128)(2,1)} %dynamic-slice_convert_fusion.2), channel_id=1, source_target_pairs={{0,16},{4,20},{8,24},{12,28},{16,0},{20,4},{24,8},{28,12},{1,17},{... | collective-permute-start | bytes 2359304 | tf_op jit(solution)/shard_map/ppermute | solution.py:37
  360.1 13.8 %copy-start.4 = (f32[256,1536]{1,0:T(8,128)S(1)}, f32[256,1536]{1,0:T(8,128)}, u32[]{:S(2)}) copy-start(f32[256,1536]{1,0:T(8,128)} %copy-done.3) | copy-start | bytes 4718596
  370.6 5.0 copy-start.13
  377.5 4.4 copy-start.14
  377.5 242.0 %reduce-scatter.9.cloned.1.call-start = ((), (), s32[]{:S(2)}) async-start(), calls=%async_computation.10 | async-start | bytes 3932160 | tf_op jit(solution)/shard_map/reduce_scatter | solution.py:592
  380.3 19.2 %collective-permute-start.6 = (bf16[192,2048]{1,0:T(8,128)(2,1)}, bf16[192,2048]{1,0:T(8,128)(2,1)}, u32[]{:S(2)}, u32[]{:S(2)}) collective-permute-start(bf16[192,2048]{1,0:T(8,128)(2,1)} %dynamic-slice_convert_fusion.1), channel_id=1, source_target_pairs={{0,16},{4,20},{8,24},{12,28},{16,0},{20,4},{24,8},{28,12},{1,17},{... | collective-permute-start | bytes 2359304 | tf_op jit(solution)/shard_map/ppermute | solution.py:37
  381.9 21.9 %collective-permute-start.8 = (bf16[128,1536]{1,0:T(8,128)(2,1)S(1)}, bf16[128,1536]{1,0:T(8,128)(2,1)S(1)}, u32[]{:S(2)}, u32[]{:S(2)}) collective-permute-start(bf16[128,1536]{1,0:T(8,128)(2,1)S(1)} %dynamic-slice_convert_fusion.5), channel_id=1, source_target_pairs={{0,8},{4,12},{8,0},{12,4},{16,24},{20,28},{24,16},{28,20},{1,9},{5... | collective-permute-start | bytes 1179656 | tf_op jit(solution)/shard_map/ppermute | solution.py:37
  402.3 18.3 %collective-permute-start.7 = (bf16[192,2048]{1,0:T(8,128)(2,1)}, bf16[192,2048]{1,0:T(8,128)(2,1)}, u32[]{:S(2)}, u32[]{:S(2)}) collective-permute-start(bf16[192,2048]{1,0:T(8,128)(2,1)} %add_convert_fusion.1), channel_id=1, source_target_pairs={{0,16},{4,20},{8,24},{12,28},{16,0},{20,4},{24,8},{28,12},{1,17},{... | collective-permute-start | bytes 2359304 | tf_op jit(solution)/shard_map/ppermute | solution.py:37
  403.9 9.4 %collective-permute-start.9 = (bf16[128,1536]{1,0:T(8,128)(2,1)S(1)}, bf16[128,1536]{1,0:T(8,128)(2,1)S(1)}, u32[]{:S(2)}, u32[]{:S(2)}) collective-permute-start(bf16[128,1536]{1,0:T(8,128)(2,1)S(1)} %add_convert_fusion.3), channel_id=1, source_target_pairs={{0,8},{4,12},{8,0},{12,4},{16,24},{20,28},{24,16},{28,20},{1,9},{5... | collective-permute-start | bytes 1179656 | tf_op jit(solution)/shard_map/ppermute | solution.py:37
  446.1 36.1 %collective-permute-start.10 = (bf16[384,2048]{1,0:T(8,128)(2,1)S(1)}, bf16[384,2048]{1,0:T(8,128)(2,1)}, u32[]{:S(2)}, u32[]{:S(2)}) collective-permute-start(bf16[384,2048]{1,0:T(8,128)(2,1)S(1)} %maximum_select_fusion.4), channel_id=1, source_target_pairs={{0,8},{4,12},{8,0},{12,4},{16,24},{20,28},{24,16},{28,20},{1,9},{5... | collective-permute-start | bytes 4718600 | tf_op jit(solution)/shard_map/ppermute | solution.py:37
  447.6 22.1 %collective-permute-start.11 = (bf16[256,1536]{1,0:T(8,128)(2,1)}, bf16[256,1536]{1,0:T(8,128)(2,1)}, u32[]{:S(2)}, u32[]{:S(2)}) collective-permute-start(bf16[256,1536]{1,0:T(8,128)(2,1)} %maximum_select_fusion.9), channel_id=1, source_target_pairs={{0,16},{4,20},{8,24},{12,28},{16,0},{20,4},{24,8},{28,12},{1,17},{... | collective-permute-start | bytes 2359304 | tf_op jit(solution)/shard_map/ppermute | solution.py:37
  449.1 182.9 %reduce-scatter.11.cloned.1.call-start = ((), (), s32[]{:S(2)}) async-start(), calls=%async_computation.11 | async-start | bytes 3932160 | tf_op jit(solution)/shard_map/reduce_scatter | solution.py:632
  482.2 5.3 copy-start.39
  486.4 44.6 %collective-permute-start.14 = (bf16[768,2048]{1,0:T(8,128)(2,1)}, bf16[768,2048]{1,0:T(8,128)(2,1)}, u32[]{:S(2)}, u32[]{:S(2)}) collective-permute-start(bf16[768,2048]{1,0:T(8,128)(2,1)} %maximum_select_fusion), channel_id=1, source_target_pairs={{0,4},{4,0},{8,12},{12,8},{16,20},{20,16},{24,28},{28,24},{1,5},{5... | collective-permute-start | bytes 9437192 | tf_op jit(solution)/shard_map/ppermute | solution.py:37
  490.0 4.2 copy-start.10
  490.1 39.8 %collective-permute-start.15 = (bf16[512,1536]{1,0:T(8,128)(2,1)S(1)}, bf16[512,1536]{1,0:T(8,128)(2,1)S(1)}, u32[]{:S(2)}, u32[]{:S(2)}) collective-permute-start(bf16[512,1536]{1,0:T(8,128)(2,1)S(1)} %maximum_select_fusion.5), channel_id=1, source_target_pairs={{0,4},{4,0},{8,12},{12,8},{16,20},{20,16},{24,28},{28,24},{1,5},{5... | collective-permute-start | bytes 4718600 | tf_op jit(solution)/shard_map/ppermute | solution.py:37
  490.3 5.0 copy-start.27
  490.3 11.8 %collective-permute-start.12 = (bf16[2,1024,256]{2,1,0:T(8,128)(2,1)S(1)}, bf16[2,1024,256]{2,1,0:T(8,128)(2,1)S(1)}, u32[]{:S(2)}, u32[]{:S(2)}) collective-permute-start(bf16[2,1024,256]{2,1,0:T(8,128)(2,1)S(1)} %get-tuple-element.113), channel_id=1, source_target_pairs={{4,0},{8,4},{12,8},{16,12},{20,16},{24,20},{28,24},{5,1},{9,5},{13... | collective-permute-start | bytes 3145736 | tf_op jit(solution)/shard_map/ppermute | solution.py:32
  491.9 38.0 %collective-permute-start.13 = (bf16[2,1024,256]{2,1,0:T(8,128)(2,1)S(1)}, bf16[2,1024,256]{2,1,0:T(8,128)(2,1)S(1)}, u32[]{:S(2)}, u32[]{:S(2)}) collective-permute-start(bf16[2,1024,256]{2,1,0:T(8,128)(2,1)S(1)} %get-tuple-element.112), channel_id=1, source_target_pairs={{8,0},{12,4},{16,8},{20,12},{24,16},{28,20},{9,1},{13,5},{17,9},{2... | collective-permute-start | bytes 3145736 | tf_op jit(solution)/shard_map/ppermute | solution.py:32
  494.2 6.0 collective-permute-start.16
  502.1 28.9 %copy-start.29 = (bf16[2,1024,256]{2,1,0:T(8,128)(2,1)}, bf16[2,1024,256]{2,1,0:T(8,128)(2,1)S(1)}, u32[]{:S(2)}) copy-start(bf16[2,1024,256]{2,1,0:T(8,128)(2,1)S(1)} %collective-permute-done.12.refs_0_) | copy-start | bytes 3145732
  535.9 3.7 copy-start.28
  535.9 3.9 copy-start.32
  539.9 5.5 copy-start.31
  543.6 5.1 collective-permute-start.28
  544.8 14.8 %collective-permute-start.23 = (bf16[96,1536]{1,0:T(8,128)(2,1)S(1)}, bf16[96,1536]{1,0:T(8,128)(2,1)}, u32[]{:S(2)}, u32[]{:S(2)}) collective-permute-start(bf16[96,1536]{1,0:T(8,128)(2,1)S(1)} %dynamic-slice_convert_fusion.6), channel_id=1, source_target_pairs={{0,16},{4,20},{8,24},{12,28},{16,0},{20,4},{24,8},{28,12},{1,17},{... | collective-permute-start | bytes 884744 | tf_op jit(solution)/shard_map/ppermute | solution.py:37
  546.1 4.3 copy-start.11
  546.1 4.3 copy-start.24
  548.6 5.1 collective-permute-start.17
  548.7 4.8 collective-permute-start.29
  553.5 6.1 copy-start.17
  553.5 37.4 %collective-permute-start.30 = (f32[2,1536]{1,0:T(2,128)S(1)}, f32[2,1536]{1,0:T(2,128)S(1)}, u32[]{:S(2)}, u32[]{:S(2)}) collective-permute-start(f32[2,1536]{1,0:T(2,128)S(1)} %fusion.114), channel_id=1, source_target_pairs={{0,4},{4,0},{8,12},{12,8},{16,20},{20,16},{24,28},{28,24},{1,5},{5... | collective-permute-start | bytes 36872 | tf_op jit(solution)/shard_map/ppermute | solution.py:37
  557.7 17.3 %collective-permute-start.18 = (bf16[384,832]{0,1:T(8,128)(2,1)S(1)}, bf16[384,832]{0,1:T(8,128)(2,1)S(1)}, u32[]{:S(2)}, u32[]{:S(2)}) collective-permute-start(bf16[384,832]{0,1:T(8,128)(2,1)S(1)} %dynamic-slice_convert_fusion.3), channel_id=1, source_target_pairs={{0,8},{4,12},{8,0},{12,4},{16,24},{20,28},{24,16},{28,20},{1,9},{5... | collective-permute-start | bytes 1916936 | tf_op jit(solution)/shard_map/ppermute | solution.py:37
  560.7 16.9 %collective-permute-start.24 = (bf16[48,1536]{1,0:T(8,128)(2,1)S(1)}, bf16[48,1536]{1,0:T(8,128)(2,1)S(1)}, u32[]{:S(2)}, u32[]{:S(2)}) collective-permute-start(bf16[48,1536]{1,0:T(8,128)(2,1)S(1)} %dynamic-slice_convert_fusion.7), channel_id=1, source_target_pairs={{0,8},{4,12},{8,0},{12,4},{16,24},{20,28},{24,16},{28,20},{1,9},{5... | collective-permute-start | bytes 442376 | tf_op jit(solution)/shard_map/ppermute | solution.py:37
  575.4 11.2 %collective-permute-start.19 = (bf16[192,832]{0,1:T(8,128)(2,1)S(1)}, bf16[192,832]{0,1:T(8,128)(2,1)S(1)}, u32[]{:S(2)}, u32[]{:S(2)}) collective-permute-start(bf16[192,832]{0,1:T(8,128)(2,1)S(1)} %dynamic-slice_convert_fusion.4), channel_id=1, source_target_pairs={{0,16},{4,20},{8,24},{12,28},{16,0},{20,4},{24,8},{28,12},{1,17},{... | collective-permute-start | bytes 958472 | tf_op jit(solution)/shard_map/ppermute | solution.py:37
  577.6 14.9 %collective-permute-start.25 = (bf16[48,1536]{1,0:T(8,128)(2,1)S(1)}, bf16[48,1536]{1,0:T(8,128)(2,1)S(1)}, u32[]{:S(2)}, u32[]{:S(2)}) collective-permute-start(bf16[48,1536]{1,0:T(8,128)(2,1)S(1)} %add_convert_fusion.4), channel_id=1, source_target_pairs={{0,8},{4,12},{8,0},{12,4},{16,24},{20,28},{24,16},{28,20},{1,9},{5... | collective-permute-start | bytes 442376 | tf_op jit(solution)/shard_map/ppermute | solution.py:37
  586.9 12.8 %collective-permute-start.20 = (bf16[192,832]{0,1:T(8,128)(2,1)S(1)}, bf16[192,832]{0,1:T(8,128)(2,1)S(1)}, u32[]{:S(2)}, u32[]{:S(2)}) collective-permute-start(bf16[192,832]{0,1:T(8,128)(2,1)S(1)} %add_convert_fusion.2), channel_id=1, source_target_pairs={{0,16},{4,20},{8,24},{12,28},{16,0},{20,4},{24,8},{28,12},{1,17},{... | collective-permute-start | bytes 958472 | tf_op jit(solution)/shard_map/ppermute | solution.py:37
  590.9 10.8 %copy-start.9 = (bf16[768,1024]{1,0:T(8,128)(2,1)S(1)}, bf16[768,1024]{1,0:T(8,128)(2,1)}, u32[]{:S(2)}) copy-start(bf16[768,1024]{1,0:T(8,128)(2,1)} %get-tuple-element.110) | copy-start | bytes 4718596
  590.9 14.2 %collective-permute-start.31 = (f32[2,1536]{1,0:T(2,128)S(1)}, f32[2,1536]{1,0:T(2,128)S(1)}, u32[]{:S(2)}, u32[]{:S(2)}) collective-permute-start(f32[2,1536]{1,0:T(2,128)S(1)} %add.321), channel_id=1, source_target_pairs={{0,8},{4,12},{8,0},{12,4},{16,24},{20,28},{24,16},{28,20},{1,9},{5... | collective-permute-start | bytes 36872 | tf_op jit(solution)/shard_map/ppermute | solution.py:37
  592.5 14.5 %collective-permute-start.26 = (bf16[96,1536]{1,0:T(8,128)(2,1)S(1)}, bf16[96,1536]{1,0:T(8,128)(2,1)S(1)}, u32[]{:S(2)}, u32[]{:S(2)}) collective-permute-start(bf16[96,1536]{1,0:T(8,128)(2,1)S(1)} %maximum_select_fusion.14), channel_id=1, source_target_pairs={{0,16},{4,20},{8,24},{12,28},{16,0},{20,4},{24,8},{28,12},{1,17},{... | collective-permute-start | bytes 884744 | tf_op jit(solution)/shard_map/ppermute | solution.py:37
  600.2 11.9 %collective-permute-start.21 = (bf16[384,832]{0,1:T(8,128)(2,1)S(1)}, bf16[384,832]{0,1:T(8,128)(2,1)S(1)}, u32[]{:S(2)}, u32[]{:S(2)}) collective-permute-start(bf16[384,832]{0,1:T(8,128)(2,1)S(1)} %maximum_select_fusion.10), channel_id=1, source_target_pairs={{0,8},{4,12},{8,0},{12,4},{16,24},{20,28},{24,16},{28,20},{1,9},{5... | collective-permute-start | bytes 1916936 | tf_op jit(solution)/shard_map/ppermute | solution.py:37
  605.2 12.0 %collective-permute-start.32 = (f32[2,1536]{1,0:T(2,128)S(1)}, f32[2,1536]{1,0:T(2,128)S(1)}, u32[]{:S(2)}, u32[]{:S(2)}) collective-permute-start(f32[2,1536]{1,0:T(2,128)S(1)} %add.322), channel_id=1, source_target_pairs={{0,16},{4,20},{8,24},{12,28},{16,0},{20,4},{24,8},{28,12},{1,17},{... | collective-permute-start | bytes 36872 | tf_op jit(solution)/shard_map/ppermute | solution.py:37
  607.1 10.7 %collective-permute-start.27 = (bf16[192,1536]{1,0:T(8,128)(2,1)S(1)}, bf16[192,1536]{1,0:T(8,128)(2,1)S(1)}, u32[]{:S(2)}, u32[]{:S(2)}) collective-permute-start(bf16[192,1536]{1,0:T(8,128)(2,1)S(1)} %maximum_select_fusion.13), channel_id=1, source_target_pairs={{0,4},{4,0},{8,12},{12,8},{16,20},{20,16},{24,28},{28,24},{1,5},{5... | collective-permute-start | bytes 1769480 | tf_op jit(solution)/shard_map/ppermute | solution.py:37
  613.5 11.4 %collective-permute-start.22 = (bf16[768,832]{0,1:T(8,128)(2,1)}, bf16[768,832]{0,1:T(8,128)(2,1)}, u32[]{:S(2)}, u32[]{:S(2)}) collective-permute-start(bf16[768,832]{0,1:T(8,128)(2,1)} %maximum_select_fusion.6), channel_id=1, source_target_pairs={{0,4},{4,0},{8,12},{12,8},{16,20},{20,16},{24,28},{28,24},{1,5},{5... | collective-permute-start | bytes 3833864 | tf_op jit(solution)/shard_map/ppermute | solution.py:37
  (21 other events, 52.6 us)
Sparse Core Ops, SparseCore 0:
  13.2 66.1 all-gather.4
  81.5 62.0 all-gather.6
  146.5 66.2 reduce-scatter.4
  217.1 63.3 all-gather.8
  314.7 59.1 reduce-scatter.6
  377.6 63.3 all-gather.10
  449.2 57.2 reduce-scatter.8
  553.6 61.6 reduce-scatter.10

commit v6 on v5

--- a/solution.py
+++ b/solution.py
@@ -431,12 +431,14 @@
         part = lax.dynamic_slice_in_dim(self.left, offset, self.size, 1)
         return jnp.dot(part.T, self.right, preferred_element_type=f32)
 
-    def meet(self):
+    def meet(self, *others):
         got = exchange(self.sent, self.axis, 1 << self.order[0])
+        if others:
+            got, *others = lax.optimization_barrier((got,) + others)
         self.value = self.times(0, False) + got.astype(f32)
         self.down = list(self.order[1:])
         self.up = list(reversed(self.order))
-        return self.value
+        return others
 
     def step(self):
         if self.down:
@@ -547,7 +549,14 @@
         attention_normed, w_joined, cosine, sine, heads + kv_heads,
         (heads * LANES, 2 * kv_heads * LANES), rows,
     )
-    windows = [(from_behind(key_value, "dp", d), 0) for d in range(reach, -1, -1)]
+    paired = reach == 2 and lax.axis_size("dp") % 2 == 0
+    odd = lax.axis_index("dp") % 2 == 1
+    if paired:
+        two_back = from_behind(key_value, "dp", 2)
+        one_back = exchange(jnp.where(odd, two_back, key_value), "dp", 1)
+        windows = [(two_back, 0), (one_back, 0), (key_value, 0)]
+    else:
+        windows = [(from_behind(key_value, "dp", d), 0) for d in range(reach, -1, -1)]
     attended, logs = attend(queries, windows, firsts, low, kv_heads, group, rows, tile_rows)
     hidden_grad = jnp.dot(out_low, w_down.T, preferred_element_type=f32)
     mixed = scatter_low(jnp.dot(attended, w_out_spread, preferred_element_type=f32))
@@ -606,17 +615,19 @@
         while len(shared.up) > 2:
             shared.step()
         shared.begin_up()
-    earlier, pair_shared.got, down_shared.got, attended_plain = tied(
-        (earlier, pair_shared.got, down_shared.got, attended_plain)
-    )
+    earlier = [earlier[reach - d] for d in range(1, reach + 1)]
+    if paired:
+        crossing = exchange(earlier[0], "dp", 1)
+        both_back = earlier[1] + jnp.where(odd, crossing, 0)
+        both_back, crossing, attended_plain = tied((both_back, crossing, attended_plain))
+        received = [from_behind(both_back, "dp", -2), jnp.where(odd, 0, crossing)]
+    else:
+        earlier, attended_plain = tied((earlier, attended_plain))
+        received = [from_behind(earlier[d - 1], "dp", -d) for d in range(1, reach + 1)]
+    out_shared = SharedProduct(attended_plain, residual_low, "dp", crossed)
+    pair_shared.got, down_shared.got = out_shared.meet(pair_shared.got, down_shared.got)
     for shared in wide:
         shared.end_up()
-    received = [
-        from_behind(earlier[reach - d], "dp", -d) for d in range(1, reach + 1)
-    ]
-    out_shared = SharedProduct(attended_plain, residual_low, "dp", crossed)
-    out_shared.meet()
-    for shared in wide:
         shared.begin_up()
     received, pair_shared.got, down_shared.got, out_shared.value = tied(
         (received, pair_shared.got, down_shared.got, out_shared.value)
@@ -636,6 +647,16 @@
         attention_normed, jnp.concatenate([query_plain, kv_plain], axis=1), "dp", places
     )
     joined_shared.meet()
+    grad_gate, grad_up = pair_shared.finish((0, width), (width, 2 * width))
+    (grad_down,) = down_shared.finish((0, out_grad.shape[1]))
+    joined_shared.step()
+    joined_shared.value, grad_down = tied((joined_shared.value, grad_down))
+    joined_shared.step()
+    joined_shared.value, grad_gate = tied((joined_shared.value, grad_gate))
+    joined_shared.step()
+    joined_shared.value, grad_up, block_output = tied(
+        (joined_shared.value, grad_up, block_output)
+    )
     query_width = w_query.shape[1]
     kv_width = key_weight.shape[1]
     value_from = query_width + kv_width + gap
@@ -644,8 +665,6 @@
         (query_width, query_width + kv_width),
         (value_from, value_from + kv_width),
     )
-    grad_gate, grad_up = pair_shared.finish((0, width), (width, 2 * width))
-    (grad_down,) = down_shared.finish((0, out_grad.shape[1]))
     (grad_out,) = out_shared.finish((0, out_grad.shape[1]))
     attn_gain_part = (
         jnp.sum(

time: 653 us -> 688 us (1.054)
  waiting for transfers between devices: 339 us -> 353 us
  other arithmetic: 69.1 us -> 78.6 us
  starting transfers between devices: 40.9 us -> 49.8 us
    ppermute x29 -> x31, waiting for transfers between devices: 91 us -> 123 us  [exchange(): return lax.ppermute(value, axis, [(i, i ^ distance) for i in range(count)])]
    ppermute x29 -> x31, starting transfers between devices: 30.2 us -> 42.8 us  [exchange(): return lax.ppermute(value, axis, [(i, i ^ distance) for i in range(count)])]
    ppermute x4 -> x2, waiting for transfers between devices: 44 us -> 35.3 us  [from_behind(): lax.ppermute(value, axis, [(source, source + steps) for source in range(l...]
    unnamed x92 -> x98, local copies, waits for them, and re-layouts: 15.6 us -> 16.6 us
  transfers between devices with their start and end apart: 41 -> 41, of which waited for: 19 -> 23; matrix products, arithmetic and copies ran while one was open for 22% -> 22% of each run, Pallas kernels for 7% -> 4%
where the time goes in v6:
time: 688 us; the launch traced here: 679 us
  waiting for transfers between devices  353 us (51%)
  matrix products  100 us (15%)
  other arithmetic  78.6 us (11%)
  starting transfers between devices  49.8 us (7%)
  Pallas kernels  45.1 us (7%)
  local copies, waits for them, and re-layouts  38.3 us (6%)
  between operations  15 us (2%)
    all_gather x4, waiting for transfers between devices, gather_rows(): return lax.all_gather(rows, 'tensor', axis=0, tiled=True)  132 us
    ppermute x31, waiting for transfers between devices, exchange(): return lax.ppermute(value, axis, [(i, i ^ distance) for i in range(count)])  123 us
    reduce_scatter x2, waiting for transfers between devices, scatter_low(): lax.psum_scatter(product.astype(bf16), 'tensor', scatter_dimension=0, til...  60.9 us
    ppermute x31, starting transfers between devices, exchange(): return lax.ppermute(value, axis, [(i, i ^ distance) for i in range(count)])  42.8 us
    ppermute x2, waiting for transfers between devices, from_behind(): lax.ppermute(value, axis, [(source, source + steps) for source in range(l...  35.3 us
    dot_general x8, matrix products, times(): return jnp.dot(part.T, self.right, preferred_element_type=f32)  33.6 us
    pallas_call x1, Pallas kernels, attend_back(): pl.pallas_call(functools.partial(attend_back_kernel, tiles, chunks, group...  20.1 us
    unnamed x98, local copies, waits for them, and re-layouts  16.6 us
  transfers between devices with their start and end apart: 41, of which 23 were waited for; matrix products, arithmetic and copies ran while one was open for 22% of the time, Pallas kernels for 4%

profile of v6, /device:TPU:0, one launch (start us, length us, event | category | flops | bytes accessed | tf_op | source)
XLA Modules:
  0.0 679.5 jit_solution(9924876181489169340)
XLA Ops:
  10.5 2.5 multiply_convert_fusion.4
  18.4 3.1 fusion.44
  21.5 6.4 fusion.4.weight_ref
  27.9 51.4 %all-gather.5.cloned.1.call-done.rows_ref = bf16[1024,1536]{1,0:T(8,128)(2,1)} async-done(((bf16[256,1536]{1,0:T(8,128)(2,1)}), bf16[1024,1536]{1,0:T(8,128)(2,1)}) %all-gather.5.cloned.1.call-update) | async-done | bytes 3145744 | tf_op jit(solution)/shard_map/all_gather | solution.py:498
  79.4 7.5 %project.1 = (bf16[1024,512]{1,0:T(8,128)(2,1)}, bf16[1024,512]{1,0:T(8,128)(2,1)}) custom-call(bf16[1024,1536]{1,0:T(8,128)(2,1)} %all-gather.5.cloned.1.call-done.rows_ref, bf16[1536,1024]{1,0:T(8,128)(2,1)} %fusion.4.weight_ref, f32[1024,128]{1,0:T(8,128)} %get-tuple-element.135.cosine_ref.refs_2_, f32[1024,128]{1,0:T(8,128)} %get-tuple-element.134.sine_ref.refs_3_), custom_call_target="tpu_custom_call" | custom-call | flops 3221225472 | bytes 8388608 | tf_op jit(solution)/shard_map/project/pallas_call | solution.py:100
  86.9 4.3 collective-permute-start
  91.3 21.6 %collective-permute-done.refs_0_.refs_3_.refs_5_.refs_8_ = bf16[1024,512]{1,0:T(8,128)(2,1)} collective-permute-done((bf16[1024,512]{1,0:T(8,128)(2,1)}, bf16[1024,512]{1,0:T(8,128)(2,1)}, u32[]{:S(2)}, u32[]{:S(2)}) %collective-permute-start) | collective-permute-done | bytes 1048608 | tf_op jit(solution)/shard_map/ppermute | solution.py:32
  115.9 3.5 fusion.41
  119.4 13.1 %attend.1 = (bf16[1024,512]{1,0:T(8,128)(2,1)}, f32[2,4,1,512]{3,2,1,0:T(1,128)}) custom-call(s32[4]{0:T(128)} %and_select_fusion.low_ref, bf16[1024,512]{1,0:T(8,128)(2,1)} %get-tuple-element.53.query_ref, s32[4,1,256]{2,1,0:T(1,128)} %bitcast.28, bf16[1024,512]{1,0:T(8,128)(2,1)} %collective-permute-done.refs_0_.refs_3_.refs_5_.refs_8_, ...), custom_call_target="tpu_custom_call" | custom-call | flops 8589934592 | bytes 8388608 | tf_op jit(solution)/shard_map/attend/pallas_call | solution.py:229
  132.5 5.2 convolution_convert_fusion.1
  137.8 5.8 all-gather.7.cloned.1.call-done
  143.6 6.9 %fusion.89 = f32[1024,1024]{1,0:T(8,128)} fusion(bf16[1024,1536]{1,0:T(8,128)(2,1)} %all-gather.7.cloned.1.call-done, bf16[1024,1536]{1,0:T(8,128)(2,1)S(1)} %copy-done), kind=kOutput, calls=%fused_computation.183 | convolution fusion | flops 3221225472 | bytes 10485760 | tf_op jit(solution)/shard_map/dot_general | solution.py:561
  150.5 57.6 %reduce-scatter.5.cloned.1.call-done = bf16[256,1536]{1,0:T(8,128)(2,1)} async-done(((bf16[1024,1536]{1,0:T(8,128)(2,1)}), bf16[256,1536]{1,0:T(8,128)(2,1)}) %reduce-scatter.5.cloned.1.call-update) | async-done | bytes 786448 | tf_op jit(solution)/shard_map/reduce_scatter | solution.py:494
  212.5 4.0 constant_dynamic-update-slice_fusion.1
  218.5 57.3 %all-gather.9.cloned.1.call-done = bf16[1024,1536]{1,0:T(8,128)(2,1)} async-done(((bf16[256,1536]{1,0:T(8,128)(2,1)}), bf16[1024,1536]{1,0:T(8,128)(2,1)}) %all-gather.9.cloned.1.call-update) | async-done | bytes 3145744 | tf_op jit(solution)/shard_map/all_gather | solution.py:498
  275.7 9.8 %fusion.90 = f32[1024,2048]{1,0:T(8,128)S(1)} fusion(bf16[1024,1536]{1,0:T(8,128)(2,1)} %all-gather.9.cloned.1.call-done, bf16[1536,2048]{1,0:T(8,128)(2,1)} %constant_dynamic-update-slice_fusion), kind=kOutput, calls=%fused_computation.184 | convolution fusion | flops 6442450944 | bytes 17825792 | tf_op jit(solution)/shard_map/dot_general | solution.py:569
  285.6 3.9 multiply_convert_fusion.2
  289.5 2.4 pad_maximum_fusion
  291.9 10.0 %convolution_convert_fusion = bf16[1024,1536]{1,0:T(8,128)(2,1)} fusion(bf16[1536,2048]{1,0:T(8,128)(2,1)} %constant_dynamic-update-slice_fusion, bf16[1024,1024]{1,0:T(8,128)(2,1)S(1)} %get-tuple-element.124, bf16[1024,1024]{1,0:T(8,128)(2,1)S(1)} %get-tuple-element.123), kind=kOutput, calls=%fused_computation.9 | convolution fusion | flops 6452412416 | bytes 13631488 | tf_op jit(solution)/shard_map/dot_general | solution.py:577
  301.9 7.8 %convolution_convert_fusion.3 = bf16[768,2048]{1,0:T(8,128)(2,1)} fusion(bf16[1024,2048]{1,0:T(8,128)(2,1)} %pad_maximum_fusion, bf16[1024,1536]{1,0:T(8,128)(2,1)} %all-gather.9.cloned.1.call-done, s32[]{:T(128)S(6)} %select_n.307), kind=kOutput, calls=%fused_computation.12 | convolution fusion | flops 3222798336 | bytes 8912900 | tf_op jit(solution)/shard_map/dot_general | solution.py:432
  310.0 5.2 convolution_convert_fusion.4
  315.7 7.2 %convert_add_fusion = f32[768,2048]{1,0:T(8,128)S(1)} fusion(bf16[768,2048]{1,0:T(8,128)(2,1)} %collective-permute-done.2, bf16[1024,2048]{1,0:T(8,128)(2,1)} %pad_maximum_fusion, bf16[1024,1536]{1,0:T(8,128)(2,1)} %all-gather.9.cloned.1.call-done, s32[]{:T(128)S(6)} %select_n.295), kind=kOutput, calls=%fused_computation.2 | convolution fusion | flops 3224371200 | bytes 15204356 | tf_op jit(solution)/shard_map/dot_general | solution.py:432
  327.2 3.3 convert_add_fusion.1
  333.9 6.4 convolution_convert_fusion.2
  340.3 12.1 %collective-permute-done.5 = bf16[256,1536]{1,0:T(8,128)(2,1)} collective-permute-done((bf16[256,1536]{1,0:T(8,128)(2,1)}, bf16[256,1536]{1,0:T(8,128)(2,1)}, u32[]{:S(2)}, u32[]{:S(2)}) %collective-permute-start.5) | collective-permute-done | bytes 786464 | tf_op jit(solution)/shard_map/ppermute | solution.py:37
  352.3 3.0 convert_add_fusion.5
  355.3 5.8 collective-permute-done.3
  361.1 4.7 convert_add_fusion.2
  365.8 3.3 reduce-scatter.7.cloned.1.call-done
  373.1 2.4 dynamic-slice_convert_fusion.1
  378.6 16.1 %collective-permute-done.6 = bf16[192,2048]{1,0:T(8,128)(2,1)} collective-permute-done((bf16[192,2048]{1,0:T(8,128)(2,1)}, bf16[192,2048]{1,0:T(8,128)(2,1)}, u32[]{:S(2)}, u32[]{:S(2)}) %collective-permute-start.6) | collective-permute-done | bytes 786464 | tf_op jit(solution)/shard_map/ppermute | solution.py:37
  394.7 2.7 add_convert_fusion.1
  400.6 7.9 %collective-permute-done.9 = bf16[128,1536]{1,0:T(8,128)(2,1)S(1)} collective-permute-done((bf16[128,1536]{1,0:T(8,128)(2,1)S(1)}, bf16[128,1536]{1,0:T(8,128)(2,1)S(1)}, u32[]{:S(2)}, u32[]{:S(2)}) %collective-permute-start.9) | collective-permute-done | bytes 393248 | tf_op jit(solution)/shard_map/ppermute | solution.py:37
  409.5 6.3 collective-permute-done.7
  415.8 2.5 maximum_select_fusion.4
  418.4 17.8 %all-gather.11.cloned.1.call-done = bf16[1024,1536]{1,0:T(8,128)(2,1)} async-done(((bf16[256,1536]{1,0:T(8,128)(2,1)}), bf16[1024,1536]{1,0:T(8,128)(2,1)}) %all-gather.11.cloned.1.call-update) | async-done | bytes 3145744 | tf_op jit(solution)/shard_map/all_gather | solution.py:498
  436.2 5.1 convolution_convert_fusion.7.refs_4_
  441.8 20.1 %attend_back.1 = (bf16[1024,512]{1,0:T(8,128)(2,1)}, f32[1024,256]{1,0:T(8,128)}, f32[1024,256]{1,0:T(8,128)}, bf16[2,2,1024,256]{3,2,1,0:T(8,128)(2,1)}) custom-call(s32[4]{0:T(128)} %and_select_fusion.low_ref, s32[4]{0:T(128)} %iota.46.slot_ref, bf16[1024,512]{1,0:T(8,128)(2,1)} %get-tuple-element.53.query_ref, s32[4,1,256]{2,1,0:T(1,128)} %bitcast.29, ...), custom_call_target="tpu_custom_call" | custom-call | flops 21474836480 | bytes 16777216 | tf_op jit(solution)/shard_map/attend_back/pallas_call | solution.py:374
  464.2 14.3 %collective-permute-start.10 = (bf16[2,1024,256]{2,1,0:T(8,128)(2,1)}, bf16[2,1024,256]{2,1,0:T(8,128)(2,1)}, u32[]{:S(2)}, u32[]{:S(2)}) collective-permute-start(bf16[2,1024,256]{2,1,0:T(8,128)(2,1)} %slice_bitcast_fusion), channel_id=1, source_target_pairs={{0,4},{4,0},{8,12},{12,8},{16,20},{20,16},{24,28},{28,24},{1,5},{5... | collective-permute-start | bytes 3145736 | tf_op jit(solution)/shard_map/ppermute | solution.py:37
  482.6 2.5 bitcast_add_fusion
  487.4 15.1 %collective-permute-done.14 = bf16[256,1536]{1,0:T(8,128)(2,1)} collective-permute-done((bf16[256,1536]{1,0:T(8,128)(2,1)}, bf16[256,1536]{1,0:T(8,128)(2,1)}, u32[]{:S(2)}, u32[]{:S(2)}) %collective-permute-start.14) | collective-permute-done | bytes 786464 | tf_op jit(solution)/shard_map/ppermute | solution.py:37
  502.6 12.9 %collective-permute-done.13 = bf16[384,2048]{1,0:T(8,128)(2,1)} collective-permute-done((bf16[384,2048]{1,0:T(8,128)(2,1)S(1)}, bf16[384,2048]{1,0:T(8,128)(2,1)}, u32[]{:S(2)}, u32[]{:S(2)}) %collective-permute-start.13) | collective-permute-done | bytes 1572896 | tf_op jit(solution)/shard_map/ppermute | solution.py:37
  515.5 4.1 maximum_select_fusion
  524.0 2.7 fusion.40
  529.0 4.0 fusion.84
  533.1 3.0 convolution_add_fusion
  536.0 13.8 %collective-permute-done.11.refs_0_ = bf16[2,1024,256]{2,1,0:T(8,128)(2,1)S(1)} collective-permute-done((bf16[2,1024,256]{2,1,0:T(8,128)(2,1)}, bf16[2,1024,256]{2,1,0:T(8,128)(2,1)S(1)}, u32[]{:S(2)}, u32[]{:S(2)}) %collective-permute-start.11) | collective-permute-done | bytes 1048608 | tf_op jit(solution)/shard_map/ppermute | solution.py:32
  551.3 4.3 gather_back.1
  555.6 3.7 fusion.17
  559.6 3.6 multiply_reduce_fusion
  566.1 2.6 convolution_convert_fusion.6
  568.7 3.8 fusion.83
  572.6 4.5 fusion.1
  577.1 3.6 fusion.3
  580.8 3.8 fusion.2
  584.7 2.9 convert_add_fusion.3
  590.9 14.1 %collective-permute-done.18 = bf16[384,832]{0,1:T(8,128)(2,1)S(1)} collective-permute-done((bf16[384,832]{0,1:T(8,128)(2,1)S(1)}, bf16[384,832]{0,1:T(8,128)(2,1)S(1)}, u32[]{:S(2)}, u32[]{:S(2)}) %collective-permute-start.18) | collective-permute-done | bytes 639008 | tf_op jit(solution)/shard_map/ppermute | solution.py:37
  609.6 7.3 %collective-permute-done.19 = bf16[192,832]{0,1:T(8,128)(2,1)S(1)} collective-permute-done((bf16[192,832]{0,1:T(8,128)(2,1)S(1)}, bf16[192,832]{0,1:T(8,128)(2,1)S(1)}, u32[]{:S(2)}, u32[]{:S(2)}) %collective-permute-start.19) | collective-permute-done | bytes 319520 | tf_op jit(solution)/shard_map/ppermute | solution.py:37
  619.7 2.5 convert_add_fusion.4
  622.2 6.8 collective-permute-done.20
  635.1 10.2 %collective-permute-done.21 = bf16[384,832]{0,1:T(8,128)(2,1)S(1)} collective-permute-done((bf16[384,832]{0,1:T(8,128)(2,1)S(1)}, bf16[384,832]{0,1:T(8,128)(2,1)S(1)}, u32[]{:S(2)}, u32[]{:S(2)}) %collective-permute-start.21) | collective-permute-done | bytes 639008 | tf_op jit(solution)/shard_map/ppermute | solution.py:37
  646.5 3.1 collective-permute-done.30
  650.3 3.0 collective-permute-done.31
  668.8 3.6 subtract_add_fusion
  (231 shorter events, 92.3 us)
Async XLA Ops:
  7.2 136.5 %copy-start = (bf16[1024,1536]{1,0:T(8,128)(2,1)S(1)}, bf16[1024,1536]{1,0:T(8,128)(2,1)}, u32[]{:S(2)}) copy-start(bf16[1024,1536]{1,0:T(8,128)(2,1)} %param.22) | copy-start | bytes 9437188
  7.2 72.2 %all-gather.5.cloned.1.call-start = ((), (), s32[]{:S(2)}) async-start(), calls=%async_computation.4 | async-start | bytes 3932160 | tf_op jit(solution)/shard_map/all_gather | solution.py:498
  13.1 130.6 %all-gather.7.cloned.1.call-start = ((), (), s32[]{:S(2)}) async-start(), calls=%async_computation.6 | async-start | bytes 3932160 | tf_op jit(solution)/shard_map/all_gather | solution.py:498
  13.8 194.3 %reduce-scatter.5.cloned.1.call-start = ((), (), s32[]{:S(2)}) async-start(), calls=%async_computation.5 | async-start | bytes 3932160 | tf_op jit(solution)/shard_map/reduce_scatter | solution.py:494
  13.9 101.2 %copy-start.36 = (s32[1024]{0:T(1024)}, s32[1024]{0:T(1024)S(1)}, u32[]{:S(2)}) copy-start(s32[1024]{0:T(1024)S(1)} %get-tuple-element.137) | copy-start | bytes 12292
  86.9 25.9 %collective-permute-start = (bf16[1024,512]{1,0:T(8,128)(2,1)}, bf16[1024,512]{1,0:T(8,128)(2,1)}, u32[]{:S(2)}, u32[]{:S(2)}) collective-permute-start(bf16[1024,512]{1,0:T(8,128)(2,1)} %get-tuple-element.54.refs_2_.refs_5_.refs_7_.refs_10_), channel_id=1, source_target_pairs={{0,8},{4,12},{8,16},{12,20},{16,24},{20,28},{1,9},{5,13},{9,17},{1... | collective-permute-start | bytes 3145736 | tf_op jit(solution)/shard_map/ppermute | solution.py:32
  115.1 4.3 collective-permute-start.1
  137.7 138.0 %all-gather.9.cloned.1.call-start = ((), (), s32[]{:S(2)}) async-start(), calls=%async_computation.7 | async-start | bytes 3932160 | tf_op jit(solution)/shard_map/all_gather | solution.py:498
  150.5 60.6 %copy-start.35 = (f32[1536]{0:T(1024)S(1)}, f32[1536]{0:T(1024)}, u32[]{:S(2)}) copy-start(f32[1536]{0:T(1024)} %param.19) | copy-start | bytes 18436
  212.2 156.8 %reduce-scatter.7.cloned.1.call-start = ((), (), s32[]{:S(2)}) async-start(), calls=%async_computation.8 | async-start | bytes 3932160 | tf_op jit(solution)/shard_map/reduce_scatter | solution.py:494
  212.5 4.0 copy-start.20
  275.7 9.9 %copy-start.18 = (f32[1024,1024]{1,0:T(8,128)S(1)}, f32[1024,1024]{1,0:T(8,128)}, u32[]{:S(2)}) copy-start(f32[1024,1024]{1,0:T(8,128)} %fusion.89) | copy-start | bytes 12582916
  309.7 6.0 collective-permute-start.2
  309.7 126.4 %all-gather.11.cloned.1.call-start = ((), (), s32[]{:S(2)}) async-start(), calls=%async_computation.9 | async-start | bytes 3932160 | tf_op jit(solution)/shard_map/all_gather | solution.py:498
  315.2 10.7 %collective-permute-start.4 = (bf16[512,1536]{1,0:T(8,128)(2,1)}, bf16[512,1536]{1,0:T(8,128)(2,1)}, u32[]{:S(2)}, u32[]{:S(2)}) collective-permute-start(bf16[512,1536]{1,0:T(8,128)(2,1)} %convolution_convert_fusion.4), channel_id=1, source_target_pairs={{0,4},{4,0},{8,12},{12,8},{16,20},{20,16},{24,28},{28,24},{1,5},{5... | collective-permute-start | bytes 4718600 | tf_op jit(solution)/shard_map/ppermute | solution.py:37
  315.7 10.1 %copy-start.17 = (bf16[1024,1024]{1,0:T(8,128)(2,1)S(1)}, bf16[1024,1024]{1,0:T(8,128)(2,1)}, u32[]{:S(2)}) copy-start(bf16[1024,1024]{1,0:T(8,128)(2,1)} %get-tuple-element.61) | copy-start | bytes 6291460
  323.0 7.5 %copy-start.5 = (f32[768,2048]{1,0:T(8,128)}, f32[768,2048]{1,0:T(8,128)S(1)}, u32[]{:S(2)}) copy-start(f32[768,2048]{1,0:T(8,128)S(1)} %convert_add_fusion) | copy-start | bytes 18874372
  323.0 4.2 copy-start.9
  324.4 36.8 %collective-permute-start.3 = (bf16[384,2048]{1,0:T(8,128)(2,1)}, bf16[384,2048]{1,0:T(8,128)(2,1)}, u32[]{:S(2)}, u32[]{:S(2)}) collective-permute-start(bf16[384,2048]{1,0:T(8,128)(2,1)} %dynamic-slice_convert_fusion), channel_id=1, source_target_pairs={{0,8},{4,12},{8,0},{12,4},{16,24},{20,28},{24,16},{28,20},{1,9},{5... | collective-permute-start | bytes 4718600 | tf_op jit(solution)/shard_map/ppermute | solution.py:37
  332.4 19.9 %collective-permute-start.5 = (bf16[256,1536]{1,0:T(8,128)(2,1)}, bf16[256,1536]{1,0:T(8,128)(2,1)}, u32[]{:S(2)}, u32[]{:S(2)}) collective-permute-start(bf16[256,1536]{1,0:T(8,128)(2,1)} %dynamic-slice_convert_fusion.2), channel_id=1, source_target_pairs={{0,16},{4,20},{8,24},{12,28},{16,0},{20,4},{24,8},{28,12},{1,17},{... | collective-permute-start | bytes 2359304 | tf_op jit(solution)/shard_map/ppermute | solution.py:37
  355.3 13.8 %copy-start.4 = (f32[256,1536]{1,0:T(8,128)S(1)}, f32[256,1536]{1,0:T(8,128)}, u32[]{:S(2)}) copy-start(f32[256,1536]{1,0:T(8,128)} %copy-done.3) | copy-start | bytes 4718596
  365.8 5.0 copy-start.15
  372.6 4.4 copy-start.16
  372.7 247.1 %reduce-scatter.9.cloned.1.call-start = ((), (), s32[]{:S(2)}) async-start(), calls=%async_computation.10 | async-start | bytes 3932160 | tf_op jit(solution)/shard_map/reduce_scatter | solution.py:601
  375.5 19.2 %collective-permute-start.6 = (bf16[192,2048]{1,0:T(8,128)(2,1)}, bf16[192,2048]{1,0:T(8,128)(2,1)}, u32[]{:S(2)}, u32[]{:S(2)}) collective-permute-start(bf16[192,2048]{1,0:T(8,128)(2,1)} %dynamic-slice_convert_fusion.1), channel_id=1, source_target_pairs={{0,16},{4,20},{8,24},{12,28},{16,0},{20,4},{24,8},{28,12},{1,17},{... | collective-permute-start | bytes 2359304 | tf_op jit(solution)/shard_map/ppermute | solution.py:37
  377.0 21.9 %collective-permute-start.8 = (bf16[128,1536]{1,0:T(8,128)(2,1)S(1)}, bf16[128,1536]{1,0:T(8,128)(2,1)S(1)}, u32[]{:S(2)}, u32[]{:S(2)}) collective-permute-start(bf16[128,1536]{1,0:T(8,128)(2,1)S(1)} %dynamic-slice_convert_fusion.5), channel_id=1, source_target_pairs={{0,8},{4,12},{8,0},{12,4},{16,24},{20,28},{24,16},{28,20},{1,9},{5... | collective-permute-start | bytes 1179656 | tf_op jit(solution)/shard_map/ppermute | solution.py:37
  397.5 18.3 %collective-permute-start.7 = (bf16[192,2048]{1,0:T(8,128)(2,1)}, bf16[192,2048]{1,0:T(8,128)(2,1)}, u32[]{:S(2)}, u32[]{:S(2)}) collective-permute-start(bf16[192,2048]{1,0:T(8,128)(2,1)} %add_convert_fusion.1), channel_id=1, source_target_pairs={{0,16},{4,20},{8,24},{12,28},{16,0},{20,4},{24,8},{28,12},{1,17},{... | collective-permute-start | bytes 2359304 | tf_op jit(solution)/shard_map/ppermute | solution.py:37
  399.0 9.4 %collective-permute-start.9 = (bf16[128,1536]{1,0:T(8,128)(2,1)S(1)}, bf16[128,1536]{1,0:T(8,128)(2,1)S(1)}, u32[]{:S(2)}, u32[]{:S(2)}) collective-permute-start(bf16[128,1536]{1,0:T(8,128)(2,1)S(1)} %add_convert_fusion.2), channel_id=1, source_target_pairs={{0,8},{4,12},{8,0},{12,4},{16,24},{20,28},{24,16},{28,20},{1,9},{5... | collective-permute-start | bytes 1179656 | tf_op jit(solution)/shard_map/ppermute | solution.py:37
  441.8 38.5 %copy-start.40 = (s32[384]{0:T(512)S(1)}, s32[384]{0:T(512)}, u32[]{:S(2)}) copy-start(s32[384]{0:T(512)} %copy-done.39) | copy-start | bytes 4612
  464.2 18.4 %collective-permute-start.10 = (bf16[2,1024,256]{2,1,0:T(8,128)(2,1)}, bf16[2,1024,256]{2,1,0:T(8,128)(2,1)}, u32[]{:S(2)}, u32[]{:S(2)}) collective-permute-start(bf16[2,1024,256]{2,1,0:T(8,128)(2,1)} %slice_bitcast_fusion), channel_id=1, source_target_pairs={{0,4},{4,0},{8,12},{12,8},{16,20},{20,16},{24,28},{28,24},{1,5},{5... | collective-permute-start | bytes 3145736 | tf_op jit(solution)/shard_map/ppermute | solution.py:37
  478.5 37.0 %collective-permute-start.13 = (bf16[384,2048]{1,0:T(8,128)(2,1)S(1)}, bf16[384,2048]{1,0:T(8,128)(2,1)}, u32[]{:S(2)}, u32[]{:S(2)}) collective-permute-start(bf16[384,2048]{1,0:T(8,128)(2,1)S(1)} %maximum_select_fusion.4), channel_id=1, source_target_pairs={{0,8},{4,12},{8,0},{12,4},{16,24},{20,28},{24,16},{28,20},{1,9},{5... | collective-permute-start | bytes 4718600 | tf_op jit(solution)/shard_map/ppermute | solution.py:37
  480.3 4.8 copy-start.6
  482.5 4.3 copy-start.26
  482.5 20.1 %collective-permute-start.14 = (bf16[256,1536]{1,0:T(8,128)(2,1)}, bf16[256,1536]{1,0:T(8,128)(2,1)}, u32[]{:S(2)}, u32[]{:S(2)}) collective-permute-start(bf16[256,1536]{1,0:T(8,128)(2,1)} %maximum_select_fusion.9), channel_id=1, source_target_pairs={{0,16},{4,20},{8,24},{12,28},{16,0},{20,4},{24,8},{28,12},{1,17},{... | collective-permute-start | bytes 2359304 | tf_op jit(solution)/shard_map/ppermute | solution.py:37
  486.8 28.6 %collective-permute-start.12 = (bf16[192,1536]{1,0:T(8,128)(2,1)}, bf16[192,1536]{1,0:T(8,128)(2,1)}, u32[]{:S(2)}, u32[]{:S(2)}) collective-permute-start(bf16[192,1536]{1,0:T(8,128)(2,1)} %convolution_convert_fusion.5), channel_id=1, source_target_pairs={{0,4},{4,0},{8,12},{12,8},{16,20},{20,16},{24,28},{28,24},{1,5},{5... | collective-permute-start | bytes 1769480 | tf_op jit(solution)/shard_map/ppermute | solution.py:37
  487.4 179.9 %reduce-scatter.11.cloned.1.call-start = ((), (), s32[]{:S(2)}) async-start(), calls=%async_computation.11 | async-start | bytes 3932160 | tf_op jit(solution)/shard_map/reduce_scatter | solution.py:643
  519.6 31.4 %collective-permute-start.15 = (bf16[768,2048]{1,0:T(8,128)(2,1)}, bf16[768,2048]{1,0:T(8,128)(2,1)}, u32[]{:S(2)}, u32[]{:S(2)}) collective-permute-start(bf16[768,2048]{1,0:T(8,128)(2,1)} %maximum_select_fusion), channel_id=1, source_target_pairs={{0,4},{4,0},{8,12},{12,8},{16,20},{20,16},{24,28},{28,24},{1,5},{5... | collective-permute-start | bytes 9437192 | tf_op jit(solution)/shard_map/ppermute | solution.py:37
  521.8 27.9 %collective-permute-start.16 = (bf16[512,1536]{1,0:T(8,128)(2,1)S(1)}, bf16[512,1536]{1,0:T(8,128)(2,1)S(1)}, u32[]{:S(2)}, u32[]{:S(2)}) collective-permute-start(bf16[512,1536]{1,0:T(8,128)(2,1)S(1)} %maximum_select_fusion.5), channel_id=1, source_target_pairs={{0,4},{4,0},{8,12},{12,8},{16,20},{20,16},{24,28},{28,24},{1,5},{5... | collective-permute-start | bytes 4718600 | tf_op jit(solution)/shard_map/ppermute | solution.py:37
  522.6 27.2 %collective-permute-start.11 = (bf16[2,1024,256]{2,1,0:T(8,128)(2,1)}, bf16[2,1024,256]{2,1,0:T(8,128)(2,1)S(1)}, u32[]{:S(2)}, u32[]{:S(2)}) collective-permute-start(bf16[2,1024,256]{2,1,0:T(8,128)(2,1)} %bitcast_add_fusion), channel_id=1, source_target_pairs={{8,0},{12,4},{16,8},{20,12},{24,16},{28,20},{9,1},{13,5},{17,9},{2... | collective-permute-start | bytes 3145736 | tf_op jit(solution)/shard_map/ppermute | solution.py:32
  529.0 4.0 copy-start.7
  529.0 4.0 copy-start.27
  555.6 3.9 copy-start.33
  559.6 5.8 copy-start.32
  563.2 70.2 %collective-permute-start.28 = (f32[2,1536]{1,0:T(2,128)S(1)}, f32[2,1536]{1,0:T(2,128)S(1)}, u32[]{:S(2)}, u32[]{:S(2)}) collective-permute-start(f32[2,1536]{1,0:T(2,128)S(1)} %pad_maximum_fusion.4), channel_id=1, source_target_pairs={{0,1},{1,0},{2,3},{3,2},{4,5},{5,4},{6,7},{7,6},{8,9},{9,8},{10,11... | collective-permute-start | bytes 36872 | tf_op jit(solution)/shard_map/ppermute | solution.py:37
  564.5 25.1 %collective-permute-start.23 = (bf16[96,1536]{1,0:T(8,128)(2,1)S(1)}, bf16[96,1536]{1,0:T(8,128)(2,1)}, u32[]{:S(2)}, u32[]{:S(2)}) collective-permute-start(bf16[96,1536]{1,0:T(8,128)(2,1)S(1)} %dynamic-slice_convert_fusion.6), channel_id=1, source_target_pairs={{0,16},{4,20},{8,24},{12,28},{16,0},{20,4},{24,8},{28,12},{1,17},{... | collective-permute-start | bytes 884744 | tf_op jit(solution)/shard_map/ppermute | solution.py:37
  568.7 16.0 %collective-permute-start.17 = (bf16[768,832]{0,1:T(8,128)(2,1)}, bf16[768,832]{0,1:T(8,128)(2,1)}, u32[]{:S(2)}, u32[]{:S(2)}) collective-permute-start(bf16[768,832]{0,1:T(8,128)(2,1)} %convolution_convert_fusion.6), channel_id=1, source_target_pairs={{0,4},{4,0},{8,12},{12,8},{16,20},{20,16},{24,28},{28,24},{1,5},{5... | collective-permute-start | bytes 3833864 | tf_op jit(solution)/shard_map/ppermute | solution.py:37
  572.5 4.6 copy-start.11
  572.6 4.6 copy-start.13
  580.8 3.9 copy-start.44
  580.8 3.9 copy-start.46
  584.6 5.0 copy-start.19
  587.7 17.3 %collective-permute-start.18 = (bf16[384,832]{0,1:T(8,128)(2,1)S(1)}, bf16[384,832]{0,1:T(8,128)(2,1)S(1)}, u32[]{:S(2)}, u32[]{:S(2)}) collective-permute-start(bf16[384,832]{0,1:T(8,128)(2,1)S(1)} %dynamic-slice_convert_fusion.3), channel_id=1, source_target_pairs={{0,8},{4,12},{8,0},{12,4},{16,24},{20,28},{24,16},{28,20},{1,9},{5... | collective-permute-start | bytes 1916936 | tf_op jit(solution)/shard_map/ppermute | solution.py:37
  590.6 17.1 %collective-permute-start.24 = (bf16[48,1536]{1,0:T(8,128)(2,1)S(1)}, bf16[48,1536]{1,0:T(8,128)(2,1)S(1)}, u32[]{:S(2)}, u32[]{:S(2)}) collective-permute-start(bf16[48,1536]{1,0:T(8,128)(2,1)S(1)} %dynamic-slice_convert_fusion.7), channel_id=1, source_target_pairs={{0,8},{4,12},{8,0},{12,4},{16,24},{20,28},{24,16},{28,20},{1,9},{5... | collective-permute-start | bytes 442376 | tf_op jit(solution)/shard_map/ppermute | solution.py:37
  605.3 11.6 %collective-permute-start.19 = (bf16[192,832]{0,1:T(8,128)(2,1)S(1)}, bf16[192,832]{0,1:T(8,128)(2,1)S(1)}, u32[]{:S(2)}, u32[]{:S(2)}) collective-permute-start(bf16[192,832]{0,1:T(8,128)(2,1)S(1)} %dynamic-slice_convert_fusion.4), channel_id=1, source_target_pairs={{0,16},{4,20},{8,24},{12,28},{16,0},{20,4},{24,8},{28,12},{1,17},{... | collective-permute-start | bytes 958472 | tf_op jit(solution)/shard_map/ppermute | solution.py:37
  607.8 24.0 %collective-permute-start.25 = (bf16[48,1536]{1,0:T(8,128)(2,1)S(1)}, bf16[48,1536]{1,0:T(8,128)(2,1)S(1)}, u32[]{:S(2)}, u32[]{:S(2)}) collective-permute-start(bf16[48,1536]{1,0:T(8,128)(2,1)S(1)} %add_convert_fusion.3), channel_id=1, source_target_pairs={{0,8},{4,12},{8,0},{12,4},{16,24},{20,28},{24,16},{28,20},{1,9},{5... | collective-permute-start | bytes 442376 | tf_op jit(solution)/shard_map/ppermute | solution.py:37
  618.0 11.0 %collective-permute-start.20 = (bf16[192,832]{0,1:T(8,128)(2,1)}, bf16[192,832]{0,1:T(8,128)(2,1)S(1)}, u32[]{:S(2)}, u32[]{:S(2)}) collective-permute-start(bf16[192,832]{0,1:T(8,128)(2,1)} %convert_add_fusion.8), channel_id=1, source_target_pairs={{0,16},{4,20},{8,24},{12,28},{16,0},{20,4},{24,8},{28,12},{1,17},{... | collective-permute-start | bytes 958472 | tf_op jit(solution)/shard_map/ppermute | solution.py:37
  630.7 14.7 %collective-permute-start.21 = (bf16[384,832]{0,1:T(8,128)(2,1)S(1)}, bf16[384,832]{0,1:T(8,128)(2,1)S(1)}, u32[]{:S(2)}, u32[]{:S(2)}) collective-permute-start(bf16[384,832]{0,1:T(8,128)(2,1)S(1)} %maximum_select_fusion.10), channel_id=1, source_target_pairs={{0,8},{4,12},{8,0},{12,4},{16,24},{20,28},{24,16},{28,20},{1,9},{5... | collective-permute-start | bytes 1916936 | tf_op jit(solution)/shard_map/ppermute | solution.py:37
  631.9 13.8 %collective-permute-start.26 = (bf16[96,1536]{1,0:T(8,128)(2,1)S(1)}, bf16[96,1536]{1,0:T(8,128)(2,1)S(1)}, u32[]{:S(2)}, u32[]{:S(2)}) collective-permute-start(bf16[96,1536]{1,0:T(8,128)(2,1)S(1)} %maximum_select_fusion.14), channel_id=1, source_target_pairs={{0,16},{4,20},{8,24},{12,28},{16,0},{20,4},{24,8},{28,12},{1,17},{... | collective-permute-start | bytes 884744 | tf_op jit(solution)/shard_map/ppermute | solution.py:37
  633.5 12.9 %collective-permute-start.29 = (f32[2,1536]{1,0:T(2,128)S(1)}, f32[2,1536]{1,0:T(2,128)S(1)}, u32[]{:S(2)}, u32[]{:S(2)}) collective-permute-start(f32[2,1536]{1,0:T(2,128)S(1)} %fusion.80), channel_id=1, source_target_pairs={{0,2},{1,3},{2,0},{3,1},{4,6},{5,7},{6,4},{7,5},{8,10},{9,11},{10,... | collective-permute-start | bytes 36872 | tf_op jit(solution)/shard_map/ppermute | solution.py:37
  645.6 14.6 %collective-permute-start.22 = (bf16[768,832]{0,1:T(8,128)(2,1)S(1)}, bf16[768,832]{0,1:T(8,128)(2,1)S(1)}, u32[]{:S(2)}, u32[]{:S(2)}) collective-permute-start(bf16[768,832]{0,1:T(8,128)(2,1)S(1)} %maximum_select_fusion.6), channel_id=1, source_target_pairs={{0,4},{4,0},{8,12},{12,8},{16,20},{20,16},{24,28},{28,24},{1,5},{5... | collective-permute-start | bytes 3833864 | tf_op jit(solution)/shard_map/ppermute | solution.py:37
  645.8 11.9 %collective-permute-start.27 = (bf16[192,1536]{1,0:T(8,128)(2,1)S(1)}, bf16[192,1536]{1,0:T(8,128)(2,1)S(1)}, u32[]{:S(2)}, u32[]{:S(2)}) collective-permute-start(bf16[192,1536]{1,0:T(8,128)(2,1)S(1)} %maximum_select_fusion.13), channel_id=1, source_target_pairs={{0,4},{4,0},{8,12},{12,8},{16,20},{20,16},{24,28},{28,24},{1,5},{5... | collective-permute-start | bytes 1769480 | tf_op jit(solution)/shard_map/ppermute | solution.py:37
  646.4 3.1 collective-permute-start.30
  649.6 3.8 collective-permute-start.31
  653.3 3.8 collective-permute-start.32
  (24 other events, 62.9 us)
Sparse Core Ops, SparseCore 0:
  13.2 66.1 all-gather.4
  81.5 62.0 all-gather.6
  146.5 61.5 reduce-scatter.4
  212.4 63.3 all-gather.8
  309.9 59.1 reduce-scatter.6
  372.8 63.3 all-gather.10
  487.5 58.2 reduce-scatter.8
  572.7 61.4 reduce-scatter.10

commit v7 on v6

--- a/solution.py
+++ b/solution.py
@@ -480,16 +480,6 @@
         ]
 
 
-def sum_everywhere(value, axes):
-    for axis in axes:
-        count = lax.axis_size(axis)
-        place = 1
-        while place < count:
-            value = value + exchange(value, axis, place)
-            place *= 2
-    return value
-
-
 def scatter_low(product):
     return lax.psum_scatter(product.astype(bf16), "tensor", scatter_dimension=0, tiled=True)
 
@@ -595,8 +585,8 @@
     for shared in wide:
         for _ in range(len(places) - 1):
             shared.step()
-    residual_low, down_product, pair_shared.value, down_shared.value = tied(
-        (residual_low, down_product, pair_shared.value, down_shared.value)
+    residual_low, down_product, pair_shared.value, down_shared.value, attended_plain = tied(
+        (residual_low, down_product, pair_shared.value, down_shared.value, attended_plain)
     )
     block_scattered = lax.psum_scatter(
         down_product, "tensor", scatter_dimension=0, tiled=True
@@ -620,7 +610,8 @@
         crossing = exchange(earlier[0], "dp", 1)
         both_back = earlier[1] + jnp.where(odd, crossing, 0)
         both_back, crossing, attended_plain = tied((both_back, crossing, attended_plain))
-        received = [from_behind(both_back, "dp", -2), jnp.where(odd, 0, crossing)]
+        both_received = from_behind(both_back, "dp", -2)
+        received = [both_received, jnp.where(odd, 0, crossing)]
     else:
         earlier, attended_plain = tied((earlier, attended_plain))
         received = [from_behind(earlier[d - 1], "dp", -d) for d in range(1, reach + 1)]
@@ -629,8 +620,11 @@
     for shared in wide:
         shared.end_up()
         shared.begin_up()
-    received, pair_shared.got, down_shared.got, out_shared.value = tied(
-        (received, pair_shared.got, down_shared.got, out_shared.value)
+    query_plain = jnp.dot(query_grad, query_spread.T, preferred_element_type=bf16)
+    query_shared = SharedProduct(attention_normed, query_plain, "dp", places)
+    query_shared.meet()
+    received, pair_shared.got, down_shared.got, out_shared.value, query_shared.value = tied(
+        (received, pair_shared.got, down_shared.got, out_shared.value, query_shared.value)
     )
     key_value_grad = gather_back(
         key_own, value_own, received, cosine, sine, kv_heads, stretch, rows
@@ -641,31 +635,6 @@
         + jnp.dot(key_value_grad, w_joined[:, split:].T, preferred_element_type=f32)
     ).astype(bf16)
     attn_scattered = lax.psum_scatter(attn_normed_part, "tensor", scatter_dimension=0, tiled=True)
-    query_plain = jnp.dot(query_grad, query_spread.T, preferred_element_type=bf16)
-    kv_plain = jnp.dot(key_value_grad, kv_spread.T, preferred_element_type=bf16)
-    joined_shared = SharedProduct(
-        attention_normed, jnp.concatenate([query_plain, kv_plain], axis=1), "dp", places
-    )
-    joined_shared.meet()
-    grad_gate, grad_up = pair_shared.finish((0, width), (width, 2 * width))
-    (grad_down,) = down_shared.finish((0, out_grad.shape[1]))
-    joined_shared.step()
-    joined_shared.value, grad_down = tied((joined_shared.value, grad_down))
-    joined_shared.step()
-    joined_shared.value, grad_gate = tied((joined_shared.value, grad_gate))
-    joined_shared.step()
-    joined_shared.value, grad_up, block_output = tied(
-        (joined_shared.value, grad_up, block_output)
-    )
-    query_width = w_query.shape[1]
-    kv_width = key_weight.shape[1]
-    value_from = query_width + kv_width + gap
-    grad_query, grad_key, grad_value = joined_shared.finish(
-        (0, query_width),
-        (query_width, query_width + kv_width),
-        (value_from, value_from + kv_width),
-    )
-    (grad_out,) = out_shared.finish((0, out_grad.shape[1]))
     attn_gain_part = (
         jnp.sum(
             attn_normed_part.astype(f32) * attention_normed.astype(f32), axis=0, keepdims=True
@@ -673,11 +642,38 @@
         / attn_gain
     )
     mlp_gain_part = jnp.sum(mlp_normed_grad * residual * inv_rms_mlp, axis=0, keepdims=True)
-    gains = sum_everywhere(
-        jnp.concatenate([attn_gain_part, mlp_gain_part], axis=0), ("tensor", "dp")
-    )
+    gains = jnp.concatenate([attn_gain_part, mlp_gain_part], axis=0)
+    rounds = [
+        (axis, 1 << place)
+        for axis in ("tensor", "dp")
+        for place in range((lax.axis_size(axis) - 1).bit_length())
+    ]
+    kv_plain = jnp.dot(key_value_grad, kv_spread.T, preferred_element_type=bf16)
+    kv_shared = SharedProduct(attention_normed, kv_plain, "dp", crossed)
+    kv_shared.meet()
+    grad_gate, grad_up = pair_shared.finish((0, width), (width, 2 * width))
+    (grad_down,) = down_shared.finish((0, out_grad.shape[1]))
+    outputs = [grad_down, grad_gate, grad_up, block_output]
+    for place in range(len(outputs)):
+        query_shared.step()
+        kv_shared.step()
+        if rounds:
+            axis, distance = rounds.pop(0)
+            gains = gains + exchange(gains, axis, distance)
+        kv_shared.value, query_shared.value, gains, outputs[place] = tied(
+            (kv_shared.value, query_shared.value, gains, outputs[place])
+        )
+    grad_down, grad_gate, grad_up, block_output = outputs
+    for axis, distance in rounds:
+        gains = gains + exchange(gains, axis, distance)
     grad_attn_gain, grad_mlp_gain = gains[0], gains[1]
-
+    query_width = w_query.shape[1]
+    kv_width = key_weight.shape[1]
+    (grad_query,) = query_shared.finish((0, query_width))
+    grad_key, grad_value = kv_shared.finish(
+        (0, kv_width), (kv_width + gap, 2 * kv_width + gap)
+    )
+    (grad_out,) = out_shared.finish((0, out_grad.shape[1]))
     attn_normed_grad = attn_scattered.astype(f32)
     input_part = normalize_back(block_input, inv_rms_attn, attn_gain, attn_normed_grad)
     input_grad = residual_grad + input_part

time: 688 us -> 667 us (0.969)
  waiting for transfers between devices: 353 us -> 329 us
    ppermute x31 -> x37, waiting for transfers between devices: 123 us -> 99.2 us  [exchange(): return lax.ppermute(value, axis, [(i, i ^ distance) for i in range(count)])]
    dot_general x8 -> x10, matrix products: 33.6 us -> 37.1 us  [times(): return jnp.dot(part.T, self.right, preferred_element_type=f32)]
    ppermute x31 -> x37, starting transfers between devices: 42.8 us -> 45.8 us  [exchange(): return lax.ppermute(value, axis, [(i, i ^ distance) for i in range(count)])]
    unnamed x98 -> x97, local copies, waits for them, and re-layouts: 16.6 us -> 14.8 us
  transfers between devices with their start and end apart: 41 -> 47, of which waited for: 23 -> 25; matrix products, arithmetic and copies ran while one was open for 22% -> 22% of each run, Pallas kernels for 4% -> 4%
where the time goes in v7:
time: 667 us; the launch traced here: 658 us
  waiting for transfers between devices  329 us (49%)
  matrix products  102 us (15%)
  other arithmetic  78.2 us (12%)
  starting transfers between devices  52.9 us (8%)
  Pallas kernels  45 us (7%)
  local copies, waits for them, and re-layouts  35.5 us (5%)
  between operations  15.1 us (2%)
    all_gather x4, waiting for transfers between devices, gather_rows(): return lax.all_gather(rows, 'tensor', axis=0, tiled=True)  132 us
    ppermute x37, waiting for transfers between devices, exchange(): return lax.ppermute(value, axis, [(i, i ^ distance) for i in range(count)])  99.2 us
    reduce_scatter x2, waiting for transfers between devices, scatter_low(): lax.psum_scatter(product.astype(bf16), 'tensor', scatter_dimension=0, til...  60.9 us
    ppermute x37, starting transfers between devices, exchange(): return lax.ppermute(value, axis, [(i, i ^ distance) for i in range(count)])  45.8 us
    dot_general x10, matrix products, times(): return jnp.dot(part.T, self.right, preferred_element_type=f32)  37.1 us
    ppermute x2, waiting for transfers between devices, from_behind(): lax.ppermute(value, axis, [(source, source + steps) for source in range(l...  36.1 us
    pallas_call x1, Pallas kernels, attend_back(): pl.pallas_call(functools.partial(attend_back_kernel, tiles, chunks, group...  19.9 us
    convert_element_type x7, other arithmetic, finish(): self.joined(self.value[:, a:b], self.got[:, a:b]).astype(f32)  17.2 us
  transfers between devices with their start and end apart: 47, of which 25 were waited for; matrix products, arithmetic and copies ran while one was open for 22% of the time, Pallas kernels for 4%

profile of v7, /device:TPU:0, one launch (start us, length us, event | category | flops | bytes accessed | tf_op | source)
XLA Modules:
  0.0 658.2 jit_solution(11726669097161524520)
XLA Ops:
  10.6 2.5 multiply_convert_fusion.4
  18.5 3.1 fusion.53
  21.6 6.4 fusion.4.weight_ref
  28.0 51.5 %all-gather.5.cloned.1.call-done.rows_ref = bf16[1024,1536]{1,0:T(8,128)(2,1)} async-done(((bf16[256,1536]{1,0:T(8,128)(2,1)}), bf16[1024,1536]{1,0:T(8,128)(2,1)}) %all-gather.5.cloned.1.call-update) | async-done | bytes 3145744 | tf_op jit(solution)/shard_map/all_gather | solution.py:488
  79.4 7.5 %project.1 = (bf16[1024,512]{1,0:T(8,128)(2,1)}, bf16[1024,512]{1,0:T(8,128)(2,1)}) custom-call(bf16[1024,1536]{1,0:T(8,128)(2,1)} %all-gather.5.cloned.1.call-done.rows_ref, bf16[1536,1024]{1,0:T(8,128)(2,1)} %fusion.4.weight_ref, f32[1024,128]{1,0:T(8,128)} %get-tuple-element.135.cosine_ref.refs_2_, f32[1024,128]{1,0:T(8,128)} %get-tuple-element.134.sine_ref.refs_3_), custom_call_target="tpu_custom_call" | custom-call | flops 3221225472 | bytes 8388608 | tf_op jit(solution)/shard_map/project/pallas_call | solution.py:100
  87.0 4.3 collective-permute-start
  91.3 21.6 %collective-permute-done.refs_0_.refs_3_.refs_5_.refs_8_ = bf16[1024,512]{1,0:T(8,128)(2,1)} collective-permute-done((bf16[1024,512]{1,0:T(8,128)(2,1)}, bf16[1024,512]{1,0:T(8,128)(2,1)}, u32[]{:S(2)}, u32[]{:S(2)}) %collective-permute-start) | collective-permute-done | bytes 1048608 | tf_op jit(solution)/shard_map/ppermute | solution.py:32
  112.9 2.3 broadcast_select_fusion.1
  115.9 3.5 fusion.50
  119.4 13.2 %attend.1 = (bf16[1024,512]{1,0:T(8,128)(2,1)}, f32[2,4,1,512]{3,2,1,0:T(1,128)}) custom-call(s32[4]{0:T(128)} %and_select_fusion.low_ref, bf16[1024,512]{1,0:T(8,128)(2,1)} %get-tuple-element.64.query_ref, s32[4,1,256]{2,1,0:T(1,128)} %bitcast.32, bf16[1024,512]{1,0:T(8,128)(2,1)} %collective-permute-done.refs_0_.refs_3_.refs_5_.refs_8_, ...), custom_call_target="tpu_custom_call" | custom-call | flops 8589934592 | bytes 8388608 | tf_op jit(solution)/shard_map/attend/pallas_call | solution.py:229
  132.6 5.2 convolution_convert_fusion.1
  137.9 5.8 all-gather.7.cloned.1.call-done
  143.7 6.9 %fusion.102 = f32[1024,1024]{1,0:T(8,128)} fusion(bf16[1024,1536]{1,0:T(8,128)(2,1)} %all-gather.7.cloned.1.call-done, bf16[1024,1536]{1,0:T(8,128)(2,1)S(1)} %copy-done), kind=kOutput, calls=%fused_computation.195 | convolution fusion | flops 3221225472 | bytes 10485760 | tf_op jit(solution)/shard_map/dot_general | solution.py:551
  150.5 57.6 %reduce-scatter.5.cloned.1.call-done = bf16[256,1536]{1,0:T(8,128)(2,1)} async-done(((bf16[1024,1536]{1,0:T(8,128)(2,1)}), bf16[256,1536]{1,0:T(8,128)(2,1)}) %reduce-scatter.5.cloned.1.call-update) | async-done | bytes 786448 | tf_op jit(solution)/shard_map/reduce_scatter | solution.py:484
  212.6 4.0 constant_dynamic-update-slice_fusion.1
  218.5 57.3 %all-gather.9.cloned.1.call-done = bf16[1024,1536]{1,0:T(8,128)(2,1)} async-done(((bf16[256,1536]{1,0:T(8,128)(2,1)}), bf16[1024,1536]{1,0:T(8,128)(2,1)}) %all-gather.9.cloned.1.call-update) | async-done | bytes 3145744 | tf_op jit(solution)/shard_map/all_gather | solution.py:488
  275.8 9.8 %fusion.103 = f32[1024,2048]{1,0:T(8,128)S(1)} fusion(bf16[1024,1536]{1,0:T(8,128)(2,1)} %all-gather.9.cloned.1.call-done, bf16[1536,2048]{1,0:T(8,128)(2,1)} %constant_dynamic-update-slice_fusion), kind=kOutput, calls=%fused_computation.196 | convolution fusion | flops 6442450944 | bytes 17825792 | tf_op jit(solution)/shard_map/dot_general | solution.py:559
  285.7 3.9 multiply_convert_fusion.2
  289.6 2.4 pad_maximum_fusion
  292.0 10.0 %convolution_convert_fusion = bf16[1024,1536]{1,0:T(8,128)(2,1)} fusion(bf16[1536,2048]{1,0:T(8,128)(2,1)} %constant_dynamic-update-slice_fusion, bf16[1024,1024]{1,0:T(8,128)(2,1)S(1)} %get-tuple-element.124, bf16[1024,1024]{1,0:T(8,128)(2,1)S(1)} %get-tuple-element.123), kind=kOutput, calls=%fused_computation.9 | convolution fusion | flops 6452412416 | bytes 13631488 | tf_op jit(solution)/shard_map/dot_general | solution.py:567
  302.0 7.8 %convolution_convert_fusion.3 = bf16[768,2048]{1,0:T(8,128)(2,1)} fusion(bf16[1024,2048]{1,0:T(8,128)(2,1)} %pad_maximum_fusion, bf16[1024,1536]{1,0:T(8,128)(2,1)} %all-gather.9.cloned.1.call-done, s32[]{:T(128)S(6)} %select_n.338), kind=kOutput, calls=%fused_computation.12 | convolution fusion | flops 3222798336 | bytes 8912900 | tf_op jit(solution)/shard_map/dot_general | solution.py:432
  310.1 5.2 convolution_convert_fusion.4
  315.8 7.2 %convert_add_fusion = f32[768,2048]{1,0:T(8,128)S(1)} fusion(bf16[768,2048]{1,0:T(8,128)(2,1)} %collective-permute-done.2, bf16[1024,2048]{1,0:T(8,128)(2,1)} %pad_maximum_fusion, bf16[1024,1536]{1,0:T(8,128)(2,1)} %all-gather.9.cloned.1.call-done, s32[]{:T(128)S(6)} %select_n.326), kind=kOutput, calls=%fused_computation.2 | convolution fusion | flops 3224371200 | bytes 15204356 | tf_op jit(solution)/shard_map/dot_general | solution.py:432
  327.2 3.3 convert_add_fusion.1
  333.9 6.4 convolution_convert_fusion.2
  340.3 12.1 %collective-permute-done.5 = bf16[256,1536]{1,0:T(8,128)(2,1)} collective-permute-done((bf16[256,1536]{1,0:T(8,128)(2,1)}, bf16[256,1536]{1,0:T(8,128)(2,1)}, u32[]{:S(2)}, u32[]{:S(2)}) %collective-permute-start.5) | collective-permute-done | bytes 786464 | tf_op jit(solution)/shard_map/ppermute | solution.py:37
  352.4 3.0 convert_add_fusion.4
  355.4 5.8 collective-permute-done.3
  361.2 4.7 convert_add_fusion.2
  365.8 3.3 reduce-scatter.7.cloned.1.call-done
  373.2 2.4 dynamic-slice_convert_fusion.1
  378.6 16.2 %collective-permute-done.6 = bf16[192,2048]{1,0:T(8,128)(2,1)} collective-permute-done((bf16[192,2048]{1,0:T(8,128)(2,1)}, bf16[192,2048]{1,0:T(8,128)(2,1)}, u32[]{:S(2)}, u32[]{:S(2)}) %collective-permute-start.6) | collective-permute-done | bytes 786464 | tf_op jit(solution)/shard_map/ppermute | solution.py:37
  394.8 2.7 add_convert_fusion.1
  400.6 3.0 fusion.49
  403.6 4.9 collective-permute-done.9
  409.5 6.3 collective-permute-done.7
  415.9 2.7 maximum_select_fusion.4
  418.6 17.6 %all-gather.11.cloned.1.call-done = bf16[1024,1536]{1,0:T(8,128)(2,1)} async-done(((bf16[256,1536]{1,0:T(8,128)(2,1)}), bf16[1024,1536]{1,0:T(8,128)(2,1)}) %all-gather.11.cloned.1.call-update) | async-done | bytes 3145744 | tf_op jit(solution)/shard_map/all_gather | solution.py:488
  436.2 5.1 convolution_convert_fusion.6.refs_4_
  441.9 19.9 %attend_back.1 = (bf16[1024,512]{1,0:T(8,128)(2,1)}, f32[1024,256]{1,0:T(8,128)}, f32[1024,256]{1,0:T(8,128)}, bf16[2,2,1024,256]{3,2,1,0:T(8,128)(2,1)}) custom-call(s32[4]{0:T(128)} %and_select_fusion.low_ref, s32[4]{0:T(128)} %iota.46.slot_ref, bf16[1024,512]{1,0:T(8,128)(2,1)} %get-tuple-element.64.query_ref, s32[4,1,256]{2,1,0:T(1,128)} %bitcast.33, ...), custom_call_target="tpu_custom_call" | custom-call | flops 21474836480 | bytes 16777216 | tf_op jit(solution)/shard_map/attend_back/pallas_call | solution.py:374
  464.1 14.3 %collective-permute-start.10 = (bf16[2,1024,256]{2,1,0:T(8,128)(2,1)}, bf16[2,1024,256]{2,1,0:T(8,128)(2,1)}, u32[]{:S(2)}, u32[]{:S(2)}) collective-permute-start(bf16[2,1024,256]{2,1,0:T(8,128)(2,1)} %slice_bitcast_fusion), channel_id=1, source_target_pairs={{0,4},{4,0},{8,12},{12,8},{16,20},{20,16},{24,28},{28,24},{1,5},{5... | collective-permute-start | bytes 3145736 | tf_op jit(solution)/shard_map/ppermute | solution.py:37
  481.1 2.4 bitcast_add_fusion
  486.2 13.9 %collective-permute-done.14 = bf16[256,1536]{1,0:T(8,128)(2,1)S(1)} collective-permute-done((bf16[256,1536]{1,0:T(8,128)(2,1)}, bf16[256,1536]{1,0:T(8,128)(2,1)S(1)}, u32[]{:S(2)}, u32[]{:S(2)}) %collective-permute-start.14) | collective-permute-done | bytes 786464 | tf_op jit(solution)/shard_map/ppermute | solution.py:37
  500.1 15.3 %collective-permute-done.13 = bf16[384,2048]{1,0:T(8,128)(2,1)} collective-permute-done((bf16[384,2048]{1,0:T(8,128)(2,1)S(1)}, bf16[384,2048]{1,0:T(8,128)(2,1)}, u32[]{:S(2)}, u32[]{:S(2)}) %collective-permute-start.13) | collective-permute-done | bytes 1572896 | tf_op jit(solution)/shard_map/ppermute | solution.py:37
  515.4 4.2 maximum_select_fusion
  521.6 2.6 fusion.37
  531.6 3.5 fusion.97
  535.1 3.0 convolution_add_fusion
  538.1 14.6 %collective-permute-done.11.refs_0_ = bf16[2,1024,256]{2,1,0:T(8,128)(2,1)S(1)} collective-permute-done((bf16[2,1024,256]{2,1,0:T(8,128)(2,1)S(1)}, bf16[2,1024,256]{2,1,0:T(8,128)(2,1)S(1)}, u32[]{:S(2)}, u32[]{:S(2)}) %collective-permute-start.11) | collective-permute-done | bytes 1048608 | tf_op jit(solution)/shard_map/ppermute | solution.py:32
  554.2 4.4 gather_back.1
  558.6 3.7 fusion.17
  562.5 3.7 multiply_reduce_fusion
  567.4 2.7 collective-permute-start.20
  574.4 3.5 fusion.96
  577.9 3.1 fusion.1
  580.9 3.5 fusion.2
  593.6 6.5 collective-permute-done.19
  605.9 3.6 collective-permute-done.24
  613.9 3.7 fusion.3
  624.0 2.5 convert_add_fusion.3
  626.4 5.0 collective-permute-done.29
  634.5 3.0 fusion.41
  638.3 3.0 collective-permute-done.38
  647.5 3.6 subtract_add_fusion
  (248 shorter events, 95.6 us)
Async XLA Ops:
  7.2 136.5 %copy-start = (bf16[1024,1536]{1,0:T(8,128)(2,1)S(1)}, bf16[1024,1536]{1,0:T(8,128)(2,1)}, u32[]{:S(2)}) copy-start(bf16[1024,1536]{1,0:T(8,128)(2,1)} %param.22) | copy-start | bytes 9437188
  7.2 72.2 %all-gather.5.cloned.1.call-start = ((), (), s32[]{:S(2)}) async-start(), calls=%async_computation.4 | async-start | bytes 3932160 | tf_op jit(solution)/shard_map/all_gather | solution.py:488
  13.1 130.6 %all-gather.7.cloned.1.call-start = ((), (), s32[]{:S(2)}) async-start(), calls=%async_computation.6 | async-start | bytes 3932160 | tf_op jit(solution)/shard_map/all_gather | solution.py:488
  13.9 194.3 %reduce-scatter.5.cloned.1.call-start = ((), (), s32[]{:S(2)}) async-start(), calls=%async_computation.5 | async-start | bytes 3932160 | tf_op jit(solution)/shard_map/reduce_scatter | solution.py:484
  14.0 101.2 %copy-start.39 = (s32[1024]{0:T(1024)}, s32[1024]{0:T(1024)S(1)}, u32[]{:S(2)}) copy-start(s32[1024]{0:T(1024)S(1)} %get-tuple-element.137) | copy-start | bytes 12292
  87.0 25.9 %collective-permute-start = (bf16[1024,512]{1,0:T(8,128)(2,1)}, bf16[1024,512]{1,0:T(8,128)(2,1)}, u32[]{:S(2)}, u32[]{:S(2)}) collective-permute-start(bf16[1024,512]{1,0:T(8,128)(2,1)} %get-tuple-element.65.refs_2_.refs_5_.refs_7_.refs_10_), channel_id=1, source_target_pairs={{0,8},{4,12},{8,16},{12,20},{16,24},{20,28},{1,9},{5,13},{9,17},{1... | collective-permute-start | bytes 3145736 | tf_op jit(solution)/shard_map/ppermute | solution.py:32
  115.2 4.3 collective-permute-start.1
  137.8 138.0 %all-gather.9.cloned.1.call-start = ((), (), s32[]{:S(2)}) async-start(), calls=%async_computation.7 | async-start | bytes 3932160 | tf_op jit(solution)/shard_map/all_gather | solution.py:488
  150.5 60.7 %copy-start.38 = (f32[1536]{0:T(1024)S(1)}, f32[1536]{0:T(1024)}, u32[]{:S(2)}) copy-start(f32[1536]{0:T(1024)} %param.19) | copy-start | bytes 18436
  212.3 156.8 %reduce-scatter.7.cloned.1.call-start = ((), (), s32[]{:S(2)}) async-start(), calls=%async_computation.8 | async-start | bytes 3932160 | tf_op jit(solution)/shard_map/reduce_scatter | solution.py:484
  212.5 4.0 copy-start.19
  275.8 9.9 %copy-start.18 = (f32[1024,1024]{1,0:T(8,128)S(1)}, f32[1024,1024]{1,0:T(8,128)}, u32[]{:S(2)}) copy-start(f32[1024,1024]{1,0:T(8,128)} %fusion.102) | copy-start | bytes 12582916
  309.8 6.0 collective-permute-start.2
  309.8 126.4 %all-gather.11.cloned.1.call-start = ((), (), s32[]{:S(2)}) async-start(), calls=%async_computation.9 | async-start | bytes 3932160 | tf_op jit(solution)/shard_map/all_gather | solution.py:488
  315.3 10.6 %collective-permute-start.4 = (bf16[512,1536]{1,0:T(8,128)(2,1)}, bf16[512,1536]{1,0:T(8,128)(2,1)}, u32[]{:S(2)}, u32[]{:S(2)}) collective-permute-start(bf16[512,1536]{1,0:T(8,128)(2,1)} %convolution_convert_fusion.4), channel_id=1, source_target_pairs={{0,4},{4,0},{8,12},{12,8},{16,20},{20,16},{24,28},{28,24},{1,5},{5... | collective-permute-start | bytes 4718600 | tf_op jit(solution)/shard_map/ppermute | solution.py:37
  315.8 10.1 %copy-start.17 = (bf16[1024,1024]{1,0:T(8,128)(2,1)S(1)}, bf16[1024,1024]{1,0:T(8,128)(2,1)}, u32[]{:S(2)}) copy-start(bf16[1024,1024]{1,0:T(8,128)(2,1)} %get-tuple-element.72) | copy-start | bytes 6291460
  323.0 7.5 %copy-start.5 = (f32[768,2048]{1,0:T(8,128)}, f32[768,2048]{1,0:T(8,128)S(1)}, u32[]{:S(2)}) copy-start(f32[768,2048]{1,0:T(8,128)S(1)} %convert_add_fusion) | copy-start | bytes 18874372
  323.0 4.2 copy-start.9
  324.4 36.8 %collective-permute-start.3 = (bf16[384,2048]{1,0:T(8,128)(2,1)}, bf16[384,2048]{1,0:T(8,128)(2,1)}, u32[]{:S(2)}, u32[]{:S(2)}) collective-permute-start(bf16[384,2048]{1,0:T(8,128)(2,1)} %dynamic-slice_convert_fusion), channel_id=1, source_target_pairs={{0,8},{4,12},{8,0},{12,4},{16,24},{20,28},{24,16},{28,20},{1,9},{5... | collective-permute-start | bytes 4718600 | tf_op jit(solution)/shard_map/ppermute | solution.py:37
  332.4 19.9 %collective-permute-start.5 = (bf16[256,1536]{1,0:T(8,128)(2,1)}, bf16[256,1536]{1,0:T(8,128)(2,1)}, u32[]{:S(2)}, u32[]{:S(2)}) collective-permute-start(bf16[256,1536]{1,0:T(8,128)(2,1)} %dynamic-slice_convert_fusion.2), channel_id=1, source_target_pairs={{0,16},{4,20},{8,24},{12,28},{16,0},{20,4},{24,8},{28,12},{1,17},{... | collective-permute-start | bytes 2359304 | tf_op jit(solution)/shard_map/ppermute | solution.py:37
  355.4 13.8 %copy-start.4 = (f32[256,1536]{1,0:T(8,128)S(1)}, f32[256,1536]{1,0:T(8,128)}, u32[]{:S(2)}) copy-start(f32[256,1536]{1,0:T(8,128)} %copy-done.3) | copy-start | bytes 4718596
  365.8 5.0 copy-start.15
  372.7 4.4 copy-start.16
  372.7 251.2 %reduce-scatter.9.cloned.1.call-start = ((), (), s32[]{:S(2)}) async-start(), calls=%async_computation.10 | async-start | bytes 3932160 | tf_op jit(solution)/shard_map/reduce_scatter | solution.py:591
  375.6 19.2 %collective-permute-start.6 = (bf16[192,2048]{1,0:T(8,128)(2,1)}, bf16[192,2048]{1,0:T(8,128)(2,1)}, u32[]{:S(2)}, u32[]{:S(2)}) collective-permute-start(bf16[192,2048]{1,0:T(8,128)(2,1)} %dynamic-slice_convert_fusion.1), channel_id=1, source_target_pairs={{0,16},{4,20},{8,24},{12,28},{16,0},{20,4},{24,8},{28,12},{1,17},{... | collective-permute-start | bytes 2359304 | tf_op jit(solution)/shard_map/ppermute | solution.py:37
  377.1 21.9 %collective-permute-start.8 = (bf16[128,1536]{1,0:T(8,128)(2,1)S(1)}, bf16[128,1536]{1,0:T(8,128)(2,1)S(1)}, u32[]{:S(2)}, u32[]{:S(2)}) collective-permute-start(bf16[128,1536]{1,0:T(8,128)(2,1)S(1)} %dynamic-slice_convert_fusion.3), channel_id=1, source_target_pairs={{0,8},{4,12},{8,0},{12,4},{16,24},{20,28},{24,16},{28,20},{1,9},{5... | collective-permute-start | bytes 1179656 | tf_op jit(solution)/shard_map/ppermute | solution.py:37
  397.5 18.3 %collective-permute-start.7 = (bf16[192,2048]{1,0:T(8,128)(2,1)}, bf16[192,2048]{1,0:T(8,128)(2,1)}, u32[]{:S(2)}, u32[]{:S(2)}) collective-permute-start(bf16[192,2048]{1,0:T(8,128)(2,1)} %add_convert_fusion.1), channel_id=1, source_target_pairs={{0,16},{4,20},{8,24},{12,28},{16,0},{20,4},{24,8},{28,12},{1,17},{... | collective-permute-start | bytes 2359304 | tf_op jit(solution)/shard_map/ppermute | solution.py:37
  399.1 9.4 %collective-permute-start.9 = (bf16[128,1536]{1,0:T(8,128)(2,1)S(1)}, bf16[128,1536]{1,0:T(8,128)(2,1)S(1)}, u32[]{:S(2)}, u32[]{:S(2)}) collective-permute-start(bf16[128,1536]{1,0:T(8,128)(2,1)S(1)} %add_convert_fusion.2), channel_id=1, source_target_pairs={{0,8},{4,12},{8,0},{12,4},{16,24},{20,28},{24,16},{28,20},{1,9},{5... | collective-permute-start | bytes 1179656 | tf_op jit(solution)/shard_map/ppermute | solution.py:37
  464.1 17.0 %collective-permute-start.10 = (bf16[2,1024,256]{2,1,0:T(8,128)(2,1)}, bf16[2,1024,256]{2,1,0:T(8,128)(2,1)}, u32[]{:S(2)}, u32[]{:S(2)}) collective-permute-start(bf16[2,1024,256]{2,1,0:T(8,128)(2,1)} %slice_bitcast_fusion), channel_id=1, source_target_pairs={{0,4},{4,0},{8,12},{12,8},{16,20},{20,16},{24,28},{28,24},{1,5},{5... | collective-permute-start | bytes 3145736 | tf_op jit(solution)/shard_map/ppermute | solution.py:37
  478.4 37.0 %collective-permute-start.13 = (bf16[384,2048]{1,0:T(8,128)(2,1)S(1)}, bf16[384,2048]{1,0:T(8,128)(2,1)}, u32[]{:S(2)}, u32[]{:S(2)}) collective-permute-start(bf16[384,2048]{1,0:T(8,128)(2,1)S(1)} %maximum_select_fusion.4), channel_id=1, source_target_pairs={{0,8},{4,12},{8,0},{12,4},{16,24},{20,28},{24,16},{28,20},{1,9},{5... | collective-permute-start | bytes 4718600 | tf_op jit(solution)/shard_map/ppermute | solution.py:37
  480.2 19.9 %collective-permute-start.14 = (bf16[256,1536]{1,0:T(8,128)(2,1)}, bf16[256,1536]{1,0:T(8,128)(2,1)S(1)}, u32[]{:S(2)}, u32[]{:S(2)}) collective-permute-start(bf16[256,1536]{1,0:T(8,128)(2,1)} %maximum_select_fusion.8), channel_id=1, source_target_pairs={{0,16},{4,20},{8,24},{12,28},{16,0},{20,4},{24,8},{28,12},{1,17},{... | collective-permute-start | bytes 2359304 | tf_op jit(solution)/shard_map/ppermute | solution.py:37
  485.4 30.0 %collective-permute-start.12 = (bf16[192,1536]{1,0:T(8,128)(2,1)S(1)}, bf16[192,1536]{1,0:T(8,128)(2,1)}, u32[]{:S(2)}, u32[]{:S(2)}) collective-permute-start(bf16[192,1536]{1,0:T(8,128)(2,1)S(1)} %convolution_convert_fusion.5), channel_id=1, source_target_pairs={{0,4},{4,0},{8,12},{12,8},{16,20},{20,16},{24,28},{28,24},{1,5},{5... | collective-permute-start | bytes 1769480 | tf_op jit(solution)/shard_map/ppermute | solution.py:37
  500.1 15.3 %copy-start.35 = (bf16[256,1536]{1,0:T(8,128)(2,1)}, bf16[256,1536]{1,0:T(8,128)(2,1)S(1)}, u32[]{:S(2)}) copy-start(bf16[256,1536]{1,0:T(8,128)(2,1)S(1)} %collective-permute-done.14) | copy-start | bytes 2359300
  519.5 34.3 %collective-permute-start.15 = (bf16[768,2048]{1,0:T(8,128)(2,1)}, bf16[768,2048]{1,0:T(8,128)(2,1)}, u32[]{:S(2)}, u32[]{:S(2)}) collective-permute-start(bf16[768,2048]{1,0:T(8,128)(2,1)} %maximum_select_fusion), channel_id=1, source_target_pairs={{0,4},{4,0},{8,12},{12,8},{16,20},{20,16},{24,28},{28,24},{1,5},{5... | collective-permute-start | bytes 9437192 | tf_op jit(solution)/shard_map/ppermute | solution.py:37
  519.6 126.4 %reduce-scatter.11.cloned.1.call-start = ((), (), s32[]{:S(2)}) async-start(), calls=%async_computation.11 | async-start | bytes 3932160 | tf_op jit(solution)/shard_map/reduce_scatter | solution.py:637
  521.6 4.0 copy-start.31
  524.2 3.1 collective-permute-start.17
  525.0 4.4 copy-start.11
  525.0 27.7 %collective-permute-start.16 = (bf16[512,1536]{1,0:T(8,128)(2,1)S(1)}, bf16[512,1536]{1,0:T(8,128)(2,1)S(1)}, u32[]{:S(2)}, u32[]{:S(2)}) collective-permute-start(bf16[512,1536]{1,0:T(8,128)(2,1)S(1)} %maximum_select_fusion.5), channel_id=1, source_target_pairs={{0,4},{4,0},{8,12},{12,8},{16,20},{20,16},{24,28},{28,24},{1,5},{5... | collective-permute-start | bytes 4718600 | tf_op jit(solution)/shard_map/ppermute | solution.py:37
  525.7 27.0 %collective-permute-start.11 = (bf16[2,1024,256]{2,1,0:T(8,128)(2,1)S(1)}, bf16[2,1024,256]{2,1,0:T(8,128)(2,1)S(1)}, u32[]{:S(2)}, u32[]{:S(2)}) collective-permute-start(bf16[2,1024,256]{2,1,0:T(8,128)(2,1)S(1)} %copy-done.31), channel_id=1, source_target_pairs={{8,0},{12,4},{16,8},{20,12},{24,16},{28,20},{9,1},{13,5},{17,9},{2... | collective-permute-start | bytes 3145736 | tf_op jit(solution)/shard_map/ppermute | solution.py:32
  558.5 4.0 copy-start.34
  562.5 7.6 %copy-start.33 = (bf16[1024,512]{1,0:T(8,128)(2,1)S(1)}, bf16[1024,512]{1,0:T(8,128)(2,1)}, u32[]{:S(2)}) copy-start(bf16[1024,512]{1,0:T(8,128)(2,1)} %gather_back.1) | copy-start | bytes 3145732
  566.2 18.2 %collective-permute-start.21 = (f32[2,1536]{1,0:T(2,128)S(1)}, f32[2,1536]{1,0:T(2,128)S(1)}, u32[]{:S(2)}, u32[]{:S(2)}) collective-permute-start(f32[2,1536]{1,0:T(2,128)S(1)} %pad_maximum_fusion.1), channel_id=1, source_target_pairs={{0,1},{1,0},{2,3},{3,2},{4,5},{5,4},{6,7},{7,6},{8,9},{9,8},{10,11... | collective-permute-start | bytes 36872 | tf_op jit(solution)/shard_map/ppermute | solution.py:37
  567.4 18.8 %collective-permute-start.20 = (bf16[384,384]{1,0:T(8,128)(2,1)S(1)}, bf16[384,384]{1,0:T(8,128)(2,1)}, u32[]{:S(2)}, u32[]{:S(2)}) collective-permute-start(bf16[384,384]{1,0:T(8,128)(2,1)S(1)} %dynamic-slice_convert_fusion.6), channel_id=1, source_target_pairs={{0,8},{4,12},{8,0},{12,4},{16,24},{20,28},{24,16},{28,20},{1,9},{5... | collective-permute-start | bytes 884744 | tf_op jit(solution)/shard_map/ppermute | solution.py:37
  572.5 14.9 %collective-permute-start.18 = (bf16[768,448]{0,1:T(8,128)(2,1)}, bf16[768,448]{0,1:T(8,128)(2,1)}, u32[]{:S(2)}, u32[]{:S(2)}) collective-permute-start(bf16[768,448]{0,1:T(8,128)(2,1)} %fusion.34), channel_id=1, source_target_pairs={{0,4},{4,0},{8,12},{12,8},{16,20},{20,16},{24,28},{28,24},{1,5},{5... | collective-permute-start | bytes 2064392 | tf_op jit(solution)/shard_map/ppermute | solution.py:37
  574.3 10.1 %collective-permute-start.33 = (bf16[96,1536]{1,0:T(8,128)(2,1)}, bf16[96,1536]{1,0:T(8,128)(2,1)}, u32[]{:S(2)}, u32[]{:S(2)}) collective-permute-start(bf16[96,1536]{1,0:T(8,128)(2,1)} %dynamic-slice_convert_fusion.5), channel_id=1, source_target_pairs={{0,16},{4,20},{8,24},{12,28},{16,0},{20,4},{24,8},{28,12},{1,17},{... | collective-permute-start | bytes 884744 | tf_op jit(solution)/shard_map/ppermute | solution.py:37
  585.9 6.3 collective-permute-start.34
  589.8 10.3 %collective-permute-start.19 = (bf16[384,448]{0,1:T(8,128)(2,1)S(1)}, bf16[384,448]{0,1:T(8,128)(2,1)S(1)}, u32[]{:S(2)}, u32[]{:S(2)}) collective-permute-start(bf16[384,448]{0,1:T(8,128)(2,1)S(1)} %dynamic-slice_convert_fusion.4), channel_id=1, source_target_pairs={{0,16},{4,20},{8,24},{12,28},{16,0},{20,4},{24,8},{28,12},{1,17},{... | collective-permute-start | bytes 1032200 | tf_op jit(solution)/shard_map/ppermute | solution.py:37
  592.3 21.6 %copy-start.10 = (bf16[768,1024]{1,0:T(8,128)(2,1)S(1)}, bf16[768,1024]{1,0:T(8,128)(2,1)}, u32[]{:S(2)}) copy-start(bf16[768,1024]{1,0:T(8,128)(2,1)} %get-tuple-element.126) | copy-start | bytes 4718596
  592.3 9.6 %collective-permute-start.35 = (bf16[48,1536]{1,0:T(8,128)(2,1)S(1)}, bf16[48,1536]{1,0:T(8,128)(2,1)S(1)}, u32[]{:S(2)}, u32[]{:S(2)}) collective-permute-start(bf16[48,1536]{1,0:T(8,128)(2,1)S(1)} %add_convert_fusion.3), channel_id=1, source_target_pairs={{0,8},{4,12},{8,0},{12,4},{16,24},{20,28},{24,16},{28,20},{1,9},{5... | collective-permute-start | bytes 442376 | tf_op jit(solution)/shard_map/ppermute | solution.py:37
  600.2 9.3 %collective-permute-start.23 = (bf16[192,384]{1,0:T(8,128)(2,1)S(1)}, bf16[192,384]{1,0:T(8,128)(2,1)S(1)}, u32[]{:S(2)}, u32[]{:S(2)}) collective-permute-start(bf16[192,384]{1,0:T(8,128)(2,1)S(1)} %dynamic-slice_convert_fusion.9), channel_id=1, source_target_pairs={{0,16},{4,20},{8,24},{12,28},{16,0},{20,4},{24,8},{28,12},{1,17},{... | collective-permute-start | bytes 442376 | tf_op jit(solution)/shard_map/ppermute | solution.py:37
  601.9 19.9 %collective-permute-start.36 = (bf16[96,1536]{1,0:T(8,128)(2,1)S(1)}, bf16[96,1536]{1,0:T(8,128)(2,1)S(1)}, u32[]{:S(2)}, u32[]{:S(2)}) collective-permute-start(bf16[96,1536]{1,0:T(8,128)(2,1)S(1)} %maximum_select_fusion.16), channel_id=1, source_target_pairs={{0,16},{4,20},{8,24},{12,28},{16,0},{20,4},{24,8},{28,12},{1,17},{... | collective-permute-start | bytes 884744 | tf_op jit(solution)/shard_map/ppermute | solution.py:37
  602.4 7.1 %collective-permute-start.24 = (f32[2,1536]{1,0:T(2,128)S(1)}, f32[2,1536]{1,0:T(2,128)S(1)}, u32[]{:S(2)}, u32[]{:S(2)}) collective-permute-start(f32[2,1536]{1,0:T(2,128)S(1)} %fusion.93), channel_id=1, source_target_pairs={{0,2},{1,3},{2,0},{3,1},{4,6},{5,7},{6,4},{7,5},{8,10},{9,11},{10,... | collective-permute-start | bytes 36872 | tf_op jit(solution)/shard_map/ppermute | solution.py:37
  604.1 6.4 collective-permute-start.22
  610.7 6.8 %collective-permute-start.27 = (f32[2,1536]{1,0:T(2,128)S(1)}, f32[2,1536]{1,0:T(2,128)S(1)}, u32[]{:S(2)}, u32[]{:S(2)}) collective-permute-start(f32[2,1536]{1,0:T(2,128)S(1)} %add.351), channel_id=1, source_target_pairs={{0,4},{4,0},{8,12},{12,8},{16,20},{20,16},{24,28},{28,24},{1,5},{5... | collective-permute-start | bytes 36872 | tf_op jit(solution)/shard_map/ppermute | solution.py:37
  610.8 6.8 %collective-permute-start.26 = (bf16[192,384]{1,0:T(8,128)(2,1)S(1)}, bf16[192,384]{1,0:T(8,128)(2,1)S(1)}, u32[]{:S(2)}, u32[]{:S(2)}) collective-permute-start(bf16[192,384]{1,0:T(8,128)(2,1)S(1)} %convert_add_fusion.12), channel_id=1, source_target_pairs={{0,16},{4,20},{8,24},{12,28},{16,0},{20,4},{24,8},{28,12},{1,17},{... | collective-permute-start | bytes 442376 | tf_op jit(solution)/shard_map/ppermute | solution.py:37
  612.2 7.7 %collective-permute-start.25 = (bf16[192,448]{0,1:T(8,128)(2,1)S(1)}, bf16[192,448]{0,1:T(8,128)(2,1)S(1)}, u32[]{:S(2)}, u32[]{:S(2)}) collective-permute-start(bf16[192,448]{0,1:T(8,128)(2,1)S(1)} %convert_add_fusion.11), channel_id=1, source_target_pairs={{0,8},{4,12},{8,0},{12,4},{16,24},{20,28},{24,16},{28,20},{1,9},{5... | collective-permute-start | bytes 516104 | tf_op jit(solution)/shard_map/ppermute | solution.py:37
  620.2 3.8 collective-permute-start.30
  622.0 12.6 %collective-permute-start.37 = (bf16[192,1536]{1,0:T(8,128)(2,1)S(1)}, bf16[192,1536]{1,0:T(8,128)(2,1)}, u32[]{:S(2)}, u32[]{:S(2)}) collective-permute-start(bf16[192,1536]{1,0:T(8,128)(2,1)S(1)} %maximum_select_fusion.13), channel_id=1, source_target_pairs={{0,4},{4,0},{8,12},{12,8},{16,20},{20,16},{24,28},{28,24},{1,5},{5... | collective-permute-start | bytes 1769480 | tf_op jit(solution)/shard_map/ppermute | solution.py:37
  622.1 9.4 %collective-permute-start.29 = (bf16[384,384]{1,0:T(8,128)(2,1)S(1)}, bf16[384,384]{1,0:T(8,128)(2,1)S(1)}, u32[]{:S(2)}, u32[]{:S(2)}) collective-permute-start(bf16[384,384]{1,0:T(8,128)(2,1)S(1)} %maximum_select_fusion.15), channel_id=1, source_target_pairs={{0,8},{4,12},{8,0},{12,4},{16,24},{20,28},{24,16},{28,20},{1,9},{5... | collective-permute-start | bytes 884744 | tf_op jit(solution)/shard_map/ppermute | solution.py:37
  622.5 10.2 %collective-permute-start.28 = (bf16[384,448]{0,1:T(8,128)(2,1)S(1)}, bf16[384,448]{0,1:T(8,128)(2,1)}, u32[]{:S(2)}, u32[]{:S(2)}) collective-permute-start(bf16[384,448]{0,1:T(8,128)(2,1)S(1)} %maximum_select_fusion.14), channel_id=1, source_target_pairs={{0,16},{4,20},{8,24},{12,28},{16,0},{20,4},{24,8},{28,12},{1,17},{... | collective-permute-start | bytes 1032200 | tf_op jit(solution)/shard_map/ppermute | solution.py:37
  634.0 9.6 %collective-permute-start.32 = (bf16[768,448]{0,1:T(8,128)(2,1)S(1)}, bf16[768,448]{0,1:T(8,128)(2,1)S(1)}, u32[]{:S(2)}, u32[]{:S(2)}) collective-permute-start(bf16[768,448]{0,1:T(8,128)(2,1)S(1)} %maximum_select_fusion.9), channel_id=1, source_target_pairs={{0,4},{4,0},{8,12},{12,8},{16,20},{20,16},{24,28},{28,24},{1,5},{5... | collective-permute-start | bytes 2064392 | tf_op jit(solution)/shard_map/ppermute | solution.py:37
  634.0 7.8 %collective-permute-start.31 = (bf16[768,384]{1,0:T(8,128)(2,1)S(1)}, bf16[768,384]{1,0:T(8,128)(2,1)S(1)}, u32[]{:S(2)}, u32[]{:S(2)}) collective-permute-start(bf16[768,384]{1,0:T(8,128)(2,1)S(1)} %maximum_select_fusion.10), channel_id=1, source_target_pairs={{0,4},{4,0},{8,12},{12,8},{16,20},{20,16},{24,28},{28,24},{1,5},{5... | collective-permute-start | bytes 1769480 | tf_op jit(solution)/shard_map/ppermute | solution.py:37
  637.6 3.7 collective-permute-start.38
  (30 other events, 77.1 us)
Sparse Core Ops, SparseCore 0:
  13.2 66.1 all-gather.4
  81.6 62.0 all-gather.6
  146.6 61.5 reduce-scatter.4
  212.4 63.3 all-gather.8
  309.9 59.1 reduce-scatter.6
  372.8 63.3 all-gather.10
  519.7 58.7 reduce-scatter.8
  584.6 60.2 reduce-scatter.10

commit v8 on v7

--- a/solution.py
+++ b/solution.py
@@ -134,7 +134,21 @@
 
 def bounds(low_ref, query_block, rows, tile_rows, offset):
     high = (offset + (query_block + 1) * rows - 1) // tile_rows + 1
-    return low_ref[query_block], high
+    return low_ref[0, query_block], high
+
+
+def sweep(low_ref, query_block, rows, tile_rows, offset, step):
+    low, high = bounds(low_ref, query_block, rows, tile_rows, offset)
+    full_from = low_ref[1, query_block]
+    full_to = (offset + query_block * rows) // tile_rows
+
+    def turn_over(tile, unused):
+        whole = (tile >= full_from) & (tile < full_to)
+        pl.when(whole)(lambda: step(tile, False))
+        pl.when(jnp.logical_not(whole))(lambda: step(tile, True))
+        return unused
+
+    lax.fori_loop(low, high, turn_over, 0)
 
 
 def attend_kernel(tiles, group, factor, low_ref, query_ref, first_ref, *refs):
@@ -151,9 +165,12 @@
     def _():
         for tile in range(tiles):
             for part in range(per_tile):
-                at = pl.ds(part * tile_rows, tile_rows)
-                key_window[tile * per_tile + part] = keys[tile][at, :]
-                value_turned[tile * per_tile + part] = values[tile][at, :].T
+                place = tile * per_tile + part
+
+                @pl.when(place >= low_ref[0, 0])
+                def _(tile=tile, place=place, at=pl.ds(part * tile_rows, tile_rows)):
+                    key_window[place] = keys[tile][at, :]
+                    value_turned[place] = values[tile][at, :].T
 
     offset = (tiles - 1) * stretch
     query = pair_rows(query_ref, group)
@@ -163,13 +180,13 @@
     top[...] = jnp.full_like(top, FAR)
     total[...] = jnp.zeros_like(total)
     mixed[...] = jnp.zeros_like(mixed)
-    low, high = bounds(low_ref, query_block, rows, tile_rows, offset)
-
-    def step(tile, unused):
+
+    def step(tile, check):
         scores = lax.dot_general(
             key_window[tile], query, (((1,), (1,)), ((), ())), preferred_element_type=f32
         )
-        scores = masked(scores, first, last, tile * tile_rows)
+        if check:
+            scores = masked(scores, first, last, tile * tile_rows)
         before = top[...]
         after = jnp.maximum(before, jnp.max(scores, axis=0, keepdims=True))
         weights = jnp.exp2(scores * factor - after * factor)
@@ -179,9 +196,8 @@
         mixed[...] = mixed[...] * fade + jnp.dot(
             value_turned[tile], weights.astype(bf16), preferred_element_type=f32
         )
-        return unused
-
-    lax.fori_loop(low, high, step, 0)
+
+    sweep(low_ref, query_block, rows, tile_rows, offset, step)
     result = (mixed[...] / total[...]).T.astype(bf16)
     for head in range(group):
         out_ref[:, head * LANES : (head + 1) * LANES] = result[head * rows : (head + 1) * rows]
@@ -248,18 +264,17 @@
     refs = refs[4 + chunks :]
     keys = refs[:tiles]
     values = refs[tiles : 2 * tiles]
+    refs = refs[2 * tiles :]
+    earlier_outs = refs[3 : 2 + tiles]
+    query_out, key_own, value_own = refs[:3]
     (
-        query_out,
-        key_own,
-        value_own,
-        earlier_out,
         key_out,
         value_out,
         key_window,
         value_window,
         key_turned,
         query_total,
-    ) = refs[2 * tiles :]
+    ) = refs[2 + tiles :]
     query_block = pl.program_id(1)
     rows = query_ref.shape[0]
     stretch = keys[0].shape[0]
@@ -272,10 +287,13 @@
         value_out[...] = jnp.zeros_like(value_out)
         for tile in range(tiles):
             for part in range(per_tile):
-                at = pl.ds(part * tile_rows, tile_rows)
-                key_window[tile * per_tile + part] = keys[tile][at, :]
-                key_turned[tile * per_tile + part] = keys[tile][at, :].T
-                value_window[tile * per_tile + part] = values[tile][at, :]
+                place = tile * per_tile + part
+
+                @pl.when(place >= low_ref[0, 0])
+                def _(tile=tile, place=place, at=pl.ds(part * tile_rows, tile_rows)):
+                    key_window[place] = keys[tile][at, :]
+                    key_turned[place] = keys[tile][at, :].T
+                    value_window[place] = values[tile][at, :]
 
     offset = (tiles - 1) * stretch
     query = pair_rows(query_ref, group)
@@ -289,12 +307,12 @@
     lane = lax.broadcasted_iota(jnp.int32, (1, rows), 1)
     last = jnp.concatenate([lane] * group, axis=1) + (offset + query_block * rows)
     query_total[...] = jnp.zeros_like(query_total)
-    low, high = bounds(low_ref, query_block, rows, tile_rows, offset)
     both_last = (((1,), (1,)), ((), ()))
 
-    def step(tile, unused):
+    def step(tile, check):
         scores = lax.dot_general(key_window[tile], query, both_last, preferred_element_type=f32)
-        scores = masked(scores, first, last, tile * tile_rows)
+        if check:
+            scores = masked(scores, first, last, tile * tile_rows)
         weights = jnp.exp2(scores * factor - log_total)
         weight_grad = lax.dot_general(
             value_window[tile], grad, both_last, preferred_element_type=f32
@@ -304,9 +322,8 @@
         value_out[at, :] += jnp.dot(weights.astype(bf16), grad, preferred_element_type=f32)
         key_out[at, :] += jnp.dot(score_grad, query, preferred_element_type=f32)
         query_total[...] += jnp.dot(key_turned[tile], score_grad, preferred_element_type=f32)
-        return unused
-
-    lax.fori_loop(low, high, step, 0)
+
+    sweep(low_ref, query_block, rows, tile_rows, offset, step)
     result = query_total[...].T
     for head in range(group):
         part = result[head * rows : (head + 1) * rows]
@@ -318,8 +335,8 @@
     def _():
         for tile in range(tiles - 1):
             at = pl.ds(tile * stretch, stretch)
-            earlier_out[tile, 0] = key_out[at, :].astype(bf16)
-            earlier_out[tile, 1] = value_out[at, :].astype(bf16)
+            earlier_outs[tile][0] = key_out[at, :].astype(bf16)
+            earlier_outs[tile][1] = value_out[at, :].astype(bf16)
         key_own[...] = key_out[pl.ds(offset, stretch), :]
         value_own[...] = value_out[pl.ds(offset, stretch), :]
 
@@ -342,7 +359,7 @@
     heads_spec = pl.BlockSpec((rows, group * LANES), lambda g, i, *s: (i, g))
     table_spec = pl.BlockSpec((rows, LANES), lambda g, i, *s: (i, 0))
     own_spec = pl.BlockSpec((stretch, LANES), lambda g, i, *s: (0, g))
-    earlier_spec = pl.BlockSpec((tiles - 1, 2, stretch, LANES), lambda g, i, *s: (0, 0, 0, g))
+    earlier_spec = pl.BlockSpec((2, stretch, LANES), lambda g, i, *s: (0, 0, g))
     grid_spec = pltpu.PrefetchScalarGridSpec(
         num_scalar_prefetch=2,
         grid=(kv_heads, blocks),
@@ -360,7 +377,7 @@
         * chunks
         + window_specs(stretch, key_columns)
         + window_specs(stretch, value_columns),
-        out_specs=[heads_spec, own_spec, own_spec, earlier_spec],
+        out_specs=[heads_spec, own_spec, own_spec] + [earlier_spec] * (tiles - 1),
         scratch_shapes=[
             pltpu.VMEM((tiles * stretch, LANES), f32),
             pltpu.VMEM((tiles * stretch, LANES), f32),
@@ -378,8 +395,8 @@
             jax.ShapeDtypeStruct((stretch, kv_heads * group * LANES), bf16),
             jax.ShapeDtypeStruct((stretch, kv_heads * LANES), f32),
             jax.ShapeDtypeStruct((stretch, kv_heads * LANES), f32),
-            jax.ShapeDtypeStruct((tiles - 1, 2, stretch, kv_heads * LANES), bf16),
-        ],
+        ]
+        + [jax.ShapeDtypeStruct((2, stretch, kv_heads * LANES), bf16)] * (tiles - 1),
         cost_estimate=pl.CostEstimate(
             flops=40 * LANES * work, bytes_accessed=16 * stretch * stretch, transcendentals=work
         ),
@@ -507,7 +524,7 @@
     heads = w_query.shape[1] // HEAD_SIZE
     kv_heads = key_weight.shape[1] // HEAD_SIZE
     group = heads // kv_heads
-    rows = min(256, stretch)
+    rows = min(512, stretch)
     tile_rows = min(512, stretch)
     blocks = stretch // rows
     places = list(range((lax.axis_size("dp") - 1).bit_length()))
@@ -533,11 +550,17 @@
     local = jnp.arange(stretch, dtype=jnp.int32)
     window_first = reach * stretch + local - positions
     firsts = window_first.reshape(blocks, 1, rows)
-    low = jnp.min(window_first.reshape(blocks, rows), axis=1) // tile_rows
+    cut_first = window_first.reshape(blocks, rows)
+    low = jnp.stack(
+        [
+            jnp.min(cut_first, axis=1) // tile_rows,
+            (jnp.max(cut_first, axis=1) + tile_rows - 1) // tile_rows,
+        ]
+    )
 
     queries, key_value = project(
         attention_normed, w_joined, cosine, sine, heads + kv_heads,
-        (heads * LANES, 2 * kv_heads * LANES), rows,
+        (heads * LANES, 2 * kv_heads * LANES), min(256, stretch),
     )
     paired = reach == 2 and lax.axis_size("dp") % 2 == 0
     odd = lax.axis_index("dp") % 2 == 1
@@ -597,7 +620,7 @@
         bf16
     )
     slots = jnp.arange(blocks, dtype=jnp.int32)
-    query_grad, key_own, value_own, earlier = attend_back(
+    query_grad, key_own, value_own, *earlier = attend_back(
         queries, windows, firsts, low, slots, attended, [attended_gradient], logs, cosine,
         sine, kv_heads, group, rows, tile_rows,
     )
@@ -627,7 +650,7 @@
         (received, pair_shared.got, down_shared.got, out_shared.value, query_shared.value)
     )
     key_value_grad = gather_back(
-        key_own, value_own, received, cosine, sine, kv_heads, stretch, rows
+        key_own, value_own, received, cosine, sine, kv_heads, stretch, min(256, stretch)
     )
     split = heads * LANES
     attn_normed_part = (

time: 667 us -> 666 us (level)
  transfers between devices with their start and end apart: 47 -> 47, of which waited for: 25 -> 24; matrix products, arithmetic and copies ran while one was open for 22% -> 22% of each run, Pallas kernels for 4% -> 4%
where the time goes in v8:
time: 666 us; the launch traced here: 656 us
  waiting for transfers between devices  330 us (50%)
  matrix products  102 us (15%)
  other arithmetic  78.5 us (12%)
  starting transfers between devices  52.8 us (8%)
  Pallas kernels  43.1 us (6%)
  local copies, waits for them, and re-layouts  33.8 us (5%)
  between operations  15.3 us (2%)
    all_gather x4, waiting for transfers between devices, gather_rows(): return lax.all_gather(rows, 'tensor', axis=0, tiled=True)  132 us
    ppermute x37, waiting for transfers between devices, exchange(): return lax.ppermute(value, axis, [(i, i ^ distance) for i in range(count)])  99 us
    reduce_scatter x2, waiting for transfers between devices, scatter_low(): lax.psum_scatter(product.astype(bf16), 'tensor', scatter_dimension=0, til...  62.5 us
    ppermute x37, starting transfers between devices, exchange(): return lax.ppermute(value, axis, [(i, i ^ distance) for i in range(count)])  45.7 us
    dot_general x10, matrix products, times(): return jnp.dot(part.T, self.right, preferred_element_type=f32)  37.1 us
    ppermute x2, waiting for transfers between devices, from_behind(): lax.ppermute(value, axis, [(source, source + steps) for source in range(l...  36.1 us
    pallas_call x1, Pallas kernels, attend_back(): pl.pallas_call(functools.partial(attend_back_kernel, tiles, chunks, group...  18.3 us
    convert_element_type x7, other arithmetic, finish(): self.joined(self.value[:, a:b], self.got[:, a:b]).astype(f32)  17.3 us
  transfers between devices with their start and end apart: 47, of which 24 were waited for; matrix products, arithmetic and copies ran while one was open for 22% of the time, Pallas kernels for 4%

profile of v8, /device:TPU:0, one launch (start us, length us, event | category | flops | bytes accessed | tf_op | source)
XLA Modules:
  0.0 656.3 jit_solution(13738582028949502926)
XLA Ops:
  10.6 2.5 multiply_convert_fusion.4
  18.5 3.1 fusion.53
  21.5 6.4 fusion.4.weight_ref
  28.0 51.5 %all-gather.5.cloned.1.call-done.rows_ref = bf16[1024,1536]{1,0:T(8,128)(2,1)} async-done(((bf16[256,1536]{1,0:T(8,128)(2,1)}), bf16[1024,1536]{1,0:T(8,128)(2,1)}) %all-gather.5.cloned.1.call-update) | async-done | bytes 3145744 | tf_op jit(solution)/shard_map/all_gather | solution.py:505
  79.4 7.5 %project.1 = (bf16[1024,512]{1,0:T(8,128)(2,1)}, bf16[1024,512]{1,0:T(8,128)(2,1)}) custom-call(bf16[1024,1536]{1,0:T(8,128)(2,1)} %all-gather.5.cloned.1.call-done.rows_ref, bf16[1536,1024]{1,0:T(8,128)(2,1)} %fusion.4.weight_ref, f32[1024,128]{1,0:T(8,128)} %get-tuple-element.139.cosine_ref.refs_2_, f32[1024,128]{1,0:T(8,128)} %get-tuple-element.138.sine_ref.refs_3_), custom_call_target="tpu_custom_call" | custom-call | flops 3221225472 | bytes 8388608 | tf_op jit(solution)/shard_map/project/pallas_call | solution.py:100
  86.9 4.3 collective-permute-start
  91.3 21.6 %collective-permute-done.refs_0_.refs_3_.refs_5_.refs_8_ = bf16[1024,512]{1,0:T(8,128)(2,1)} collective-permute-done((bf16[1024,512]{1,0:T(8,128)(2,1)}, bf16[1024,512]{1,0:T(8,128)(2,1)}, u32[]{:S(2)}, u32[]{:S(2)}) %collective-permute-start) | collective-permute-done | bytes 1048608 | tf_op jit(solution)/shard_map/ppermute | solution.py:32
  116.6 3.5 fusion.50
  120.1 12.9 %attend.1 = (bf16[1024,512]{1,0:T(8,128)(2,1)}, f32[2,2,1,1024]{3,2,1,0:T(1,128)}) custom-call(s32[2,2]{1,0:T(2,128)} %pad_add_fusion.1.low_ref, bf16[1024,512]{1,0:T(8,128)(2,1)} %get-tuple-element.65.query_ref, s32[2,1,512]{2,1,0:T(1,128)} %bitcast.44, bf16[1024,512]{1,0:T(8,128)(2,1)} %collective-permute-done.refs_0_.refs_3_.refs_5_.refs_8_, ...), custom_call_target="tpu_custom_call" | custom-call | flops 8589934592 | bytes 8388608 | tf_op jit(solution)/shard_map/attend/pallas_call | solution.py:245
  133.0 5.2 convolution_convert_fusion.1
  138.2 5.5 all-gather.7.cloned.1.call-done
  143.7 6.9 %fusion.103 = f32[1024,1024]{1,0:T(8,128)} fusion(bf16[1024,1536]{1,0:T(8,128)(2,1)} %all-gather.7.cloned.1.call-done, bf16[1024,1536]{1,0:T(8,128)(2,1)S(1)} %copy-done), kind=kOutput, calls=%fused_computation.202 | convolution fusion | flops 3221225472 | bytes 10485760 | tf_op jit(solution)/shard_map/dot_general | solution.py:574
  150.5 59.3 %reduce-scatter.5.cloned.1.call-done = bf16[256,1536]{1,0:T(8,128)(2,1)} async-done(((bf16[1024,1536]{1,0:T(8,128)(2,1)}), bf16[256,1536]{1,0:T(8,128)(2,1)}) %reduce-scatter.5.cloned.1.call-update) | async-done | bytes 786448 | tf_op jit(solution)/shard_map/reduce_scatter | solution.py:501
  214.2 4.0 constant_dynamic-update-slice_fusion.1
  220.2 57.2 %all-gather.9.cloned.1.call-done = bf16[1024,1536]{1,0:T(8,128)(2,1)} async-done(((bf16[256,1536]{1,0:T(8,128)(2,1)}), bf16[1024,1536]{1,0:T(8,128)(2,1)}) %all-gather.9.cloned.1.call-update) | async-done | bytes 3145744 | tf_op jit(solution)/shard_map/all_gather | solution.py:505
  277.5 9.8 %fusion.104 = f32[1024,2048]{1,0:T(8,128)S(1)} fusion(bf16[1024,1536]{1,0:T(8,128)(2,1)} %all-gather.9.cloned.1.call-done, bf16[1536,2048]{1,0:T(8,128)(2,1)} %constant_dynamic-update-slice_fusion), kind=kOutput, calls=%fused_computation.203 | convolution fusion | flops 6442450944 | bytes 17825792 | tf_op jit(solution)/shard_map/dot_general | solution.py:582
  287.3 3.9 multiply_convert_fusion.2
  291.2 2.4 pad_maximum_fusion
  293.6 10.1 %convolution_convert_fusion = bf16[1024,1536]{1,0:T(8,128)(2,1)} fusion(bf16[1536,2048]{1,0:T(8,128)(2,1)} %constant_dynamic-update-slice_fusion, bf16[1024,1024]{1,0:T(8,128)(2,1)S(1)} %get-tuple-element.128, bf16[1024,1024]{1,0:T(8,128)(2,1)S(1)} %get-tuple-element.127), kind=kOutput, calls=%fused_computation.9 | convolution fusion | flops 6452412416 | bytes 13631488 | tf_op jit(solution)/shard_map/dot_general | solution.py:590
  303.7 7.8 %convolution_convert_fusion.3 = bf16[768,2048]{1,0:T(8,128)(2,1)} fusion(bf16[1024,2048]{1,0:T(8,128)(2,1)} %pad_maximum_fusion, bf16[1024,1536]{1,0:T(8,128)(2,1)} %all-gather.9.cloned.1.call-done, s32[]{:T(128)S(6)} %select_n.356), kind=kOutput, calls=%fused_computation.12 | convolution fusion | flops 3222798336 | bytes 8912900 | tf_op jit(solution)/shard_map/dot_general | solution.py:449
  312.0 5.2 convolution_convert_fusion.4
  317.7 7.2 %convert_add_fusion = f32[768,2048]{1,0:T(8,128)S(1)} fusion(bf16[768,2048]{1,0:T(8,128)(2,1)} %collective-permute-done.2, bf16[1024,2048]{1,0:T(8,128)(2,1)} %pad_maximum_fusion, bf16[1024,1536]{1,0:T(8,128)(2,1)} %all-gather.9.cloned.1.call-done, s32[]{:T(128)S(6)} %select_n.343), kind=kOutput, calls=%fused_computation.2 | convolution fusion | flops 3224371200 | bytes 15204356 | tf_op jit(solution)/shard_map/dot_general | solution.py:449
  329.2 3.3 convert_add_fusion.1
  335.8 6.4 convolution_convert_fusion.2
  342.2 11.9 %collective-permute-done.5 = bf16[256,1536]{1,0:T(8,128)(2,1)} collective-permute-done((bf16[256,1536]{1,0:T(8,128)(2,1)}, bf16[256,1536]{1,0:T(8,128)(2,1)}, u32[]{:S(2)}, u32[]{:S(2)}) %collective-permute-start.5) | collective-permute-done | bytes 786464 | tf_op jit(solution)/shard_map/ppermute | solution.py:37
  354.2 3.0 convert_add_fusion.4
  357.1 5.8 collective-permute-done.3
  363.0 4.7 convert_add_fusion.2
  367.7 3.2 reduce-scatter.7.cloned.1.call-done
  374.7 2.5 dynamic-slice_convert_fusion.1
  380.3 16.2 %collective-permute-done.6 = bf16[192,2048]{1,0:T(8,128)(2,1)} collective-permute-done((bf16[192,2048]{1,0:T(8,128)(2,1)}, bf16[192,2048]{1,0:T(8,128)(2,1)}, u32[]{:S(2)}, u32[]{:S(2)}) %collective-permute-start.6) | collective-permute-done | bytes 786464 | tf_op jit(solution)/shard_map/ppermute | solution.py:37
  396.4 2.7 add_convert_fusion.1
  402.3 3.0 fusion.49
  405.2 4.9 collective-permute-done.9
  411.2 6.3 collective-permute-done.7
  417.5 2.7 maximum_select_fusion.4
  420.2 17.8 %all-gather.11.cloned.1.call-done = bf16[1024,1536]{1,0:T(8,128)(2,1)} async-done(((bf16[256,1536]{1,0:T(8,128)(2,1)}), bf16[1024,1536]{1,0:T(8,128)(2,1)}) %all-gather.11.cloned.1.call-update) | async-done | bytes 3145744 | tf_op jit(solution)/shard_map/all_gather | solution.py:505
  438.0 5.1 convolution_convert_fusion.6.refs_4_
  443.6 18.3 %attend_back.1 = (bf16[1024,512]{1,0:T(8,128)(2,1)}, f32[1024,256]{1,0:T(8,128)}, f32[1024,256]{1,0:T(8,128)}, bf16[2,1024,256]{2,1,0:T(8,128)(2,1)}, bf16[2,1024,256]{2,1,0:T(8,128)(2,1)}) custom-call(s32[2,2]{1,0:T(2,128)} %pad_add_fusion.1.low_ref, s32[2]{0:T(128)} %iota.46.slot_ref, bf16[1024,512]{1,0:T(8,128)(2,1)} %get-tuple-element.65.query_ref, ...), custom_call_target="tpu_custom_call" | custom-call | flops 21474836480 | bytes 16777216 | tf_op jit(solution)/shard_map/attend_back/pallas_call | solution.py:391
  461.9 12.1 %collective-permute-start.10 = (bf16[2,1024,256]{2,1,0:T(8,128)(2,1)}, bf16[2,1024,256]{2,1,0:T(8,128)(2,1)}, u32[]{:S(2)}, u32[]{:S(2)}) collective-permute-start(bf16[2,1024,256]{2,1,0:T(8,128)(2,1)} %get-tuple-element.83), channel_id=1, source_target_pairs={{0,4},{4,0},{8,12},{12,8},{16,20},{20,16},{24,28},{28,24},{1,5},{5... | collective-permute-start | bytes 3145736 | tf_op jit(solution)/shard_map/ppermute | solution.py:37
  474.1 4.1 collective-permute-start.13
  478.1 2.5 select_add_fusion
  483.2 14.8 %collective-permute-done.14 = bf16[256,1536]{1,0:T(8,128)(2,1)S(1)} collective-permute-done((bf16[256,1536]{1,0:T(8,128)(2,1)}, bf16[256,1536]{1,0:T(8,128)(2,1)S(1)}, u32[]{:S(2)}, u32[]{:S(2)}) %collective-permute-start.14) | collective-permute-done | bytes 786464 | tf_op jit(solution)/shard_map/ppermute | solution.py:37
  498.0 15.3 %collective-permute-done.13 = bf16[384,2048]{1,0:T(8,128)(2,1)} collective-permute-done((bf16[384,2048]{1,0:T(8,128)(2,1)S(1)}, bf16[384,2048]{1,0:T(8,128)(2,1)}, u32[]{:S(2)}, u32[]{:S(2)}) %collective-permute-start.13) | collective-permute-done | bytes 1572896 | tf_op jit(solution)/shard_map/ppermute | solution.py:37
  513.2 4.2 maximum_select_fusion
  519.5 2.6 fusion.37
  529.5 3.5 fusion.98
  533.0 3.0 convolution_add_fusion
  536.0 14.5 %collective-permute-done.11.refs_0_ = bf16[2,1024,256]{2,1,0:T(8,128)(2,1)S(1)} collective-permute-done((bf16[2,1024,256]{2,1,0:T(8,128)(2,1)S(1)}, bf16[2,1024,256]{2,1,0:T(8,128)(2,1)S(1)}, u32[]{:S(2)}, u32[]{:S(2)}) %collective-permute-start.11) | collective-permute-done | bytes 1048608 | tf_op jit(solution)/shard_map/ppermute | solution.py:32
  552.0 4.4 gather_back.1
  556.4 3.7 fusion.17
  560.4 3.7 multiply_reduce_fusion
  565.3 2.7 collective-permute-start.20
  572.2 3.5 fusion.97
  575.7 3.1 fusion.1
  578.8 3.5 fusion.2
  591.5 6.5 collective-permute-done.19
  603.8 3.6 collective-permute-done.24
  611.7 3.7 fusion.3
  621.8 2.5 convert_add_fusion.3
  624.3 5.0 collective-permute-done.29
  632.4 3.0 fusion.41
  636.1 3.0 collective-permute-done.38
  645.4 3.6 subtract_add_fusion
  (248 shorter events, 93.5 us)
Async XLA Ops:
  7.2 136.5 %copy-start = (bf16[1024,1536]{1,0:T(8,128)(2,1)S(1)}, bf16[1024,1536]{1,0:T(8,128)(2,1)}, u32[]{:S(2)}) copy-start(bf16[1024,1536]{1,0:T(8,128)(2,1)} %param.22) | copy-start | bytes 9437188
  7.2 72.2 %all-gather.5.cloned.1.call-start = ((), (), s32[]{:S(2)}) async-start(), calls=%async_computation.4 | async-start | bytes 3932160 | tf_op jit(solution)/shard_map/all_gather | solution.py:505
  13.1 130.6 %all-gather.7.cloned.1.call-start = ((), (), s32[]{:S(2)}) async-start(), calls=%async_computation.6 | async-start | bytes 3932160 | tf_op jit(solution)/shard_map/all_gather | solution.py:505
  13.9 196.0 %reduce-scatter.5.cloned.1.call-start = ((), (), s32[]{:S(2)}) async-start(), calls=%async_computation.5 | async-start | bytes 3932160 | tf_op jit(solution)/shard_map/reduce_scatter | solution.py:501
  14.0 101.2 %copy-start.39 = (s32[1024]{0:T(1024)}, s32[1024]{0:T(1024)S(1)}, u32[]{:S(2)}) copy-start(s32[1024]{0:T(1024)S(1)} %get-tuple-element.141) | copy-start | bytes 12292
  86.9 25.9 %collective-permute-start = (bf16[1024,512]{1,0:T(8,128)(2,1)}, bf16[1024,512]{1,0:T(8,128)(2,1)}, u32[]{:S(2)}, u32[]{:S(2)}) collective-permute-start(bf16[1024,512]{1,0:T(8,128)(2,1)} %get-tuple-element.66.refs_2_.refs_5_.refs_7_.refs_10_), channel_id=1, source_target_pairs={{0,8},{4,12},{8,16},{12,20},{16,24},{20,28},{1,9},{5,13},{9,17},{1... | collective-permute-start | bytes 3145736 | tf_op jit(solution)/shard_map/ppermute | solution.py:32
  115.2 4.9 collective-permute-start.1
  138.2 139.3 %all-gather.9.cloned.1.call-start = ((), (), s32[]{:S(2)}) async-start(), calls=%async_computation.7 | async-start | bytes 3932160 | tf_op jit(solution)/shard_map/all_gather | solution.py:505
  150.5 62.3 %copy-start.38 = (f32[1536]{0:T(1024)S(1)}, f32[1536]{0:T(1024)}, u32[]{:S(2)}) copy-start(f32[1536]{0:T(1024)} %param.19) | copy-start | bytes 18436
  214.0 156.9 %reduce-scatter.7.cloned.1.call-start = ((), (), s32[]{:S(2)}) async-start(), calls=%async_computation.8 | async-start | bytes 3932160 | tf_op jit(solution)/shard_map/reduce_scatter | solution.py:501
  214.2 4.0 copy-start.19
  277.5 9.9 %copy-start.18 = (f32[1024,1024]{1,0:T(8,128)S(1)}, f32[1024,1024]{1,0:T(8,128)}, u32[]{:S(2)}) copy-start(f32[1024,1024]{1,0:T(8,128)} %fusion.103) | copy-start | bytes 12582916
  311.5 6.2 collective-permute-start.2
  311.5 126.4 %all-gather.11.cloned.1.call-start = ((), (), s32[]{:S(2)}) async-start(), calls=%async_computation.9 | async-start | bytes 3932160 | tf_op jit(solution)/shard_map/all_gather | solution.py:505
  317.2 10.6 %collective-permute-start.4 = (bf16[512,1536]{1,0:T(8,128)(2,1)}, bf16[512,1536]{1,0:T(8,128)(2,1)}, u32[]{:S(2)}, u32[]{:S(2)}) collective-permute-start(bf16[512,1536]{1,0:T(8,128)(2,1)} %convolution_convert_fusion.4), channel_id=1, source_target_pairs={{0,4},{4,0},{8,12},{12,8},{16,20},{20,16},{24,28},{28,24},{1,5},{5... | collective-permute-start | bytes 4718600 | tf_op jit(solution)/shard_map/ppermute | solution.py:37
  317.7 10.1 %copy-start.17 = (bf16[1024,1024]{1,0:T(8,128)(2,1)S(1)}, bf16[1024,1024]{1,0:T(8,128)(2,1)}, u32[]{:S(2)}) copy-start(bf16[1024,1024]{1,0:T(8,128)(2,1)} %get-tuple-element.73) | copy-start | bytes 6291460
  324.9 7.5 %copy-start.5 = (f32[768,2048]{1,0:T(8,128)}, f32[768,2048]{1,0:T(8,128)S(1)}, u32[]{:S(2)}) copy-start(f32[768,2048]{1,0:T(8,128)S(1)} %convert_add_fusion) | copy-start | bytes 18874372
  325.0 4.2 copy-start.9
  326.4 36.6 %collective-permute-start.3 = (bf16[384,2048]{1,0:T(8,128)(2,1)}, bf16[384,2048]{1,0:T(8,128)(2,1)}, u32[]{:S(2)}, u32[]{:S(2)}) collective-permute-start(bf16[384,2048]{1,0:T(8,128)(2,1)} %dynamic-slice_convert_fusion), channel_id=1, source_target_pairs={{0,8},{4,12},{8,0},{12,4},{16,24},{20,28},{24,16},{28,20},{1,9},{5... | collective-permute-start | bytes 4718600 | tf_op jit(solution)/shard_map/ppermute | solution.py:37
  334.4 19.8 %collective-permute-start.5 = (bf16[256,1536]{1,0:T(8,128)(2,1)}, bf16[256,1536]{1,0:T(8,128)(2,1)}, u32[]{:S(2)}, u32[]{:S(2)}) collective-permute-start(bf16[256,1536]{1,0:T(8,128)(2,1)} %dynamic-slice_convert_fusion.2), channel_id=1, source_target_pairs={{0,16},{4,20},{8,24},{12,28},{16,0},{20,4},{24,8},{28,12},{1,17},{... | collective-permute-start | bytes 2359304 | tf_op jit(solution)/shard_map/ppermute | solution.py:37
  357.1 13.7 %copy-start.4 = (f32[256,1536]{1,0:T(8,128)S(1)}, f32[256,1536]{1,0:T(8,128)}, u32[]{:S(2)}) copy-start(f32[256,1536]{1,0:T(8,128)} %copy-done.3) | copy-start | bytes 4718596
  367.7 4.9 copy-start.15
  374.4 4.3 copy-start.16
  374.5 247.4 %reduce-scatter.9.cloned.1.call-start = ((), (), s32[]{:S(2)}) async-start(), calls=%async_computation.10 | async-start | bytes 3932160 | tf_op jit(solution)/shard_map/reduce_scatter | solution.py:614
  377.2 19.2 %collective-permute-start.6 = (bf16[192,2048]{1,0:T(8,128)(2,1)}, bf16[192,2048]{1,0:T(8,128)(2,1)}, u32[]{:S(2)}, u32[]{:S(2)}) collective-permute-start(bf16[192,2048]{1,0:T(8,128)(2,1)} %dynamic-slice_convert_fusion.1), channel_id=1, source_target_pairs={{0,16},{4,20},{8,24},{12,28},{16,0},{20,4},{24,8},{28,12},{1,17},{... | collective-permute-start | bytes 2359304 | tf_op jit(solution)/shard_map/ppermute | solution.py:37
  378.8 21.9 %collective-permute-start.8 = (bf16[128,1536]{1,0:T(8,128)(2,1)S(1)}, bf16[128,1536]{1,0:T(8,128)(2,1)S(1)}, u32[]{:S(2)}, u32[]{:S(2)}) collective-permute-start(bf16[128,1536]{1,0:T(8,128)(2,1)S(1)} %dynamic-slice_convert_fusion.3), channel_id=1, source_target_pairs={{0,8},{4,12},{8,0},{12,4},{16,24},{20,28},{24,16},{28,20},{1,9},{5... | collective-permute-start | bytes 1179656 | tf_op jit(solution)/shard_map/ppermute | solution.py:37
  399.2 18.3 %collective-permute-start.7 = (bf16[192,2048]{1,0:T(8,128)(2,1)}, bf16[192,2048]{1,0:T(8,128)(2,1)}, u32[]{:S(2)}, u32[]{:S(2)}) collective-permute-start(bf16[192,2048]{1,0:T(8,128)(2,1)} %add_convert_fusion.1), channel_id=1, source_target_pairs={{0,16},{4,20},{8,24},{12,28},{16,0},{20,4},{24,8},{28,12},{1,17},{... | collective-permute-start | bytes 2359304 | tf_op jit(solution)/shard_map/ppermute | solution.py:37
  400.7 9.4 %collective-permute-start.9 = (bf16[128,1536]{1,0:T(8,128)(2,1)S(1)}, bf16[128,1536]{1,0:T(8,128)(2,1)S(1)}, u32[]{:S(2)}, u32[]{:S(2)}) collective-permute-start(bf16[128,1536]{1,0:T(8,128)(2,1)S(1)} %add_convert_fusion.2), channel_id=1, source_target_pairs={{0,8},{4,12},{8,0},{12,4},{16,24},{20,28},{24,16},{28,20},{1,9},{5... | collective-permute-start | bytes 1179656 | tf_op jit(solution)/shard_map/ppermute | solution.py:37
  461.9 16.2 %collective-permute-start.10 = (bf16[2,1024,256]{2,1,0:T(8,128)(2,1)}, bf16[2,1024,256]{2,1,0:T(8,128)(2,1)}, u32[]{:S(2)}, u32[]{:S(2)}) collective-permute-start(bf16[2,1024,256]{2,1,0:T(8,128)(2,1)} %get-tuple-element.83), channel_id=1, source_target_pairs={{0,4},{4,0},{8,12},{12,8},{16,20},{20,16},{24,28},{28,24},{1,5},{5... | collective-permute-start | bytes 3145736 | tf_op jit(solution)/shard_map/ppermute | solution.py:37
  474.1 39.2 %collective-permute-start.13 = (bf16[384,2048]{1,0:T(8,128)(2,1)S(1)}, bf16[384,2048]{1,0:T(8,128)(2,1)}, u32[]{:S(2)}, u32[]{:S(2)}) collective-permute-start(bf16[384,2048]{1,0:T(8,128)(2,1)S(1)} %maximum_select_fusion.4), channel_id=1, source_target_pairs={{0,8},{4,12},{8,0},{12,4},{16,24},{20,28},{24,16},{28,20},{1,9},{5... | collective-permute-start | bytes 4718600 | tf_op jit(solution)/shard_map/ppermute | solution.py:37
  478.1 19.8 %collective-permute-start.14 = (bf16[256,1536]{1,0:T(8,128)(2,1)}, bf16[256,1536]{1,0:T(8,128)(2,1)S(1)}, u32[]{:S(2)}, u32[]{:S(2)}) collective-permute-start(bf16[256,1536]{1,0:T(8,128)(2,1)} %maximum_select_fusion.8), channel_id=1, source_target_pairs={{0,16},{4,20},{8,24},{12,28},{16,0},{20,4},{24,8},{28,12},{1,17},{... | collective-permute-start | bytes 2359304 | tf_op jit(solution)/shard_map/ppermute | solution.py:37
  482.6 30.7 %collective-permute-start.12 = (bf16[192,1536]{1,0:T(8,128)(2,1)S(1)}, bf16[192,1536]{1,0:T(8,128)(2,1)}, u32[]{:S(2)}, u32[]{:S(2)}) collective-permute-start(bf16[192,1536]{1,0:T(8,128)(2,1)S(1)} %convolution_convert_fusion.5), channel_id=1, source_target_pairs={{0,4},{4,0},{8,12},{12,8},{16,20},{20,16},{24,28},{28,24},{1,5},{5... | collective-permute-start | bytes 1769480 | tf_op jit(solution)/shard_map/ppermute | solution.py:37
  497.9 15.3 %copy-start.35 = (bf16[256,1536]{1,0:T(8,128)(2,1)}, bf16[256,1536]{1,0:T(8,128)(2,1)S(1)}, u32[]{:S(2)}) copy-start(bf16[256,1536]{1,0:T(8,128)(2,1)S(1)} %collective-permute-done.14) | copy-start | bytes 2359300
  517.4 34.3 %collective-permute-start.15 = (bf16[768,2048]{1,0:T(8,128)(2,1)}, bf16[768,2048]{1,0:T(8,128)(2,1)}, u32[]{:S(2)}, u32[]{:S(2)}) collective-permute-start(bf16[768,2048]{1,0:T(8,128)(2,1)} %maximum_select_fusion), channel_id=1, source_target_pairs={{0,4},{4,0},{8,12},{12,8},{16,20},{20,16},{24,28},{28,24},{1,5},{5... | collective-permute-start | bytes 9437192 | tf_op jit(solution)/shard_map/ppermute | solution.py:37
  517.4 126.4 %reduce-scatter.11.cloned.1.call-start = ((), (), s32[]{:S(2)}) async-start(), calls=%async_computation.11 | async-start | bytes 3932160 | tf_op jit(solution)/shard_map/reduce_scatter | solution.py:660
  519.5 4.0 copy-start.31
  522.1 3.1 collective-permute-start.17
  522.8 4.4 copy-start.11
  522.8 27.7 %collective-permute-start.16 = (bf16[512,1536]{1,0:T(8,128)(2,1)S(1)}, bf16[512,1536]{1,0:T(8,128)(2,1)S(1)}, u32[]{:S(2)}, u32[]{:S(2)}) collective-permute-start(bf16[512,1536]{1,0:T(8,128)(2,1)S(1)} %maximum_select_fusion.5), channel_id=1, source_target_pairs={{0,4},{4,0},{8,12},{12,8},{16,20},{20,16},{24,28},{28,24},{1,5},{5... | collective-permute-start | bytes 4718600 | tf_op jit(solution)/shard_map/ppermute | solution.py:37
  523.5 27.0 %collective-permute-start.11 = (bf16[2,1024,256]{2,1,0:T(8,128)(2,1)S(1)}, bf16[2,1024,256]{2,1,0:T(8,128)(2,1)S(1)}, u32[]{:S(2)}, u32[]{:S(2)}) collective-permute-start(bf16[2,1024,256]{2,1,0:T(8,128)(2,1)S(1)} %copy-done.31), channel_id=1, source_target_pairs={{8,0},{12,4},{16,8},{20,12},{24,16},{28,20},{9,1},{13,5},{17,9},{2... | collective-permute-start | bytes 3145736 | tf_op jit(solution)/shard_map/ppermute | solution.py:32
  556.4 4.0 copy-start.34
  560.4 7.6 %copy-start.33 = (bf16[1024,512]{1,0:T(8,128)(2,1)S(1)}, bf16[1024,512]{1,0:T(8,128)(2,1)}, u32[]{:S(2)}) copy-start(bf16[1024,512]{1,0:T(8,128)(2,1)} %gather_back.1) | copy-start | bytes 3145732
  564.1 18.2 %collective-permute-start.21 = (f32[2,1536]{1,0:T(2,128)S(1)}, f32[2,1536]{1,0:T(2,128)S(1)}, u32[]{:S(2)}, u32[]{:S(2)}) collective-permute-start(f32[2,1536]{1,0:T(2,128)S(1)} %pad_maximum_fusion.1), channel_id=1, source_target_pairs={{0,1},{1,0},{2,3},{3,2},{4,5},{5,4},{6,7},{7,6},{8,9},{9,8},{10,11... | collective-permute-start | bytes 36872 | tf_op jit(solution)/shard_map/ppermute | solution.py:37
  565.3 18.8 %collective-permute-start.20 = (bf16[384,384]{1,0:T(8,128)(2,1)S(1)}, bf16[384,384]{1,0:T(8,128)(2,1)}, u32[]{:S(2)}, u32[]{:S(2)}) collective-permute-start(bf16[384,384]{1,0:T(8,128)(2,1)S(1)} %dynamic-slice_convert_fusion.6), channel_id=1, source_target_pairs={{0,8},{4,12},{8,0},{12,4},{16,24},{20,28},{24,16},{28,20},{1,9},{5... | collective-permute-start | bytes 884744 | tf_op jit(solution)/shard_map/ppermute | solution.py:37
  570.4 14.9 %collective-permute-start.18 = (bf16[768,448]{0,1:T(8,128)(2,1)}, bf16[768,448]{0,1:T(8,128)(2,1)}, u32[]{:S(2)}, u32[]{:S(2)}) collective-permute-start(bf16[768,448]{0,1:T(8,128)(2,1)} %fusion.34), channel_id=1, source_target_pairs={{0,4},{4,0},{8,12},{12,8},{16,20},{20,16},{24,28},{28,24},{1,5},{5... | collective-permute-start | bytes 2064392 | tf_op jit(solution)/shard_map/ppermute | solution.py:37
  572.2 10.1 %collective-permute-start.33 = (bf16[96,1536]{1,0:T(8,128)(2,1)}, bf16[96,1536]{1,0:T(8,128)(2,1)}, u32[]{:S(2)}, u32[]{:S(2)}) collective-permute-start(bf16[96,1536]{1,0:T(8,128)(2,1)} %dynamic-slice_convert_fusion.5), channel_id=1, source_target_pairs={{0,16},{4,20},{8,24},{12,28},{16,0},{20,4},{24,8},{28,12},{1,17},{... | collective-permute-start | bytes 884744 | tf_op jit(solution)/shard_map/ppermute | solution.py:37
  583.8 6.3 collective-permute-start.34
  587.6 10.3 %collective-permute-start.19 = (bf16[384,448]{0,1:T(8,128)(2,1)S(1)}, bf16[384,448]{0,1:T(8,128)(2,1)S(1)}, u32[]{:S(2)}, u32[]{:S(2)}) collective-permute-start(bf16[384,448]{0,1:T(8,128)(2,1)S(1)} %dynamic-slice_convert_fusion.4), channel_id=1, source_target_pairs={{0,16},{4,20},{8,24},{12,28},{16,0},{20,4},{24,8},{28,12},{1,17},{... | collective-permute-start | bytes 1032200 | tf_op jit(solution)/shard_map/ppermute | solution.py:37
  590.1 21.6 %copy-start.10 = (bf16[768,1024]{1,0:T(8,128)(2,1)S(1)}, bf16[768,1024]{1,0:T(8,128)(2,1)}, u32[]{:S(2)}) copy-start(bf16[768,1024]{1,0:T(8,128)(2,1)} %get-tuple-element.130) | copy-start | bytes 4718596
  590.2 9.6 %collective-permute-start.35 = (bf16[48,1536]{1,0:T(8,128)(2,1)S(1)}, bf16[48,1536]{1,0:T(8,128)(2,1)S(1)}, u32[]{:S(2)}, u32[]{:S(2)}) collective-permute-start(bf16[48,1536]{1,0:T(8,128)(2,1)S(1)} %add_convert_fusion.3), channel_id=1, source_target_pairs={{0,8},{4,12},{8,0},{12,4},{16,24},{20,28},{24,16},{28,20},{1,9},{5... | collective-permute-start | bytes 442376 | tf_op jit(solution)/shard_map/ppermute | solution.py:37
  598.1 9.3 %collective-permute-start.23 = (bf16[192,384]{1,0:T(8,128)(2,1)S(1)}, bf16[192,384]{1,0:T(8,128)(2,1)S(1)}, u32[]{:S(2)}, u32[]{:S(2)}) collective-permute-start(bf16[192,384]{1,0:T(8,128)(2,1)S(1)} %dynamic-slice_convert_fusion.9), channel_id=1, source_target_pairs={{0,16},{4,20},{8,24},{12,28},{16,0},{20,4},{24,8},{28,12},{1,17},{... | collective-permute-start | bytes 442376 | tf_op jit(solution)/shard_map/ppermute | solution.py:37
  599.8 19.9 %collective-permute-start.36 = (bf16[96,1536]{1,0:T(8,128)(2,1)S(1)}, bf16[96,1536]{1,0:T(8,128)(2,1)S(1)}, u32[]{:S(2)}, u32[]{:S(2)}) collective-permute-start(bf16[96,1536]{1,0:T(8,128)(2,1)S(1)} %maximum_select_fusion.16), channel_id=1, source_target_pairs={{0,16},{4,20},{8,24},{12,28},{16,0},{20,4},{24,8},{28,12},{1,17},{... | collective-permute-start | bytes 884744 | tf_op jit(solution)/shard_map/ppermute | solution.py:37
  600.3 7.1 %collective-permute-start.24 = (f32[2,1536]{1,0:T(2,128)S(1)}, f32[2,1536]{1,0:T(2,128)S(1)}, u32[]{:S(2)}, u32[]{:S(2)}) collective-permute-start(f32[2,1536]{1,0:T(2,128)S(1)} %fusion.93), channel_id=1, source_target_pairs={{0,2},{1,3},{2,0},{3,1},{4,6},{5,7},{6,4},{7,5},{8,10},{9,11},{10,... | collective-permute-start | bytes 36872 | tf_op jit(solution)/shard_map/ppermute | solution.py:37
  602.0 6.4 collective-permute-start.22
  608.6 6.8 %collective-permute-start.27 = (f32[2,1536]{1,0:T(2,128)S(1)}, f32[2,1536]{1,0:T(2,128)S(1)}, u32[]{:S(2)}, u32[]{:S(2)}) collective-permute-start(f32[2,1536]{1,0:T(2,128)S(1)} %add.379), channel_id=1, source_target_pairs={{0,4},{4,0},{8,12},{12,8},{16,20},{20,16},{24,28},{28,24},{1,5},{5... | collective-permute-start | bytes 36872 | tf_op jit(solution)/shard_map/ppermute | solution.py:37
  608.7 6.8 %collective-permute-start.26 = (bf16[192,384]{1,0:T(8,128)(2,1)S(1)}, bf16[192,384]{1,0:T(8,128)(2,1)S(1)}, u32[]{:S(2)}, u32[]{:S(2)}) collective-permute-start(bf16[192,384]{1,0:T(8,128)(2,1)S(1)} %convert_add_fusion.12), channel_id=1, source_target_pairs={{0,16},{4,20},{8,24},{12,28},{16,0},{20,4},{24,8},{28,12},{1,17},{... | collective-permute-start | bytes 442376 | tf_op jit(solution)/shard_map/ppermute | solution.py:37
  610.1 7.7 %collective-permute-start.25 = (bf16[192,448]{0,1:T(8,128)(2,1)S(1)}, bf16[192,448]{0,1:T(8,128)(2,1)S(1)}, u32[]{:S(2)}, u32[]{:S(2)}) collective-permute-start(bf16[192,448]{0,1:T(8,128)(2,1)S(1)} %convert_add_fusion.11), channel_id=1, source_target_pairs={{0,8},{4,12},{8,0},{12,4},{16,24},{20,28},{24,16},{28,20},{1,9},{5... | collective-permute-start | bytes 516104 | tf_op jit(solution)/shard_map/ppermute | solution.py:37
  618.0 3.8 collective-permute-start.30
  619.8 12.6 %collective-permute-start.37 = (bf16[192,1536]{1,0:T(8,128)(2,1)S(1)}, bf16[192,1536]{1,0:T(8,128)(2,1)}, u32[]{:S(2)}, u32[]{:S(2)}) collective-permute-start(bf16[192,1536]{1,0:T(8,128)(2,1)S(1)} %maximum_select_fusion.13), channel_id=1, source_target_pairs={{0,4},{4,0},{8,12},{12,8},{16,20},{20,16},{24,28},{28,24},{1,5},{5... | collective-permute-start | bytes 1769480 | tf_op jit(solution)/shard_map/ppermute | solution.py:37
  619.9 9.4 %collective-permute-start.29 = (bf16[384,384]{1,0:T(8,128)(2,1)S(1)}, bf16[384,384]{1,0:T(8,128)(2,1)S(1)}, u32[]{:S(2)}, u32[]{:S(2)}) collective-permute-start(bf16[384,384]{1,0:T(8,128)(2,1)S(1)} %maximum_select_fusion.15), channel_id=1, source_target_pairs={{0,8},{4,12},{8,0},{12,4},{16,24},{20,28},{24,16},{28,20},{1,9},{5... | collective-permute-start | bytes 884744 | tf_op jit(solution)/shard_map/ppermute | solution.py:37
  620.4 10.2 %collective-permute-start.28 = (bf16[384,448]{0,1:T(8,128)(2,1)S(1)}, bf16[384,448]{0,1:T(8,128)(2,1)}, u32[]{:S(2)}, u32[]{:S(2)}) collective-permute-start(bf16[384,448]{0,1:T(8,128)(2,1)S(1)} %maximum_select_fusion.14), channel_id=1, source_target_pairs={{0,16},{4,20},{8,24},{12,28},{16,0},{20,4},{24,8},{28,12},{1,17},{... | collective-permute-start | bytes 1032200 | tf_op jit(solution)/shard_map/ppermute | solution.py:37
  631.8 9.6 %collective-permute-start.32 = (bf16[768,448]{0,1:T(8,128)(2,1)S(1)}, bf16[768,448]{0,1:T(8,128)(2,1)S(1)}, u32[]{:S(2)}, u32[]{:S(2)}) collective-permute-start(bf16[768,448]{0,1:T(8,128)(2,1)S(1)} %maximum_select_fusion.9), channel_id=1, source_target_pairs={{0,4},{4,0},{8,12},{12,8},{16,20},{20,16},{24,28},{28,24},{1,5},{5... | collective-permute-start | bytes 2064392 | tf_op jit(solution)/shard_map/ppermute | solution.py:37
  631.9 7.8 %collective-permute-start.31 = (bf16[768,384]{1,0:T(8,128)(2,1)S(1)}, bf16[768,384]{1,0:T(8,128)(2,1)S(1)}, u32[]{:S(2)}, u32[]{:S(2)}) collective-permute-start(bf16[768,384]{1,0:T(8,128)(2,1)S(1)} %maximum_select_fusion.10), channel_id=1, source_target_pairs={{0,4},{4,0},{8,12},{12,8},{16,20},{20,16},{24,28},{28,24},{1,5},{5... | collective-permute-start | bytes 1769480 | tf_op jit(solution)/shard_map/ppermute | solution.py:37
  635.4 3.7 collective-permute-start.38
  (30 other events, 76.3 us)
Sparse Core Ops, SparseCore 0:
  13.2 66.1 all-gather.4
  81.6 62.0 all-gather.6
  146.6 63.2 reduce-scatter.4
  214.1 63.3 all-gather.8
  311.7 59.1 reduce-scatter.6
  374.6 63.3 all-gather.10
  517.6 58.7 reduce-scatter.8
  582.4 60.2 reduce-scatter.10

commit v9 on v8

--- a/solution.py
+++ b/solution.py
@@ -404,20 +404,25 @@
     )(low, slots, queries_joined, firsts, mixed, logs, cosine, sine, *grads, *arrays, *arrays)
 
 
-def gather_back_kernel(kv_heads, parts, key_ref, value_ref, cosine_ref, sine_ref, *refs):
+def gather_back_kernel(
+    kv_heads, parts, key_ref, value_ref, cosine_ref, sine_ref, share_ref, *refs
+):
     out_ref = refs[parts]
     for head in range(kv_heads):
         at = pl.ds(head * LANES, LANES)
         key = key_ref[:, at]
         value = value_ref[:, at]
         for part in range(parts):
-            key = key + refs[part][0, :, at].astype(f32)
-            value = value + refs[part][1, :, at].astype(f32)
+            share = share_ref[part : part + 1, :]
+            key = key + share * refs[part][0, :, at].astype(f32)
+            value = value + share * refs[part][1, :, at].astype(f32)
         out_ref[:, at] = turn_back(key, cosine_ref[...], sine_ref[...]).astype(bf16)
         out_ref[:, pl.ds((kv_heads + head) * LANES, LANES)] = value.astype(bf16)
 
 
-def gather_back(key_totals, value_totals, received, cosine, sine, kv_heads, stretch, block):
+def gather_back(
+    key_totals, value_totals, received, shares, cosine, sine, kv_heads, stretch, block
+):
     width = kv_heads * LANES
     own = pl.BlockSpec((block, width), lambda i: (i, 0))
     other = pl.BlockSpec((2, block, width), lambda i: (0, i, 0))
@@ -425,11 +430,12 @@
     return pl.pallas_call(
         functools.partial(gather_back_kernel, kv_heads, len(received)),
         grid=(stretch // block,),
-        in_specs=[own, own, table, table] + [other] * len(received),
+        in_specs=[own, own, table, table, pl.BlockSpec(shares.shape, lambda i: (0, 0))]
+        + [other] * len(received),
         out_specs=pl.BlockSpec((block, 2 * width), lambda i: (i, 0)),
         out_shape=jax.ShapeDtypeStruct((stretch, 2 * width), bf16),
         name="gather_back",
-    )(key_totals, value_totals, cosine, sine, *received)
+    )(key_totals, value_totals, cosine, sine, shares, *received)
 
 
 class SharedProduct:
@@ -448,14 +454,11 @@
         part = lax.dynamic_slice_in_dim(self.left, offset, self.size, 1)
         return jnp.dot(part.T, self.right, preferred_element_type=f32)
 
-    def meet(self, *others):
+    def meet(self):
         got = exchange(self.sent, self.axis, 1 << self.order[0])
-        if others:
-            got, *others = lax.optimization_barrier((got,) + others)
         self.value = self.times(0, False) + got.astype(f32)
         self.down = list(self.order[1:])
         self.up = list(reversed(self.order))
-        return others
 
     def step(self):
         if self.down:
@@ -634,12 +637,15 @@
         both_back = earlier[1] + jnp.where(odd, crossing, 0)
         both_back, crossing, attended_plain = tied((both_back, crossing, attended_plain))
         both_received = from_behind(both_back, "dp", -2)
-        received = [both_received, jnp.where(odd, 0, crossing)]
+        received = [both_received, crossing]
+        counts = [1.0, jnp.where(odd, 0.0, 1.0)]
     else:
         earlier, attended_plain = tied((earlier, attended_plain))
         received = [from_behind(earlier[d - 1], "dp", -d) for d in range(1, reach + 1)]
+        counts = [1.0] * reach
+    shares = jnp.stack([jnp.full((LANES,), count, f32) for count in counts])
     out_shared = SharedProduct(attended_plain, residual_low, "dp", crossed)
-    pair_shared.got, down_shared.got = out_shared.meet(pair_shared.got, down_shared.got)
+    out_shared.meet()
     for shared in wide:
         shared.end_up()
         shared.begin_up()
@@ -650,7 +656,7 @@
         (received, pair_shared.got, down_shared.got, out_shared.value, query_shared.value)
     )
     key_value_grad = gather_back(
-        key_own, value_own, received, cosine, sine, kv_heads, stretch, min(256, stretch)
+        key_own, value_own, received, shares, cosine, sine, kv_heads, stretch, min(256, stretch)
     )
     split = heads * LANES
     attn_normed_part = (
@@ -676,6 +682,9 @@
     kv_shared.meet()
     grad_gate, grad_up = pair_shared.finish((0, width), (width, 2 * width))
     (grad_down,) = down_shared.finish((0, out_grad.shape[1]))
+    if rounds:
+        axis, distance = rounds.pop(0)
+        gains = gains + exchange(gains, axis, distance)
     outputs = [grad_down, grad_gate, grad_up, block_output]
     for place in range(len(outputs)):
         query_shared.step()

time: 666 us -> 677 us (1.017)
  waiting for transfers between devices: 330 us -> 350 us
    ppermute x37, waiting for transfers between devices: 99 us -> 111 us  [exchange(): return lax.ppermute(value, axis, [(i, i ^ distance) for i in range(count)])]
    unnamed x97 -> x93, local copies, waits for them, and re-layouts: 15.3 us -> 14.6 us
  transfers between devices with their start and end apart: 47 -> 47, of which waited for: 24 -> 24; matrix products, arithmetic and copies ran while one was open for 22% -> 22% of each run, Pallas kernels for 4% -> 6%
where the time goes in v9:
time: 677 us; the launch traced here: 667 us
  waiting for transfers between devices  350 us (52%)
  matrix products  100 us (15%)
  other arithmetic  75.1 us (11%)
  starting transfers between devices  50.7 us (7%)
  Pallas kernels  43.2 us (6%)
  local copies, waits for them, and re-layouts  32.5 us (5%)
  between operations  15.4 us (2%)
    all_gather x4, waiting for transfers between devices, gather_rows(): return lax.all_gather(rows, 'tensor', axis=0, tiled=True)  132 us
    ppermute x37, waiting for transfers between devices, exchange(): return lax.ppermute(value, axis, [(i, i ^ distance) for i in range(count)])  111 us
    reduce_scatter x2, waiting for transfers between devices, scatter_low(): lax.psum_scatter(product.astype(bf16), 'tensor', scatter_dimension=0, til...  62.5 us
    ppermute x37, starting transfers between devices, exchange(): return lax.ppermute(value, axis, [(i, i ^ distance) for i in range(count)])  43.4 us
    ppermute x2, waiting for transfers between devices, from_behind(): lax.ppermute(value, axis, [(source, source + steps) for source in range(l...  41.4 us
    dot_general x10, matrix products, times(): return jnp.dot(part.T, self.right, preferred_element_type=f32)  33.8 us
    pallas_call x1, Pallas kernels, attend_back(): pl.pallas_call(functools.partial(attend_back_kernel, tiles, chunks, group...  18.4 us
    convert_element_type x7, other arithmetic, finish(): self.joined(self.value[:, a:b], self.got[:, a:b]).astype(f32)  17.3 us
  transfers between devices with their start and end apart: 47, of which 24 were waited for; matrix products, arithmetic and copies ran while one was open for 22% of the time, Pallas kernels for 6%

profile of v9, /device:TPU:0, one launch (start us, length us, event | category | flops | bytes accessed | tf_op | source)
XLA Modules:
  0.0 667.4 jit_solution(11022370563167343784)
XLA Ops:
  10.6 2.5 multiply_convert_fusion.4
  18.5 3.0 fusion.53
  21.5 6.4 fusion.4.weight_ref
  27.9 51.5 %all-gather.5.cloned.1.call-done.rows_ref = bf16[1024,1536]{1,0:T(8,128)(2,1)} async-done(((bf16[256,1536]{1,0:T(8,128)(2,1)}), bf16[1024,1536]{1,0:T(8,128)(2,1)}) %all-gather.5.cloned.1.call-update) | async-done | bytes 3145744 | tf_op jit(solution)/shard_map/all_gather | solution.py:508
  79.4 7.5 %project.1 = (bf16[1024,512]{1,0:T(8,128)(2,1)}, bf16[1024,512]{1,0:T(8,128)(2,1)}) custom-call(bf16[1024,1536]{1,0:T(8,128)(2,1)} %all-gather.5.cloned.1.call-done.rows_ref, bf16[1536,1024]{1,0:T(8,128)(2,1)} %fusion.4.weight_ref, f32[1024,128]{1,0:T(8,128)} %get-tuple-element.133.cosine_ref.refs_2_, f32[1024,128]{1,0:T(8,128)} %get-tuple-element.132.sine_ref.refs_3_), custom_call_target="tpu_custom_call" | custom-call | flops 3221225472 | bytes 8388608 | tf_op jit(solution)/shard_map/project/pallas_call | solution.py:100
  86.9 4.3 collective-permute-start
  91.3 21.6 %collective-permute-done.refs_0_.refs_3_.refs_5_.refs_8_ = bf16[1024,512]{1,0:T(8,128)(2,1)} collective-permute-done((bf16[1024,512]{1,0:T(8,128)(2,1)}, bf16[1024,512]{1,0:T(8,128)(2,1)}, u32[]{:S(2)}, u32[]{:S(2)}) %collective-permute-start) | collective-permute-done | bytes 1048608 | tf_op jit(solution)/shard_map/ppermute | solution.py:32
  112.9 2.3 broadcast_select_fusion
  116.5 3.5 fusion.50
  120.1 12.9 %attend.1 = (bf16[1024,512]{1,0:T(8,128)(2,1)}, f32[2,2,1,1024]{3,2,1,0:T(1,128)}) custom-call(s32[2,2]{1,0:T(2,128)} %pad_add_fusion.1.low_ref, bf16[1024,512]{1,0:T(8,128)(2,1)} %get-tuple-element.62.query_ref, s32[2,1,512]{2,1,0:T(1,128)} %bitcast.44, bf16[1024,512]{1,0:T(8,128)(2,1)} %collective-permute-done.refs_0_.refs_3_.refs_5_.refs_8_, ...), custom_call_target="tpu_custom_call" | custom-call | flops 8589934592 | bytes 8388608 | tf_op jit(solution)/shard_map/attend/pallas_call | solution.py:245
  132.9 5.2 convolution_convert_fusion.1
  138.2 5.5 all-gather.7.cloned.1.call-done
  143.7 6.9 %fusion.103 = f32[1024,1024]{1,0:T(8,128)} fusion(bf16[1024,1536]{1,0:T(8,128)(2,1)} %all-gather.7.cloned.1.call-done, bf16[1024,1536]{1,0:T(8,128)(2,1)S(1)} %copy-done), kind=kOutput, calls=%fused_computation.201 | convolution fusion | flops 3221225472 | bytes 10485760 | tf_op jit(solution)/shard_map/dot_general | solution.py:577
  150.5 59.3 %reduce-scatter.5.cloned.1.call-done = bf16[256,1536]{1,0:T(8,128)(2,1)} async-done(((bf16[1024,1536]{1,0:T(8,128)(2,1)}), bf16[256,1536]{1,0:T(8,128)(2,1)}) %reduce-scatter.5.cloned.1.call-update) | async-done | bytes 786448 | tf_op jit(solution)/shard_map/reduce_scatter | solution.py:504
  214.2 4.0 constant_dynamic-update-slice_fusion.1
  220.2 57.2 %all-gather.9.cloned.1.call-done = bf16[1024,1536]{1,0:T(8,128)(2,1)} async-done(((bf16[256,1536]{1,0:T(8,128)(2,1)}), bf16[1024,1536]{1,0:T(8,128)(2,1)}) %all-gather.9.cloned.1.call-update) | async-done | bytes 3145744 | tf_op jit(solution)/shard_map/all_gather | solution.py:508
  277.4 9.8 %fusion.104 = f32[1024,2048]{1,0:T(8,128)S(1)} fusion(bf16[1024,1536]{1,0:T(8,128)(2,1)} %all-gather.9.cloned.1.call-done, bf16[1536,2048]{1,0:T(8,128)(2,1)} %constant_dynamic-update-slice_fusion), kind=kOutput, calls=%fused_computation.202 | convolution fusion | flops 6442450944 | bytes 17825792 | tf_op jit(solution)/shard_map/dot_general | solution.py:585
  287.3 3.9 multiply_convert_fusion.2
  291.2 2.4 pad_maximum_fusion
  293.6 10.0 %convolution_convert_fusion = bf16[1024,1536]{1,0:T(8,128)(2,1)} fusion(bf16[1536,2048]{1,0:T(8,128)(2,1)} %constant_dynamic-update-slice_fusion, bf16[1024,1024]{1,0:T(8,128)(2,1)S(1)} %get-tuple-element.122, bf16[1024,1024]{1,0:T(8,128)(2,1)S(1)} %get-tuple-element.121), kind=kOutput, calls=%fused_computation.9 | convolution fusion | flops 6452412416 | bytes 13631488 | tf_op jit(solution)/shard_map/dot_general | solution.py:593
  303.6 7.8 %convolution_convert_fusion.3 = bf16[768,2048]{1,0:T(8,128)(2,1)} fusion(bf16[1024,2048]{1,0:T(8,128)(2,1)} %pad_maximum_fusion, bf16[1024,1536]{1,0:T(8,128)(2,1)} %all-gather.9.cloned.1.call-done, s32[]{:T(128)S(6)} %select_n.354), kind=kOutput, calls=%fused_computation.12 | convolution fusion | flops 3222798336 | bytes 8912900 | tf_op jit(solution)/shard_map/dot_general | solution.py:455
  311.9 5.2 convolution_convert_fusion.4
  317.6 7.2 %convert_add_fusion = f32[768,2048]{1,0:T(8,128)S(1)} fusion(bf16[768,2048]{1,0:T(8,128)(2,1)} %collective-permute-done.2, bf16[1024,2048]{1,0:T(8,128)(2,1)} %pad_maximum_fusion, bf16[1024,1536]{1,0:T(8,128)(2,1)} %all-gather.9.cloned.1.call-done, s32[]{:T(128)S(6)} %select_n.341), kind=kOutput, calls=%fused_computation.2 | convolution fusion | flops 3224371200 | bytes 15204356 | tf_op jit(solution)/shard_map/dot_general | solution.py:455
  329.0 3.3 convert_add_fusion.1
  335.7 6.4 convolution_convert_fusion.2
  342.1 11.9 %collective-permute-done.5 = bf16[256,1536]{1,0:T(8,128)(2,1)} collective-permute-done((bf16[256,1536]{1,0:T(8,128)(2,1)}, bf16[256,1536]{1,0:T(8,128)(2,1)}, u32[]{:S(2)}, u32[]{:S(2)}) %collective-permute-start.5) | collective-permute-done | bytes 786464 | tf_op jit(solution)/shard_map/ppermute | solution.py:37
  354.0 3.0 convert_add_fusion.4
  357.0 5.8 collective-permute-done.3
  362.9 4.7 convert_add_fusion.2
  367.5 3.2 reduce-scatter.7.cloned.1.call-done
  374.6 2.5 dynamic-slice_convert_fusion.1
  380.2 16.2 %collective-permute-done.6 = bf16[192,2048]{1,0:T(8,128)(2,1)} collective-permute-done((bf16[192,2048]{1,0:T(8,128)(2,1)}, bf16[192,2048]{1,0:T(8,128)(2,1)}, u32[]{:S(2)}, u32[]{:S(2)}) %collective-permute-start.6) | collective-permute-done | bytes 786464 | tf_op jit(solution)/shard_map/ppermute | solution.py:37
  396.3 2.7 add_convert_fusion.1
  402.1 3.0 fusion.49
  405.1 4.9 collective-permute-done.9
  411.1 6.3 collective-permute-done.7
  417.4 2.5 maximum_select_fusion.4
  419.9 17.9 %all-gather.11.cloned.1.call-done = bf16[1024,1536]{1,0:T(8,128)(2,1)} async-done(((bf16[256,1536]{1,0:T(8,128)(2,1)}), bf16[1024,1536]{1,0:T(8,128)(2,1)}) %all-gather.11.cloned.1.call-update) | async-done | bytes 3145744 | tf_op jit(solution)/shard_map/all_gather | solution.py:508
  439.3 5.1 convolution_convert_fusion.6.refs_4_
  444.5 29.5 %collective-permute-done.12 = bf16[384,2048]{1,0:T(8,128)(2,1)} collective-permute-done((bf16[384,2048]{1,0:T(8,128)(2,1)S(1)}, bf16[384,2048]{1,0:T(8,128)(2,1)}, u32[]{:S(2)}, u32[]{:S(2)}) %collective-permute-start.12) | collective-permute-done | bytes 1572896 | tf_op jit(solution)/shard_map/ppermute | solution.py:37
  473.9 4.2 maximum_select_fusion
  478.7 18.4 %attend_back.1 = (bf16[1024,512]{1,0:T(8,128)(2,1)}, f32[1024,256]{1,0:T(8,128)}, f32[1024,256]{1,0:T(8,128)}, bf16[2,1024,256]{2,1,0:T(8,128)(2,1)}, bf16[2,1024,256]{2,1,0:T(8,128)(2,1)}) custom-call(s32[2,2]{1,0:T(2,128)} %pad_add_fusion.1.low_ref, s32[2]{0:T(128)} %iota.46.slot_ref, bf16[1024,512]{1,0:T(8,128)(2,1)} %get-tuple-element.62.query_ref, ...), custom_call_target="tpu_custom_call" | custom-call | flops 21474836480 | bytes 16777216 | tf_op jit(solution)/shard_map/attend_back/pallas_call | solution.py:391
  497.1 13.0 %collective-permute-start.10 = (bf16[2,1024,256]{2,1,0:T(8,128)(2,1)}, bf16[2,1024,256]{2,1,0:T(8,128)(2,1)S(1)}, u32[]{:S(2)}, u32[]{:S(2)}) collective-permute-start(bf16[2,1024,256]{2,1,0:T(8,128)(2,1)} %get-tuple-element.80), channel_id=1, source_target_pairs={{0,4},{4,0},{8,12},{12,8},{16,20},{20,16},{24,28},{28,24},{1,5},{5... | collective-permute-start | bytes 3145736 | tf_op jit(solution)/shard_map/ppermute | solution.py:37
  512.4 2.5 fusion.37
  515.1 14.8 %collective-permute-done.14 = bf16[256,1536]{1,0:T(8,128)(2,1)} collective-permute-done((bf16[256,1536]{1,0:T(8,128)(2,1)}, bf16[256,1536]{1,0:T(8,128)(2,1)}, u32[]{:S(2)}, u32[]{:S(2)}) %collective-permute-start.14) | collective-permute-done | bytes 786464 | tf_op jit(solution)/shard_map/ppermute | solution.py:37
  537.8 3.3 fusion.98
  542.0 19.8 %collective-permute-done.11.refs_0_ = bf16[2,1024,256]{2,1,0:T(8,128)(2,1)S(1)} collective-permute-done((bf16[2,1024,256]{2,1,0:T(8,128)(2,1)S(1)}, bf16[2,1024,256]{2,1,0:T(8,128)(2,1)S(1)}, u32[]{:S(2)}, u32[]{:S(2)}) %collective-permute-start.11) | collective-permute-done | bytes 1048608 | tf_op jit(solution)/shard_map/ppermute | solution.py:32
  564.2 4.4 gather_back.1
  568.6 3.7 fusion.17
  572.5 3.7 multiply_reduce_fusion
  578.2 2.3 collective-permute-start.20
  582.9 3.5 fusion.97
  586.4 3.1 fusion.1
  591.4 3.5 fusion.2
  603.9 6.2 collective-permute-done.19
  614.3 2.6 collective-permute-done.24
  617.0 3.6 collective-permute-done.23
  624.6 3.7 fusion.3
  628.5 2.6 collective-permute-done.26
  635.1 2.5 convert_add_fusion.3
  637.6 3.7 collective-permute-done.30
  644.5 3.0 fusion.41
  652.3 2.7 reduce-scatter.11.cloned.1.call-done
  656.5 3.6 subtract_add_fusion
  (245 shorter events, 88.8 us)
Async XLA Ops:
  7.2 136.5 %copy-start = (bf16[1024,1536]{1,0:T(8,128)(2,1)S(1)}, bf16[1024,1536]{1,0:T(8,128)(2,1)}, u32[]{:S(2)}) copy-start(bf16[1024,1536]{1,0:T(8,128)(2,1)} %param.22) | copy-start | bytes 9437188
  7.2 72.2 %all-gather.5.cloned.1.call-start = ((), (), s32[]{:S(2)}) async-start(), calls=%async_computation.4 | async-start | bytes 3932160 | tf_op jit(solution)/shard_map/all_gather | solution.py:508
  13.1 130.6 %all-gather.7.cloned.1.call-start = ((), (), s32[]{:S(2)}) async-start(), calls=%async_computation.6 | async-start | bytes 3932160 | tf_op jit(solution)/shard_map/all_gather | solution.py:508
  13.8 195.9 %reduce-scatter.5.cloned.1.call-start = ((), (), s32[]{:S(2)}) async-start(), calls=%async_computation.5 | async-start | bytes 3932160 | tf_op jit(solution)/shard_map/reduce_scatter | solution.py:504
  13.9 101.2 %copy-start.37 = (s32[1024]{0:T(1024)}, s32[1024]{0:T(1024)S(1)}, u32[]{:S(2)}) copy-start(s32[1024]{0:T(1024)S(1)} %get-tuple-element.135) | copy-start | bytes 12292
  86.9 25.9 %collective-permute-start = (bf16[1024,512]{1,0:T(8,128)(2,1)}, bf16[1024,512]{1,0:T(8,128)(2,1)}, u32[]{:S(2)}, u32[]{:S(2)}) collective-permute-start(bf16[1024,512]{1,0:T(8,128)(2,1)} %get-tuple-element.63.refs_2_.refs_5_.refs_7_.refs_10_), channel_id=1, source_target_pairs={{0,8},{4,12},{8,16},{12,20},{16,24},{20,28},{1,9},{5,13},{9,17},{1... | collective-permute-start | bytes 3145736 | tf_op jit(solution)/shard_map/ppermute | solution.py:32
  115.2 4.9 collective-permute-start.1
  138.1 139.3 %all-gather.9.cloned.1.call-start = ((), (), s32[]{:S(2)}) async-start(), calls=%async_computation.7 | async-start | bytes 3932160 | tf_op jit(solution)/shard_map/all_gather | solution.py:508
  150.5 62.3 %copy-start.36 = (f32[1536]{0:T(1024)S(1)}, f32[1536]{0:T(1024)}, u32[]{:S(2)}) copy-start(f32[1536]{0:T(1024)} %param.19) | copy-start | bytes 18436
  213.9 156.8 %reduce-scatter.7.cloned.1.call-start = ((), (), s32[]{:S(2)}) async-start(), calls=%async_computation.8 | async-start | bytes 3932160 | tf_op jit(solution)/shard_map/reduce_scatter | solution.py:504
  277.4 9.9 %copy-start.18 = (f32[1024,1024]{1,0:T(8,128)S(1)}, f32[1024,1024]{1,0:T(8,128)}, u32[]{:S(2)}) copy-start(f32[1024,1024]{1,0:T(8,128)} %fusion.103) | copy-start | bytes 12582916
  311.4 6.2 collective-permute-start.2
  311.4 126.4 %all-gather.11.cloned.1.call-start = ((), (), s32[]{:S(2)}) async-start(), calls=%async_computation.9 | async-start | bytes 3932160 | tf_op jit(solution)/shard_map/all_gather | solution.py:508
  317.1 10.6 %collective-permute-start.4 = (bf16[512,1536]{1,0:T(8,128)(2,1)}, bf16[512,1536]{1,0:T(8,128)(2,1)}, u32[]{:S(2)}, u32[]{:S(2)}) collective-permute-start(bf16[512,1536]{1,0:T(8,128)(2,1)} %convolution_convert_fusion.4), channel_id=1, source_target_pairs={{0,4},{4,0},{8,12},{12,8},{16,20},{20,16},{24,28},{28,24},{1,5},{5... | collective-permute-start | bytes 4718600 | tf_op jit(solution)/shard_map/ppermute | solution.py:37
  317.6 10.1 %copy-start.16 = (bf16[1024,1024]{1,0:T(8,128)(2,1)S(1)}, bf16[1024,1024]{1,0:T(8,128)(2,1)}, u32[]{:S(2)}) copy-start(bf16[1024,1024]{1,0:T(8,128)(2,1)} %get-tuple-element.70) | copy-start | bytes 6291460
  324.8 7.5 %copy-start.5 = (f32[768,2048]{1,0:T(8,128)}, f32[768,2048]{1,0:T(8,128)S(1)}, u32[]{:S(2)}) copy-start(f32[768,2048]{1,0:T(8,128)S(1)} %convert_add_fusion) | copy-start | bytes 18874372
  326.2 36.6 %collective-permute-start.3 = (bf16[384,2048]{1,0:T(8,128)(2,1)}, bf16[384,2048]{1,0:T(8,128)(2,1)}, u32[]{:S(2)}, u32[]{:S(2)}) collective-permute-start(bf16[384,2048]{1,0:T(8,128)(2,1)} %dynamic-slice_convert_fusion), channel_id=1, source_target_pairs={{0,8},{4,12},{8,0},{12,4},{16,24},{20,28},{24,16},{28,20},{1,9},{5... | collective-permute-start | bytes 4718600 | tf_op jit(solution)/shard_map/ppermute | solution.py:37
  334.2 19.8 %collective-permute-start.5 = (bf16[256,1536]{1,0:T(8,128)(2,1)}, bf16[256,1536]{1,0:T(8,128)(2,1)}, u32[]{:S(2)}, u32[]{:S(2)}) collective-permute-start(bf16[256,1536]{1,0:T(8,128)(2,1)} %dynamic-slice_convert_fusion.2), channel_id=1, source_target_pairs={{0,16},{4,20},{8,24},{12,28},{16,0},{20,4},{24,8},{28,12},{1,17},{... | collective-permute-start | bytes 2359304 | tf_op jit(solution)/shard_map/ppermute | solution.py:37
  357.0 13.8 %copy-start.4 = (f32[256,1536]{1,0:T(8,128)S(1)}, f32[256,1536]{1,0:T(8,128)}, u32[]{:S(2)}) copy-start(f32[256,1536]{1,0:T(8,128)} %copy-done.3) | copy-start | bytes 4718596
  374.4 260.8 %reduce-scatter.9.cloned.1.call-start = ((), (), s32[]{:S(2)}) async-start(), calls=%async_computation.10 | async-start | bytes 3932160 | tf_op jit(solution)/shard_map/reduce_scatter | solution.py:617
  377.1 19.2 %collective-permute-start.6 = (bf16[192,2048]{1,0:T(8,128)(2,1)}, bf16[192,2048]{1,0:T(8,128)(2,1)}, u32[]{:S(2)}, u32[]{:S(2)}) collective-permute-start(bf16[192,2048]{1,0:T(8,128)(2,1)} %dynamic-slice_convert_fusion.1), channel_id=1, source_target_pairs={{0,16},{4,20},{8,24},{12,28},{16,0},{20,4},{24,8},{28,12},{1,17},{... | collective-permute-start | bytes 2359304 | tf_op jit(solution)/shard_map/ppermute | solution.py:37
  378.6 21.9 %collective-permute-start.8 = (bf16[128,1536]{1,0:T(8,128)(2,1)S(1)}, bf16[128,1536]{1,0:T(8,128)(2,1)S(1)}, u32[]{:S(2)}, u32[]{:S(2)}) collective-permute-start(bf16[128,1536]{1,0:T(8,128)(2,1)S(1)} %dynamic-slice_convert_fusion.3), channel_id=1, source_target_pairs={{0,8},{4,12},{8,0},{12,4},{16,24},{20,28},{24,16},{28,20},{1,9},{5... | collective-permute-start | bytes 1179656 | tf_op jit(solution)/shard_map/ppermute | solution.py:37
  399.0 18.3 %collective-permute-start.7 = (bf16[192,2048]{1,0:T(8,128)(2,1)}, bf16[192,2048]{1,0:T(8,128)(2,1)}, u32[]{:S(2)}, u32[]{:S(2)}) collective-permute-start(bf16[192,2048]{1,0:T(8,128)(2,1)} %add_convert_fusion.1), channel_id=1, source_target_pairs={{0,16},{4,20},{8,24},{12,28},{16,0},{20,4},{24,8},{28,12},{1,17},{... | collective-permute-start | bytes 2359304 | tf_op jit(solution)/shard_map/ppermute | solution.py:37
  400.6 9.4 %collective-permute-start.9 = (bf16[128,1536]{1,0:T(8,128)(2,1)S(1)}, bf16[128,1536]{1,0:T(8,128)(2,1)S(1)}, u32[]{:S(2)}, u32[]{:S(2)}) collective-permute-start(bf16[128,1536]{1,0:T(8,128)(2,1)S(1)} %add_convert_fusion.2), channel_id=1, source_target_pairs={{0,8},{4,12},{8,0},{12,4},{16,24},{20,28},{24,16},{28,20},{1,9},{5... | collective-permute-start | bytes 1179656 | tf_op jit(solution)/shard_map/ppermute | solution.py:37
  437.8 36.1 %collective-permute-start.12 = (bf16[384,2048]{1,0:T(8,128)(2,1)S(1)}, bf16[384,2048]{1,0:T(8,128)(2,1)}, u32[]{:S(2)}, u32[]{:S(2)}) collective-permute-start(bf16[384,2048]{1,0:T(8,128)(2,1)S(1)} %maximum_select_fusion.4), channel_id=1, source_target_pairs={{0,8},{4,12},{8,0},{12,4},{16,24},{20,28},{24,16},{28,20},{1,9},{5... | collective-permute-start | bytes 4718600 | tf_op jit(solution)/shard_map/ppermute | solution.py:37
  478.2 83.6 %collective-permute-start.13 = (bf16[768,2048]{1,0:T(8,128)(2,1)}, bf16[768,2048]{1,0:T(8,128)(2,1)}, u32[]{:S(2)}, u32[]{:S(2)}) collective-permute-start(bf16[768,2048]{1,0:T(8,128)(2,1)} %maximum_select_fusion), channel_id=1, source_target_pairs={{0,4},{4,0},{8,12},{12,8},{16,20},{20,16},{24,28},{28,24},{1,5},{5... | collective-permute-start | bytes 9437192 | tf_op jit(solution)/shard_map/ppermute | solution.py:37
  478.7 31.4 %copy-start.41 = (s32[384]{0:T(512)S(1)}, s32[384]{0:T(512)}, u32[]{:S(2)}) copy-start(s32[384]{0:T(512)} %copy-done.40) | copy-start | bytes 4612
  497.1 34.8 %collective-permute-start.10 = (bf16[2,1024,256]{2,1,0:T(8,128)(2,1)}, bf16[2,1024,256]{2,1,0:T(8,128)(2,1)S(1)}, u32[]{:S(2)}, u32[]{:S(2)}) collective-permute-start(bf16[2,1024,256]{2,1,0:T(8,128)(2,1)} %get-tuple-element.80), channel_id=1, source_target_pairs={{0,4},{4,0},{8,12},{12,8},{16,20},{20,16},{24,28},{28,24},{1,5},{5... | collective-permute-start | bytes 3145736 | tf_op jit(solution)/shard_map/ppermute | solution.py:37
  510.1 19.8 %collective-permute-start.14 = (bf16[256,1536]{1,0:T(8,128)(2,1)}, bf16[256,1536]{1,0:T(8,128)(2,1)}, u32[]{:S(2)}, u32[]{:S(2)}) collective-permute-start(bf16[256,1536]{1,0:T(8,128)(2,1)} %maximum_select_fusion.8), channel_id=1, source_target_pairs={{0,16},{4,20},{8,24},{12,28},{16,0},{20,4},{24,8},{28,12},{1,17},{... | collective-permute-start | bytes 2359304 | tf_op jit(solution)/shard_map/ppermute | solution.py:37
  510.3 144.7 %reduce-scatter.11.cloned.1.call-start = ((), (), s32[]{:S(2)}) async-start(), calls=%async_computation.11 | async-start | bytes 3932160 | tf_op jit(solution)/shard_map/reduce_scatter | solution.py:666
  512.4 17.5 %copy-start.25 = (bf16[256,1536]{1,0:T(8,128)(2,1)S(1)}, bf16[256,1536]{1,0:T(8,128)(2,1)}, u32[]{:S(2)}) copy-start(bf16[256,1536]{1,0:T(8,128)(2,1)} %maximum_select_fusion.8) | copy-start | bytes 2359300
  514.9 17.0 %copy-start.31 = (bf16[2,1024,256]{2,1,0:T(8,128)(2,1)S(1)}, bf16[2,1024,256]{2,1,0:T(8,128)(2,1)}, u32[]{:S(2)}) copy-start(bf16[2,1024,256]{2,1,0:T(8,128)(2,1)} %get-tuple-element.79) | copy-start | bytes 3145732
  514.9 20.8 %collective-permute-start.17 = (bf16[768,384]{1,0:T(8,128)(2,1)S(1)}, bf16[768,384]{1,0:T(8,128)(2,1)S(1)}, u32[]{:S(2)}, u32[]{:S(2)}) collective-permute-start(bf16[768,384]{1,0:T(8,128)(2,1)S(1)} %fusion.37), channel_id=1, source_target_pairs={{0,4},{4,0},{8,12},{12,8},{16,20},{20,16},{24,28},{28,24},{1,5},{5... | collective-permute-start | bytes 1769480 | tf_op jit(solution)/shard_map/ppermute | solution.py:37
  531.8 30.0 %collective-permute-start.15 = (bf16[512,1536]{1,0:T(8,128)(2,1)S(1)}, bf16[512,1536]{1,0:T(8,128)(2,1)S(1)}, u32[]{:S(2)}, u32[]{:S(2)}) collective-permute-start(bf16[512,1536]{1,0:T(8,128)(2,1)S(1)} %maximum_select_fusion.5), channel_id=1, source_target_pairs={{0,4},{4,0},{8,12},{12,8},{16,20},{20,16},{24,28},{28,24},{1,5},{5... | collective-permute-start | bytes 4718600 | tf_op jit(solution)/shard_map/ppermute | solution.py:37
  532.1 29.7 %collective-permute-start.11 = (bf16[2,1024,256]{2,1,0:T(8,128)(2,1)S(1)}, bf16[2,1024,256]{2,1,0:T(8,128)(2,1)S(1)}, u32[]{:S(2)}, u32[]{:S(2)}) collective-permute-start(bf16[2,1024,256]{2,1,0:T(8,128)(2,1)S(1)} %select_add_fusion), channel_id=1, source_target_pairs={{8,0},{12,4},{16,8},{20,12},{24,16},{28,20},{9,1},{13,5},{17,9},{2... | collective-permute-start | bytes 3145736 | tf_op jit(solution)/shard_map/ppermute | solution.py:32
  535.6 5.5 collective-permute-start.16
  542.0 19.8 %copy-start.19 = (f32[192,1536]{1,0:T(8,128)}, f32[192,1536]{1,0:T(8,128)S(1)}, u32[]{:S(2)}) copy-start(f32[192,1536]{1,0:T(8,128)S(1)} %convolution_add_fusion) | copy-start | bytes 3538948
  562.9 32.0 %collective-permute-start.34 = (bf16[96,1536]{1,0:T(8,128)(2,1)S(1)}, bf16[96,1536]{1,0:T(8,128)(2,1)}, u32[]{:S(2)}, u32[]{:S(2)}) collective-permute-start(bf16[96,1536]{1,0:T(8,128)(2,1)S(1)} %dynamic-slice_convert_fusion.5), channel_id=1, source_target_pairs={{0,16},{4,20},{8,24},{12,28},{16,0},{20,4},{24,8},{28,12},{1,17},{... | collective-permute-start | bytes 884744 | tf_op jit(solution)/shard_map/ppermute | solution.py:37
  572.5 7.9 %copy-start.33 = (bf16[1024,512]{1,0:T(8,128)(2,1)S(1)}, bf16[1024,512]{1,0:T(8,128)(2,1)}, u32[]{:S(2)}) copy-start(bf16[1024,512]{1,0:T(8,128)(2,1)} %gather_back.1) | copy-start | bytes 3145732
  576.3 13.3 %collective-permute-start.21 = (f32[2,1536]{1,0:T(2,128)S(1)}, f32[2,1536]{1,0:T(2,128)S(1)}, u32[]{:S(2)}, u32[]{:S(2)}) collective-permute-start(f32[2,1536]{1,0:T(2,128)S(1)} %pad_maximum_fusion.1), channel_id=1, source_target_pairs={{0,1},{1,0},{2,3},{3,2},{4,5},{5,4},{6,7},{7,6},{8,9},{9,8},{10,11... | collective-permute-start | bytes 36872 | tf_op jit(solution)/shard_map/ppermute | solution.py:37
  578.2 18.2 %collective-permute-start.20 = (bf16[384,384]{1,0:T(8,128)(2,1)}, bf16[384,384]{1,0:T(8,128)(2,1)}, u32[]{:S(2)}, u32[]{:S(2)}) collective-permute-start(bf16[384,384]{1,0:T(8,128)(2,1)} %dynamic-slice_convert_fusion.6), channel_id=1, source_target_pairs={{0,8},{4,12},{8,0},{12,4},{16,24},{20,28},{24,16},{28,20},{1,9},{5... | collective-permute-start | bytes 884744 | tf_op jit(solution)/shard_map/ppermute | solution.py:37
  582.9 14.7 %collective-permute-start.18 = (bf16[768,448]{0,1:T(8,128)(2,1)}, bf16[768,448]{0,1:T(8,128)(2,1)}, u32[]{:S(2)}, u32[]{:S(2)}) collective-permute-start(bf16[768,448]{0,1:T(8,128)(2,1)} %fusion.34), channel_id=1, source_target_pairs={{0,4},{4,0},{8,12},{12,8},{16,20},{20,16},{24,28},{28,24},{1,5},{5... | collective-permute-start | bytes 2064392 | tf_op jit(solution)/shard_map/ppermute | solution.py:37
  586.4 4.9 copy-start.12
  589.6 5.3 collective-permute-start.22
  596.3 5.9 collective-permute-start.35
  600.0 10.1 %collective-permute-start.19 = (bf16[384,448]{0,1:T(8,128)(2,1)S(1)}, bf16[384,448]{0,1:T(8,128)(2,1)S(1)}, u32[]{:S(2)}, u32[]{:S(2)}) collective-permute-start(bf16[384,448]{0,1:T(8,128)(2,1)S(1)} %dynamic-slice_convert_fusion.4), channel_id=1, source_target_pairs={{0,16},{4,20},{8,24},{12,28},{16,0},{20,4},{24,8},{28,12},{1,17},{... | collective-permute-start | bytes 1032200 | tf_op jit(solution)/shard_map/ppermute | solution.py:37
  602.2 22.4 %copy-start.9 = (bf16[768,1024]{1,0:T(8,128)(2,1)S(1)}, bf16[768,1024]{1,0:T(8,128)(2,1)}, u32[]{:S(2)}) copy-start(bf16[768,1024]{1,0:T(8,128)(2,1)} %get-tuple-element.124) | copy-start | bytes 4718596
  602.2 9.7 %collective-permute-start.36 = (bf16[48,1536]{1,0:T(8,128)(2,1)S(1)}, bf16[48,1536]{1,0:T(8,128)(2,1)S(1)}, u32[]{:S(2)}, u32[]{:S(2)}) collective-permute-start(bf16[48,1536]{1,0:T(8,128)(2,1)S(1)} %add_convert_fusion.3), channel_id=1, source_target_pairs={{0,8},{4,12},{8,0},{12,4},{16,24},{20,28},{24,16},{28,20},{1,9},{5... | collective-permute-start | bytes 442376 | tf_op jit(solution)/shard_map/ppermute | solution.py:37
  610.2 6.8 %collective-permute-start.24 = (bf16[192,384]{1,0:T(8,128)(2,1)S(1)}, bf16[192,384]{1,0:T(8,128)(2,1)S(1)}, u32[]{:S(2)}, u32[]{:S(2)}) collective-permute-start(bf16[192,384]{1,0:T(8,128)(2,1)S(1)} %dynamic-slice_convert_fusion.9), channel_id=1, source_target_pairs={{0,16},{4,20},{8,24},{12,28},{16,0},{20,4},{24,8},{28,12},{1,17},{... | collective-permute-start | bytes 442376 | tf_op jit(solution)/shard_map/ppermute | solution.py:37
  612.0 19.6 %collective-permute-start.37 = (bf16[96,1536]{1,0:T(8,128)(2,1)S(1)}, bf16[96,1536]{1,0:T(8,128)(2,1)S(1)}, u32[]{:S(2)}, u32[]{:S(2)}) collective-permute-start(bf16[96,1536]{1,0:T(8,128)(2,1)S(1)} %maximum_select_fusion.16), channel_id=1, source_target_pairs={{0,16},{4,20},{8,24},{12,28},{16,0},{20,4},{24,8},{28,12},{1,17},{... | collective-permute-start | bytes 884744 | tf_op jit(solution)/shard_map/ppermute | solution.py:37
  612.4 1.9 collective-permute-start.25
  612.5 8.1 %collective-permute-start.23 = (bf16[192,448]{0,1:T(8,128)(2,1)S(1)}, bf16[192,448]{0,1:T(8,128)(2,1)S(1)}, u32[]{:S(2)}, u32[]{:S(2)}) collective-permute-start(bf16[192,448]{0,1:T(8,128)(2,1)S(1)} %dynamic-slice_convert_fusion.7), channel_id=1, source_target_pairs={{0,8},{4,12},{8,0},{12,4},{16,24},{20,28},{24,16},{28,20},{1,9},{5... | collective-permute-start | bytes 516104 | tf_op jit(solution)/shard_map/ppermute | solution.py:37
  620.8 7.6 %collective-permute-start.28 = (f32[2,1536]{1,0:T(2,128)S(1)}, f32[2,1536]{1,0:T(2,128)S(1)}, u32[]{:S(2)}, u32[]{:S(2)}) collective-permute-start(f32[2,1536]{1,0:T(2,128)S(1)} %add.382), channel_id=1, source_target_pairs={{0,8},{4,12},{8,0},{12,4},{16,24},{20,28},{24,16},{28,20},{1,9},{5... | collective-permute-start | bytes 36872 | tf_op jit(solution)/shard_map/ppermute | solution.py:37
  622.6 5.8 collective-permute-start.27
  624.3 6.7 %collective-permute-start.26 = (bf16[192,448]{0,1:T(8,128)(2,1)S(1)}, bf16[192,448]{0,1:T(8,128)(2,1)S(1)}, u32[]{:S(2)}, u32[]{:S(2)}) collective-permute-start(bf16[192,448]{0,1:T(8,128)(2,1)S(1)} %convert_add_fusion.11), channel_id=1, source_target_pairs={{0,8},{4,12},{8,0},{12,4},{16,24},{20,28},{24,16},{28,20},{1,9},{5... | collective-permute-start | bytes 516104 | tf_op jit(solution)/shard_map/ppermute | solution.py:37
  631.3 3.8 collective-permute-start.31
  631.8 12.8 %collective-permute-start.38 = (bf16[192,1536]{1,0:T(8,128)(2,1)S(1)}, bf16[192,1536]{1,0:T(8,128)(2,1)}, u32[]{:S(2)}, u32[]{:S(2)}) collective-permute-start(bf16[192,1536]{1,0:T(8,128)(2,1)S(1)} %maximum_select_fusion.13), channel_id=1, source_target_pairs={{0,4},{4,0},{8,12},{12,8},{16,20},{20,16},{24,28},{28,24},{1,5},{5... | collective-permute-start | bytes 1769480 | tf_op jit(solution)/shard_map/ppermute | solution.py:37
  631.9 9.4 %collective-permute-start.30 = (bf16[384,384]{1,0:T(8,128)(2,1)S(1)}, bf16[384,384]{1,0:T(8,128)(2,1)S(1)}, u32[]{:S(2)}, u32[]{:S(2)}) collective-permute-start(bf16[384,384]{1,0:T(8,128)(2,1)S(1)} %maximum_select_fusion.15), channel_id=1, source_target_pairs={{0,8},{4,12},{8,0},{12,4},{16,24},{20,28},{24,16},{28,20},{1,9},{5... | collective-permute-start | bytes 884744 | tf_op jit(solution)/shard_map/ppermute | solution.py:37
  632.5 10.2 %collective-permute-start.29 = (bf16[384,448]{0,1:T(8,128)(2,1)S(1)}, bf16[384,448]{0,1:T(8,128)(2,1)}, u32[]{:S(2)}, u32[]{:S(2)}) collective-permute-start(bf16[384,448]{0,1:T(8,128)(2,1)S(1)} %maximum_select_fusion.14), channel_id=1, source_target_pairs={{0,16},{4,20},{8,24},{12,28},{16,0},{20,4},{24,8},{28,12},{1,17},{... | collective-permute-start | bytes 1032200 | tf_op jit(solution)/shard_map/ppermute | solution.py:37
  644.0 5.9 collective-permute-start.33
  644.0 4.2 collective-permute-start.32
  649.9 5.1 copy-start.2
  651.1 5.4 copy-start.39
  651.1 5.4 copy-start.43
  (28 other events, 84.3 us)
Sparse Core Ops, SparseCore 0:
  13.2 66.1 all-gather.4
  81.5 62.0 all-gather.6
  146.6 63.1 reduce-scatter.4
  214.1 63.3 all-gather.8
  311.5 59.1 reduce-scatter.6
  374.5 63.3 all-gather.10
  510.4 61.5 reduce-scatter.8
  595.0 59.9 reduce-scatter.10
